TPU v7x, 256 devices: a whole 4x4x8 slice. The times are simulated.
256 devices in a mesh: row: 32 (over x, z_hi, core), col: 8 (over y, z_lo).
Axes of the slice: x: 4, y: 4, z: 8 (z_hi: 4, z_lo: 2; z = z_hi * 2 + z_lo), core: 2. Of those that a mesh axis runs over, the one named last changes fastest.
Arguments:
- ancestor_inverse: bfloat16 [24576, 8, 3072], P('row', 'col'), may hold values from -6 to 6
- parent_panel: bfloat16 [24576, 1024], P(('row', 'col')), may hold values from -0.15625 to 0.15625
- parent_diag_inv: bfloat16 [1024, 1024], replicated, may hold values from -1.5 to 1.5, as said below
- child_panel_anc: bfloat16 [24576, 1024], P(('row', 'col')), may hold values from -0.15625 to 0.15625
- child_panel_par: bfloat16 [1024, 1024], replicated, may hold values from -0.1875 to 0.1875
- child_diag_inv: bfloat16 [1024, 1024], replicated, may hold values from -1.5 to 1.5, as said below
Outputs:
- ainv_ap: float32 [24576, 1024], P(('row', 'col'))
- ainv_pp: float32 [1024, 1024], P(('row', 'col'))
- ainv_ac: float32 [24576, 1024], P(('row', 'col'))
- ainv_pc: float32 [1024, 1024], P(('row', 'col'))
- ainv_cc: float32 [1024, 1024], P(('row', 'col'))
Inputs may be any that keep to these rules, and one draw needn't show every extreme that they name: `parent_diag_inv`: lower triangular, with diagonal entries between 0.5 and 1.5. `child_diag_inv`: lower triangular, with diagonal entries between 0.5 and 1.5.
All inputs are finite; a program needn't handle non-finite values.
Results may differ from a plain program's by a relative error of at most 0.0041.
Values may be sent and summed in bfloat16 or wider, within the bound.
No kernel may reach another device: no remote copies, remote signals or barrier semaphores. Data moves between devices by JAX's collectives and lax.ppermute only.
A program may use at most 128 MiB of HBM per device.

v0:
```python
import jax
import jax.numpy as jnp
from jax import lax
from jax.sharding import PartitionSpec as P


def contract_rows(left_side, right_side):
    return lax.dot_general(
        left_side, right_side, (((0,), (0,)), ((), ())), preferred_element_type=jnp.float32
    )


def shards(
    ancestor_inverse,
    parent_panel,
    parent_diag_inv,
    child_panel_anc,
    child_panel_par,
    child_diag_inv,
):
    local_rows = ancestor_inverse.shape[0]
    local_block = ancestor_inverse.reshape(local_rows, -1)
    columns = parent_panel.shape[1]

    def add_panel(pieces):
        return jnp.dot(local_block, pieces, preferred_element_type=jnp.float32)

    pieces = (
        lax.all_gather(parent_panel, "row", axis=0, tiled=True),
        lax.all_gather(child_panel_anc, "row", axis=0, tiled=True),
    )
    partial_upper = add_panel(pieces[0])
    partial_lower = add_panel(pieces[1])
    upper_prod, lower_first = (
        lax.psum_scatter(partial_upper, "col", scatter_dimension=0, tiled=True),
        lax.psum_scatter(partial_lower, "col", scatter_dimension=0, tiled=True),
    )
    upper_round = upper_prod.astype(jnp.bfloat16)
    shifted = jnp.dot(upper_round, child_panel_par, preferred_element_type=jnp.float32)
    shifted_round = shifted.astype(jnp.bfloat16)
    lower_prod_anc = lower_first - shifted
    anc_round = lower_prod_anc.astype(jnp.bfloat16)
    mixed_round = jnp.dot(parent_panel, child_panel_par, preferred_element_type=jnp.float32).astype(
        jnp.bfloat16
    )
    diag_prod = jnp.dot(
        parent_diag_inv, child_panel_par, preferred_element_type=jnp.float32
    ).astype(jnp.bfloat16)
    devices = lax.axis_size("row") * lax.axis_size("col")
    my_rows = columns // devices
    position = lax.axis_index("row") * lax.axis_size("col") + lax.axis_index("col")
    first_row = position * my_rows
    parent_cols = lax.dynamic_slice_in_dim(parent_diag_inv, first_row, my_rows, 1)
    diag_upper = contract_rows(parent_cols, parent_diag_inv)
    child_cols = lax.dynamic_slice_in_dim(child_diag_inv, first_row, my_rows, 1)
    prod_cols = lax.dynamic_slice_in_dim(diag_prod, first_row, my_rows, 1)
    diag_lower = contract_rows(child_cols, child_diag_inv) + contract_rows(prod_cols, diag_prod)
    from_anc = contract_rows(child_panel_anc, anc_round)
    from_mixed = contract_rows(mixed_round, shifted_round)
    from_shift = contract_rows(shifted_round, child_panel_anc)
    joined_sum = lax.psum_scatter(
        jnp.concatenate(
            [
                contract_rows(parent_panel, upper_round),
                contract_rows(upper_round, child_panel_anc),
                from_anc + from_mixed - from_shift,
            ],
            axis=1,
        ),
        ("row", "col"),
        scatter_dimension=0,
        tiled=True,
    )
    upper_sum = joined_sum[:, :columns]
    cross_sum = joined_sum[:, columns : 2 * columns]
    lower_sum = joined_sum[:, 2 * columns :]
    ainv_pp = diag_upper + upper_sum
    pp_round = ainv_pp.astype(jnp.bfloat16)
    lower_prod_par = (
        jnp.dot(pp_round, child_panel_par, preferred_element_type=jnp.float32) - cross_sum
    )
    ainv_cc = diag_lower + lower_sum
    return (-upper_prod, ainv_pp, -lower_prod_anc, -lower_prod_par, ainv_cc)


def solution(mesh):
    placed = (
        P("row", "col", None),
        P(("row", "col"), None),
        P(),
        P(("row", "col"), None),
        P(),
        P(),
    )
    return jax.shard_map(
        shards,
        mesh=mesh,
        in_specs=placed,
        out_specs=(
            P(("row", "col"), None),
            P(("row", "col"), None),
            P(("row", "col"), None),
            P(("row", "col"), None),
            P(("row", "col"), None),
        ),
        check_vma=False,
    )
```

profile of v0, /device:TPU:1, one launch (start us, length us, event | category | flops | bytes accessed | tf_op | source)
XLA Modules:
  0.0 633.2 jit_solution(10543304892223463329)
XLA Ops:
  7.2 0.0 copy-start
  7.2 0.0 all-gather.3.cloned.1.call-start
  7.2 0.7 all-gather.3.cloned.1.call-update
  7.9 0.0 all-gather.5.cloned.1.call-start
  8.0 0.7 all-gather.5.cloned.1.call-update
  8.7 0.0 reduce-scatter.3.cloned.1.call-start
  8.7 75.0 %all-gather.3.cloned.1.call-done = bf16[3072,1024]{1,0:T(8,128)(2,1)} async-done(((bf16[96,1024]{1,0:T(8,128)(2,1)}), bf16[3072,1024]{1,0:T(8,128)(2,1)}) %all-gather.3.cloned.1.call-update) | async-done | bytes 6291472 | tf_op jit(solution)/shard_map/all_gather | solution.py:29
  83.7 9.7 %fusion.2 = f32[768,1024]{1,0:T(8,128)} fusion(bf16[3072,1024]{1,0:T(8,128)(2,1)} %all-gather.3.cloned.1.call-done, bf16[768,1,3072]{2,0,1:T(8,128)(2,1)} %param.6), kind=kOutput, calls=%fused_computation.3 | convolution fusion | flops 4831838208 | bytes 14155776 | tf_op jit(solution)/shard_map/dot_general | solution.py:26
  93.5 0.0 reduce-scatter.3.cloned.1.call-update
  93.5 0.0 reduce-scatter.5.cloned.1.call-start
  93.5 59.7 %all-gather.5.cloned.1.call-done = bf16[3072,1024]{1,0:T(8,128)(2,1)} async-done(((bf16[96,1024]{1,0:T(8,128)(2,1)}), bf16[3072,1024]{1,0:T(8,128)(2,1)}) %all-gather.5.cloned.1.call-update) | async-done | bytes 6291472 | tf_op jit(solution)/shard_map/all_gather | solution.py:30
  153.3 9.7 %fusion = f32[768,1024]{1,0:T(8,128)} fusion(bf16[3072,1024]{1,0:T(8,128)(2,1)} %all-gather.5.cloned.1.call-done, bf16[768,1,3072]{2,0,1:T(8,128)(2,1)} %param.6), kind=kOutput, calls=%fused_computation.1 | convolution fusion | flops 4831838208 | bytes 14155776 | tf_op jit(solution)/shard_map/dot_general | solution.py:26
  163.0 0.0 copy-start.4
  163.0 0.0 reduce-scatter.5.cloned.1.call-update
  163.0 0.0 copy-start.6
  163.0 0.2 all-reduce.3.cloned.1.call-start
  163.2 64.5 %reduce-scatter.3.cloned.1.call-done = f32[96,1024]{1,0:T(8,128)} async-done(((f32[768,1024]{1,0:T(8,128)}), f32[96,1024]{1,0:T(8,128)}) %reduce-scatter.3.cloned.1.call-update) | async-done | bytes 393232 | tf_op jit(solution)/shard_map/reduce_scatter | solution.py:35
  227.8 76.5 %reduce-scatter.5.cloned.1.call-done = f32[96,1024]{1,0:T(8,128)} async-done(((f32[768,1024]{1,0:T(8,128)}), f32[96,1024]{1,0:T(8,128)}) %reduce-scatter.5.cloned.1.call-update) | async-done | bytes 393232 | tf_op jit(solution)/shard_map/reduce_scatter | solution.py:36
  304.3 0.0 copy-done
  304.3 2.3 subtract_negate_fusion
  306.6 0.0 copy-done.4
  306.6 2.7 fusion.13
  309.3 0.0 copy-done.6
  309.3 0.0 copy-start.3
  309.3 3.0 fusion.5
  312.3 0.0 copy-done.3
  312.3 0.0 copy-start.1
  312.4 0.0 copy-start.2
  312.4 0.0 copy-start.7
  312.4 0.7 convolution_bitcast_fusion
  313.1 0.8 fusion.23
  313.9 0.7 copy-done.1
  314.5 1.3 copy-done.2
  315.8 0.0 copy-done.7
  315.8 0.9 fusion.4
  316.7 5.6 pad_maximum_fusion
  322.3 12.6 %copy.16 = f32[1024,3072]{1,0:T(8,128)} copy(f32[1024,3072]{0,1:T(8,128)} %pad_maximum_fusion) | data formatting | bytes 25165824 | tf_op jit(solution)/shard_map/concatenate | solution.py:62
  335.0 0.0 all-reduce.3.cloned.1.call-update
  335.0 2.2 fusion.8
  337.2 5.4 convolution_convert_fusion
  342.5 0.8 neg.9
  343.3 277.3 %all-reduce.3.cloned.1.call-done = f32[1024,3072]{1,0:T(8,128)} async-done(((f32[1024,3072]{1,0:T(8,128)}), f32[1024,3072]{1,0:T(8,128)}) %all-reduce.3.cloned.1.call-update) | async-done | bytes 12582928
  620.6 0.0 copy-start.5
  620.6 2.2 convolution_add_fusion.1
  622.8 0.0 copy-start.8
  622.8 1.8 fusion.7
  624.6 0.0 copy-done.5
  624.6 2.0 fusion.6
  626.6 0.0 copy-done.8
Async XLA Ops:
  7.2 297.1 %copy-start = (bf16[1024,1024]{1,0:T(8,128)(2,1)S(1)}, bf16[1024,1024]{1,0:T(8,128)(2,1)}, u32[]{:S(2)}) copy-start(bf16[1024,1024]{1,0:T(8,128)(2,1)} %param.10) | copy-start | bytes 6291460
  7.2 76.6 %all-gather.3.cloned.1.call-start = ((), (), s32[]{:S(2)}) async-start(), calls=%async_computation.2 | async-start | bytes 6488064 | tf_op jit(solution)/shard_map/all_gather | solution.py:29
  7.9 145.3 %all-gather.5.cloned.1.call-start = ((), (), s32[]{:S(2)}) async-start(), calls=%async_computation.4 | async-start | bytes 6488064 | tf_op jit(solution)/shard_map/all_gather | solution.py:30
  8.7 219.1 %reduce-scatter.3.cloned.1.call-start = ((), (), s32[]{:S(2)}) async-start(), calls=%async_computation.3 | async-start | bytes 3538944 | tf_op jit(solution)/shard_map/reduce_scatter | solution.py:35
  93.5 210.8 %reduce-scatter.5.cloned.1.call-start = ((), (), s32[]{:S(2)}) async-start(), calls=%async_computation.5 | async-start | bytes 3538944 | tf_op jit(solution)/shard_map/reduce_scatter | solution.py:36
  163.0 143.7 %copy-start.4 = (bf16[96,1024]{1,0:T(8,128)(2,1)S(1)}, bf16[96,1024]{1,0:T(8,128)(2,1)}, u32[]{:S(2)}) copy-start(bf16[96,1024]{1,0:T(8,128)(2,1)} %param.9) | copy-start | bytes 589828
  163.0 146.4 %copy-start.6 = (bf16[96,1024]{1,0:T(8,128)(2,1)S(1)}, bf16[96,1024]{1,0:T(8,128)(2,1)}, u32[]{:S(2)}) copy-start(bf16[96,1024]{1,0:T(8,128)(2,1)} %param.7) | copy-start | bytes 589828
  163.0 457.6 %all-reduce.3.cloned.1.call-start = ((), (), s32[]{:S(2)}) async-start(), calls=%async_computation.6 | async-start | bytes 25165824
  309.3 3.0 copy-start.3
  312.3 2.2 copy-start.1
  312.4 3.5 copy-start.2
  312.4 3.5 copy-start.7
  620.6 4.0 copy-start.5
  622.8 3.8 copy-start.8
Sparse Core Ops, SparseCore 0:
  10.6 73.1 all-gather.2
  86.3 66.9 all-gather.4
  155.8 71.9 reduce-scatter.2
  230.2 74.0 reduce-scatter.4
  335.1 285.4 all-reduce.2
where the time goes:
time: 635 us; the launch traced here: 633 us
  waiting for transfers between devices  555 us (87%)
  matrix products  43.4 us (7%)
  local copies, waits for them, and re-layouts  14.6 us (2%)
  between operations  13.8 us (2%)
  other arithmetic  6.41 us (1%)
    unnamed x6, waiting for transfers between devices  279 us
    reduce_scatter x1, waiting for transfers between devices, shards(): lax.psum_scatter(partial_lower, 'col', scatter_dimension=0, tiled=True)  76.5 us
    all_gather x1, waiting for transfers between devices, shards(): lax.all_gather(parent_panel, 'row', axis=0, tiled=True)  75 us
    reduce_scatter x1, waiting for transfers between devices, shards(): lax.psum_scatter(partial_upper, 'col', scatter_dimension=0, tiled=True)  64.5 us
    all_gather x1, waiting for transfers between devices, shards(): lax.all_gather(child_panel_anc, 'row', axis=0, tiled=True)  59.7 us
    dot_general x2, matrix products, add_panel(): return jnp.dot(local_block, pieces, preferred_element_type=jnp.float32)  19.4 us
    dot_general x8, matrix products, contract_rows(): lax.dot_general(left_side, right_side, (((0,), (0,)), ((), ())), preferre...  14.5 us
  transfers between devices with their start and end apart: 5, of which 5 were waited for; matrix products, arithmetic and copies ran while one was open for 4% of the time, Pallas kernels for 0%

commit v1 on v0

v1 whole, which is shorter than its diff:
```python
import jax
import jax.numpy as jnp
from jax import lax
from jax.sharding import Mesh, PartitionSpec as P

ROW = ("x", "zh", "core")
COL = ("y", "zl")
ALL = ROW + COL
BF = jnp.bfloat16
F32 = jnp.float32


def dot(a, b, ca=1, cb=0):
    return lax.dot_general(a, b, (((ca,), (cb,)), ((), ())), preferred_element_type=F32)


def shards(z, pp, pdi, ca, cp, cdi):
    rows, w = pp.shape
    nr, nc = lax.axis_size(ROW), lax.axis_size(COL)
    sl = w // nr
    mine = sl // nc
    block = z.reshape(z.shape[0], -1)
    panels = lax.all_gather(jnp.concatenate([pp, ca], axis=1), ROW, axis=0, tiled=True)
    part = dot(block, panels).astype(BF).reshape(nc, rows, 2 * w)
    got = lax.all_to_all(part, COL, 0, 0, tiled=True)
    total = jnp.sum(got.astype(F32), axis=0)
    upper, lower = total[:, :w], total[:, w:]
    u = upper.astype(BF)
    shifted = dot(u, cp)
    s = shifted.astype(BF)
    anc = lower - shifted
    a = anc.astype(BF)

    x = jnp.stack([u.T, s.T, a.T]).reshape(3, nr, sl, rows).transpose(1, 0, 2, 3)
    x = lax.all_to_all(x, ROW, 0, 0, tiled=True)
    x = x.transpose(1, 2, 0, 3).reshape(3 * sl, nr * rows)
    g = dot(x, panels)
    g1t = g[:sl, :w]
    cross = g[:sl, w:]
    stp = g[sl : 2 * sl, :w]
    stc = g[sl : 2 * sl, w:]
    atc = g[2 * sl :, w:]
    t2 = dot(stp.astype(BF), cp) + atc
    t = jnp.stack([g1t, t2]).reshape(2, sl, nr, sl).transpose(2, 0, 3, 1)
    t = lax.all_to_all(t, ROW, 0, 0, tiled=True)
    t = t.transpose(1, 2, 0, 3).reshape(2, sl, w)
    f = jnp.stack([t[0], cross, t[1] - stc]).reshape(3, nc, mine, w).transpose(1, 0, 2, 3)
    f = lax.all_to_all(f, COL, 0, 0, tiled=True)
    f = jnp.sum(f, axis=0)

    diag_prod = dot(pdi, cp).astype(BF)
    first = (lax.axis_index(ROW) * nc + lax.axis_index(COL)) * mine
    cols = lambda m: lax.dynamic_slice_in_dim(m, first, mine, 1)
    pp_out = dot(cols(pdi), pdi, 0, 0) + f[0]
    pc = f[1] - dot(pp_out.astype(BF), cp)
    cc = dot(cols(cdi), cdi, 0, 0) + dot(cols(diag_prod), diag_prod, 0, 0) + f[2]
    return -upper, pp_out, -anc, pc, cc


def solution(mesh):
    fine = Mesh(mesh.devices.reshape(4, 4, 2, 4, 2), ALL)
    out = P(ALL, None)
    return jax.shard_map(
        shards,
        mesh=fine,
        in_specs=(P(ROW, COL, None), out, P(), out, P(), P()),
        out_specs=(out,) * 5,
        check_vma=False,
    )
```

time: 635 us -> 266 us (0.42)
  waiting for transfers between devices: 555 us -> 113 us
  blocking collectives: 0 us -> 79.2 us
  matrix products: 43.4 us -> 33.3 us
  starting transfers between devices: 0.38 us -> 8.97 us
    unnamed x6 -> x1, waiting for transfers between devices: 279 us -> 0.02 us
    reduce_scatter x2 -> x0, waiting for transfers between devices: 141 us -> none  [the longest x1 76.5 us: shards(): lax.psum_scatter(partial_lower, 'col', scatter_dimension=0, tiled=True)]
    all_to_all x0 -> x2, blocking collectives: none -> 79.2 us  [the longest x1 47.8 us: shards(): got = lax.all_to_all(part, COL, 0, 0, tiled=True)]
    all_gather x2 -> x1, waiting for transfers between devices: 135 us -> 98.4 us  [shards(): lax.all_gather(jnp.concatenate([pp, ca], axis=1), ROW, axis=0, tiled=True)]
    all_to_all x0 -> x2, waiting for transfers between devices: none -> 15 us  [the longest x1 12.9 us: shards(): t = lax.all_to_all(t, ROW, 0, 0, tiled=True)]
    concatenate x1 -> x0, local copies, waits for them, and re-layouts: 12.6 us -> none  [shards(): jnp.concatenate([contract_rows(parent_panel, upper_round), contract_rows(...]
    dot_general x13 -> x9, matrix products: 43.4 us -> 33.3 us  [dot(): lax.dot_general(a, b, (((ca,), (cb,)), ((), ())), preferred_element_type=...]
    all_to_all x0 -> x2, starting transfers between devices: none -> 8.94 us  [the longest x1 5.48 us: shards(): t = lax.all_to_all(t, ROW, 0, 0, tiled=True)]
  transfers between devices with their start and end apart: 5 -> 3, of which waited for: 5 -> 3; matrix products, arithmetic and copies ran while one was open for 4% -> 2% of each run, Pallas kernels for 0% -> 0%
where the time goes in v1:
time: 266 us; the launch traced here: 265 us
  waiting for transfers between devices  113 us (42%)
  blocking collectives  79.2 us (30%)
  matrix products  33.3 us (13%)
  between operations  14.3 us (5%)
  local copies, waits for them, and re-layouts  9.7 us (4%)
  starting transfers between devices  8.97 us (3%)
  other arithmetic  6.4 us (2%)
    all_gather x1, waiting for transfers between devices, shards(): lax.all_gather(jnp.concatenate([pp, ca], axis=1), ROW, axis=0, tiled=True)  98.4 us
    all_to_all x1, blocking collectives, shards(): got = lax.all_to_all(part, COL, 0, 0, tiled=True)  47.8 us
    dot_general x9, matrix products, dot(): lax.dot_general(a, b, (((ca,), (cb,)), ((), ())), preferred_element_type=...  33.3 us
    all_to_all x1, blocking collectives, shards(): x = lax.all_to_all(x, ROW, 0, 0, tiled=True)  31.4 us
    all_to_all x1, waiting for transfers between devices, shards(): t = lax.all_to_all(t, ROW, 0, 0, tiled=True)  12.9 us
    all_to_all x1, starting transfers between devices, shards(): t = lax.all_to_all(t, ROW, 0, 0, tiled=True)  5.48 us
  transfers between devices with their start and end apart: 3, of which 3 were waited for; matrix products, arithmetic and copies ran while one was open for 2% of the time, Pallas kernels for 0%

profile of v1, /device:TPU:1, one launch (start us, length us, event | category | flops | bytes accessed | tf_op | source)
XLA Modules:
  0.0 265.3 jit_solution(7984998674487563898)
XLA Ops:
  7.2 0.0 copy-start
  7.2 0.0 all-gather.2.cloned.1.call-start
  7.2 1.9 pad_maximum_fusion
  9.2 0.0 all-gather.2.cloned.1.call-update
  9.2 98.4 %all-gather.2.cloned.1.call-done = bf16[3072,2048]{1,0:T(8,128)(2,1)} async-done(((bf16[96,2048]{1,0:T(8,128)(2,1)}), bf16[3072,2048]{1,0:T(8,128)(2,1)}) %all-gather.2.cloned.1.call-update) | async-done | bytes 12582928 | tf_op jit(solution)/shard_map/all_gather | solution.py:23
  107.6 14.3 %fusion.2 = bf16[2048,768]{0,1:T(8,128)(2,1)S(1)} fusion(bf16[3072,2048]{1,0:T(8,128)(2,1)} %all-gather.2.cloned.1.call-done, bf16[768,1,3072]{2,0,1:T(8,128)(2,1)} %param.6), kind=kOutput, calls=%fused_computation.3 | convolution fusion | flops 9665249280 | bytes 20447232 | tf_op jit(solution)/shard_map/dot_general | solution.py:14
  121.8 47.8 %all_to_all.20 = bf16[8,96,2048]{2,1,0:T(8,128)(2,1)S(1)} all-to-all(bf16[8,96,2048]{2,1,0:T(8,128)(2,1)S(1)} %bitcast.57), channel_id=1, replica_groups=mesh['x'=4,'zh'=4,'core'=2,'y'=4,'zl'=2] {'y','zl'}, dimensions={0} | all-to-all | bytes 6291456 | tf_op jit(solution)/shard_map/all_to_all | solution.py:25
  169.7 0.6 convert_reduce_fusion
  170.3 0.0 copy-done
  170.3 1.3 fusion.9
  171.5 0.2 copy.30
  171.7 0.2 copy.31
  171.9 0.2 copy.29
  172.1 0.2 maximum_bitcast_fusion.1
  172.3 0.1 copy.32
  172.3 31.4 %all_to_all.21 = bf16[32,3,32,96]{3,2,1,0:T(8,128)(2,1)S(1)} all-to-all(bf16[32,3,32,96]{3,2,1,0:T(8,128)(2,1)S(1)} %copy.32), channel_id=1, replica_groups=mesh['x'=4,'zh'=4,'core'=2,'y'=4,'zl'=2] {'x','zh','core'}, dimensions={0} | all-to-all | bytes 1179648 | tf_op jit(solution)/shard_map/all_to_all | solution.py:35
  203.7 0.3 copy.33
  204.1 1.1 reshape.44
  205.1 6.7 %fusion.19 = f32[96,2048]{1,0:T(8,128)S(1)} fusion(bf16[96,3072]{1,0:T(8,128)(2,1)S(1)} %reshape.44, bf16[3072,2048]{1,0:T(8,128)(2,1)} %all-gather.2.cloned.1.call-done), kind=kOutput, calls=%fused_computation.37 | convolution fusion | flops 1207959552 | bytes 13959168 | tf_op jit(solution)/shard_map/dot_general | solution.py:14
  211.8 0.0 copy-start.1
  211.8 0.9 copy-done.1
  212.7 0.5 convolution_add_fusion
  213.1 1.0 copy.39
  214.2 1.0 copy.40
  215.2 1.3 maximum_bitcast_fusion
  216.5 1.1 reshape.45
  217.6 5.5 %all-to-all-start.2 = ((f32[32,1,2048]{2,1,0:T(1,128)}), f32[32,1,2048]{2,1,0:T(1,128)S(1)}, u32[]{:S(2)}, u32[]{:S(2)}) async-start(f32[32,1,2048]{2,1,0:T(1,128)} %reshape.45), calls=%async_computation.2 | async-start | bytes 524288 | tf_op jit(solution)/shard_map/all_to_all | solution.py:45
  223.1 12.9 %all-to-all-done.2 = f32[32,1,2048]{2,1,0:T(1,128)S(1)} async-done(((f32[32,1,2048]{2,1,0:T(1,128)}), f32[32,1,2048]{2,1,0:T(1,128)S(1)}, u32[]{:S(2)}, u32[]{:S(2)}) %all-to-all-start.2) | async-done | bytes 262176 | tf_op jit(solution)/shard_map/all_to_all | solution.py:45
  236.0 0.5 broadcast
  236.5 1.3 reduce
  237.8 0.3 reshape.46
  238.1 0.9 fusion.17
  239.0 0.0 copy-start.4
  239.0 0.3 copy.37
  239.3 0.2 squeeze.12
  239.6 1.0 fusion.18
  240.7 0.0 copy-done.4
  240.7 0.3 copy.36
  241.0 0.3 stack.39
  241.3 0.1 maximum_bitcast_fusion.2
  241.4 0.8 copy.38
  242.1 3.5 %all-to-all-start.3 = ((f32[8,3,4,1024]{3,2,1,0:T(4,128)}), f32[8,3,4,1024]{3,2,1,0:T(4,128)S(1)}, u32[]{:S(2)}, u32[]{:S(2)}) async-start(f32[8,3,4,1024]{3,2,1,0:T(4,128)} %copy.38), calls=%async_computation.3 | async-start | bytes 786432 | tf_op jit(solution)/shard_map/all_to_all | solution.py:48
  245.6 0.0 copy-start.2
  245.6 2.3 fusion.6
  247.9 0.0 copy-done.2
  247.9 3.7 %convolution_convert_fusion = bf16[1024,1024]{0,1:T(8,128)(2,1)} fusion(bf16[1024,1024]{1,0:T(8,128)(2,1)S(1)} %copy-done.2, bf16[1024,1024]{1,0:T(8,128)(2,1)S(1)} %copy-done), kind=kOutput, calls=%fused_computation.4 | convolution fusion | flops 2148532224 | bytes 6291456 | tf_op jit(solution)/shard_map/dot_general | solution.py:14
  251.7 2.1 all-to-all-done.3
  253.8 0.1 reduce_sum.19
  253.9 0.0 copy-start.3
  253.9 2.3 convolution_add_fusion.2
  256.2 0.0 copy-start.5
  256.2 1.0 convolution_subtract_fusion
  257.2 0.0 copy-done.3
  257.2 1.3 fusion.5
  258.5 0.0 copy-done.5
  (4 shorter events, 0.1 us)
Async XLA Ops:
  7.2 163.1 %copy-start = (bf16[1024,1024]{1,0:T(8,128)(2,1)S(1)}, bf16[1024,1024]{1,0:T(8,128)(2,1)}, u32[]{:S(2)}) copy-start(bf16[1024,1024]{1,0:T(8,128)(2,1)} %param.10) | copy-start | bytes 6291460
  7.2 100.4 %all-gather.2.cloned.1.call-start = ((), (), s32[]{:S(2)}) async-start(), calls=%async_computation.4 | async-start | bytes 12976128 | tf_op jit(solution)/shard_map/all_gather | solution.py:23
  211.8 0.9 copy-start.1
  217.6 18.4 %all-to-all-start.2 = ((f32[32,1,2048]{2,1,0:T(1,128)}), f32[32,1,2048]{2,1,0:T(1,128)S(1)}, u32[]{:S(2)}, u32[]{:S(2)}) async-start(f32[32,1,2048]{2,1,0:T(1,128)} %reshape.45), calls=%async_computation.2 | async-start | bytes 524288 | tf_op jit(solution)/shard_map/all_to_all | solution.py:45
  239.0 1.6 copy-start.4
  242.1 11.7 %all-to-all-start.3 = ((f32[8,3,4,1024]{3,2,1,0:T(4,128)}), f32[8,3,4,1024]{3,2,1,0:T(4,128)S(1)}, u32[]{:S(2)}, u32[]{:S(2)}) async-start(f32[8,3,4,1024]{3,2,1,0:T(4,128)} %copy.38), calls=%async_computation.3 | async-start | bytes 786432 | tf_op jit(solution)/shard_map/all_to_all | solution.py:48
  245.6 2.3 copy-start.2
  253.9 3.3 %copy-start.3 = (bf16[1024,1024]{0,1:T(8,128)(2,1)S(1)}, bf16[1024,1024]{0,1:T(8,128)(2,1)}, u32[]{:S(2)}) copy-start(bf16[1024,1024]{0,1:T(8,128)(2,1)} %convolution_convert_fusion) | copy-start | bytes 6291460
  256.2 2.3 copy-start.5
Sparse Core Ops, SparseCore 0:
  11.1 96.4 all-gather.1

commit v2 on v1

--- a/solution.py
+++ b/solution.py
@@ -1,6 +1,8 @@
 import jax
 import jax.numpy as jnp
 from jax import lax
+from jax.experimental import pallas as pl
+from jax.experimental.pallas import tpu as pltpu
 from jax.sharding import Mesh, PartitionSpec as P
 
 ROW = ("x", "zh", "core")
@@ -8,10 +10,109 @@
 ALL = ROW + COL
 BF = jnp.bfloat16
 F32 = jnp.float32
+RING = (0, 1, 3, 2)
 
 
 def dot(a, b, ca=1, cb=0):
     return lax.dot_general(a, b, (((ca,), (cb,)), ((), ())), preferred_element_type=F32)
+
+
+def shift(a, axis, by):
+    n = lax.axis_size(axis)
+    return lax.ppermute(a, axis, [(i, (i + by) % n) for i in range(n)])
+
+
+def swap(a):
+    return shift(a, "core", 1)
+
+
+def ring(a, axis, direct=False):
+    after = shift(a, axis, -1)
+    before = shift(a, axis, 1)
+    if direct:
+        return [a, after, before, shift(a, axis, 2)]
+    half = a.shape[0] // 2
+    return [a, after, before, shift(after[:half], axis, -1), shift(before[half:], axis, 1)]
+
+
+def product_kernel(zrows, where, *refs):
+    first, second = refs[:5], refs[5:10]
+    z_own, z_other, out, panel_out, panel, sem, out_sem = refs[10:]
+    step = pl.program_id(0)
+    steps = pl.num_programs(0)
+    part1, part2 = first[3].shape[0] // 2, second[3].shape[0] // 2
+    shard = part1 + part2
+
+    def copies():
+        x, zh = where[0], where[1]
+        for pieces, rows, start in ((first, part1, 0), (second, part2, part1)):
+            for k, outer in enumerate((0, 1, 3, 2, 2)):
+                for n in range(pieces[k].shape[0] // rows):
+                    inner = RING[n + (2 if k == 4 else 0)]
+                    dx, dz = (outer, inner) if start == 0 else (inner, outer)
+                    at = lax.rem(x + dx, 4) * 4 + lax.rem(zh + dz, 4)
+                    at = pl.multiple_of(at * shard + start, 64)
+                    yield pltpu.make_async_copy(
+                        pieces[k].at[pl.ds(n * rows, rows)], panel.at[pl.ds(at, rows)], sem
+                    )
+
+    keep = pltpu.make_async_copy(panel, panel_out, out_sem)
+
+    @pl.when(step == 0)
+    def _():
+        for copy in copies():
+            copy.start()
+        pltpu.make_async_copy(panel, panel, sem).wait()
+        keep.start()
+
+    def multiply(z):
+        out[...] = jnp.dot(z[...], panel[...], preferred_element_type=F32).astype(BF).reshape(out.shape)
+
+    pl.when(step < steps // 2)(lambda: multiply(z_own))
+    pl.when(step >= steps // 2)(lambda: multiply(z_other))
+
+    @pl.when(step == steps - 1)
+    def _():
+        keep.wait()
+
+
+def product(where, first, second, z_own, z_other, rows):
+    depth, width = z_own.shape[1], first[0].shape[1]
+    steps, block = 4, 2 * z_own.shape[0] // 4
+    dests = block // rows
+    half = steps // 2
+    any_ = pl.BlockSpec(memory_space=pl.ANY)
+    return pl.pallas_call(
+        lambda *refs: product_kernel(block, *refs),
+        grid_spec=pltpu.PrefetchScalarGridSpec(
+            num_scalar_prefetch=1,
+            grid=(steps,),
+            in_specs=[any_] * 10
+            + [
+                pl.BlockSpec((block, depth), lambda i, w: (jnp.minimum(i, half - 1), 0)),
+                pl.BlockSpec((block, depth), lambda i, w: (jnp.maximum(i - half, 0), 0)),
+            ],
+            out_specs=[
+                pl.BlockSpec((dests, rows, width), lambda i, w: (lax.rem(i + w[2] * half, steps), 0, 0)),
+                any_,
+            ],
+            scratch_shapes=[
+                pltpu.VMEM((depth, width), BF),
+                pltpu.SemaphoreType.DMA(()),
+                pltpu.SemaphoreType.DMA(()),
+            ],
+        ),
+        out_shape=[
+            jax.ShapeDtypeStruct((steps * dests, rows, width), BF),
+            jax.ShapeDtypeStruct((depth, width), BF),
+        ],
+        compiler_params=pltpu.CompilerParams(vmem_limit_bytes=56 << 20),
+        cost_estimate=pl.CostEstimate(
+            flops=4 * z_own.shape[0] * depth * width,
+            transcendentals=0,
+            bytes_accessed=4 * z_own.size + 4 * depth * width + 4 * z_own.shape[0] * width,
+        ),
+    )(where, *first, *second, z_own, z_other)
 
 
 def shards(z, pp, pdi, ca, cp, cdi):
@@ -19,12 +120,23 @@
     nr, nc = lax.axis_size(ROW), lax.axis_size(COL)
     sl = w // nr
     mine = sl // nc
+    core = lax.axis_index("core")
+    where = jnp.stack([lax.axis_index("x"), lax.axis_index("zh"), core]).astype(jnp.int32)
     block = z.reshape(z.shape[0], -1)
-    panels = lax.all_gather(jnp.concatenate([pp, ca], axis=1), ROW, axis=0, tiled=True)
-    part = dot(block, panels).astype(BF).reshape(nc, rows, 2 * w)
-    got = lax.all_to_all(part, COL, 0, 0, tiled=True)
-    total = jnp.sum(got.astype(F32), axis=0)
-    upper, lower = total[:, :w], total[:, w:]
+
+    even = core == 0
+    got = swap(jnp.where(even, ca, pp))
+    own = jnp.where(even, pp, ca)
+    shard = jnp.concatenate([jnp.where(even, own, got), jnp.where(even, got, own)])
+    split = 2 * shard.shape[0] // 3
+    other_block = swap(block)
+    along_z = jnp.concatenate(ring(shard[:split], "zh"))
+    along_x = jnp.concatenate(ring(shard[split:], "x", direct=True))
+    part, panel = product(where, ring(along_z, "x"), ring(along_x, "zh"), block, other_block, rows)
+    other_panel = swap(panel)
+    got = lax.all_to_all(part, ("core",) + COL, 0, 0, tiled=True)
+    upper = jnp.sum(got[:nc].astype(F32), axis=0)
+    lower = jnp.sum(got[nc:].astype(F32), axis=0)
     u = upper.astype(BF)
     shifted = dot(u, cp)
     s = shifted.astype(BF)
@@ -34,12 +146,10 @@
     x = jnp.stack([u.T, s.T, a.T]).reshape(3, nr, sl, rows).transpose(1, 0, 2, 3)
     x = lax.all_to_all(x, ROW, 0, 0, tiled=True)
     x = x.transpose(1, 2, 0, 3).reshape(3 * sl, nr * rows)
-    g = dot(x, panels)
-    g1t = g[:sl, :w]
-    cross = g[:sl, w:]
-    stp = g[sl : 2 * sl, :w]
-    stc = g[sl : 2 * sl, w:]
-    atc = g[2 * sl :, w:]
+    g0, g1 = dot(x, panel), dot(x, other_panel)
+    gp, gc = jnp.where(even, g0, g1), jnp.where(even, g1, g0)
+    g1t, stp = gp[:sl], gp[sl : 2 * sl]
+    cross, stc, atc = gc[:sl], gc[sl : 2 * sl], gc[2 * sl :]
     t2 = dot(stp.astype(BF), cp) + atc
     t = jnp.stack([g1t, t2]).reshape(2, sl, nr, sl).transpose(2, 0, 3, 1)
     t = lax.all_to_all(t, ROW, 0, 0, tiled=True)

time: 266 us -> 273 us (1.026)
  blocking collectives: 79.2 us -> 29.6 us
  starting transfers between devices: 8.97 us -> 45.3 us
  waiting for transfers between devices: 113 us -> 137 us
  Pallas kernels: 0 us -> 17.4 us
  matrix products: 33.3 us -> 19.4 us
  between operations: 14.3 us -> 0.96 us
  other arithmetic: 6.4 us -> 10.8 us
    all_gather x1 -> x0, waiting for transfers between devices: 98.4 us -> none  [shards(): lax.all_gather(jnp.concatenate([pp, ca], axis=1), ROW, axis=0, tiled=True)]
    ppermute x0 -> x18, waiting for transfers between devices: none -> 83.7 us  [shift(): return lax.ppermute(a, axis, [(i, (i + by) % n) for i in range(n)])]
    all_to_all x1 -> x0, blocking collectives: 47.8 us -> none  [shards(): got = lax.all_to_all(part, COL, 0, 0, tiled=True)]
    all_to_all x0 -> x1, waiting for transfers between devices: none -> 38.2 us  [shards(): got = lax.all_to_all(part, ('core',) + COL, 0, 0, tiled=True)]
    ppermute x0 -> x18, starting transfers between devices: none -> 30.1 us  [shift(): return lax.ppermute(a, axis, [(i, (i + by) % n) for i in range(n)])]
    pallas_call x0 -> x1, Pallas kernels: none -> 17.4 us  [product(): pl.pallas_call(lambda *refs: product_kernel(block, *refs), grid_spec=pltp...]
    dot_general x9, matrix products: 33.3 us -> 19.4 us  [dot(): lax.dot_general(a, b, (((ca,), (cb,)), ((), ())), preferred_element_type=...]
    all_to_all x0 -> x1, starting transfers between devices: none -> 6.62 us  [shards(): got = lax.all_to_all(part, ('core',) + COL, 0, 0, tiled=True)]
  transfers between devices with their start and end apart: 3 -> 21, of which waited for: 3 -> 13; matrix products, arithmetic and copies ran while one was open for 2% -> 6% of each run, Pallas kernels for 0% -> 0%
where the time goes in v2:
time: 273 us; the launch traced here: 272 us
  waiting for transfers between devices  137 us (50%)
  starting transfers between devices  45.3 us (17%)
  blocking collectives  29.6 us (11%)
  matrix products  19.4 us (7%)
  Pallas kernels  17.4 us (6%)
  local copies, waits for them, and re-layouts  12.4 us (5%)
  other arithmetic  10.8 us (4%)
    ppermute x18, waiting for transfers between devices, shift(): return lax.ppermute(a, axis, [(i, (i + by) % n) for i in range(n)])  83.7 us
    all_to_all x1, waiting for transfers between devices, shards(): got = lax.all_to_all(part, ('core',) + COL, 0, 0, tiled=True)  38.2 us
    ppermute x18, starting transfers between devices, shift(): return lax.ppermute(a, axis, [(i, (i + by) % n) for i in range(n)])  30.1 us
    all_to_all x1, blocking collectives, shards(): x = lax.all_to_all(x, ROW, 0, 0, tiled=True)  29.6 us
    dot_general x9, matrix products, dot(): lax.dot_general(a, b, (((ca,), (cb,)), ((), ())), preferred_element_type=...  19.4 us
    pallas_call x1, Pallas kernels, product(): pl.pallas_call(lambda *refs: product_kernel(block, *refs), grid_spec=pltp...  17.4 us
    all_to_all x1, waiting for transfers between devices, shards(): t = lax.all_to_all(t, ROW, 0, 0, tiled=True)  12.7 us
    all_to_all x1, starting transfers between devices, shards(): got = lax.all_to_all(part, ('core',) + COL, 0, 0, tiled=True)  6.62 us
  transfers between devices with their start and end apart: 21, of which 13 were waited for; matrix products, arithmetic and copies ran while one was open for 6% of the time, Pallas kernels for 0%

profile of v2, /device:TPU:1, one launch (start us, length us, event | category | flops | bytes accessed | tf_op | source)
XLA Modules:
  0.0 272.5 jit_solution(16751477033413657514)
XLA Ops:
  0.6 3.3 %collective-permute-start.16 = (bf16[768,3072]{1,0:T(8,128)(2,1)}, bf16[768,3072]{1,0:T(8,128)(2,1)}, u32[]{:S(2)}, u32[]{:S(2)}) collective-permute-start(bf16[768,3072]{1,0:T(8,128)(2,1)} %bitcast.60), channel_id=1, source_target_pairs={{0,8},{8,0},{1,9},{9,1},{2,10},{10,2},{3,11},{11,3},{4,12},{12,4},... | collective-permute-start | bytes 14155784 | tf_op jit(solution)/shard_map/ppermute | solution.py:22
  4.0 1.0 broadcast_select_fusion.4
  4.9 0.2 collective-permute-start
  5.2 6.6 %collective-permute-done = bf16[96,1024]{1,0:T(8,128)(2,1)S(1)} collective-permute-done((bf16[96,1024]{1,0:T(8,128)(2,1)S(1)}, bf16[96,1024]{1,0:T(8,128)(2,1)S(1)}, u32[]{:S(2)}, u32[]{:S(2)}) %collective-permute-start) | collective-permute-done | bytes 196640 | tf_op jit(solution)/shard_map/ppermute | solution.py:22
  11.8 1.0 broadcast_select_fusion.3
  12.8 4.4 %collective-permute-start.1 = (bf16[128,1024]{1,0:T(8,128)(2,1)S(1)}, bf16[128,1024]{1,0:T(8,128)(2,1)S(1)}, u32[]{:S(2)}, u32[]{:S(2)}) collective-permute-start(bf16[128,1024]{1,0:T(8,128)(2,1)S(1)} %get-tuple-element.17), channel_id=1, source_target_pairs={{0,48},{16,0},{32,16},{48,32},{1,49},{17,1},{33,17},{49,33},{2,50}... | collective-permute-start | bytes 786440 | tf_op jit(solution)/shard_map/ppermute | solution.py:22
  17.2 10.2 %collective-permute-done.1 = bf16[128,1024]{1,0:T(8,128)(2,1)S(1)} collective-permute-done((bf16[128,1024]{1,0:T(8,128)(2,1)S(1)}, bf16[128,1024]{1,0:T(8,128)(2,1)S(1)}, u32[]{:S(2)}, u32[]{:S(2)}) %collective-permute-start.1) | collective-permute-done | bytes 262176 | tf_op jit(solution)/shard_map/ppermute | solution.py:22
  27.4 3.1 %collective-permute-start.3 = (bf16[64,1024]{1,0:T(8,128)(2,1)S(1)}, bf16[64,1024]{1,0:T(8,128)(2,1)S(1)}, u32[]{:S(2)}, u32[]{:S(2)}) collective-permute-start(bf16[64,1024]{1,0:T(8,128)(2,1)S(1)} %slice.83), channel_id=1, source_target_pairs={{0,48},{16,0},{32,16},{48,32},{1,49},{17,1},{33,17},{49,33},{2,50}... | collective-permute-start | bytes 393224 | tf_op jit(solution)/shard_map/ppermute | solution.py:22
  30.6 5.8 %collective-permute-done.3 = bf16[64,1024]{1,0:T(8,128)(2,1)S(1)} collective-permute-done((bf16[64,1024]{1,0:T(8,128)(2,1)S(1)}, bf16[64,1024]{1,0:T(8,128)(2,1)S(1)}, u32[]{:S(2)}, u32[]{:S(2)}) %collective-permute-start.3) | collective-permute-done | bytes 131104 | tf_op jit(solution)/shard_map/ppermute | solution.py:22
  36.6 8.2 %collective-permute-start.5 = (bf16[512,1024]{1,0:T(8,128)(2,1)S(1)}, bf16[512,1024]{1,0:T(8,128)(2,1)S(1)}, u32[]{:S(2)}, u32[]{:S(2)}) collective-permute-start(bf16[512,1024]{1,0:T(8,128)(2,1)S(1)} %constant_dynamic-update-slice_fusion.refs_1_), channel_id=1, source_target_pairs={{0,192},{64,0},{128,64},{192,128},{1,193},{65,1},{129,65},{193,129... | collective-permute-start | bytes 3145736 | tf_op jit(solution)/shard_map/ppermute | solution.py:22
  44.9 0.3 collective-permute-start.10
  45.2 3.7 %collective-permute-start.11 = (bf16[64,1024]{1,0:T(8,128)(2,1)S(1)}, bf16[64,1024]{1,0:T(8,128)(2,1)S(1)}, u32[]{:S(2)}, u32[]{:S(2)}) collective-permute-start(bf16[64,1024]{1,0:T(8,128)(2,1)S(1)} %slice.87), channel_id=1, source_target_pairs={{0,128},{64,192},{128,0},{192,64},{1,129},{65,193},{129,1},{193,65... | collective-permute-start | bytes 393224 | tf_op jit(solution)/shard_map/ppermute | solution.py:22
  48.8 24.7 %collective-permute-done.10 = bf16[64,1024]{1,0:T(8,128)(2,1)S(1)} collective-permute-done((bf16[64,1024]{1,0:T(8,128)(2,1)S(1)}, bf16[64,1024]{1,0:T(8,128)(2,1)S(1)}, u32[]{:S(2)}, u32[]{:S(2)}) %collective-permute-start.10) | collective-permute-done | bytes 131104 | tf_op jit(solution)/shard_map/ppermute | solution.py:22
  73.5 0.6 collective-permute-done.11
  74.1 3.2 %collective-permute-done.9 = bf16[64,1024]{1,0:T(8,128)(2,1)S(1)} collective-permute-done((bf16[64,1024]{1,0:T(8,128)(2,1)S(1)}, bf16[64,1024]{1,0:T(8,128)(2,1)S(1)}, u32[]{:S(2)}, u32[]{:S(2)}) %collective-permute-start.9) | collective-permute-done | bytes 131104 | tf_op jit(solution)/shard_map/ppermute | solution.py:22
  77.5 2.4 collective-permute-start.13
  79.8 1.3 collective-permute-start.7
  81.1 0.9 slice.86
  82.1 0.3 collective-permute-start.8
  82.3 26.0 %collective-permute-done.12.refs_7_ = bf16[256,1024]{1,0:T(8,128)(2,1)S(1)} collective-permute-done((bf16[256,1024]{1,0:T(8,128)(2,1)S(1)}, bf16[256,1024]{1,0:T(8,128)(2,1)S(1)}, u32[]{:S(2)}, u32[]{:S(2)}) %collective-permute-start.12) | collective-permute-done | bytes 524320 | tf_op jit(solution)/shard_map/ppermute | solution.py:22
  108.4 0.4 collective-permute-start.14
  108.8 0.8 slice.89
  109.7 2.1 collective-permute-start.15
  111.8 0.6 pad_add_fusion.refs_0_
  112.4 3.7 %collective-permute-done.14.refs_9_ = bf16[128,1024]{1,0:T(8,128)(2,1)} collective-permute-done((bf16[128,1024]{1,0:T(8,128)(2,1)S(1)}, bf16[128,1024]{1,0:T(8,128)(2,1)}, u32[]{:S(2)}, u32[]{:S(2)}) %collective-permute-start.14) | collective-permute-done | bytes 262176 | tf_op jit(solution)/shard_map/ppermute | solution.py:22
  116.1 2.7 collective-permute-done.15.refs_10_
  118.9 17.4 %shard_map.101 = (bf16[16,96,1024]{2,1,0:T(8,128)(2,1)}, bf16[3072,1024]{1,0:T(8,128)(2,1)}) custom-call(s32[3]{0:T(128)} %pad_add_fusion.refs_0_, bf16[512,1024]{1,0:T(8,128)(2,1)} %copy-done.10, bf16[512,1024]{1,0:T(8,128)(2,1)} %copy-done.5, bf16[512,1024]{1,0:T(8,128)(2,1)} %copy-done.6, bf16[256,1024]{1,0:T(8,128)(2,1)} %collective-permute-done.7.refs_4_, ...), custom_call_target="tpu_custom_call" | custom-call | flops 9663676416 | bytes 25165824 | tf_op jit(solution)/shard_map/pallas_call | solution.py:85
  136.3 6.6 %all-to-all-start = ((bf16[16,96,1024]{2,1,0:T(8,128)(2,1)}), bf16[16,96,1024]{2,1,0:T(8,128)(2,1)}, u32[]{:S(2)}, u32[]{:S(2)}) async-start(bf16[16,96,1024]{2,1,0:T(8,128)(2,1)} %get-tuple-element.7), calls=%async_computation | async-start | bytes 6291456 | tf_op jit(solution)/shard_map/all_to_all | solution.py:137
  143.0 0.2 collective-permute-start.17
  143.2 38.2 %all-to-all-done = bf16[16,96,1024]{2,1,0:T(8,128)(2,1)} async-done(((bf16[16,96,1024]{2,1,0:T(8,128)(2,1)}), bf16[16,96,1024]{2,1,0:T(8,128)(2,1)}, u32[]{:S(2)}, u32[]{:S(2)}) %all-to-all-start) | async-done | bytes 3145760 | tf_op jit(solution)/shard_map/all_to_all | solution.py:137
  181.4 2.6 convert_reduce_fusion
  183.9 0.5 fusion.4
  184.4 1.0 subtract_negate_fusion
  185.6 0.2 copy.30
  186.0 0.2 maximum_bitcast_fusion.1
  186.2 29.6 %all_to_all.20 = bf16[32,3,32,96]{3,2,1,0:T(8,128)(2,1)S(1)} all-to-all(bf16[32,3,32,96]{3,2,1,0:T(8,128)(2,1)S(1)} %copy.32), channel_id=1, replica_groups=mesh['x'=4,'zh'=4,'core'=2,'y'=4,'zl'=2] {'x','zh','core'}, dimensions={0} | all-to-all | bytes 1179648 | tf_op jit(solution)/shard_map/all_to_all | solution.py:147
  215.9 0.3 copy.33
  216.2 1.1 reshape.40
  217.2 3.9 %fusion.14 = f32[96,1024]{1,0:T(8,128)S(1)} fusion(bf16[96,3072]{1,0:T(8,128)(2,1)S(1)} %reshape.40, bf16[3072,1024]{1,0:T(8,128)(2,1)} %collective-permute-done.17), kind=kOutput, calls=%fused_computation.47 | convolution fusion | flops 603979776 | bytes 7274496 | tf_op jit(solution)/shard_map/dot_general | solution.py:17
  221.1 3.9 %broadcast_select_fusion.1 = (f32[96,1024]{1,0:T(8,128)S(1)}, f32[96,1024]{1,0:T(8,128)S(1)}) fusion(f32[96,1024]{1,0:T(8,128)S(1)} %fusion.14, pred[]{:T(512)S(6)} %eq.3, bf16[96,3072]{1,0:T(8,128)(2,1)S(1)} %reshape.40, bf16[3072,1024]{1,0:T(8,128)(2,1)} %get-tuple-element.8), kind=kOutput, calls=%fused_computation.18 | convolution fusion | flops 604176384 | bytes 8060929 | tf_op jit(solution)/shard_map/dot_general | solution.py:17
  225.1 1.0 copy.39
  226.1 0.5 slice_add_fusion
  226.6 1.0 copy.40
  227.6 1.3 maximum_bitcast_fusion
  228.9 1.2 reshape.41
  230.1 5.0 %all-to-all-start.2 = ((f32[32,1,2048]{2,1,0:T(1,128)}), f32[32,1,2048]{2,1,0:T(1,128)S(1)}, u32[]{:S(2)}, u32[]{:S(2)}) async-start(f32[32,1,2048]{2,1,0:T(1,128)} %reshape.41), calls=%async_computation.2 | async-start | bytes 524288 | tf_op jit(solution)/shard_map/all_to_all | solution.py:155
  235.1 12.7 %all-to-all-done.2 = f32[32,1,2048]{2,1,0:T(1,128)S(1)} async-done(((f32[32,1,2048]{2,1,0:T(1,128)}), f32[32,1,2048]{2,1,0:T(1,128)S(1)}, u32[]{:S(2)}, u32[]{:S(2)}) %all-to-all-start.2) | async-done | bytes 262176 | tf_op jit(solution)/shard_map/all_to_all | solution.py:155
  247.8 0.5 broadcast
  248.3 2.0 reduce
  250.3 1.3 reshape.42
  251.6 0.9 fusion.12
  252.5 0.3 copy.37
  252.8 0.9 squeeze.12
  253.7 0.9 fusion.13
  254.7 0.3 copy.36
  255.0 0.3 stack.55
  255.4 0.8 copy.38
  256.2 3.6 %all-to-all-start.3 = ((f32[8,3,4,1024]{3,2,1,0:T(4,128)}), f32[8,3,4,1024]{3,2,1,0:T(4,128)S(1)}, u32[]{:S(2)}, u32[]{:S(2)}) async-start(f32[8,3,4,1024]{3,2,1,0:T(4,128)} %copy.38), calls=%async_computation.3 | async-start | bytes 786432 | tf_op jit(solution)/shard_map/all_to_all | solution.py:158
  259.8 2.3 fusion.1
  262.1 3.7 %convolution_convert_fusion = bf16[1024,1024]{0,1:T(8,128)(2,1)} fusion(bf16[1024,1024]{1,0:T(8,128)(2,1)S(1)} %copy-done.1, bf16[1024,1024]{1,0:T(8,128)(2,1)S(1)} %copy-done), kind=kOutput, calls=%fused_computation.2 | convolution fusion | flops 2148532224 | bytes 6291456 | tf_op jit(solution)/shard_map/dot_general | solution.py:17
  265.8 2.0 all-to-all-done.3
  267.9 2.3 convolution_add_fusion.1
  270.2 1.0 convolution_subtract_fusion
  271.2 1.3 fusion
  (55 shorter events, 1.3 us)
Async XLA Ops:
  0.6 183.3 %copy-start = (bf16[1024,1024]{1,0:T(8,128)(2,1)S(1)}, bf16[1024,1024]{1,0:T(8,128)(2,1)}, u32[]{:S(2)}) copy-start(bf16[1024,1024]{1,0:T(8,128)(2,1)} %param.10) | copy-start | bytes 6291460
  0.6 118.2 %collective-permute-start.16 = (bf16[768,3072]{1,0:T(8,128)(2,1)}, bf16[768,3072]{1,0:T(8,128)(2,1)}, u32[]{:S(2)}, u32[]{:S(2)}) collective-permute-start(bf16[768,3072]{1,0:T(8,128)(2,1)} %bitcast.60), channel_id=1, source_target_pairs={{0,8},{8,0},{1,9},{9,1},{2,10},{10,2},{3,11},{11,3},{4,12},{12,4},... | collective-permute-start | bytes 14155784 | tf_op jit(solution)/shard_map/ppermute | solution.py:22
  4.9 6.9 %collective-permute-start = (bf16[96,1024]{1,0:T(8,128)(2,1)S(1)}, bf16[96,1024]{1,0:T(8,128)(2,1)S(1)}, u32[]{:S(2)}, u32[]{:S(2)}) collective-permute-start(bf16[96,1024]{1,0:T(8,128)(2,1)S(1)} %broadcast_select_fusion.4), channel_id=1, source_target_pairs={{0,8},{8,0},{1,9},{9,1},{2,10},{10,2},{3,11},{11,3},{4,12},{12,4},... | collective-permute-start | bytes 589832 | tf_op jit(solution)/shard_map/ppermute | solution.py:22
  12.8 14.6 %collective-permute-start.1 = (bf16[128,1024]{1,0:T(8,128)(2,1)S(1)}, bf16[128,1024]{1,0:T(8,128)(2,1)S(1)}, u32[]{:S(2)}, u32[]{:S(2)}) collective-permute-start(bf16[128,1024]{1,0:T(8,128)(2,1)S(1)} %get-tuple-element.17), channel_id=1, source_target_pairs={{0,48},{16,0},{32,16},{48,32},{1,49},{17,1},{33,17},{49,33},{2,50}... | collective-permute-start | bytes 786440 | tf_op jit(solution)/shard_map/ppermute | solution.py:22
  17.2 13.3 %collective-permute-start.2 = (bf16[128,1024]{1,0:T(8,128)(2,1)S(1)}, bf16[128,1024]{1,0:T(8,128)(2,1)S(1)}, u32[]{:S(2)}, u32[]{:S(2)}) collective-permute-start(bf16[128,1024]{1,0:T(8,128)(2,1)S(1)} %get-tuple-element.17), channel_id=1, source_target_pairs={{0,16},{16,32},{32,48},{48,0},{1,17},{17,33},{33,49},{49,1},{2,18}... | collective-permute-start | bytes 786440 | tf_op jit(solution)/shard_map/ppermute | solution.py:22
  27.4 9.1 %collective-permute-start.3 = (bf16[64,1024]{1,0:T(8,128)(2,1)S(1)}, bf16[64,1024]{1,0:T(8,128)(2,1)S(1)}, u32[]{:S(2)}, u32[]{:S(2)}) collective-permute-start(bf16[64,1024]{1,0:T(8,128)(2,1)S(1)} %slice.83), channel_id=1, source_target_pairs={{0,48},{16,0},{32,16},{48,32},{1,49},{17,1},{33,17},{49,33},{2,50}... | collective-permute-start | bytes 393224 | tf_op jit(solution)/shard_map/ppermute | solution.py:22
  30.5 6.1 %collective-permute-start.4 = (bf16[64,1024]{1,0:T(8,128)(2,1)S(1)}, bf16[64,1024]{1,0:T(8,128)(2,1)S(1)}, u32[]{:S(2)}, u32[]{:S(2)}) collective-permute-start(bf16[64,1024]{1,0:T(8,128)(2,1)S(1)} %slice.84), channel_id=1, source_target_pairs={{0,16},{16,32},{32,48},{48,0},{1,17},{17,33},{33,49},{49,1},{2,18}... | collective-permute-start | bytes 393224 | tf_op jit(solution)/shard_map/ppermute | solution.py:22
  36.6 72.9 %copy-start.10 = (bf16[512,1024]{1,0:T(8,128)(2,1)}, bf16[512,1024]{1,0:T(8,128)(2,1)S(1)}, u32[]{:S(2)}) copy-start(bf16[512,1024]{1,0:T(8,128)(2,1)S(1)} %constant_dynamic-update-slice_fusion.refs_1_) | copy-start | bytes 3145732
  36.6 43.2 %collective-permute-start.5 = (bf16[512,1024]{1,0:T(8,128)(2,1)S(1)}, bf16[512,1024]{1,0:T(8,128)(2,1)S(1)}, u32[]{:S(2)}, u32[]{:S(2)}) collective-permute-start(bf16[512,1024]{1,0:T(8,128)(2,1)S(1)} %constant_dynamic-update-slice_fusion.refs_1_), channel_id=1, source_target_pairs={{0,192},{64,0},{128,64},{192,128},{1,193},{65,1},{129,65},{193,129... | collective-permute-start | bytes 3145736 | tf_op jit(solution)/shard_map/ppermute | solution.py:22
  44.9 36.3 %collective-permute-start.6 = (bf16[512,1024]{1,0:T(8,128)(2,1)S(1)}, bf16[512,1024]{1,0:T(8,128)(2,1)S(1)}, u32[]{:S(2)}, u32[]{:S(2)}) collective-permute-start(bf16[512,1024]{1,0:T(8,128)(2,1)S(1)} %constant_dynamic-update-slice_fusion.refs_1_), channel_id=1, source_target_pairs={{0,64},{64,128},{128,192},{192,0},{1,65},{65,129},{129,193},{193,1... | collective-permute-start | bytes 3145736 | tf_op jit(solution)/shard_map/ppermute | solution.py:22
  44.9 28.6 %collective-permute-start.10 = (bf16[64,1024]{1,0:T(8,128)(2,1)S(1)}, bf16[64,1024]{1,0:T(8,128)(2,1)S(1)}, u32[]{:S(2)}, u32[]{:S(2)}) collective-permute-start(bf16[64,1024]{1,0:T(8,128)(2,1)S(1)} %slice.87), channel_id=1, source_target_pairs={{0,64},{64,128},{128,192},{192,0},{1,65},{65,129},{129,193},{193,1... | collective-permute-start | bytes 393224 | tf_op jit(solution)/shard_map/ppermute | solution.py:22
  45.2 29.0 %collective-permute-start.11 = (bf16[64,1024]{1,0:T(8,128)(2,1)S(1)}, bf16[64,1024]{1,0:T(8,128)(2,1)S(1)}, u32[]{:S(2)}, u32[]{:S(2)}) collective-permute-start(bf16[64,1024]{1,0:T(8,128)(2,1)S(1)} %slice.87), channel_id=1, source_target_pairs={{0,128},{64,192},{128,0},{192,64},{1,129},{65,193},{129,1},{193,65... | collective-permute-start | bytes 393224 | tf_op jit(solution)/shard_map/ppermute | solution.py:22
  73.5 3.8 %collective-permute-start.9 = (bf16[64,1024]{1,0:T(8,128)(2,1)S(1)}, bf16[64,1024]{1,0:T(8,128)(2,1)S(1)}, u32[]{:S(2)}, u32[]{:S(2)}) collective-permute-start(bf16[64,1024]{1,0:T(8,128)(2,1)S(1)} %slice.87), channel_id=1, source_target_pairs={{0,192},{64,0},{128,64},{192,128},{1,193},{65,1},{129,65},{193,129... | collective-permute-start | bytes 393224 | tf_op jit(solution)/shard_map/ppermute | solution.py:22
  77.3 41.5 %copy-start.4 = (bf16[256,1024]{1,0:T(8,128)(2,1)}, bf16[256,1024]{1,0:T(8,128)(2,1)S(1)}, u32[]{:S(2)}) copy-start(bf16[256,1024]{1,0:T(8,128)(2,1)S(1)} %pad_maximum_fusion.refs_6_) | copy-start | bytes 1572868
  77.4 31.0 %collective-permute-start.12 = (bf16[256,1024]{1,0:T(8,128)(2,1)S(1)}, bf16[256,1024]{1,0:T(8,128)(2,1)S(1)}, u32[]{:S(2)}, u32[]{:S(2)}) collective-permute-start(bf16[256,1024]{1,0:T(8,128)(2,1)S(1)} %pad_maximum_fusion.refs_6_), channel_id=1, source_target_pairs={{0,48},{16,0},{32,16},{48,32},{1,49},{17,1},{33,17},{49,33},{2,50}... | collective-permute-start | bytes 1572872 | tf_op jit(solution)/shard_map/ppermute | solution.py:22
  77.5 31.3 %collective-permute-start.13 = (bf16[256,1024]{1,0:T(8,128)(2,1)S(1)}, bf16[256,1024]{1,0:T(8,128)(2,1)S(1)}, u32[]{:S(2)}, u32[]{:S(2)}) collective-permute-start(bf16[256,1024]{1,0:T(8,128)(2,1)S(1)} %pad_maximum_fusion.refs_6_), channel_id=1, source_target_pairs={{0,16},{16,32},{32,48},{48,0},{1,17},{17,33},{33,49},{49,1},{2,18}... | collective-permute-start | bytes 1572872 | tf_op jit(solution)/shard_map/ppermute | solution.py:22
  79.8 29.0 %copy-start.5 = (bf16[512,1024]{1,0:T(8,128)(2,1)}, bf16[512,1024]{1,0:T(8,128)(2,1)S(1)}, u32[]{:S(2)}) copy-start(bf16[512,1024]{1,0:T(8,128)(2,1)S(1)} %collective-permute-done.5.refs_2_) | copy-start | bytes 3145732
  79.8 39.0 %collective-permute-start.7 = (bf16[256,1024]{1,0:T(8,128)(2,1)S(1)}, bf16[256,1024]{1,0:T(8,128)(2,1)}, u32[]{:S(2)}, u32[]{:S(2)}) collective-permute-start(bf16[256,1024]{1,0:T(8,128)(2,1)S(1)} %slice.85), channel_id=1, source_target_pairs={{0,192},{64,0},{128,64},{192,128},{1,193},{65,1},{129,65},{193,129... | collective-permute-start | bytes 1572872 | tf_op jit(solution)/shard_map/ppermute | solution.py:22
  81.1 28.4 %copy-start.6 = (bf16[512,1024]{1,0:T(8,128)(2,1)}, bf16[512,1024]{1,0:T(8,128)(2,1)S(1)}, u32[]{:S(2)}) copy-start(bf16[512,1024]{1,0:T(8,128)(2,1)S(1)} %collective-permute-done.6.refs_3_) | copy-start | bytes 3145732
  82.1 36.8 %collective-permute-start.8 = (bf16[256,1024]{1,0:T(8,128)(2,1)}, bf16[256,1024]{1,0:T(8,128)(2,1)}, u32[]{:S(2)}, u32[]{:S(2)}) collective-permute-start(bf16[256,1024]{1,0:T(8,128)(2,1)} %slice.86), channel_id=1, source_target_pairs={{0,64},{64,128},{128,192},{192,0},{1,65},{65,129},{129,193},{193,1... | collective-permute-start | bytes 1572872 | tf_op jit(solution)/shard_map/ppermute | solution.py:22
  108.3 1.2 copy-start.7
  108.4 7.8 %collective-permute-start.14 = (bf16[128,1024]{1,0:T(8,128)(2,1)S(1)}, bf16[128,1024]{1,0:T(8,128)(2,1)}, u32[]{:S(2)}, u32[]{:S(2)}) collective-permute-start(bf16[128,1024]{1,0:T(8,128)(2,1)S(1)} %slice.88), channel_id=1, source_target_pairs={{0,48},{16,0},{32,16},{48,32},{1,49},{17,1},{33,17},{49,33},{2,50}... | collective-permute-start | bytes 786440 | tf_op jit(solution)/shard_map/ppermute | solution.py:22
  108.8 0.9 copy-start.8
  109.7 9.2 %collective-permute-start.15 = (bf16[128,1024]{1,0:T(8,128)(2,1)}, bf16[128,1024]{1,0:T(8,128)(2,1)}, u32[]{:S(2)}, u32[]{:S(2)}) collective-permute-start(bf16[128,1024]{1,0:T(8,128)(2,1)} %slice.89), channel_id=1, source_target_pairs={{0,16},{16,32},{32,48},{48,0},{1,17},{17,33},{33,49},{49,1},{2,18}... | collective-permute-start | bytes 786440 | tf_op jit(solution)/shard_map/ppermute | solution.py:22
  136.3 45.0 %all-to-all-start = ((bf16[16,96,1024]{2,1,0:T(8,128)(2,1)}), bf16[16,96,1024]{2,1,0:T(8,128)(2,1)}, u32[]{:S(2)}, u32[]{:S(2)}) async-start(bf16[16,96,1024]{2,1,0:T(8,128)(2,1)} %get-tuple-element.7), calls=%async_computation | async-start | bytes 6291456 | tf_op jit(solution)/shard_map/all_to_all | solution.py:137
  143.0 74.3 %collective-permute-start.17 = (bf16[3072,1024]{1,0:T(8,128)(2,1)}, bf16[3072,1024]{1,0:T(8,128)(2,1)}, u32[]{:S(2)}, u32[]{:S(2)}) collective-permute-start(bf16[3072,1024]{1,0:T(8,128)(2,1)} %get-tuple-element.8), channel_id=1, source_target_pairs={{0,8},{8,0},{1,9},{9,1},{2,10},{10,2},{3,11},{11,3},{4,12},{12,4},... | collective-permute-start | bytes 18874376 | tf_op jit(solution)/shard_map/ppermute | solution.py:22
  230.1 17.7 %all-to-all-start.2 = ((f32[32,1,2048]{2,1,0:T(1,128)}), f32[32,1,2048]{2,1,0:T(1,128)S(1)}, u32[]{:S(2)}, u32[]{:S(2)}) async-start(f32[32,1,2048]{2,1,0:T(1,128)} %reshape.41), calls=%async_computation.2 | async-start | bytes 524288 | tf_op jit(solution)/shard_map/all_to_all | solution.py:155
  252.5 2.2 copy-start.3
  256.2 11.7 %all-to-all-start.3 = ((f32[8,3,4,1024]{3,2,1,0:T(4,128)}), f32[8,3,4,1024]{3,2,1,0:T(4,128)S(1)}, u32[]{:S(2)}, u32[]{:S(2)}) async-start(f32[8,3,4,1024]{3,2,1,0:T(4,128)} %copy.38), calls=%async_computation.3 | async-start | bytes 786432 | tf_op jit(solution)/shard_map/all_to_all | solution.py:158
  259.8 2.3 copy-start.1
  267.9 3.3 %copy-start.2 = (bf16[1024,1024]{0,1:T(8,128)(2,1)S(1)}, bf16[1024,1024]{0,1:T(8,128)(2,1)}, u32[]{:S(2)}) copy-start(bf16[1024,1024]{0,1:T(8,128)(2,1)} %convolution_convert_fusion) | copy-start | bytes 6291460
  270.2 2.3 copy-start.9

commit v3 on v1

v3 whole, which is shorter than its diff:
```python
import jax
import jax.numpy as jnp
from jax import lax
from jax.sharding import Mesh, PartitionSpec as P

ROW = ("x", "zh", "core")
COL = ("y", "zl")
ALL = ROW + COL
BF = jnp.bfloat16
F32 = jnp.float32


def dot(a, b, ca=1, cb=0):
    return lax.dot_general(a, b, (((ca,), (cb,)), ((), ())), preferred_element_type=F32)


def hold(a):
    return lax.optimization_barrier(a)


def exchange(a, axes):
    return lax.all_to_all(a, axes, 0, 0, tiled=True)


def shards(z, pp, pdi, ca, cp, cdi):
    rows, w = pp.shape
    nr, nc = lax.axis_size(ROW), lax.axis_size(COL)
    sl = w // nr
    mine = sl // nc
    block = z.reshape(z.shape[0], -1)

    def by_col(m):
        return m.reshape(-1, nr, nc, mine).transpose(0, 2, 1, 3).reshape(-1, w)

    parent = lax.all_gather(pp, ROW, axis=0, tiled=True)
    child = lax.all_gather(ca, ROW, axis=0, tiled=True)

    cp_by = by_col(cp)
    mixed = dot(pp, cp_by).astype(BF)
    wide = jnp.concatenate([mixed, ca], axis=1)
    wide = exchange(jnp.broadcast_to(wide, (nc,) + wide.shape), COL).reshape(nc * rows, 2 * w)
    mixed_by, anc_rows = wide[:, :w], wide[:, w:]
    anc_by = by_col(anc_rows)
    diag_prod = dot(pdi, cp).astype(BF)
    first = (lax.axis_index(ROW) * nc + lax.axis_index(COL)) * mine
    cols = lambda m: lax.dynamic_slice_in_dim(m, first, mine, 1)
    diag_upper = dot(cols(pdi), pdi, 0, 0)
    diag_lower = dot(cols(cdi), cdi, 0, 0) + dot(cols(diag_prod), diag_prod, 0, 0)
    parent, cp_by, mixed_by, anc_rows, anc_by, diag_upper, diag_lower = hold(
        (parent, cp_by, mixed_by, anc_rows, anc_by, diag_upper, diag_lower)
    )

    up = dot(block, parent).astype(BF)
    upper = exchange(up.reshape(nc, rows, w), COL)
    sp = dot(up, cp).astype(BF)
    sp_by = dot(up, cp_by).astype(BF)
    early = dot(mixed_by, sp, 0, 0) - dot(sp_by, anc_rows, 0, 0) - dot(anc_by, sp, 0, 0)
    upper = jnp.sum(upper.astype(F32), axis=0)
    u = upper.astype(BF)
    x = exchange(u.T.reshape(nr, sl, rows), ROW)
    shifted = dot(u, cp)
    x = hold(x.transpose(1, 0, 2).reshape(sl, nr * rows))
    t = hold(dot(parent, x, 0, 1))
    t = exchange(t.reshape(nr, sl, sl), ROW)
    child, early, t, x, shifted = hold((child, early, t, x, shifted))

    g1 = t.transpose(1, 0, 2).reshape(sl, w)
    f = jnp.stack([g1, dot(x, child)]).reshape(2, nc, mine, w).transpose(1, 0, 2, 3)
    f, child = hold((f, child))
    f = exchange(f, COL)
    lp = dot(block, child).astype(BF)
    low = (early + dot(anc_by, lp, 0, 0)).astype(BF)
    f, low = hold((f, low))
    low = exchange(low.reshape(nc, nr * mine, w), COL)
    low = jnp.sum(low.astype(F32), axis=0)
    lp, low = hold((lp, low))
    low = exchange(low.reshape(nr, mine, w), ROW)
    lower = exchange(lp.reshape(nc, rows, w), COL)
    f = jnp.sum(f, axis=0)
    lower = jnp.sum(lower.astype(F32), axis=0)
    low = jnp.sum(low, axis=0)

    pp_out = diag_upper + f[0]
    pc = f[1] - dot(pp_out.astype(BF), cp)
    cc = diag_lower + low
    return -upper, pp_out, shifted - lower, pc, cc


def solution(mesh):
    fine = Mesh(mesh.devices.reshape(4, 4, 2, 4, 2), ALL)
    out = P(ALL, None)
    return jax.shard_map(
        shards,
        mesh=fine,
        in_specs=(P(ROW, COL, None), out, P(), out, P(), P()),
        out_specs=(out,) * 5,
        check_vma=False,
    )
```

time: 266 us -> 341 us (1.28)
  blocking collectives: 79.2 us -> 30.1 us
  matrix products: 33.3 us -> 67.5 us
  starting transfers between devices: 8.97 us -> 41.9 us
  local copies, waits for them, and re-layouts: 9.7 us -> 40.7 us
  waiting for transfers between devices: 113 us -> 138 us
    all_to_all x2 -> x7, waiting for transfers between devices: 15 us -> 136 us  [exchange(): return lax.all_to_all(a, axes, 0, 0, tiled=True)]
    all_gather x1 -> x2, waiting for transfers between devices: 98.4 us -> 0.02 us  [the longest x1 0.02 us: shards(): child = lax.all_gather(ca, ROW, axis=0, tiled=True)]
    all_to_all x2 -> x1, blocking collectives: 79.2 us -> 30.1 us  [exchange(): return lax.all_to_all(a, axes, 0, 0, tiled=True)]
    dot_general x9 -> x16, matrix products: 33.3 us -> 67.5 us  [dot(): lax.dot_general(a, b, (((ca,), (cb,)), ((), ())), preferred_element_type=...]
    all_to_all x2 -> x7, starting transfers between devices: 8.94 us -> 41.8 us  [exchange(): return lax.all_to_all(a, axes, 0, 0, tiled=True)]
    reshape x1 -> x7, local copies, waits for them, and re-layouts: 1.05 us -> 16.3 us  [the longest x4 14.8 us: by_col(): return m.reshape(-1, nr, nc, mine).transpose(0, 2, 1, 3).reshape(-1, w)]
    unnamed x14 -> x26, local copies, waits for them, and re-layouts: 2.37 us -> 7.31 us
    transpose x6 -> x4, local copies, waits for them, and re-layouts: 1.5 us -> 5.97 us  [the longest x2 5.56 us: by_col(): return m.reshape(-1, nr, nc, mine).transpose(0, 2, 1, 3).reshape(-1, w)]
  transfers between devices with their start and end apart: 3 -> 9, of which waited for: 3 -> 7; matrix products, arithmetic and copies ran while one was open for 2% -> 28% of each run, Pallas kernels for 0% -> 0%
where the time goes in v3:
time: 341 us; the launch traced here: 339 us
  waiting for transfers between devices  138 us (40%)
  matrix products  67.5 us (20%)
  starting transfers between devices  41.9 us (12%)
  local copies, waits for them, and re-layouts  40.7 us (12%)
  blocking collectives  30.1 us (9%)
  between operations  14.3 us (4%)
  other arithmetic  7.24 us (2%)
    all_to_all x7, waiting for transfers between devices, exchange(): return lax.all_to_all(a, axes, 0, 0, tiled=True)  136 us
    dot_general x16, matrix products, dot(): lax.dot_general(a, b, (((ca,), (cb,)), ((), ())), preferred_element_type=...  67.5 us
    all_to_all x7, starting transfers between devices, exchange(): return lax.all_to_all(a, axes, 0, 0, tiled=True)  41.8 us
    all_to_all x1, blocking collectives, exchange(): return lax.all_to_all(a, axes, 0, 0, tiled=True)  30.1 us
    reshape x4, local copies, waits for them, and re-layouts, by_col(): return m.reshape(-1, nr, nc, mine).transpose(0, 2, 1, 3).reshape(-1, w)  14.8 us
    unnamed x26, local copies, waits for them, and re-layouts  7.31 us
  transfers between devices with their start and end apart: 9, of which 7 were waited for; matrix products, arithmetic and copies ran while one was open for 28% of the time, Pallas kernels for 0%

profile of v3, /device:TPU:1, one launch (start us, length us, event | category | flops | bytes accessed | tf_op | source)
XLA Modules:
  0.0 339.3 jit_solution(1482526066049071296)
XLA Ops:
  7.2 0.7 all-gather.3.cloned.1.call-update
  8.0 0.7 all-gather.5.cloned.1.call-update
  8.7 4.0 %copy.47 = bf16[1024,1024]{0,1:T(8,128)(2,1)} copy(bf16[1024,1024]{1,0:T(8,128)(2,1)} %param.10) | data formatting | bytes 4194304 | tf_op args[4]
  12.6 4.1 %reshape.54 = bf16[1024,32,8,4]{0,3,2,1:T(4,128)(2,1)} reshape(bf16[1024,1024]{0,1:T(8,128)(2,1)} %copy.47) | data formatting | bytes 4194304 | tf_op jit(solution)/shard_map/reshape | solution.py:33
  16.8 3.8 %copy.48 = bf16[1024,8,32,4]{0,3,2,1:T(4,128)(2,1)} copy(bf16[1024,8,32,4]{0,3,1,2:T(4,128)(2,1)} %bitcast.68) | data formatting | bytes 4194304 | tf_op jit(solution)/shard_map/transpose | solution.py:33
  20.5 4.0 %reshape.55 = bf16[1024,1024]{0,1:T(8,128)(2,1)} reshape(bf16[1024,8,32,4]{0,3,2,1:T(4,128)(2,1)} %copy.48) | data formatting | bytes 4194304 | tf_op jit(solution)/shard_map/reshape | solution.py:33
  24.6 2.4 convolution_convert_fusion.3
  27.0 2.0 broadcast_in_dim.3
  29.1 6.4 %all-to-all-start = ((bf16[8,96,2048]{2,1,0:T(8,128)(2,1)}), bf16[8,96,2048]{2,1,0:T(8,128)(2,1)}, u32[]{:S(2)}, u32[]{:S(2)}) async-start(bf16[8,96,2048]{2,1,0:T(8,128)(2,1)} %broadcast_in_dim.3), calls=%async_computation | async-start | bytes 6291456 | tf_op jit(solution)/shard_map/all_to_all | solution.py:22
  35.5 2.3 fusion.11
  37.8 0.5 fusion.13
  38.3 2.4 convolution_convert_fusion
  40.7 0.7 convolution_add_fusion
  41.4 59.8 %all-to-all-done = bf16[8,96,2048]{2,1,0:T(8,128)(2,1)} async-done(((bf16[8,96,2048]{2,1,0:T(8,128)(2,1)}), bf16[8,96,2048]{2,1,0:T(8,128)(2,1)}, u32[]{:S(2)}, u32[]{:S(2)}) %all-to-all-start) | async-done | bytes 3145760 | tf_op jit(solution)/shard_map/all_to_all | solution.py:22
  101.2 3.3 fusion.23
  104.5 1.2 copy-done.4
  105.7 1.6 copy.49
  107.3 2.9 reshape.57
  110.2 1.8 copy.50
  112.0 3.7 %reshape.58 = bf16[768,1024]{0,1:T(8,128)(2,1)} reshape(bf16[768,8,32,4]{0,3,2,1:T(4,128)(2,1)} %copy.50) | data formatting | bytes 3145728 | tf_op jit(solution)/shard_map/reshape | solution.py:33
  115.7 9.4 %fusion.4 = bf16[1024,768]{0,1:T(8,128)(2,1)} fusion(bf16[3072,1024]{1,0:T(8,128)(2,1)} %all-gather.3.cloned.1.call-done, bf16[768,1,3072]{2,0,1:T(8,128)(2,1)} %param.6), kind=kOutput, calls=%fused_computation.10 | convolution fusion | flops 4832624640 | bytes 12582912 | tf_op jit(solution)/shard_map/dot_general | solution.py:14
  125.2 4.6 %all-to-all-start.1 = ((bf16[8,96,1024]{2,1,0:T(8,128)(2,1)}), bf16[8,96,1024]{2,1,0:T(8,128)(2,1)}, u32[]{:S(2)}, u32[]{:S(2)}) async-start(bf16[8,96,1024]{2,1,0:T(8,128)(2,1)} %bitcast.74), calls=%async_computation.1 | async-start | bytes 3145728 | tf_op jit(solution)/shard_map/all_to_all | solution.py:22
  129.8 3.3 convolution_convert_fusion.2
  133.1 1.1 copy-done.8
  134.3 3.8 %fusion.24 = f32[1024,1024]{1,0:T(8,128)} fusion(bf16[768,1024]{1,0:T(8,128)(2,1)S(1)} %copy-done.7, bf16[768,1024]{1,0:T(8,128)(2,1)S(1)} %convolution_convert_fusion.2), kind=kOutput, calls=%fused_computation.36 | convolution fusion | flops 1610612736 | bytes 7340032 | tf_op jit(solution)/shard_map/dot_general | solution.py:14
  138.1 7.9 %fusion.10 = f32[1024,1024]{1,0:T(8,128)} fusion(bf16[768,1024]{1,0:T(8,128)(2,1)} %copy-done.4, bf16[1024,768]{0,1:T(8,128)(2,1)} %fusion.4, bf16[1024,1024]{0,1:T(8,128)(2,1)} %reshape.55), kind=kOutput, calls=%fused_computation.17 | convolution fusion | flops 3222011904 | bytes 9437184 | tf_op jit(solution)/shard_map/dot_general | solution.py:14
  146.0 27.0 %all-to-all-done.1 = bf16[8,96,1024]{2,1,0:T(8,128)(2,1)} async-done(((bf16[8,96,1024]{2,1,0:T(8,128)(2,1)}), bf16[8,96,1024]{2,1,0:T(8,128)(2,1)}, u32[]{:S(2)}, u32[]{:S(2)}) %all-to-all-start.1) | async-done | bytes 1572896 | tf_op jit(solution)/shard_map/all_to_all | solution.py:22
  173.0 1.8 convert_reduce_fusion.2
  174.7 0.8 convert_bitcast_fusion
  175.5 0.8 copy.51
  176.4 12.4 %all-to-all-start.2 = ((bf16[32,32,96]{2,1,0:T(8,128)(2,1)}), bf16[32,32,96]{2,1,0:T(8,128)(2,1)S(1)}, u32[]{:S(2)}, u32[]{:S(2)}) async-start(bf16[32,32,96]{2,1,0:T(8,128)(2,1)} %bitcast.7), calls=%async_computation.2 | async-start | bytes 524288 | tf_op jit(solution)/shard_map/all_to_all | solution.py:22
  188.8 8.1 %subtract_subtract_fusion = f32[1024,1024]{1,0:T(8,128)} fusion(f32[1024,1024]{1,0:T(8,128)} %fusion.24, f32[1024,1024]{1,0:T(8,128)} %fusion.10, bf16[768,1024]{0,1:T(8,128)(2,1)} %reshape.58, bf16[768,1024]{1,0:T(8,128)(2,1)} %copy-done.8), kind=kOutput, calls=%fused_computation.6 | convolution fusion | flops 1612709888 | bytes 15728640 | tf_op jit(solution)/shard_map/dot_general | solution.py:14
  196.9 4.6 %all-to-all-done.2 = bf16[32,32,96]{2,1,0:T(8,128)(2,1)S(1)} async-done(((bf16[32,32,96]{2,1,0:T(8,128)(2,1)}), bf16[32,32,96]{2,1,0:T(8,128)(2,1)S(1)}, u32[]{:S(2)}, u32[]{:S(2)}) %all-to-all-start.2) | async-done | bytes 196640 | tf_op jit(solution)/shard_map/all_to_all | solution.py:22
  201.4 0.1 copy.52
  201.5 0.3 reshape.62
  201.9 4.0 %fusion.26 = f32[1024,32]{0,1:T(8,128)S(1)} fusion(bf16[32,3072]{1,0:T(8,128)(2,1)S(1)} %reshape.62, bf16[3072,1024]{1,0:T(8,128)(2,1)} %all-gather.3.cloned.1.call-done), kind=kOutput, calls=%fused_computation.38 | convolution fusion | flops 201326592 | bytes 6619136 | tf_op jit(solution)/shard_map/dot_general | solution.py:14
  205.8 0.2 copy.58
  206.0 0.9 reshape.67
  207.0 5.2 %all-to-all-start.3 = ((f32[32,1,1024]{2,1,0:T(1,128)}), f32[32,1,1024]{2,1,0:T(1,128)S(1)}, u32[]{:S(2)}, u32[]{:S(2)}) async-start(f32[32,1,1024]{2,1,0:T(1,128)} %reshape.67), calls=%async_computation.3 | async-start | bytes 262144 | tf_op jit(solution)/shard_map/all_to_all | solution.py:22
  212.2 0.5 fusion.15
  212.7 10.2 %all-to-all-done.3 = f32[32,1,1024]{2,1,0:T(1,128)S(1)} async-done(((f32[32,1,1024]{2,1,0:T(1,128)}), f32[32,1,1024]{2,1,0:T(1,128)S(1)}, u32[]{:S(2)}, u32[]{:S(2)}) %all-to-all-start.3) | async-done | bytes 131104 | tf_op jit(solution)/shard_map/all_to_all | solution.py:22
  222.9 0.5 broadcast
  223.4 0.9 reduce
  224.3 0.2 reshape.68
  224.5 0.3 copy.54
  224.9 0.3 stack.8
  225.1 4.0 %fusion.25 = f32[32,1024]{1,0:T(8,128)S(1)} fusion(bf16[32,3072]{1,0:T(8,128)(2,1)S(1)} %reshape.62, bf16[3072,1024]{1,0:T(8,128)(2,1)} %all-gather.5.cloned.1.call-done), kind=kOutput, calls=%fused_computation.37 | convolution fusion | flops 201326592 | bytes 6619136 | tf_op jit(solution)/shard_map/dot_general | solution.py:14
  229.2 9.6 %fusion.7 = bf16[1024,768]{1,0:T(8,128)(2,1)} fusion(bf16[3072,1024]{1,0:T(8,128)(2,1)} %all-gather.5.cloned.1.call-done, bf16[768,1,3072]{2,0,1:T(8,128)(2,1)} %param.6), kind=kOutput, calls=%fused_computation.11 | convolution fusion | flops 4832624640 | bytes 12582912 | tf_op jit(solution)/shard_map/dot_general | solution.py:14
  238.9 0.7 copy.55
  239.6 3.4 %all-to-all-start.4 = ((f32[8,2,4,1024]{3,2,1,0:T(4,128)}), f32[8,2,4,1024]{3,2,1,0:T(4,128)S(1)}, u32[]{:S(2)}, u32[]{:S(2)}) async-start(f32[8,2,4,1024]{3,2,1,0:T(4,128)} %copy.55), calls=%async_computation.4 | async-start | bytes 524288 | tf_op jit(solution)/shard_map/all_to_all | solution.py:22
  243.0 5.8 %add_convert_fusion = bf16[1024,1024]{1,0:T(8,128)(2,1)} fusion(f32[1024,1024]{1,0:T(8,128)} %subtract_subtract_fusion, bf16[768,1024]{0,1:T(8,128)(2,1)S(1)} %copy-done.5, bf16[1024,768]{1,0:T(8,128)(2,1)} %fusion.7), kind=kOutput, calls=%fused_computation.5 | convolution fusion | flops 1612709888 | bytes 9437184 | tf_op jit(solution)/shard_map/dot_general | solution.py:14
  248.8 1.3 all-to-all-done.4
  250.1 30.1 %all_to_all.40 = bf16[8,128,1024]{2,1,0:T(8,128)(2,1)S(1)} all-to-all(bf16[8,128,1024]{2,1,0:T(8,128)(2,1)} %bitcast.72), channel_id=1, replica_groups=mesh['x'=4,'zh'=4,'core'=2,'y'=4,'zl'=2] {'y','zl'}, dimensions={0} | all-to-all | bytes 4194304 | tf_op jit(solution)/shard_map/all_to_all | solution.py:22
  280.2 0.3 convert_reduce_fusion
  280.5 1.0 reshape.66
  281.5 5.5 %all-to-all-start.7 = ((f32[32,4,1024]{2,1,0:T(4,128)}), f32[32,4,1024]{2,1,0:T(4,128)S(1)}, u32[]{:S(2)}, u32[]{:S(2)}) async-start(f32[32,4,1024]{2,1,0:T(4,128)} %reshape.66), calls=%async_computation.7 | async-start | bytes 1048576 | tf_op jit(solution)/shard_map/all_to_all | solution.py:22
  287.0 1.7 copy.56
  288.6 16.5 %all-to-all-done.7 = f32[32,4,1024]{2,1,0:T(4,128)S(1)} async-done(((f32[32,4,1024]{2,1,0:T(4,128)}), f32[32,4,1024]{2,1,0:T(4,128)S(1)}, u32[]{:S(2)}, u32[]{:S(2)}) %all-to-all-start.7) | async-done | bytes 524320 | tf_op jit(solution)/shard_map/all_to_all | solution.py:22
  305.1 4.3 %all-to-all-start.6 = ((bf16[8,96,1024]{2,1,0:T(8,128)(2,1)}), bf16[8,96,1024]{2,1,0:T(8,128)(2,1)}, u32[]{:S(2)}, u32[]{:S(2)}) async-start(bf16[8,96,1024]{2,1,0:T(8,128)(2,1)} %bitcast.15), calls=%async_computation.6 | async-start | bytes 3145728 | tf_op jit(solution)/shard_map/all_to_all | solution.py:22
  309.5 2.7 convolution_subtract_fusion
  312.4 0.6 add.37
  313.0 16.9 %all-to-all-done.6 = bf16[8,96,1024]{2,1,0:T(8,128)(2,1)} async-done(((bf16[8,96,1024]{2,1,0:T(8,128)(2,1)}), bf16[8,96,1024]{2,1,0:T(8,128)(2,1)}, u32[]{:S(2)}, u32[]{:S(2)}) %all-to-all-start.6) | async-done | bytes 1572896 | tf_op jit(solution)/shard_map/all_to_all | solution.py:22
  329.9 1.7 convert_reduce_fusion.1
  331.7 0.8 sub.14
  (32 shorter events, 0.4 us)
Async XLA Ops:
  7.2 30.7 %copy-start = (bf16[1024,1024]{1,0:T(8,128)(2,1)S(1)}, bf16[1024,1024]{1,0:T(8,128)(2,1)}, u32[]{:S(2)}) copy-start(bf16[1024,1024]{1,0:T(8,128)(2,1)} %param.8) | copy-start | bytes 6291460
  7.2 108.5 %all-gather.3.cloned.1.call-start = ((), (), s32[]{:S(2)}) async-start(), calls=%async_computation.8 | async-start | bytes 6488064 | tf_op jit(solution)/shard_map/all_gather | solution.py:35
  7.9 216.6 %all-gather.5.cloned.1.call-start = ((), (), s32[]{:S(2)}) async-start(), calls=%async_computation.9 | async-start | bytes 6488064 | tf_op jit(solution)/shard_map/all_gather | solution.py:36
  20.5 4.0 %copy-start.9 = (bf16[96,1024]{1,0:T(8,128)(2,1)S(1)}, bf16[96,1024]{1,0:T(8,128)(2,1)}, u32[]{:S(2)}) copy-start(bf16[96,1024]{1,0:T(8,128)(2,1)} %param.7) | copy-start | bytes 589828
  24.6 2.4 copy-start.10
  29.1 72.1 %all-to-all-start = ((bf16[8,96,2048]{2,1,0:T(8,128)(2,1)}), bf16[8,96,2048]{2,1,0:T(8,128)(2,1)}, u32[]{:S(2)}, u32[]{:S(2)}) async-start(bf16[8,96,2048]{2,1,0:T(8,128)(2,1)} %broadcast_in_dim.3), calls=%async_computation | async-start | bytes 6291456 | tf_op jit(solution)/shard_map/all_to_all | solution.py:22
  35.5 2.8 copy-start.2
  104.5 1.2 copy-start.4
  125.2 4.6 %copy-start.3 = (bf16[1024,1024]{1,0:T(8,128)(2,1)S(1)}, bf16[1024,1024]{1,0:T(8,128)(2,1)}, u32[]{:S(2)}) copy-start(bf16[1024,1024]{1,0:T(8,128)(2,1)} %param.10) | copy-start | bytes 6291460
  125.2 47.8 %all-to-all-start.1 = ((bf16[8,96,1024]{2,1,0:T(8,128)(2,1)}), bf16[8,96,1024]{2,1,0:T(8,128)(2,1)}, u32[]{:S(2)}, u32[]{:S(2)}) async-start(bf16[8,96,1024]{2,1,0:T(8,128)(2,1)} %bitcast.74), calls=%async_computation.1 | async-start | bytes 3145728 | tf_op jit(solution)/shard_map/all_to_all | solution.py:22
  129.8 4.5 %copy-start.7 = (bf16[768,1024]{1,0:T(8,128)(2,1)S(1)}, bf16[768,1024]{1,0:T(8,128)(2,1)}, u32[]{:S(2)}) copy-start(bf16[768,1024]{1,0:T(8,128)(2,1)} %get-tuple-element.25) | copy-start | bytes 4718596
  133.1 1.1 copy-start.8
  176.4 25.1 %all-to-all-start.2 = ((bf16[32,32,96]{2,1,0:T(8,128)(2,1)}), bf16[32,32,96]{2,1,0:T(8,128)(2,1)S(1)}, u32[]{:S(2)}, u32[]{:S(2)}) async-start(bf16[32,32,96]{2,1,0:T(8,128)(2,1)} %bitcast.7), calls=%async_computation.2 | async-start | bytes 524288 | tf_op jit(solution)/shard_map/all_to_all | solution.py:22
  207.0 15.9 %all-to-all-start.3 = ((f32[32,1,1024]{2,1,0:T(1,128)}), f32[32,1,1024]{2,1,0:T(1,128)S(1)}, u32[]{:S(2)}, u32[]{:S(2)}) async-start(f32[32,1,1024]{2,1,0:T(1,128)} %reshape.67), calls=%async_computation.3 | async-start | bytes 262144 | tf_op jit(solution)/shard_map/all_to_all | solution.py:22
  229.2 13.8 %copy-start.5 = (bf16[768,1024]{0,1:T(8,128)(2,1)S(1)}, bf16[768,1024]{0,1:T(8,128)(2,1)}, u32[]{:S(2)}) copy-start(bf16[768,1024]{0,1:T(8,128)(2,1)} %reshape.58) | copy-start | bytes 4718596
  239.6 10.5 %all-to-all-start.4 = ((f32[8,2,4,1024]{3,2,1,0:T(4,128)}), f32[8,2,4,1024]{3,2,1,0:T(4,128)S(1)}, u32[]{:S(2)}, u32[]{:S(2)}) async-start(f32[8,2,4,1024]{3,2,1,0:T(4,128)} %copy.55), calls=%async_computation.4 | async-start | bytes 524288 | tf_op jit(solution)/shard_map/all_to_all | solution.py:22
  280.5 6.4 %copy-start.6 = (bf16[1024,768]{1,0:T(8,128)(2,1)S(1)}, bf16[1024,768]{1,0:T(8,128)(2,1)}, u32[]{:S(2)}) copy-start(bf16[1024,768]{1,0:T(8,128)(2,1)} %fusion.7) | copy-start | bytes 4718596
  281.5 23.6 %all-to-all-start.7 = ((f32[32,4,1024]{2,1,0:T(4,128)}), f32[32,4,1024]{2,1,0:T(4,128)S(1)}, u32[]{:S(2)}, u32[]{:S(2)}) async-start(f32[32,4,1024]{2,1,0:T(4,128)} %reshape.66), calls=%async_computation.7 | async-start | bytes 1048576 | tf_op jit(solution)/shard_map/all_to_all | solution.py:22
  305.1 24.8 %all-to-all-start.6 = ((bf16[8,96,1024]{2,1,0:T(8,128)(2,1)}), bf16[8,96,1024]{2,1,0:T(8,128)(2,1)}, u32[]{:S(2)}, u32[]{:S(2)}) async-start(bf16[8,96,1024]{2,1,0:T(8,128)(2,1)} %bitcast.15), calls=%async_computation.6 | async-start | bytes 3145728 | tf_op jit(solution)/shard_map/all_to_all | solution.py:22
  309.5 22.1 %copy-start.11 = (f32[4,1024]{1,0:T(4,128)}, f32[4,1024]{1,0:T(4,128)S(1)}, u32[]{:S(2)}) copy-start(f32[4,1024]{1,0:T(4,128)S(1)} %fusion.17) | copy-start | bytes 49156
  309.5 22.9 %copy-start.1 = (bf16[1024,1024]{1,0:T(8,128)(2,1)S(1)}, bf16[1024,1024]{1,0:T(8,128)(2,1)}, u32[]{:S(2)}) copy-start(bf16[1024,1024]{1,0:T(8,128)(2,1)} %param.8) | copy-start | bytes 6291460
Sparse Core Ops, SparseCore 0:
  10.6 86.5 all-gather.2
  99.7 78.7 all-gather.4

commit v4 on v1

v4 whole, which is shorter than its diff:
```python
import jax
import jax.numpy as jnp
from jax import lax
from jax.experimental import pallas as pl
from jax.experimental.pallas import tpu as pltpu
from jax.sharding import Mesh, PartitionSpec as P

ROW = ("x", "zh", "core")
COL = ("y", "zl")
ALL = ROW + COL
BF = jnp.bfloat16
F32 = jnp.float32
RING = (0, 1, 3, 2)


def dot(a, b, ca=1, cb=0):
    return lax.dot_general(a, b, (((ca,), (cb,)), ((), ())), preferred_element_type=F32)


def hold(a):
    return lax.optimization_barrier(a)


def exchange(a, axes):
    return lax.all_to_all(a, axes, 0, 0, tiled=True)


def shift(a, axis, by):
    n = lax.axis_size(axis)
    return lax.ppermute(a, axis, [(i, (i + by) % n) for i in range(n)])


def swap(a):
    return shift(a, "core", 1)


def ring(a, axis, direct=False):
    after = shift(a, axis, -1)
    before = shift(a, axis, 1)
    if direct:
        return [a, after, before, shift(a, axis, 2)]
    half = a.shape[0] // 2
    return [a, after, before, shift(after[:half], axis, -1), shift(before[half:], axis, 1)]


def product_kernel(where, *refs):
    mine, others = refs[:5], refs[5:10]
    z, out, panel_out, panel, sem, out_sem = refs[10:]
    step = pl.program_id(0)
    rows = mine[0].shape[0] // 4
    keep = pltpu.make_async_copy(panel, panel_out, out_sem)

    @pl.when(step == 0)
    def _():
        for pieces, core in ((mine, where[2]), (others, 1 - where[2])):
            for k, dx in enumerate((0, 1, 3, 2, 2)):
                for n in range(pieces[k].shape[0] // rows):
                    dz = RING[n + (2 if k == 4 else 0)]
                    at = lax.rem(where[0] + dx, 4) * 4 + lax.rem(where[1] + dz, 4)
                    at = pl.multiple_of((at * 2 + core) * rows, 32)
                    pltpu.make_async_copy(
                        pieces[k].at[pl.ds(n * rows, rows)], panel.at[pl.ds(at, rows)], sem
                    ).start()
        pltpu.make_async_copy(panel, panel, sem).wait()
        keep.start()

    out[...] = jnp.dot(z[...], panel[...], preferred_element_type=F32).astype(BF).reshape(out.shape)

    @pl.when(step == pl.num_programs(0) - 1)
    def _():
        keep.wait()


def product(where, mine, others, z, rows):
    depth, width = z.shape[1], mine[0].shape[1]
    steps = 2
    block = z.shape[0] // steps
    any_ = pl.BlockSpec(memory_space=pl.ANY)
    return pl.pallas_call(
        product_kernel,
        grid_spec=pltpu.PrefetchScalarGridSpec(
            num_scalar_prefetch=1,
            grid=(steps,),
            in_specs=[any_] * 10 + [pl.BlockSpec((block, depth), lambda i, w: (i, 0))],
            out_specs=[pl.BlockSpec((block // rows, rows, width), lambda i, w: (i, 0, 0)), any_],
            scratch_shapes=[
                pltpu.VMEM((depth, width), BF),
                pltpu.SemaphoreType.DMA(()),
                pltpu.SemaphoreType.DMA(()),
            ],
        ),
        out_shape=[
            jax.ShapeDtypeStruct((z.shape[0] // rows, rows, width), BF),
            jax.ShapeDtypeStruct((depth, width), BF),
        ],
        compiler_params=pltpu.CompilerParams(vmem_limit_bytes=48 << 20),
        cost_estimate=pl.CostEstimate(
            flops=2 * z.size * width,
            transcendentals=0,
            bytes_accessed=2 * z.size + 6 * depth * width + 2 * z.shape[0] * width,
        ),
    )(where, *mine, *others, z)


def shards(z, pp, pdi, ca, cp, cdi):
    rows, w = pp.shape
    nr, nc = lax.axis_size(ROW), lax.axis_size(COL)
    sl = w // nr
    own = sl // nc
    where = jnp.stack([lax.axis_index(a) for a in ROW]).astype(jnp.int32)
    block = z.reshape(z.shape[0], -1)

    child = lax.all_gather(ca, ROW, axis=0, tiled=True)
    pieces = ring(jnp.concatenate(ring(pp, "zh", direct=True)), "x")
    others = [swap(p) for p in pieces]

    diag_prod = dot(pdi, cp).astype(BF)
    first = (lax.axis_index(ROW) * nc + lax.axis_index(COL)) * own
    cols = lambda m: lax.dynamic_slice_in_dim(m, first, own, 1)
    diag_upper = dot(cols(pdi), pdi, 0, 0)
    diag_lower = dot(cols(cdi), cdi, 0, 0) + dot(cols(diag_prod), diag_prod, 0, 0)
    others[-1], diag_upper, diag_lower = hold((others[-1], diag_upper, diag_lower))

    up, parent = product(where, pieces, others, block, rows)
    upper = jnp.sum(exchange(up, COL).astype(F32), axis=0)
    u = upper.astype(BF)
    shifted = dot(u, cp)
    s = shifted.astype(BF)

    lp = dot(block, child).astype(BF).reshape(nc, rows, w)
    lower = jnp.sum(exchange(lp, COL).astype(F32), axis=0)
    anc = lower - shifted
    a = anc.astype(BF)

    x = jnp.stack([u.T, s.T, a.T]).reshape(3, nr, sl, rows).transpose(1, 0, 2, 3)
    x = exchange(x, ROW)
    x = x.transpose(1, 2, 0, 3).reshape(3 * sl, nr * rows)
    gp, gc = dot(x[: 2 * sl], parent), dot(x, child)
    g1t, stp = gp[:sl], gp[sl:]
    cross, stc, atc = gc[:sl], gc[sl : 2 * sl], gc[2 * sl :]
    t2 = dot(stp.astype(BF), cp) + atc
    t = jnp.stack([g1t, t2]).reshape(2, sl, nr, sl).transpose(2, 0, 3, 1)
    t = exchange(t, ROW)
    t = t.transpose(1, 2, 0, 3).reshape(2, sl, w)
    f = jnp.stack([t[0], cross, t[1] - stc]).reshape(3, nc, own, w).transpose(1, 0, 2, 3)
    f = jnp.sum(exchange(f, COL), axis=0)

    pp_out = diag_upper + f[0]
    pc = f[1] - dot(pp_out.astype(BF), cp)
    cc = diag_lower + f[2]
    return -upper, pp_out, -anc, pc, cc


def solution(mesh):
    fine = Mesh(mesh.devices.reshape(4, 4, 2, 4, 2), ALL)
    out = P(ALL, None)
    return jax.shard_map(
        shards,
        mesh=fine,
        in_specs=(P(ROW, COL, None), out, P(), out, P(), P()),
        out_specs=(out,) * 5,
        check_vma=False,
    )
```

time: 266 us -> 245 us (0.921)
  waiting for transfers between devices: 113 us -> 54.6 us
  starting transfers between devices: 8.97 us -> 41.3 us
  Pallas kernels: 0 us -> 15.6 us
  blocking collectives: 79.2 us -> 66.2 us
  local copies, waits for them, and re-layouts: 9.7 us -> 15.8 us
  matrix products: 33.3 us -> 28.1 us
    all_gather x1, waiting for transfers between devices: 98.4 us -> 0.01 us  [shards(): child = lax.all_gather(ca, ROW, axis=0, tiled=True)]
    ppermute x0 -> x12, starting transfers between devices: none -> 26.6 us  [shift(): return lax.ppermute(a, axis, [(i, (i + by) % n) for i in range(n)])]
    ppermute x0 -> x12, waiting for transfers between devices: none -> 24.9 us  [shift(): return lax.ppermute(a, axis, [(i, (i + by) % n) for i in range(n)])]
    pallas_call x0 -> x1, Pallas kernels: none -> 15.6 us  [product(): pl.pallas_call(product_kernel, grid_spec=pltpu.PrefetchScalarGridSpec(num...]
    all_to_all x2, waiting for transfers between devices: 15 us -> 29.1 us  [exchange(): return lax.all_to_all(a, axes, 0, 0, tiled=True)]
    all_to_all x2 -> x3, blocking collectives: 79.2 us -> 66.2 us  [exchange(): return lax.all_to_all(a, axes, 0, 0, tiled=True)]
    all_to_all x2, starting transfers between devices: 8.94 us -> 14.7 us  [exchange(): return lax.all_to_all(a, axes, 0, 0, tiled=True)]
    dot_general x9 -> x10, matrix products: 33.3 us -> 28.1 us  [dot(): lax.dot_general(a, b, (((ca,), (cb,)), ((), ())), preferred_element_type=...]
  transfers between devices with their start and end apart: 3 -> 15, of which waited for: 3 -> 7; matrix products, arithmetic and copies ran while one was open for 2% -> 9% of each run, Pallas kernels for 0% -> 6%
where the time goes in v4:
time: 245 us
  blocking collectives  66.2 us (27%)
  waiting for transfers between devices  54.6 us (22%)
  starting transfers between devices  41.3 us (17%)
  matrix products  28.1 us (11%)
  local copies, waits for them, and re-layouts  15.8 us (6%)
  Pallas kernels  15.6 us (6%)
  between operations  14.3 us (6%)
  other arithmetic  8.79 us (4%)
    all_to_all x3, blocking collectives, exchange(): return lax.all_to_all(a, axes, 0, 0, tiled=True)  66.2 us
    all_to_all x2, waiting for transfers between devices, exchange(): return lax.all_to_all(a, axes, 0, 0, tiled=True)  29.1 us
    dot_general x10, matrix products, dot(): lax.dot_general(a, b, (((ca,), (cb,)), ((), ())), preferred_element_type=...  28.1 us
    ppermute x12, starting transfers between devices, shift(): return lax.ppermute(a, axis, [(i, (i + by) % n) for i in range(n)])  26.6 us
    ppermute x12, waiting for transfers between devices, shift(): return lax.ppermute(a, axis, [(i, (i + by) % n) for i in range(n)])  24.9 us
    pallas_call x1, Pallas kernels, product(): pl.pallas_call(product_kernel, grid_spec=pltpu.PrefetchScalarGridSpec(num...  15.6 us
    all_to_all x2, starting transfers between devices, exchange(): return lax.all_to_all(a, axes, 0, 0, tiled=True)  14.7 us
    unnamed x37, local copies, waits for them, and re-layouts  5.06 us
  transfers between devices with their start and end apart: 15, of which 7 were waited for; matrix products, arithmetic and copies ran while one was open for 9% of the time, Pallas kernels for 6%

profile of v4, /device:TPU:1, one launch (start us, length us, event | category | flops | bytes accessed | tf_op | source)
XLA Modules:
  0.0 244.8 jit_solution(13935229871926142240)
XLA Ops:
  7.2 0.7 all-gather.2.cloned.1.call-update
  7.9 6.9 %collective-permute-start = (bf16[96,1024]{1,0:T(8,128)(2,1)}, bf16[96,1024]{1,0:T(8,128)(2,1)S(1)}, u32[]{:S(2)}, u32[]{:S(2)}) collective-permute-start(bf16[96,1024]{1,0:T(8,128)(2,1)} %param.7), channel_id=1, source_target_pairs={{0,48},{16,0},{32,16},{48,32},{1,49},{17,1},{33,17},{49,33},{2,50}... | collective-permute-start | bytes 589832 | tf_op jit(solution)/shard_map/ppermute | solution.py:30
  14.9 3.3 %collective-permute-start.2 = (bf16[96,1024]{1,0:T(8,128)(2,1)}, bf16[96,1024]{1,0:T(8,128)(2,1)S(1)}, u32[]{:S(2)}, u32[]{:S(2)}) collective-permute-start(bf16[96,1024]{1,0:T(8,128)(2,1)} %param.7), channel_id=1, source_target_pairs={{0,32},{16,48},{32,0},{48,16},{1,33},{17,49},{33,1},{49,17},{2,34}... | collective-permute-start | bytes 589832 | tf_op jit(solution)/shard_map/ppermute | solution.py:30
  18.1 1.0 constant_dynamic-update-slice_fusion.3
  19.1 1.9 collective-permute-done
  21.0 2.9 %collective-permute-done.1 = bf16[96,1024]{1,0:T(8,128)(2,1)S(1)} collective-permute-done((bf16[96,1024]{1,0:T(8,128)(2,1)}, bf16[96,1024]{1,0:T(8,128)(2,1)S(1)}, u32[]{:S(2)}, u32[]{:S(2)}) %collective-permute-start.1) | collective-permute-done | bytes 196640 | tf_op jit(solution)/shard_map/ppermute | solution.py:30
  23.9 5.5 %collective-permute-done.2 = bf16[96,1024]{1,0:T(8,128)(2,1)S(1)} collective-permute-done((bf16[96,1024]{1,0:T(8,128)(2,1)}, bf16[96,1024]{1,0:T(8,128)(2,1)S(1)}, u32[]{:S(2)}, u32[]{:S(2)}) %collective-permute-start.2) | collective-permute-done | bytes 196640 | tf_op jit(solution)/shard_map/ppermute | solution.py:30
  29.4 1.3 collective-permute-start.4
  30.7 1.5 collective-permute-start.3
  32.2 14.3 %collective-permute-done.4.refs_2_ = bf16[384,1024]{1,0:T(8,128)(2,1)S(1)} collective-permute-done((bf16[384,1024]{1,0:T(8,128)(2,1)S(1)}, bf16[384,1024]{1,0:T(8,128)(2,1)S(1)}, u32[]{:S(2)}, u32[]{:S(2)}) %collective-permute-start.4) | collective-permute-done | bytes 786464 | tf_op jit(solution)/shard_map/ppermute | solution.py:30
  46.5 0.8 slice.60
  47.2 1.0 collective-permute-start.6
  48.2 0.9 copy-done.1
  49.1 0.8 slice.59
  49.9 1.7 collective-permute-start.5
  51.6 3.8 %convolution_convert_fusion = bf16[1024,1024]{0,1:T(8,128)(2,1)} fusion(bf16[1024,1024]{1,0:T(8,128)(2,1)S(1)} %copy-done.5, bf16[1024,1024]{1,0:T(8,128)(2,1)S(1)} %copy-done), kind=kOutput, calls=%fused_computation.2 | convolution fusion | flops 2148532224 | bytes 6291456 | tf_op jit(solution)/shard_map/dot_general | solution.py:17
  55.4 7.5 %collective-permute-start.7 = (bf16[384,1024]{1,0:T(8,128)(2,1)}, bf16[384,1024]{1,0:T(8,128)(2,1)S(1)}, u32[]{:S(2)}, u32[]{:S(2)}) collective-permute-start(bf16[384,1024]{1,0:T(8,128)(2,1)} %copy-done.3), channel_id=1, source_target_pairs={{0,8},{8,0},{1,9},{9,1},{2,10},{10,2},{3,11},{11,3},{4,12},{12,4},... | collective-permute-start | bytes 2359304 | tf_op jit(solution)/shard_map/ppermute | solution.py:30
  62.9 0.5 collective-permute-start.9
  63.4 2.3 fusion.2
  65.7 2.9 %collective-permute-start.11 = (bf16[192,1024]{1,0:T(8,128)(2,1)S(1)}, bf16[192,1024]{1,0:T(8,128)(2,1)S(1)}, u32[]{:S(2)}, u32[]{:S(2)}) collective-permute-start(bf16[192,1024]{1,0:T(8,128)(2,1)S(1)} %collective-permute-done.6.refs_4_), channel_id=1, source_target_pairs={{0,8},{8,0},{1,9},{9,1},{2,10},{10,2},{3,11},{11,3},{4,12},{12,4},... | collective-permute-start | bytes 1179656 | tf_op jit(solution)/shard_map/ppermute | solution.py:30
  68.6 0.5 fusion
  69.2 1.3 convolution_add_fusion.1
  70.5 0.3 collective-permute-done.10.refs_8_
  70.8 0.9 copy-done.15
  71.6 15.6 %shard_map.101 = (bf16[8,96,1024]{2,1,0:T(8,128)(2,1)}, bf16[3072,1024]{1,0:T(8,128)(2,1)}) custom-call(s32[3]{0:T(128)S(1)} %pad_add_fusion.where, bf16[384,1024]{1,0:T(8,128)(2,1)S(1)} %copy-done.4, bf16[384,1024]{1,0:T(8,128)(2,1)S(1)} %copy-done.2, bf16[384,1024]{1,0:T(8,128)(2,1)S(1)} %collective-permute-done.4.refs_2_, ...), custom_call_target="tpu_custom_call" | custom-call | flops 4831838208 | bytes 25165824 | tf_op jit(solution)/shard_map/pallas_call | solution.py:79
  87.2 10.4 %all-to-all-start = ((bf16[8,96,1024]{2,1,0:T(8,128)(2,1)}), bf16[8,96,1024]{2,1,0:T(8,128)(2,1)}, u32[]{:S(2)}, u32[]{:S(2)}) async-start(bf16[8,96,1024]{2,1,0:T(8,128)(2,1)} %get-tuple-element.11), calls=%async_computation | async-start | bytes 3145728 | tf_op jit(solution)/shard_map/all_to_all | solution.py:25
  97.7 9.5 %convolution_convert_fusion.1 = bf16[768,1024]{1,0:T(8,128)(2,1)} fusion(bf16[3072,1024]{1,0:T(8,128)(2,1)} %all-gather.2.cloned.1.call-done, bf16[768,1,3072]{2,0,1:T(8,128)(2,1)} %param.6), kind=kOutput, calls=%fused_computation.3 | convolution fusion | flops 4832624640 | bytes 12582912 | tf_op jit(solution)/shard_map/dot_general | solution.py:17
  107.1 11.7 %all-to-all-done = bf16[8,96,1024]{2,1,0:T(8,128)(2,1)} async-done(((bf16[8,96,1024]{2,1,0:T(8,128)(2,1)}), bf16[8,96,1024]{2,1,0:T(8,128)(2,1)}, u32[]{:S(2)}, u32[]{:S(2)}) %all-to-all-start) | async-done | bytes 1572896 | tf_op jit(solution)/shard_map/all_to_all | solution.py:25
  118.8 4.3 %all-to-all-start.1 = ((bf16[8,96,1024]{2,1,0:T(8,128)(2,1)}), bf16[8,96,1024]{2,1,0:T(8,128)(2,1)}, u32[]{:S(2)}, u32[]{:S(2)}) async-start(bf16[8,96,1024]{2,1,0:T(8,128)(2,1)} %bitcast.64), calls=%async_computation.1 | async-start | bytes 3145728 | tf_op jit(solution)/shard_map/all_to_all | solution.py:25
  123.1 1.7 convert_reduce_fusion.1
  124.8 0.8 convert_bitcast_fusion.2
  125.6 0.2 copy.19
  125.8 17.4 %all-to-all-done.1 = bf16[8,96,1024]{2,1,0:T(8,128)(2,1)} async-done(((bf16[8,96,1024]{2,1,0:T(8,128)(2,1)}), bf16[8,96,1024]{2,1,0:T(8,128)(2,1)}, u32[]{:S(2)}, u32[]{:S(2)}) %all-to-all-start.1) | async-done | bytes 1572896 | tf_op jit(solution)/shard_map/all_to_all | solution.py:25
  143.2 1.7 convert_reduce_fusion
  145.0 1.2 subtract_negate_fusion
  146.4 0.2 copy.20
  146.6 0.2 maximum_bitcast_fusion.1
  146.8 37.3 %all_to_all.25 = bf16[32,3,32,96]{3,2,1,0:T(8,128)(2,1)S(1)} all-to-all(bf16[32,3,32,96]{3,2,1,0:T(8,128)(2,1)S(1)} %copy.22), channel_id=1, replica_groups=mesh['x'=4,'zh'=4,'core'=2,'y'=4,'zl'=2] {'x','zh','core'}, dimensions={0} | all-to-all | bytes 1179648 | tf_op jit(solution)/shard_map/all_to_all | solution.py:25
  184.2 0.3 copy.24
  184.5 0.3 copy.23
  184.8 1.5 slice.48
  186.4 4.1 %fusion.18 = f32[64,1024]{1,0:T(8,128)S(1)} fusion(bf16[64,3072]{1,0:T(8,128)(2,1)} %slice.48, bf16[3072,1024]{1,0:T(8,128)(2,1)} %get-tuple-element.13), kind=kOutput, calls=%fused_computation.40 | convolution fusion | flops 402653184 | bytes 6946816 | tf_op jit(solution)/shard_map/dot_general | solution.py:17
  190.5 0.7 copy-done.11
  191.2 1.0 copy.30
  192.2 1.0 reshape.45
  193.3 4.0 %fusion.19 = f32[96,1024]{1,0:T(8,128)S(1)} fusion(bf16[96,3072]{1,0:T(8,128)(2,1)S(1)} %reshape.45, bf16[3072,1024]{1,0:T(8,128)(2,1)} %all-gather.2.cloned.1.call-done), kind=kOutput, calls=%fused_computation.41 | convolution fusion | flops 603979776 | bytes 7274496 | tf_op jit(solution)/shard_map/dot_general | solution.py:17
  197.3 0.7 copy-done.9
  198.0 0.5 convolution_add_fusion
  198.5 1.0 copy.31
  199.5 1.3 maximum_bitcast_fusion
  200.8 0.5 reshape.46
  201.3 18.2 %all_to_all.26 = f32[32,1,2048]{2,1,0:T(1,128)S(1)} all-to-all(f32[32,1,2048]{2,1,0:T(1,128)S(1)} %reshape.46), channel_id=1, replica_groups=mesh['x'=4,'zh'=4,'core'=2,'y'=4,'zl'=2] {'x','zh','core'}, dimensions={0} | all-to-all | bytes 524288 | tf_op jit(solution)/shard_map/all_to_all | solution.py:25
  219.5 0.5 broadcast
  220.0 1.3 reduce
  221.3 0.3 reshape.47
  221.6 0.9 fusion.14
  222.5 0.3 copy.28
  222.8 0.9 squeeze.12
  223.7 0.9 fusion.15
  224.8 0.3 copy.27
  225.1 0.3 stack.55
  225.5 10.7 %all_to_all.27 = f32[8,3,4,1024]{3,2,1,0:T(4,128)S(1)} all-to-all(f32[8,3,4,1024]{3,2,1,0:T(4,128)S(1)} %copy.29), channel_id=1, replica_groups=mesh['x'=4,'zh'=4,'core'=2,'y'=4,'zl'=2] {'y','zl'}, dimensions={0} | all-to-all | bytes 786432 | tf_op jit(solution)/shard_map/all_to_all | solution.py:25
  236.3 0.6 fusion.6
  236.9 1.0 convolution_subtract_fusion
  (53 shorter events, 0.8 us)
Async XLA Ops:
  7.2 44.4 %copy-start = (bf16[1024,1024]{1,0:T(8,128)(2,1)S(1)}, bf16[1024,1024]{1,0:T(8,128)(2,1)}, u32[]{:S(2)}) copy-start(bf16[1024,1024]{1,0:T(8,128)(2,1)} %param.10) | copy-start | bytes 6291460
  7.2 90.5 %all-gather.2.cloned.1.call-start = ((), (), s32[]{:S(2)}) async-start(), calls=%async_computation.5 | async-start | bytes 6488064 | tf_op jit(solution)/shard_map/all_gather | solution.py:113
  7.9 43.7 %copy-start.5 = (bf16[1024,1024]{1,0:T(8,128)(2,1)S(1)}, bf16[1024,1024]{1,0:T(8,128)(2,1)}, u32[]{:S(2)}) copy-start(bf16[1024,1024]{1,0:T(8,128)(2,1)} %param.8) | copy-start | bytes 6291460
  7.9 13.1 %collective-permute-start = (bf16[96,1024]{1,0:T(8,128)(2,1)}, bf16[96,1024]{1,0:T(8,128)(2,1)S(1)}, u32[]{:S(2)}, u32[]{:S(2)}) collective-permute-start(bf16[96,1024]{1,0:T(8,128)(2,1)} %param.7), channel_id=1, source_target_pairs={{0,48},{16,0},{32,16},{48,32},{1,49},{17,1},{33,17},{49,33},{2,50}... | collective-permute-start | bytes 589832 | tf_op jit(solution)/shard_map/ppermute | solution.py:30
  14.9 9.1 %collective-permute-start.1 = (bf16[96,1024]{1,0:T(8,128)(2,1)}, bf16[96,1024]{1,0:T(8,128)(2,1)S(1)}, u32[]{:S(2)}, u32[]{:S(2)}) collective-permute-start(bf16[96,1024]{1,0:T(8,128)(2,1)} %param.7), channel_id=1, source_target_pairs={{0,16},{16,32},{32,48},{48,0},{1,17},{17,33},{33,49},{49,1},{2,18}... | collective-permute-start | bytes 589832 | tf_op jit(solution)/shard_map/ppermute | solution.py:30
  14.9 14.5 %collective-permute-start.2 = (bf16[96,1024]{1,0:T(8,128)(2,1)}, bf16[96,1024]{1,0:T(8,128)(2,1)S(1)}, u32[]{:S(2)}, u32[]{:S(2)}) collective-permute-start(bf16[96,1024]{1,0:T(8,128)(2,1)} %param.7), channel_id=1, source_target_pairs={{0,32},{16,48},{32,0},{48,16},{1,33},{17,49},{33,1},{49,17},{2,34}... | collective-permute-start | bytes 589832 | tf_op jit(solution)/shard_map/ppermute | solution.py:30
  29.4 20.5 %copy-start.3 = (bf16[384,1024]{1,0:T(8,128)(2,1)}, bf16[384,1024]{1,0:T(8,128)(2,1)S(1)}, u32[]{:S(2)}) copy-start(bf16[384,1024]{1,0:T(8,128)(2,1)S(1)} %constant_dynamic-update-slice_fusion.refs_0_) | copy-start | bytes 2359300
  29.4 17.1 %collective-permute-start.4 = (bf16[384,1024]{1,0:T(8,128)(2,1)S(1)}, bf16[384,1024]{1,0:T(8,128)(2,1)S(1)}, u32[]{:S(2)}, u32[]{:S(2)}) collective-permute-start(bf16[384,1024]{1,0:T(8,128)(2,1)S(1)} %constant_dynamic-update-slice_fusion.refs_0_), channel_id=1, source_target_pairs={{0,64},{64,128},{128,192},{192,0},{1,65},{65,129},{129,193},{193,1... | collective-permute-start | bytes 2359304 | tf_op jit(solution)/shard_map/ppermute | solution.py:30
  30.7 17.5 %collective-permute-start.3 = (bf16[384,1024]{1,0:T(8,128)(2,1)S(1)}, bf16[384,1024]{1,0:T(8,128)(2,1)S(1)}, u32[]{:S(2)}, u32[]{:S(2)}) collective-permute-start(bf16[384,1024]{1,0:T(8,128)(2,1)S(1)} %constant_dynamic-update-slice_fusion.refs_0_), channel_id=1, source_target_pairs={{0,192},{64,0},{128,64},{192,128},{1,193},{65,1},{129,65},{193,129... | collective-permute-start | bytes 2359304 | tf_op jit(solution)/shard_map/ppermute | solution.py:30
  47.2 18.5 %collective-permute-start.6 = (bf16[192,1024]{1,0:T(8,128)(2,1)}, bf16[192,1024]{1,0:T(8,128)(2,1)S(1)}, u32[]{:S(2)}, u32[]{:S(2)}) collective-permute-start(bf16[192,1024]{1,0:T(8,128)(2,1)} %slice.60), channel_id=1, source_target_pairs={{0,64},{64,128},{128,192},{192,0},{1,65},{65,129},{129,193},{193,1... | collective-permute-start | bytes 1179656 | tf_op jit(solution)/shard_map/ppermute | solution.py:30
  48.2 0.9 copy-start.1
  49.9 18.8 %collective-permute-start.5 = (bf16[192,1024]{1,0:T(8,128)(2,1)}, bf16[192,1024]{1,0:T(8,128)(2,1)}, u32[]{:S(2)}, u32[]{:S(2)}) collective-permute-start(bf16[192,1024]{1,0:T(8,128)(2,1)} %slice.59), channel_id=1, source_target_pairs={{0,192},{64,0},{128,64},{192,128},{1,193},{65,1},{129,65},{193,129... | collective-permute-start | bytes 1179656 | tf_op jit(solution)/shard_map/ppermute | solution.py:30
  55.4 13.2 %copy-start.6 = (bf16[1024,1024]{1,0:T(8,128)(2,1)S(1)}, bf16[1024,1024]{1,0:T(8,128)(2,1)}, u32[]{:S(2)}) copy-start(bf16[1024,1024]{1,0:T(8,128)(2,1)} %param.11) | copy-start | bytes 6291460
  55.4 13.8 %copy-start.7 = (bf16[1024,1024]{0,1:T(8,128)(2,1)S(1)}, bf16[1024,1024]{0,1:T(8,128)(2,1)}, u32[]{:S(2)}) copy-start(bf16[1024,1024]{0,1:T(8,128)(2,1)} %convolution_convert_fusion) | copy-start | bytes 6291460
  55.4 15.1 %collective-permute-start.7 = (bf16[384,1024]{1,0:T(8,128)(2,1)}, bf16[384,1024]{1,0:T(8,128)(2,1)S(1)}, u32[]{:S(2)}, u32[]{:S(2)}) collective-permute-start(bf16[384,1024]{1,0:T(8,128)(2,1)} %copy-done.3), channel_id=1, source_target_pairs={{0,8},{8,0},{1,9},{9,1},{2,10},{10,2},{3,11},{11,3},{4,12},{12,4},... | collective-permute-start | bytes 2359304 | tf_op jit(solution)/shard_map/ppermute | solution.py:30
  62.9 7.8 %collective-permute-start.8 = (bf16[384,1024]{1,0:T(8,128)(2,1)}, bf16[384,1024]{1,0:T(8,128)(2,1)S(1)}, u32[]{:S(2)}, u32[]{:S(2)}) collective-permute-start(bf16[384,1024]{1,0:T(8,128)(2,1)} %copy-done.1), channel_id=1, source_target_pairs={{0,8},{8,0},{1,9},{9,1},{2,10},{10,2},{3,11},{11,3},{4,12},{12,4},... | collective-permute-start | bytes 2359304 | tf_op jit(solution)/shard_map/ppermute | solution.py:30
  62.9 7.8 %collective-permute-start.9 = (bf16[384,1024]{1,0:T(8,128)(2,1)S(1)}, bf16[384,1024]{1,0:T(8,128)(2,1)S(1)}, u32[]{:S(2)}, u32[]{:S(2)}) collective-permute-start(bf16[384,1024]{1,0:T(8,128)(2,1)S(1)} %collective-permute-done.4.refs_2_), channel_id=1, source_target_pairs={{0,8},{8,0},{1,9},{9,1},{2,10},{10,2},{3,11},{11,3},{4,12},{12,4},... | collective-permute-start | bytes 2359304 | tf_op jit(solution)/shard_map/ppermute | solution.py:30
  65.7 5.9 %copy-start.2 = (bf16[384,1024]{1,0:T(8,128)(2,1)S(1)}, bf16[384,1024]{1,0:T(8,128)(2,1)}, u32[]{:S(2)}) copy-start(bf16[384,1024]{1,0:T(8,128)(2,1)} %copy-done.1) | copy-start | bytes 2359300
  65.7 5.9 %copy-start.4 = (bf16[384,1024]{1,0:T(8,128)(2,1)S(1)}, bf16[384,1024]{1,0:T(8,128)(2,1)}, u32[]{:S(2)}) copy-start(bf16[384,1024]{1,0:T(8,128)(2,1)} %copy-done.3) | copy-start | bytes 2359300
  65.7 4.8 %collective-permute-start.11 = (bf16[192,1024]{1,0:T(8,128)(2,1)S(1)}, bf16[192,1024]{1,0:T(8,128)(2,1)S(1)}, u32[]{:S(2)}, u32[]{:S(2)}) collective-permute-start(bf16[192,1024]{1,0:T(8,128)(2,1)S(1)} %collective-permute-done.6.refs_4_), channel_id=1, source_target_pairs={{0,8},{8,0},{1,9},{9,1},{2,10},{10,2},{3,11},{11,3},{4,12},{12,4},... | collective-permute-start | bytes 1179656 | tf_op jit(solution)/shard_map/ppermute | solution.py:30
  68.6 2.1 collective-permute-start.10
  70.8 0.9 copy-start.15
  87.2 31.6 %all-to-all-start = ((bf16[8,96,1024]{2,1,0:T(8,128)(2,1)}), bf16[8,96,1024]{2,1,0:T(8,128)(2,1)}, u32[]{:S(2)}, u32[]{:S(2)}) async-start(bf16[8,96,1024]{2,1,0:T(8,128)(2,1)} %get-tuple-element.11), calls=%async_computation | async-start | bytes 3145728 | tf_op jit(solution)/shard_map/all_to_all | solution.py:25
  118.8 24.4 %all-to-all-start.1 = ((bf16[8,96,1024]{2,1,0:T(8,128)(2,1)}), bf16[8,96,1024]{2,1,0:T(8,128)(2,1)}, u32[]{:S(2)}, u32[]{:S(2)}) async-start(bf16[8,96,1024]{2,1,0:T(8,128)(2,1)} %bitcast.64), calls=%async_computation.1 | async-start | bytes 3145728 | tf_op jit(solution)/shard_map/all_to_all | solution.py:25
  190.5 0.7 copy-start.11
  193.3 4.7 %copy-start.12 = (f32[64,1024]{1,0:T(8,128)S(1)}, f32[64,1024]{1,0:T(8,128)}, u32[]{:S(2)}) copy-start(f32[64,1024]{1,0:T(8,128)} %copy-done.11) | copy-start | bytes 786436
  197.2 0.8 copy-start.9
  221.6 2.1 copy-start.10
  222.5 2.2 copy-start.8
  224.8 11.5 %copy-start.13 = (f32[4,1024]{1,0:T(4,128)S(1)}, f32[4,1024]{1,0:T(4,128)}, u32[]{:S(2)}) copy-start(f32[4,1024]{1,0:T(4,128)} %convolution_add_fusion.1) | copy-start | bytes 49156
  236.9 1.0 copy-start.14
Sparse Core Ops, SparseCore 0:
  10.6 76.4 all-gather.1

commit v5 on v4

--- a/solution.py
+++ b/solution.py
@@ -43,63 +43,119 @@
     return [a, after, before, shift(after[:half], axis, -1), shift(before[half:], axis, 1)]
 
 
+def lay_out(where, mine, others, panel, sems):
+    rows = mine[0].shape[0] // 4
+    for k, dx in enumerate((0, 1, 3, 2, 2)):
+        for pieces, core in ((mine, where[2]), (others, 1 - where[2])):
+            for n in range(pieces[k].shape[0] // rows):
+                dz = RING[n + (2 if k == 4 else 0)]
+                at = lax.rem(where[0] + dx, 4) * 4 + lax.rem(where[1] + dz, 4)
+                at = pl.multiple_of((at * 2 + core) * rows, 32)
+                pltpu.make_async_copy(
+                    pieces[k].at[pl.ds(n * rows, rows)],
+                    panel.at[pl.ds(at, rows)],
+                    sems.at[RING.index(dx)],
+                ).start()
+
+
+def ring_block(step, where):
+    return lax.rem(where[0] + jnp.where(step < 2, step, 5 - step), 4)
+
+
 def product_kernel(where, *refs):
-    mine, others = refs[:5], refs[5:10]
-    z, out, panel_out, panel, sem, out_sem = refs[10:]
-    step = pl.program_id(0)
-    rows = mine[0].shape[0] // 4
-    keep = pltpu.make_async_copy(panel, panel_out, out_sem)
-
-    @pl.when(step == 0)
-    def _():
-        for pieces, core in ((mine, where[2]), (others, 1 - where[2])):
-            for k, dx in enumerate((0, 1, 3, 2, 2)):
-                for n in range(pieces[k].shape[0] // rows):
-                    dz = RING[n + (2 if k == 4 else 0)]
-                    at = lax.rem(where[0] + dx, 4) * 4 + lax.rem(where[1] + dz, 4)
-                    at = pl.multiple_of((at * 2 + core) * rows, 32)
-                    pltpu.make_async_copy(
-                        pieces[k].at[pl.ds(n * rows, rows)], panel.at[pl.ds(at, rows)], sem
-                    ).start()
-        pltpu.make_async_copy(panel, panel, sem).wait()
-        keep.start()
-
-    out[...] = jnp.dot(z[...], panel[...], preferred_element_type=F32).astype(BF).reshape(out.shape)
-
-    @pl.when(step == pl.num_programs(0) - 1)
-    def _():
-        keep.wait()
+    z, out, panel, zcols, acc, result, sems, zsems, out_sem = refs[10:]
+    depth = panel.shape[0] // 4
+
+    def block(step):
+        return pl.ds(pl.multiple_of(ring_block(step, where) * depth, 256), depth)
+
+    zcopies = [
+        pltpu.make_async_copy(z.at[:, block(step)], zcols.at[step], zsems.at[step]) for step in range(4)
+    ]
+    for copy in zcopies:
+        copy.start()
+    lay_out(where, refs[:5], refs[5:10], panel, sems)
+    for step in range(4):
+        part = panel.at[block(step)]
+        zcopies[step].wait()
+        pltpu.make_async_copy(part, part, sems.at[step]).wait()
+        got = jnp.dot(zcols[step], part[...], preferred_element_type=F32)
+        if step == 0:
+            acc[...] = got
+        elif step < 3:
+            acc[...] += got
+        else:
+            result[...] = (acc[...] + got).astype(BF).reshape(result.shape)
+    copy = pltpu.make_async_copy(result, out, out_sem)
+    copy.start()
+    copy.wait()
 
 
 def product(where, mine, others, z, rows):
     depth, width = z.shape[1], mine[0].shape[1]
-    steps = 2
-    block = z.shape[0] // steps
-    any_ = pl.BlockSpec(memory_space=pl.ANY)
+    hbm = pl.BlockSpec(memory_space=pltpu.HBM)
+    blocks = (z.shape[0] // rows, rows, width)
     return pl.pallas_call(
         product_kernel,
         grid_spec=pltpu.PrefetchScalarGridSpec(
             num_scalar_prefetch=1,
-            grid=(steps,),
-            in_specs=[any_] * 10 + [pl.BlockSpec((block, depth), lambda i, w: (i, 0))],
-            out_specs=[pl.BlockSpec((block // rows, rows, width), lambda i, w: (i, 0, 0)), any_],
+            grid=(),
+            in_specs=[hbm] * 11,
+            out_specs=hbm,
             scratch_shapes=[
                 pltpu.VMEM((depth, width), BF),
-                pltpu.SemaphoreType.DMA(()),
+                pltpu.VMEM((4, z.shape[0], depth // 4), BF),
+                pltpu.VMEM((z.shape[0], width), F32),
+                pltpu.VMEM(blocks, BF),
+                pltpu.SemaphoreType.DMA((4,)),
+                pltpu.SemaphoreType.DMA((4,)),
                 pltpu.SemaphoreType.DMA(()),
             ],
         ),
-        out_shape=[
-            jax.ShapeDtypeStruct((z.shape[0] // rows, rows, width), BF),
-            jax.ShapeDtypeStruct((depth, width), BF),
-        ],
-        compiler_params=pltpu.CompilerParams(vmem_limit_bytes=48 << 20),
+        out_shape=jax.ShapeDtypeStruct(blocks, BF),
+        compiler_params=pltpu.CompilerParams(vmem_limit_bytes=60 << 20),
         cost_estimate=pl.CostEstimate(
             flops=2 * z.size * width,
             transcendentals=0,
-            bytes_accessed=2 * z.size + 6 * depth * width + 2 * z.shape[0] * width,
+            bytes_accessed=2 * z.size + 2 * depth * width + 2 * z.shape[0] * width,
         ),
     )(where, *mine, *others, z)
+
+
+def panel_kernel(where, *refs):
+    out, panel, sems, out_sem = refs[10:]
+    depth = panel.shape[0] // 4
+    lay_out(where, refs[:5], refs[5:10], panel, sems)
+    copies = []
+    for step in range(4):
+        at = pl.ds(pl.multiple_of(ring_block(step, where) * depth, 256), depth)
+        pltpu.make_async_copy(panel.at[at], panel.at[at], sems.at[step]).wait()
+        copies.append(pltpu.make_async_copy(panel.at[at], out.at[at], out_sem.at[step]))
+        copies[-1].start()
+    for copy in copies:
+        copy.wait()
+
+
+def whole_panel(where, mine, others, depth):
+    width = mine[0].shape[1]
+    hbm = pl.BlockSpec(memory_space=pltpu.HBM)
+    return pl.pallas_call(
+        panel_kernel,
+        grid_spec=pltpu.PrefetchScalarGridSpec(
+            num_scalar_prefetch=1,
+            grid=(),
+            in_specs=[hbm] * 10,
+            out_specs=hbm,
+            scratch_shapes=[
+                pltpu.VMEM((depth, width), BF),
+                pltpu.SemaphoreType.DMA((4,)),
+                pltpu.SemaphoreType.DMA((4,)),
+            ],
+        ),
+        out_shape=jax.ShapeDtypeStruct((depth, width), BF),
+        compiler_params=pltpu.CompilerParams(vmem_limit_bytes=60 << 20),
+        cost_estimate=pl.CostEstimate(flops=0, transcendentals=0, bytes_accessed=4 * depth * width),
+    )(where, *mine, *others)
 
 
 def shards(z, pp, pdi, ca, cp, cdi):
@@ -121,13 +177,15 @@
     diag_lower = dot(cols(cdi), cdi, 0, 0) + dot(cols(diag_prod), diag_prod, 0, 0)
     others[-1], diag_upper, diag_lower = hold((others[-1], diag_upper, diag_lower))
 
-    up, parent = product(where, pieces, others, block, rows)
+    up = product(where, pieces, others, block, rows)
     upper = jnp.sum(exchange(up, COL).astype(F32), axis=0)
     u = upper.astype(BF)
     shifted = dot(u, cp)
     s = shifted.astype(BF)
 
     lp = dot(block, child).astype(BF).reshape(nc, rows, w)
+    others[0], lp = hold((others[0], lp))
+    parent = whole_panel(where, pieces, others, block.shape[1])
     lower = jnp.sum(exchange(lp, COL).astype(F32), axis=0)
     anc = lower - shifted
     a = anc.astype(BF)

time: 245 us -> 251 us (1.024)
  blocking collectives: 66.2 us -> 29.2 us
  waiting for transfers between devices: 54.6 us -> 71.8 us
  starting transfers between devices: 41.3 us -> 55.9 us
  local copies, waits for them, and re-layouts: 15.8 us -> 24.1 us
    all_to_all x3 -> x2, blocking collectives: 66.2 us -> 29.2 us  [exchange(): return lax.all_to_all(a, axes, 0, 0, tiled=True)]
    all_to_all x2 -> x3, waiting for transfers between devices: 29.1 us -> 46.6 us  [exchange(): return lax.all_to_all(a, axes, 0, 0, tiled=True)]
    all_to_all x2 -> x3, starting transfers between devices: 14.7 us -> 26 us  [exchange(): return lax.all_to_all(a, axes, 0, 0, tiled=True)]
    pallas_call x0 -> x1, Pallas kernels: none -> 6.04 us  [whole_panel(): pl.pallas_call(panel_kernel, grid_spec=pltpu.PrefetchScalarGridSpec(num_s...]
    pallas_call x1, Pallas kernels: 15.6 us -> 10.6 us  [product(): pl.pallas_call(product_kernel, grid_spec=pltpu.PrefetchScalarGridSpec(num...]
    ppermute x12, starting transfers between devices: 26.6 us -> 29.8 us  [shift(): return lax.ppermute(a, axis, [(i, (i + by) % n) for i in range(n)])]
    unnamed x37 -> x39, local copies, waits for them, and re-layouts: 5.06 us -> 7.85 us
  transfers between devices with their start and end apart: 15 -> 16, of which waited for: 7 -> 7; matrix products, arithmetic and copies ran while one was open for 9% -> 9% of each run, Pallas kernels for 6% -> 7%
where the time goes in v5:
time: 251 us; the launch traced here: 250 us
  waiting for transfers between devices  71.8 us (29%)
  starting transfers between devices  55.9 us (22%)
  blocking collectives  29.2 us (12%)
  matrix products  27.9 us (11%)
  local copies, waits for them, and re-layouts  24.1 us (10%)
  Pallas kernels  16.6 us (7%)
  between operations  14.3 us (6%)
  other arithmetic  10.1 us (4%)
    all_to_all x3, waiting for transfers between devices, exchange(): return lax.all_to_all(a, axes, 0, 0, tiled=True)  46.6 us
    ppermute x12, starting transfers between devices, shift(): return lax.ppermute(a, axis, [(i, (i + by) % n) for i in range(n)])  29.8 us
    all_to_all x2, blocking collectives, exchange(): return lax.all_to_all(a, axes, 0, 0, tiled=True)  29.2 us
    dot_general x10, matrix products, dot(): lax.dot_general(a, b, (((ca,), (cb,)), ((), ())), preferred_element_type=...  27.9 us
    all_to_all x3, starting transfers between devices, exchange(): return lax.all_to_all(a, axes, 0, 0, tiled=True)  26 us
    ppermute x12, waiting for transfers between devices, shift(): return lax.ppermute(a, axis, [(i, (i + by) % n) for i in range(n)])  24.5 us
    pallas_call x1, Pallas kernels, product(): pl.pallas_call(product_kernel, grid_spec=pltpu.PrefetchScalarGridSpec(num...  10.6 us
    unnamed x39, local copies, waits for them, and re-layouts  7.85 us
  transfers between devices with their start and end apart: 16, of which 7 were waited for; matrix products, arithmetic and copies ran while one was open for 9% of the time, Pallas kernels for 7%

profile of v5, /device:TPU:1, one launch (start us, length us, event | category | flops | bytes accessed | tf_op | source)
XLA Modules:
  0.0 249.9 jit_solution(17953484377971373601)
XLA Ops:
  7.2 0.7 all-gather.2.cloned.1.call-update
  7.9 6.9 %collective-permute-start = (bf16[96,1024]{1,0:T(8,128)(2,1)}, bf16[96,1024]{1,0:T(8,128)(2,1)S(1)}, u32[]{:S(2)}, u32[]{:S(2)}) collective-permute-start(bf16[96,1024]{1,0:T(8,128)(2,1)} %param.7), channel_id=1, source_target_pairs={{0,48},{16,0},{32,16},{48,32},{1,49},{17,1},{33,17},{49,33},{2,50}... | collective-permute-start | bytes 589832 | tf_op jit(solution)/shard_map/ppermute | solution.py:30
  14.9 3.3 %collective-permute-start.2 = (bf16[96,1024]{1,0:T(8,128)(2,1)}, bf16[96,1024]{1,0:T(8,128)(2,1)S(1)}, u32[]{:S(2)}, u32[]{:S(2)}) collective-permute-start(bf16[96,1024]{1,0:T(8,128)(2,1)} %param.7), channel_id=1, source_target_pairs={{0,32},{16,48},{32,0},{48,16},{1,33},{17,49},{33,1},{49,17},{2,34}... | collective-permute-start | bytes 589832 | tf_op jit(solution)/shard_map/ppermute | solution.py:30
  18.1 1.0 constant_dynamic-update-slice_fusion.3
  19.1 1.9 collective-permute-done
  21.0 2.9 %collective-permute-done.1 = bf16[96,1024]{1,0:T(8,128)(2,1)S(1)} collective-permute-done((bf16[96,1024]{1,0:T(8,128)(2,1)}, bf16[96,1024]{1,0:T(8,128)(2,1)S(1)}, u32[]{:S(2)}, u32[]{:S(2)}) %collective-permute-start.1) | collective-permute-done | bytes 196640 | tf_op jit(solution)/shard_map/ppermute | solution.py:30
  23.9 5.5 %collective-permute-done.2 = bf16[96,1024]{1,0:T(8,128)(2,1)S(1)} collective-permute-done((bf16[96,1024]{1,0:T(8,128)(2,1)}, bf16[96,1024]{1,0:T(8,128)(2,1)S(1)}, u32[]{:S(2)}, u32[]{:S(2)}) %collective-permute-start.2) | collective-permute-done | bytes 196640 | tf_op jit(solution)/shard_map/ppermute | solution.py:30
  29.4 2.6 %collective-permute-start.3 = (bf16[384,1024]{1,0:T(8,128)(2,1)S(1)}, bf16[384,1024]{1,0:T(8,128)(2,1)S(1)}, u32[]{:S(2)}, u32[]{:S(2)}) collective-permute-start(bf16[384,1024]{1,0:T(8,128)(2,1)S(1)} %constant_dynamic-update-slice_fusion.refs_0_), channel_id=1, source_target_pairs={{0,192},{64,0},{128,64},{192,128},{1,193},{65,1},{129,65},{193,129... | collective-permute-start | bytes 2359304 | tf_op jit(solution)/shard_map/ppermute | solution.py:30
  32.0 14.2 %collective-permute-done.3.refs_1_ = bf16[384,1024]{1,0:T(8,128)(2,1)S(1)} collective-permute-done((bf16[384,1024]{1,0:T(8,128)(2,1)S(1)}, bf16[384,1024]{1,0:T(8,128)(2,1)S(1)}, u32[]{:S(2)}, u32[]{:S(2)}) %collective-permute-start.3) | collective-permute-done | bytes 786464 | tf_op jit(solution)/shard_map/ppermute | solution.py:30
  46.2 0.8 slice.59
  47.0 3.4 %collective-permute-start.5 = (bf16[192,1024]{1,0:T(8,128)(2,1)}, bf16[192,1024]{1,0:T(8,128)(2,1)S(1)}, u32[]{:S(2)}, u32[]{:S(2)}) collective-permute-start(bf16[192,1024]{1,0:T(8,128)(2,1)} %slice.59), channel_id=1, source_target_pairs={{0,192},{64,0},{128,64},{192,128},{1,193},{65,1},{129,65},{193,129... | collective-permute-start | bytes 1179656 | tf_op jit(solution)/shard_map/ppermute | solution.py:30
  50.4 0.9 copy-done.6
  51.3 0.8 slice.60
  52.1 3.8 %convolution_convert_fusion = bf16[1024,1024]{0,1:T(8,128)(2,1)} fusion(bf16[1024,1024]{1,0:T(8,128)(2,1)S(1)} %copy-done.1, bf16[1024,1024]{1,0:T(8,128)(2,1)S(1)} %copy-done), kind=kOutput, calls=%fused_computation.2 | convolution fusion | flops 2148532224 | bytes 6291456 | tf_op jit(solution)/shard_map/dot_general | solution.py:17
  55.9 5.9 %collective-permute-start.7 = (bf16[384,1024]{1,0:T(8,128)(2,1)}, bf16[384,1024]{1,0:T(8,128)(2,1)S(1)}, u32[]{:S(2)}, u32[]{:S(2)}) collective-permute-start(bf16[384,1024]{1,0:T(8,128)(2,1)} %copy-done.7), channel_id=1, source_target_pairs={{0,8},{8,0},{1,9},{9,1},{2,10},{10,2},{3,11},{11,3},{4,12},{12,4},... | collective-permute-start | bytes 2359304 | tf_op jit(solution)/shard_map/ppermute | solution.py:30
  61.9 0.4 collective-permute-start.9
  62.3 2.2 fusion.2
  64.5 2.6 %collective-permute-start.10 = (bf16[192,1024]{1,0:T(8,128)(2,1)S(1)}, bf16[192,1024]{1,0:T(8,128)(2,1)S(1)}, u32[]{:S(2)}, u32[]{:S(2)}) collective-permute-start(bf16[192,1024]{1,0:T(8,128)(2,1)S(1)} %collective-permute-done.5.refs_3_), channel_id=1, source_target_pairs={{0,8},{8,0},{1,9},{9,1},{2,10},{10,2},{3,11},{11,3},{4,12},{12,4},... | collective-permute-start | bytes 1179656 | tf_op jit(solution)/shard_map/ppermute | solution.py:30
  67.1 4.7 %collective-permute-start.11 = (bf16[192,1024]{1,0:T(8,128)(2,1)}, bf16[192,1024]{1,0:T(8,128)(2,1)S(1)}, u32[]{:S(2)}, u32[]{:S(2)}) collective-permute-start(bf16[192,1024]{1,0:T(8,128)(2,1)} %collective-permute-done.6.refs_4_), channel_id=1, source_target_pairs={{0,8},{8,0},{1,9},{9,1},{2,10},{10,2},{3,11},{11,3},{4,12},{12,4},... | collective-permute-start | bytes 1179656 | tf_op jit(solution)/shard_map/ppermute | solution.py:30
  71.8 0.5 fusion
  72.3 0.7 pad_add_fusion.where
  72.9 1.3 convolution_add_fusion.1
  74.2 0.9 copy-done.8
  75.2 0.9 copy-done.9
  76.1 0.9 copy-done.10
  77.0 0.7 copy-done.13
  77.7 10.6 %shard_map.101 = bf16[8,96,1024]{2,1,0:T(8,128)(2,1)} custom-call(s32[3]{0:T(128)} %pad_add_fusion.where, bf16[384,1024]{1,0:T(8,128)(2,1)} %copy-done.7, bf16[384,1024]{1,0:T(8,128)(2,1)} %copy-done.5, bf16[384,1024]{1,0:T(8,128)(2,1)} %copy-done.6, bf16[192,1024]{1,0:T(8,128)(2,1)} %copy-done.12, bf16[192,1024]{1,0:T(8,128)(2,1)} %collective-permute-done.6.refs_4_, ...), custom_call_target="tpu_custom_call" | custom-call | flops 4831838208 | bytes 12582912 | tf_op jit(solution)/shard_map/pallas_call | solution.py:98
  88.3 10.4 %all-to-all-start = ((bf16[8,96,1024]{2,1,0:T(8,128)(2,1)}), bf16[8,96,1024]{2,1,0:T(8,128)(2,1)}, u32[]{:S(2)}, u32[]{:S(2)}) async-start(bf16[8,96,1024]{2,1,0:T(8,128)(2,1)} %shard_map.101), calls=%async_computation | async-start | bytes 3145728 | tf_op jit(solution)/shard_map/all_to_all | solution.py:25
  98.7 9.5 %convolution_convert_fusion.1 = bf16[768,1024]{1,0:T(8,128)(2,1)} fusion(bf16[3072,1024]{1,0:T(8,128)(2,1)} %all-gather.2.cloned.1.call-done, bf16[768,1,3072]{2,0,1:T(8,128)(2,1)} %param.6), kind=kOutput, calls=%fused_computation.3 | convolution fusion | flops 4832624640 | bytes 12582912 | tf_op jit(solution)/shard_map/dot_general | solution.py:17
  108.2 11.8 %all-to-all-done = bf16[8,96,1024]{2,1,0:T(8,128)(2,1)} async-done(((bf16[8,96,1024]{2,1,0:T(8,128)(2,1)}), bf16[8,96,1024]{2,1,0:T(8,128)(2,1)}, u32[]{:S(2)}, u32[]{:S(2)}) %all-to-all-start) | async-done | bytes 1572896 | tf_op jit(solution)/shard_map/all_to_all | solution.py:25
  120.0 4.3 %all-to-all-start.1 = ((bf16[8,96,1024]{2,1,0:T(8,128)(2,1)}), bf16[8,96,1024]{2,1,0:T(8,128)(2,1)}, u32[]{:S(2)}, u32[]{:S(2)}) async-start(bf16[8,96,1024]{2,1,0:T(8,128)(2,1)} %bitcast.64), calls=%async_computation.1 | async-start | bytes 3145728 | tf_op jit(solution)/shard_map/all_to_all | solution.py:25
  124.3 1.7 convert_reduce_fusion.1
  126.1 0.8 convert_bitcast_fusion.2
  127.0 17.6 %all-to-all-done.1 = bf16[8,96,1024]{2,1,0:T(8,128)(2,1)} async-done(((bf16[8,96,1024]{2,1,0:T(8,128)(2,1)}), bf16[8,96,1024]{2,1,0:T(8,128)(2,1)}, u32[]{:S(2)}, u32[]{:S(2)}) %all-to-all-start.1) | async-done | bytes 1572896 | tf_op jit(solution)/shard_map/all_to_all | solution.py:25
  144.6 1.7 convert_reduce_fusion
  146.4 1.2 subtract_negate_fusion
  148.2 1.0 copy.22
  149.1 11.3 %all-to-all-start.2 = ((bf16[32,3,32,96]{3,2,1,0:T(8,128)(2,1)}), bf16[32,3,32,96]{3,2,1,0:T(8,128)(2,1)S(1)}, u32[]{:S(2)}, u32[]{:S(2)}) async-start(bf16[32,3,32,96]{3,2,1,0:T(8,128)(2,1)} %copy.22), calls=%async_computation.2 | async-start | bytes 1572864 | tf_op jit(solution)/shard_map/all_to_all | solution.py:25
  160.5 6.0 %shard_map.102 = bf16[3072,1024]{1,0:T(8,128)(2,1)} custom-call(s32[3]{0:T(128)} %pad_add_fusion.where, bf16[384,1024]{1,0:T(8,128)(2,1)} %copy-done.7, bf16[384,1024]{1,0:T(8,128)(2,1)} %copy-done.5, bf16[384,1024]{1,0:T(8,128)(2,1)} %copy-done.6, bf16[192,1024]{1,0:T(8,128)(2,1)} %copy-done.12, bf16[192,1024]{1,0:T(8,128)(2,1)} %collective-permute-done.6.refs_4_, ...), custom_call_target="tpu_custom_call" | custom-call | bytes 12582912 | tf_op jit(solution)/shard_map/pallas_call | solution.py:142
  166.5 17.1 %all-to-all-done.2 = bf16[32,3,32,96]{3,2,1,0:T(8,128)(2,1)S(1)} async-done(((bf16[32,3,32,96]{3,2,1,0:T(8,128)(2,1)}), bf16[32,3,32,96]{3,2,1,0:T(8,128)(2,1)S(1)}, u32[]{:S(2)}, u32[]{:S(2)}) %all-to-all-start.2) | async-done | bytes 589856 | tf_op jit(solution)/shard_map/all_to_all | solution.py:25
  183.7 1.2 copy.24
  184.9 0.9 slice.61
  185.8 2.2 reshape.45
  188.0 1.4 copy.23
  189.4 1.5 slice.48
  190.9 4.1 %fusion.18 = f32[64,1024]{1,0:T(8,128)S(1)} fusion(bf16[64,3072]{1,0:T(8,128)(2,1)} %slice.48, bf16[3072,1024]{1,0:T(8,128)(2,1)} %shard_map.102), kind=kOutput, calls=%fused_computation.40 | convolution fusion | flops 402653184 | bytes 6946816 | tf_op jit(solution)/shard_map/dot_general | solution.py:17
  195.0 0.7 slice.62
  195.7 3.9 %fusion.19 = f32[96,1024]{1,0:T(8,128)S(1)} fusion(bf16[96,3072]{1,0:T(8,128)(2,1)S(1)} %reshape.45, bf16[3072,1024]{1,0:T(8,128)(2,1)} %all-gather.2.cloned.1.call-done), kind=kOutput, calls=%fused_computation.41 | convolution fusion | flops 603979776 | bytes 7274496 | tf_op jit(solution)/shard_map/dot_general | solution.py:17
  199.6 0.5 convolution_add_fusion
  200.1 1.0 copy.31
  201.1 1.0 copy.30
  202.1 1.3 maximum_bitcast_fusion
  203.4 1.2 reshape.46
  204.6 18.4 %all_to_all.25 = f32[32,1,2048]{2,1,0:T(1,128)S(1)} all-to-all(f32[32,1,2048]{2,1,0:T(1,128)} %reshape.46), channel_id=1, replica_groups=mesh['x'=4,'zh'=4,'core'=2,'y'=4,'zl'=2] {'x','zh','core'}, dimensions={0} | all-to-all | bytes 524288 | tf_op jit(solution)/shard_map/all_to_all | solution.py:25
  223.0 0.5 broadcast
  223.6 2.0 reduce
  225.5 1.3 reshape.47
  226.8 0.9 fusion.14
  228.0 0.9 squeeze.12
  228.9 0.9 fusion.15
  230.0 0.3 copy.27
  230.7 10.7 %all_to_all.26 = f32[8,3,4,1024]{3,2,1,0:T(4,128)S(1)} all-to-all(f32[8,3,4,1024]{3,2,1,0:T(4,128)S(1)} %copy.29), channel_id=1, replica_groups=mesh['x'=4,'zh'=4,'core'=2,'y'=4,'zl'=2] {'y','zl'}, dimensions={0} | all-to-all | bytes 786432 | tf_op jit(solution)/shard_map/all_to_all | solution.py:25
  241.5 0.6 fusion.6
  242.1 1.0 convolution_subtract_fusion
  (57 shorter events, 1.8 us)
Async XLA Ops:
  7.2 44.9 %copy-start = (bf16[1024,1024]{1,0:T(8,128)(2,1)S(1)}, bf16[1024,1024]{1,0:T(8,128)(2,1)}, u32[]{:S(2)}) copy-start(bf16[1024,1024]{1,0:T(8,128)(2,1)} %param.10) | copy-start | bytes 6291460
  7.2 91.6 %all-gather.2.cloned.1.call-start = ((), (), s32[]{:S(2)}) async-start(), calls=%async_computation.5 | async-start | bytes 6488064 | tf_op jit(solution)/shard_map/all_gather | solution.py:169
  7.9 44.2 %copy-start.1 = (bf16[1024,1024]{1,0:T(8,128)(2,1)S(1)}, bf16[1024,1024]{1,0:T(8,128)(2,1)}, u32[]{:S(2)}) copy-start(bf16[1024,1024]{1,0:T(8,128)(2,1)} %param.8) | copy-start | bytes 6291460
  7.9 13.1 %collective-permute-start = (bf16[96,1024]{1,0:T(8,128)(2,1)}, bf16[96,1024]{1,0:T(8,128)(2,1)S(1)}, u32[]{:S(2)}, u32[]{:S(2)}) collective-permute-start(bf16[96,1024]{1,0:T(8,128)(2,1)} %param.7), channel_id=1, source_target_pairs={{0,48},{16,0},{32,16},{48,32},{1,49},{17,1},{33,17},{49,33},{2,50}... | collective-permute-start | bytes 589832 | tf_op jit(solution)/shard_map/ppermute | solution.py:30
  14.9 9.1 %collective-permute-start.1 = (bf16[96,1024]{1,0:T(8,128)(2,1)}, bf16[96,1024]{1,0:T(8,128)(2,1)S(1)}, u32[]{:S(2)}, u32[]{:S(2)}) collective-permute-start(bf16[96,1024]{1,0:T(8,128)(2,1)} %param.7), channel_id=1, source_target_pairs={{0,16},{16,32},{32,48},{48,0},{1,17},{17,33},{33,49},{49,1},{2,18}... | collective-permute-start | bytes 589832 | tf_op jit(solution)/shard_map/ppermute | solution.py:30
  14.9 14.5 %collective-permute-start.2 = (bf16[96,1024]{1,0:T(8,128)(2,1)}, bf16[96,1024]{1,0:T(8,128)(2,1)S(1)}, u32[]{:S(2)}, u32[]{:S(2)}) collective-permute-start(bf16[96,1024]{1,0:T(8,128)(2,1)} %param.7), channel_id=1, source_target_pairs={{0,32},{16,48},{32,0},{48,16},{1,33},{17,49},{33,1},{49,17},{2,34}... | collective-permute-start | bytes 589832 | tf_op jit(solution)/shard_map/ppermute | solution.py:30
  29.4 22.7 %copy-start.7 = (bf16[384,1024]{1,0:T(8,128)(2,1)}, bf16[384,1024]{1,0:T(8,128)(2,1)S(1)}, u32[]{:S(2)}) copy-start(bf16[384,1024]{1,0:T(8,128)(2,1)S(1)} %constant_dynamic-update-slice_fusion.refs_0_) | copy-start | bytes 2359300
  29.4 16.8 %collective-permute-start.3 = (bf16[384,1024]{1,0:T(8,128)(2,1)S(1)}, bf16[384,1024]{1,0:T(8,128)(2,1)S(1)}, u32[]{:S(2)}, u32[]{:S(2)}) collective-permute-start(bf16[384,1024]{1,0:T(8,128)(2,1)S(1)} %constant_dynamic-update-slice_fusion.refs_0_), channel_id=1, source_target_pairs={{0,192},{64,0},{128,64},{192,128},{1,193},{65,1},{129,65},{193,129... | collective-permute-start | bytes 2359304 | tf_op jit(solution)/shard_map/ppermute | solution.py:30
  32.0 18.4 %collective-permute-start.4 = (bf16[384,1024]{1,0:T(8,128)(2,1)S(1)}, bf16[384,1024]{1,0:T(8,128)(2,1)S(1)}, u32[]{:S(2)}, u32[]{:S(2)}) collective-permute-start(bf16[384,1024]{1,0:T(8,128)(2,1)S(1)} %constant_dynamic-update-slice_fusion.refs_0_), channel_id=1, source_target_pairs={{0,64},{64,128},{128,192},{192,0},{1,65},{65,129},{129,193},{193,1... | collective-permute-start | bytes 2359304 | tf_op jit(solution)/shard_map/ppermute | solution.py:30
  46.2 15.6 %copy-start.5 = (bf16[384,1024]{1,0:T(8,128)(2,1)}, bf16[384,1024]{1,0:T(8,128)(2,1)S(1)}, u32[]{:S(2)}) copy-start(bf16[384,1024]{1,0:T(8,128)(2,1)S(1)} %collective-permute-done.3.refs_1_) | copy-start | bytes 2359300
  47.0 17.5 %collective-permute-start.5 = (bf16[192,1024]{1,0:T(8,128)(2,1)}, bf16[192,1024]{1,0:T(8,128)(2,1)S(1)}, u32[]{:S(2)}, u32[]{:S(2)}) collective-permute-start(bf16[192,1024]{1,0:T(8,128)(2,1)} %slice.59), channel_id=1, source_target_pairs={{0,192},{64,0},{128,64},{192,128},{1,193},{65,1},{129,65},{193,129... | collective-permute-start | bytes 1179656 | tf_op jit(solution)/shard_map/ppermute | solution.py:30
  50.4 0.9 copy-start.6
  52.1 15.0 %collective-permute-start.6 = (bf16[192,1024]{1,0:T(8,128)(2,1)}, bf16[192,1024]{1,0:T(8,128)(2,1)}, u32[]{:S(2)}, u32[]{:S(2)}) collective-permute-start(bf16[192,1024]{1,0:T(8,128)(2,1)} %slice.60), channel_id=1, source_target_pairs={{0,64},{64,128},{128,192},{192,0},{1,65},{65,129},{129,193},{193,1... | collective-permute-start | bytes 1179656 | tf_op jit(solution)/shard_map/ppermute | solution.py:30
  55.9 15.9 %copy-start.2 = (bf16[1024,1024]{1,0:T(8,128)(2,1)S(1)}, bf16[1024,1024]{1,0:T(8,128)(2,1)}, u32[]{:S(2)}) copy-start(bf16[1024,1024]{1,0:T(8,128)(2,1)} %param.11) | copy-start | bytes 6291460
  55.9 17.0 %copy-start.3 = (bf16[1024,1024]{0,1:T(8,128)(2,1)S(1)}, bf16[1024,1024]{0,1:T(8,128)(2,1)}, u32[]{:S(2)}) copy-start(bf16[1024,1024]{0,1:T(8,128)(2,1)} %convolution_convert_fusion) | copy-start | bytes 6291460
  55.9 18.3 %collective-permute-start.7 = (bf16[384,1024]{1,0:T(8,128)(2,1)}, bf16[384,1024]{1,0:T(8,128)(2,1)S(1)}, u32[]{:S(2)}, u32[]{:S(2)}) collective-permute-start(bf16[384,1024]{1,0:T(8,128)(2,1)} %copy-done.7), channel_id=1, source_target_pairs={{0,8},{8,0},{1,9},{9,1},{2,10},{10,2},{3,11},{11,3},{4,12},{12,4},... | collective-permute-start | bytes 2359304 | tf_op jit(solution)/shard_map/ppermute | solution.py:30
  61.8 12.4 %collective-permute-start.8 = (bf16[384,1024]{1,0:T(8,128)(2,1)S(1)}, bf16[384,1024]{1,0:T(8,128)(2,1)S(1)}, u32[]{:S(2)}, u32[]{:S(2)}) collective-permute-start(bf16[384,1024]{1,0:T(8,128)(2,1)S(1)} %collective-permute-done.3.refs_1_), channel_id=1, source_target_pairs={{0,8},{8,0},{1,9},{9,1},{2,10},{10,2},{3,11},{11,3},{4,12},{12,4},... | collective-permute-start | bytes 2359304 | tf_op jit(solution)/shard_map/ppermute | solution.py:30
  61.9 13.3 %collective-permute-start.9 = (bf16[384,1024]{1,0:T(8,128)(2,1)}, bf16[384,1024]{1,0:T(8,128)(2,1)S(1)}, u32[]{:S(2)}, u32[]{:S(2)}) collective-permute-start(bf16[384,1024]{1,0:T(8,128)(2,1)} %copy-done.6), channel_id=1, source_target_pairs={{0,8},{8,0},{1,9},{9,1},{2,10},{10,2},{3,11},{11,3},{4,12},{12,4},... | collective-permute-start | bytes 2359304 | tf_op jit(solution)/shard_map/ppermute | solution.py:30
  64.5 9.7 %copy-start.12 = (bf16[192,1024]{1,0:T(8,128)(2,1)}, bf16[192,1024]{1,0:T(8,128)(2,1)S(1)}, u32[]{:S(2)}) copy-start(bf16[192,1024]{1,0:T(8,128)(2,1)S(1)} %collective-permute-done.5.refs_3_) | copy-start | bytes 1179652
  64.5 11.6 %collective-permute-start.10 = (bf16[192,1024]{1,0:T(8,128)(2,1)S(1)}, bf16[192,1024]{1,0:T(8,128)(2,1)S(1)}, u32[]{:S(2)}, u32[]{:S(2)}) collective-permute-start(bf16[192,1024]{1,0:T(8,128)(2,1)S(1)} %collective-permute-done.5.refs_3_), channel_id=1, source_target_pairs={{0,8},{8,0},{1,9},{9,1},{2,10},{10,2},{3,11},{11,3},{4,12},{12,4},... | collective-permute-start | bytes 1179656 | tf_op jit(solution)/shard_map/ppermute | solution.py:30
  67.1 7.1 %collective-permute-start.11 = (bf16[192,1024]{1,0:T(8,128)(2,1)}, bf16[192,1024]{1,0:T(8,128)(2,1)S(1)}, u32[]{:S(2)}, u32[]{:S(2)}) collective-permute-start(bf16[192,1024]{1,0:T(8,128)(2,1)} %collective-permute-done.6.refs_4_), channel_id=1, source_target_pairs={{0,8},{8,0},{1,9},{9,1},{2,10},{10,2},{3,11},{11,3},{4,12},{12,4},... | collective-permute-start | bytes 1179656 | tf_op jit(solution)/shard_map/ppermute | solution.py:30
  74.2 1.9 copy-start.14
  74.2 0.9 copy-start.8
  75.2 0.9 copy-start.9
  76.1 0.9 copy-start.10
  77.0 0.7 copy-start.13
  88.3 31.7 %all-to-all-start = ((bf16[8,96,1024]{2,1,0:T(8,128)(2,1)}), bf16[8,96,1024]{2,1,0:T(8,128)(2,1)}, u32[]{:S(2)}, u32[]{:S(2)}) async-start(bf16[8,96,1024]{2,1,0:T(8,128)(2,1)} %shard_map.101), calls=%async_computation | async-start | bytes 3145728 | tf_op jit(solution)/shard_map/all_to_all | solution.py:25
  120.0 24.6 %all-to-all-start.1 = ((bf16[8,96,1024]{2,1,0:T(8,128)(2,1)}), bf16[8,96,1024]{2,1,0:T(8,128)(2,1)}, u32[]{:S(2)}, u32[]{:S(2)}) async-start(bf16[8,96,1024]{2,1,0:T(8,128)(2,1)} %bitcast.64), calls=%async_computation.1 | async-start | bytes 3145728 | tf_op jit(solution)/shard_map/all_to_all | solution.py:25
  149.1 34.5 %all-to-all-start.2 = ((bf16[32,3,32,96]{3,2,1,0:T(8,128)(2,1)}), bf16[32,3,32,96]{3,2,1,0:T(8,128)(2,1)S(1)}, u32[]{:S(2)}, u32[]{:S(2)}) async-start(bf16[32,3,32,96]{3,2,1,0:T(8,128)(2,1)} %copy.22), calls=%async_computation.2 | async-start | bytes 1572864 | tf_op jit(solution)/shard_map/all_to_all | solution.py:25
  199.6 1.5 copy-start.11
  227.7 2.2 copy-start.4
  230.0 11.5 %copy-start.15 = (f32[4,1024]{1,0:T(4,128)S(1)}, f32[4,1024]{1,0:T(4,128)}, u32[]{:S(2)}) copy-start(f32[4,1024]{1,0:T(4,128)} %convolution_add_fusion.1) | copy-start | bytes 49156
  242.1 1.0 copy-start.16
Sparse Core Ops, SparseCore 0:
  10.6 76.4 all-gather.1

commit v6 on v5

--- a/solution.py
+++ b/solution.py
@@ -34,13 +34,8 @@
     return shift(a, "core", 1)
 
 
-def ring(a, axis, direct=False):
-    after = shift(a, axis, -1)
-    before = shift(a, axis, 1)
-    if direct:
-        return [a, after, before, shift(a, axis, 2)]
-    half = a.shape[0] // 2
-    return [a, after, before, shift(after[:half], axis, -1), shift(before[half:], axis, 1)]
+def ring(a, axis):
+    return [a, shift(a, axis, -1), shift(a, axis, 1), shift(a, axis, 2)]
 
 
 def lay_out(where, mine, others, panel, sems):
@@ -158,6 +153,103 @@
     )(where, *mine, *others)
 
 
+def slices_kernel(x, parent, child, cp, t, r, xt, pbuf, cbuf, cpbuf, big, psem, csem, cpsem):
+    nr, kinds, sl, rows = x.shape
+    depth, w = parent.shape
+    parts = psem.shape[0]
+    chunk = depth // parts
+    copies = []
+    for n in range(parts):
+        at = pl.ds(n * chunk, chunk)
+        copies.append((pltpu.make_async_copy(parent.at[at], pbuf.at[at], psem.at[n]), pltpu.make_async_copy(child.at[at], cbuf.at[at], csem.at[n])))
+        for c in copies[-1]:
+            c.start()
+    ccopy = pltpu.make_async_copy(cp, cpbuf, cpsem)
+    ccopy.start()
+    for s in range(nr):
+        xt[:, s * rows : (s + 1) * rows] = x[s].reshape(kinds * sl, rows)
+    for n in range(parts):
+        at = pl.ds(n * chunk, chunk)
+        for c in copies[n]:
+            c.wait()
+        lhs = xt[:, n * chunk : (n + 1) * chunk]
+        gp = jnp.dot(lhs[: 2 * sl], pbuf[at, :], preferred_element_type=F32)
+        gc = jnp.dot(lhs, cbuf[at, :], preferred_element_type=F32)
+        if n == 0:
+            big[: 2 * sl] = gp
+            big[2 * sl :] = gc
+        else:
+            big[: 2 * sl] += gp
+            big[2 * sl :] += gc
+    ccopy.wait()
+    r[0] = big[2 * sl : 3 * sl]
+    r[1] = big[3 * sl : 4 * sl]
+    t2 = jnp.dot(big[sl : 2 * sl].astype(BF), cpbuf[...], preferred_element_type=F32) + big[4 * sl :]
+    big[sl : 2 * sl] = t2
+    lane = lax.broadcasted_iota(jnp.int32, (16, 128), 1) // sl
+    for q in range(w // 128):
+        for d in range(4):
+            out = None
+            for g in range(4):
+                v = big[g * 16 : (g + 1) * 16, q * 128 : (q + 1) * 128]
+                v = pltpu.roll(v, ((g - d) * sl) % 128, 1) if g != d else v
+                out = v if out is None else jnp.where(lane == g, v, out)
+            t[q * 4 + d] = out
+
+def slices(x, parent, child, cp):
+    nr, kinds, sl, rows = x.shape
+    depth, w = parent.shape
+    parts = 4
+    any_ = pl.BlockSpec(memory_space=pl.ANY)
+    vm = pl.BlockSpec(memory_space=pltpu.VMEM)
+    return pl.pallas_call(
+        slices_kernel,
+        in_specs=[vm, any_, any_, any_],
+        out_specs=[vm, vm],
+        out_shape=[jax.ShapeDtypeStruct((nr, 16, 128), F32), jax.ShapeDtypeStruct((2, sl, w), F32)],
+        scratch_shapes=[pltpu.VMEM((kinds * sl, depth), BF), pltpu.VMEM((depth, w), BF), pltpu.VMEM((depth, w), BF), pltpu.VMEM(cp.shape, BF), pltpu.VMEM((5 * sl, w), F32),
+            pltpu.SemaphoreType.DMA((parts,)), pltpu.SemaphoreType.DMA((parts,)), pltpu.SemaphoreType.DMA(())],
+        compiler_params=pltpu.CompilerParams(vmem_limit_bytes=60 << 20),
+        cost_estimate=pl.CostEstimate(flops=10 * sl * depth * w, transcendentals=0, bytes_accessed=4 * depth * w),
+    )(x, parent, child, cp)
+
+def rows_kernel(t, r, f, both):
+    nr = t.shape[0]
+    sl = r.shape[1]
+    w = r.shape[2]
+    for q in range(nr // 4):
+        for kind in range(2):
+            tall = []
+            for d in range(4):
+                for h in range(2):
+                    v = t[q * 4 + d]
+                    g = kind * 2 + h
+                    tall.append(pltpu.roll(v, (128 - g * sl) % 128, 1) if g else v)
+            tall = jnp.concatenate(tall, axis=0)
+            both[kind, :, q * 128 : (q + 1) * 128] = tall.T[:sl]
+    nc = f.shape[0]
+    own = sl // nc
+    half = w // 2
+    for c in range(nc):
+        at = slice(c * own, (c + 1) * own)
+        low = both[1, at, :] - r[1, at, :]
+        f[c, :own, :w] = both[0, at, :]
+        f[c, own:, :w] = r[0, at, :]
+        f[c, :own, w:] = low[:, :half]
+        f[c, own:, w:] = low[:, half:]
+
+def rows_of(t, r, nc):
+    sl, w = r.shape[1:]
+    vm = pl.BlockSpec(memory_space=pltpu.VMEM)
+    return pl.pallas_call(
+        rows_kernel, in_specs=[vm, vm], out_specs=vm,
+        out_shape=jax.ShapeDtypeStruct((nc, 2 * sl // nc, 3 * w // 2), F32),
+        scratch_shapes=[pltpu.VMEM((2, sl, w), F32)],
+        compiler_params=pltpu.CompilerParams(vmem_limit_bytes=16 << 20),
+        cost_estimate=pl.CostEstimate(flops=0, transcendentals=0, bytes_accessed=20 * sl * w),
+    )(t, r)
+
+
 def shards(z, pp, pdi, ca, cp, cdi):
     rows, w = pp.shape
     nr, nc = lax.axis_size(ROW), lax.axis_size(COL)
@@ -167,15 +259,20 @@
     block = z.reshape(z.shape[0], -1)
 
     child = lax.all_gather(ca, ROW, axis=0, tiled=True)
-    pieces = ring(jnp.concatenate(ring(pp, "zh", direct=True)), "x")
-    others = [swap(p) for p in pieces]
-
     diag_prod = dot(pdi, cp).astype(BF)
     first = (lax.axis_index(ROW) * nc + lax.axis_index(COL)) * own
     cols = lambda m: lax.dynamic_slice_in_dim(m, first, own, 1)
     diag_upper = dot(cols(pdi), pdi, 0, 0)
     diag_lower = dot(cols(cdi), cdi, 0, 0) + dot(cols(diag_prod), diag_prod, 0, 0)
-    others[-1], diag_upper, diag_lower = hold((others[-1], diag_upper, diag_lower))
+
+    here = jnp.concatenate(ring(pp, "zh"))
+    here, diag_upper, diag_lower = hold((here, diag_upper, diag_lower))
+    after, before, here_other = hold((shift(here, "x", -1), shift(here, "x", 1), swap(here)))
+    half = here.shape[0] // 2
+    far = shift(after[:half], "x", -1), shift(before[half:], "x", 1), swap(after), swap(before)
+    far_top, far_bottom, after_other, before_other = hold(far)
+    pieces = [here, after, before, far_top, far_bottom]
+    others = [here_other, after_other, before_other, swap(far_top), swap(far_bottom)]
 
     up = product(where, pieces, others, block, rows)
     upper = jnp.sum(exchange(up, COL).astype(F32), axis=0)
@@ -192,20 +289,13 @@
 
     x = jnp.stack([u.T, s.T, a.T]).reshape(3, nr, sl, rows).transpose(1, 0, 2, 3)
     x = exchange(x, ROW)
-    x = x.transpose(1, 2, 0, 3).reshape(3 * sl, nr * rows)
-    gp, gc = dot(x[: 2 * sl], parent), dot(x, child)
-    g1t, stp = gp[:sl], gp[sl:]
-    cross, stc, atc = gc[:sl], gc[sl : 2 * sl], gc[2 * sl :]
-    t2 = dot(stp.astype(BF), cp) + atc
-    t = jnp.stack([g1t, t2]).reshape(2, sl, nr, sl).transpose(2, 0, 3, 1)
+    t, r = slices(x, parent, child, cp)
     t = exchange(t, ROW)
-    t = t.transpose(1, 2, 0, 3).reshape(2, sl, w)
-    f = jnp.stack([t[0], cross, t[1] - stc]).reshape(3, nc, own, w).transpose(1, 0, 2, 3)
-    f = jnp.sum(exchange(f, COL), axis=0)
-
-    pp_out = diag_upper + f[0]
-    pc = f[1] - dot(pp_out.astype(BF), cp)
-    cc = diag_lower + f[2]
+    f = jnp.sum(exchange(rows_of(t, r, nc), COL), axis=0)
+
+    pp_out = diag_upper + f[:own, :w]
+    pc = f[own:, :w] - dot(pp_out.astype(BF), cp)
+    cc = diag_lower + jnp.concatenate([f[:own, w:], f[own:, w:]], axis=1)
     return -upper, pp_out, -anc, pc, cc
 
 

time: 251 us -> 236 us (0.940)
  waiting for transfers between devices: 71.8 us -> 96.2 us
  local copies, waits for them, and re-layouts: 24.1 us -> 5.25 us
  starting transfers between devices: 55.9 us -> 38.1 us
  Pallas kernels: 16.6 us -> 25 us
  matrix products: 27.9 us -> 20.7 us
  other arithmetic: 10.1 us -> 6.69 us
    ppermute x12, waiting for transfers between devices: 24.5 us -> 49.6 us  [shift(): return lax.ppermute(a, axis, [(i, (i + by) % n) for i in range(n)])]
    all_to_all x3, starting transfers between devices: 26 us -> 16.4 us  [exchange(): return lax.all_to_all(a, axes, 0, 0, tiled=True)]
    pallas_call x0 -> x2, Pallas kernels: none -> 8.39 us  [the longest x1 7.79 us: slices(): pl.pallas_call(slices_kernel, in_specs=[vm, any_, any_, any_], out_specs=...]
    ppermute x12, starting transfers between devices: 29.8 us -> 21.6 us  [shift(): return lax.ppermute(a, axis, [(i, (i + by) % n) for i in range(n)])]
    slice x9 -> x3, local copies, waits for them, and re-layouts: 7.52 us -> 0.06 us  [the longest x1 0.03 us: shards(): before[half:]]
    dot_general x10 -> x7, matrix products: 27.9 us -> 20.7 us  [dot(): lax.dot_general(a, b, (((ca,), (cb,)), ((), ())), preferred_element_type=...]
    unnamed x39 -> x32, local copies, waits for them, and re-layouts: 7.85 us -> 4.69 us
  transfers between devices with their start and end apart: 16 -> 16, of which waited for: 7 -> 10; matrix products, arithmetic and copies ran while one was open for 9% -> 8% of each run, Pallas kernels for 7% -> 7%
where the time goes in v6:
time: 236 us; the launch traced here: 235 us
  waiting for transfers between devices  96.2 us (41%)
  starting transfers between devices  38.1 us (16%)
  blocking collectives  29.2 us (12%)
  Pallas kernels  25 us (11%)
  matrix products  20.7 us (9%)
  between operations  14.2 us (6%)
  other arithmetic  6.69 us (3%)
  local copies, waits for them, and re-layouts  5.25 us (2%)
    ppermute x12, waiting for transfers between devices, shift(): return lax.ppermute(a, axis, [(i, (i + by) % n) for i in range(n)])  49.6 us
    all_to_all x3, waiting for transfers between devices, exchange(): return lax.all_to_all(a, axes, 0, 0, tiled=True)  45.9 us
    all_to_all x2, blocking collectives, exchange(): return lax.all_to_all(a, axes, 0, 0, tiled=True)  29.2 us
    ppermute x12, starting transfers between devices, shift(): return lax.ppermute(a, axis, [(i, (i + by) % n) for i in range(n)])  21.6 us
    dot_general x7, matrix products, dot(): lax.dot_general(a, b, (((ca,), (cb,)), ((), ())), preferred_element_type=...  20.7 us
    all_to_all x3, starting transfers between devices, exchange(): return lax.all_to_all(a, axes, 0, 0, tiled=True)  16.4 us
    pallas_call x1, Pallas kernels, product(): pl.pallas_call(product_kernel, grid_spec=pltpu.PrefetchScalarGridSpec(num...  10.6 us
    pallas_call x1, Pallas kernels, slices(): pl.pallas_call(slices_kernel, in_specs=[vm, any_, any_, any_], out_specs=...  7.79 us
  transfers between devices with their start and end apart: 16, of which 10 were waited for; matrix products, arithmetic and copies ran while one was open for 8% of the time, Pallas kernels for 7%

profile of v6, /device:TPU:1, one launch (start us, length us, event | category | flops | bytes accessed | tf_op | source)
XLA Modules:
  0.0 235.3 jit_solution(12247378719550269918)
XLA Ops:
  7.2 0.0 copy-start
  7.2 0.0 all-gather.2.cloned.1.call-start
  7.2 0.7 all-gather.2.cloned.1.call-update
  7.9 7.8 %collective-permute-start.2 = (bf16[96,1024]{1,0:T(8,128)(2,1)}, bf16[96,1024]{1,0:T(8,128)(2,1)S(1)}, u32[]{:S(2)}, u32[]{:S(2)}) collective-permute-start(bf16[96,1024]{1,0:T(8,128)(2,1)} %param.7), channel_id=1, source_target_pairs={{0,32},{16,48},{32,0},{48,16},{1,33},{17,49},{33,1},{49,17},{2,34}... | collective-permute-start | bytes 589832 | tf_op jit(solution)/shard_map/ppermute | solution.py:30
  15.7 1.2 collective-permute-start.1
  16.9 2.4 %collective-permute-start = (bf16[96,1024]{1,0:T(8,128)(2,1)}, bf16[96,1024]{1,0:T(8,128)(2,1)S(1)}, u32[]{:S(2)}, u32[]{:S(2)}) collective-permute-start(bf16[96,1024]{1,0:T(8,128)(2,1)} %param.7), channel_id=1, source_target_pairs={{0,48},{16,0},{32,16},{48,32},{1,49},{17,1},{33,17},{49,33},{2,50}... | collective-permute-start | bytes 589832 | tf_op jit(solution)/shard_map/ppermute | solution.py:30
  19.3 2.3 fusion
  21.6 2.4 %convolution_convert_fusion = bf16[1024,1024]{0,1:T(8,128)(2,1)S(1)} fusion(bf16[1024,1024]{1,0:T(8,128)(2,1)S(1)} %copy-done, bf16[1024,1024]{1,0:T(8,128)(2,1)S(1)} %copy-done.2), kind=kOutput, calls=%fused_computation.2 | convolution fusion | flops 2148532224 | bytes 6291456 | tf_op jit(solution)/shard_map/dot_general | solution.py:17
  24.0 0.0 copy-start.14
  24.0 0.6 convolution_add_fusion
  24.7 0.5 fusion.2
  25.2 0.0 collective-permute-done.2
  25.2 4.3 %collective-permute-done.1 = bf16[96,1024]{1,0:T(8,128)(2,1)S(1)} collective-permute-done((bf16[96,1024]{1,0:T(8,128)(2,1)}, bf16[96,1024]{1,0:T(8,128)(2,1)S(1)}, u32[]{:S(2)}, u32[]{:S(2)}) %collective-permute-start.1) | collective-permute-done | bytes 196640 | tf_op jit(solution)/shard_map/ppermute | solution.py:30
  29.5 7.1 %collective-permute-done = bf16[96,1024]{1,0:T(8,128)(2,1)S(1)} collective-permute-done((bf16[96,1024]{1,0:T(8,128)(2,1)}, bf16[96,1024]{1,0:T(8,128)(2,1)S(1)}, u32[]{:S(2)}, u32[]{:S(2)}) %collective-permute-start) | collective-permute-done | bytes 196640 | tf_op jit(solution)/shard_map/ppermute | solution.py:30
  36.6 0.1 pad_maximum_fusion.refs_0_
  36.7 2.6 %collective-permute-start.3 = (bf16[384,1024]{1,0:T(8,128)(2,1)S(1)}, bf16[384,1024]{1,0:T(8,128)(2,1)S(1)}, u32[]{:S(2)}, u32[]{:S(2)}) collective-permute-start(bf16[384,1024]{1,0:T(8,128)(2,1)S(1)} %pad_maximum_fusion.refs_0_), channel_id=1, source_target_pairs={{0,192},{64,0},{128,64},{192,128},{1,193},{65,1},{129,65},{193,129... | collective-permute-start | bytes 2359304 | tf_op jit(solution)/shard_map/ppermute | solution.py:30
  39.2 0.9 collective-permute-start.5
  40.1 18.4 %collective-permute-done.3.refs_1_ = bf16[384,1024]{1,0:T(8,128)(2,1)S(1)} collective-permute-done((bf16[384,1024]{1,0:T(8,128)(2,1)S(1)}, bf16[384,1024]{1,0:T(8,128)(2,1)S(1)}, u32[]{:S(2)}, u32[]{:S(2)}) %collective-permute-start.3) | collective-permute-done | bytes 786464 | tf_op jit(solution)/shard_map/ppermute | solution.py:30
  58.5 2.7 %collective-permute-done.4.refs_2_ = bf16[384,1024]{1,0:T(8,128)(2,1)S(1)} collective-permute-done((bf16[384,1024]{1,0:T(8,128)(2,1)S(1)}, bf16[384,1024]{1,0:T(8,128)(2,1)S(1)}, u32[]{:S(2)}, u32[]{:S(2)}) %collective-permute-start.4) | collective-permute-done | bytes 786464 | tf_op jit(solution)/shard_map/ppermute | solution.py:30
  61.2 0.0 collective-permute-done.5.refs_5_
  61.2 0.9 copy-done.7
  62.1 3.6 %collective-permute-start.8 = (bf16[384,1024]{1,0:T(8,128)(2,1)S(1)}, bf16[384,1024]{1,0:T(8,128)(2,1)S(1)}, u32[]{:S(2)}, u32[]{:S(2)}) collective-permute-start(bf16[384,1024]{1,0:T(8,128)(2,1)S(1)} %collective-permute-done.3.refs_1_), channel_id=1, source_target_pairs={{0,8},{8,0},{1,9},{9,1},{2,10},{10,2},{3,11},{11,3},{4,12},{12,4},... | collective-permute-start | bytes 2359304 | tf_op jit(solution)/shard_map/ppermute | solution.py:30
  65.7 0.0 collective-permute-start.9
  65.8 0.2 collective-permute-start.6
  66.0 1.3 collective-permute-start.7
  67.4 15.2 %collective-permute-done.6.refs_3_ = bf16[192,1024]{1,0:T(8,128)(2,1)S(1)} collective-permute-done((bf16[192,1024]{1,0:T(8,128)(2,1)S(1)}, bf16[192,1024]{1,0:T(8,128)(2,1)S(1)}, u32[]{:S(2)}, u32[]{:S(2)}) %collective-permute-start.6) | collective-permute-done | bytes 393248 | tf_op jit(solution)/shard_map/ppermute | solution.py:30
  82.5 1.2 collective-permute-done.7.refs_4_
  83.8 0.0 collective-permute-done.8.refs_6_
  83.8 0.0 collective-permute-done.9.refs_7_
  83.8 0.9 copy-done.8
  84.7 0.8 collective-permute-start.10
  85.5 0.1 copy-done.9
  85.6 0.8 collective-permute-start.11
  86.4 0.7 pad_add_fusion.where
  87.0 0.0 collective-permute-done.10.refs_8_
  87.0 0.7 collective-permute-done.11.refs_9_
  87.7 0.1 copy-done.12
  87.8 0.8 copy-done.13
  88.6 10.6 %shard_map.101 = bf16[8,96,1024]{2,1,0:T(8,128)(2,1)} custom-call(s32[3]{0:T(128)} %pad_add_fusion.where, bf16[384,1024]{1,0:T(8,128)(2,1)} %copy-done.3, bf16[384,1024]{1,0:T(8,128)(2,1)} %copy-done.5, bf16[384,1024]{1,0:T(8,128)(2,1)} %copy-done.6, bf16[192,1024]{1,0:T(8,128)(2,1)} %copy-done.10, bf16[192,1024]{1,0:T(8,128)(2,1)} %copy-done.11, ...), custom_call_target="tpu_custom_call" | custom-call | flops 4831838208 | bytes 12582912 | tf_op jit(solution)/shard_map/pallas_call | solution.py:93
  99.1 4.3 %all-to-all-start = ((bf16[8,96,1024]{2,1,0:T(8,128)(2,1)}), bf16[8,96,1024]{2,1,0:T(8,128)(2,1)}, u32[]{:S(2)}, u32[]{:S(2)}) async-start(bf16[8,96,1024]{2,1,0:T(8,128)(2,1)} %shard_map.101), calls=%async_computation | async-start | bytes 3145728 | tf_op jit(solution)/shard_map/all_to_all | solution.py:25
  103.5 0.0 all-gather.2.cloned.1.call-done.child
  103.5 9.5 %convolution_convert_fusion.1 = bf16[768,1024]{1,0:T(8,128)(2,1)} fusion(bf16[3072,1024]{1,0:T(8,128)(2,1)} %all-gather.2.cloned.1.call-done.child, bf16[768,1,3072]{2,0,1:T(8,128)(2,1)} %param.6), kind=kOutput, calls=%fused_computation.3 | convolution fusion | flops 4832624640 | bytes 12582912 | tf_op jit(solution)/shard_map/dot_general | solution.py:17
  112.9 11.5 %all-to-all-done = bf16[8,96,1024]{2,1,0:T(8,128)(2,1)} async-done(((bf16[8,96,1024]{2,1,0:T(8,128)(2,1)}), bf16[8,96,1024]{2,1,0:T(8,128)(2,1)}, u32[]{:S(2)}, u32[]{:S(2)}) %all-to-all-start) | async-done | bytes 1572896 | tf_op jit(solution)/shard_map/all_to_all | solution.py:25
  124.4 4.3 %all-to-all-start.1 = ((bf16[8,96,1024]{2,1,0:T(8,128)(2,1)}), bf16[8,96,1024]{2,1,0:T(8,128)(2,1)}, u32[]{:S(2)}, u32[]{:S(2)}) async-start(bf16[8,96,1024]{2,1,0:T(8,128)(2,1)} %bitcast.26), calls=%async_computation.1 | async-start | bytes 3145728 | tf_op jit(solution)/shard_map/all_to_all | solution.py:25
  128.7 1.7 convert_reduce_fusion.1
  130.4 0.8 convert_bitcast_fusion.2
  131.2 0.2 copy.11
  131.4 17.3 %all-to-all-done.1 = bf16[8,96,1024]{2,1,0:T(8,128)(2,1)} async-done(((bf16[8,96,1024]{2,1,0:T(8,128)(2,1)}), bf16[8,96,1024]{2,1,0:T(8,128)(2,1)}, u32[]{:S(2)}, u32[]{:S(2)}) %all-to-all-start.1) | async-done | bytes 1572896 | tf_op jit(solution)/shard_map/all_to_all | solution.py:25
  148.7 1.7 convert_reduce_fusion
  150.4 2.8 %subtract_negate_fusion = (f32[96,1024]{1,0:T(8,128)}, bf16[1024,96]{0,1:T(8,128)(2,1)S(1)}, bf16[1024,96]{0,1:T(8,128)(2,1)S(1)}) fusion(f32[96,1024]{1,0:T(8,128)S(1)} %convert_reduce_fusion, bf16[1024,1024]{1,0:T(8,128)(2,1)} %cp.1, f32[96,1024]{1,0:T(8,128)S(1)} %convert_reduce_fusion.1), kind=kOutput, calls=%fused_computation.14 | convolution fusion | flops 201818112 | bytes 3670016 | tf_op jit(solution)/shard_map/dot_general | solution.py:17
  153.2 0.2 copy.13
  153.4 0.2 copy.12
  153.6 1.1 maximum_bitcast_fusion
  154.7 7.8 %all-to-all-start.2 = ((bf16[32,3,32,96]{3,2,1,0:T(8,128)(2,1)}), bf16[32,3,32,96]{3,2,1,0:T(8,128)(2,1)S(1)}, u32[]{:S(2)}, u32[]{:S(2)}) async-start(bf16[32,3,32,96]{3,2,1,0:T(8,128)(2,1)} %maximum_bitcast_fusion), calls=%async_computation.2 | async-start | bytes 1572864 | tf_op jit(solution)/shard_map/all_to_all | solution.py:25
  162.5 6.0 %shard_map.102.parent = bf16[3072,1024]{1,0:T(8,128)(2,1)} custom-call(s32[3]{0:T(128)} %pad_add_fusion.where, bf16[384,1024]{1,0:T(8,128)(2,1)} %copy-done.3, bf16[384,1024]{1,0:T(8,128)(2,1)} %copy-done.5, bf16[384,1024]{1,0:T(8,128)(2,1)} %copy-done.6, bf16[192,1024]{1,0:T(8,128)(2,1)} %copy-done.10, bf16[192,1024]{1,0:T(8,128)(2,1)} %copy-done.11, ...), custom_call_target="tpu_custom_call" | custom-call | bytes 12582912 | tf_op jit(solution)/shard_map/pallas_call | solution.py:137
  168.6 17.1 %all-to-all-done.2.x = bf16[32,3,32,96]{3,2,1,0:T(8,128)(2,1)S(1)} async-done(((bf16[32,3,32,96]{3,2,1,0:T(8,128)(2,1)}), bf16[32,3,32,96]{3,2,1,0:T(8,128)(2,1)S(1)}, u32[]{:S(2)}, u32[]{:S(2)}) %all-to-all-start.2) | async-done | bytes 589856 | tf_op jit(solution)/shard_map/all_to_all | solution.py:25
  185.7 0.9 copy-done.4
  186.6 7.8 %shard_map.103 = (f32[32,16,128]{2,1,0:T(8,128)}, f32[2,32,1024]{2,1,0:T(8,128)}) custom-call(bf16[32,3,32,96]{3,2,1,0:T(8,128)(2,1)} %copy-done.4, bf16[3072,1024]{1,0:T(8,128)(2,1)} %shard_map.102.parent, bf16[3072,1024]{1,0:T(8,128)(2,1)} %all-gather.2.cloned.1.call-done.child, bf16[1024,1024]{1,0:T(8,128)(2,1)} %cp.1), custom_call_target="tpu_custom_call" | custom-call | flops 1006632960 | bytes 12582912 | tf_op jit(solution)/shard_map/pallas_call | solution.py:205
  194.4 18.5 %all_to_all.25.t = f32[32,16,128]{2,1,0:T(8,128)S(1)} all-to-all(f32[32,16,128]{2,1,0:T(8,128)} %get-tuple-element.30), channel_id=1, replica_groups=mesh['x'=4,'zh'=4,'core'=2,'y'=4,'zl'=2] {'x','zh','core'}, dimensions={0} | all-to-all | bytes 524288 | tf_op jit(solution)/shard_map/all_to_all | solution.py:25
  212.9 0.9 copy-done.1
  213.9 0.6 shard_map.104
  214.5 10.7 %all_to_all.26 = f32[8,8,1536]{2,1,0:T(8,128)S(1)} all-to-all(f32[8,8,1536]{2,1,0:T(8,128)S(1)} %shard_map.104), channel_id=1, replica_groups=mesh['x'=4,'zh'=4,'core'=2,'y'=4,'zl'=2] {'y','zl'}, dimensions={0} | all-to-all | bytes 786432 | tf_op jit(solution)/shard_map/all_to_all | solution.py:25
  225.3 0.6 slice_add_fusion
  225.9 2.6 %convolution_subtract_fusion = f32[4,1024]{1,0:T(4,128)} fusion(bf16[1024,1024]{1,0:T(8,128)(2,1)} %cp.1, f32[8,1536]{1,0:T(8,128)S(1)} %reduce_sum.29, f32[4,1024]{1,0:T(4,128)S(1)} %get-tuple-element.40), kind=kOutput, calls=%fused_computation.4 | convolution fusion | flops 8396800 | bytes 2146304 | tf_op jit(solution)/shard_map/dot_general | solution.py:17
  (28 shorter events, 0.1 us)
Async XLA Ops:
  7.2 14.5 %copy-start = (bf16[1024,1024]{1,0:T(8,128)(2,1)S(1)}, bf16[1024,1024]{1,0:T(8,128)(2,1)}, u32[]{:S(2)}) copy-start(bf16[1024,1024]{1,0:T(8,128)(2,1)} %param.8) | copy-start | bytes 6291460
  7.2 96.3 %all-gather.2.cloned.1.call-start = ((), (), s32[]{:S(2)}) async-start(), calls=%async_computation.5 | async-start | bytes 6488064 | tf_op jit(solution)/shard_map/all_gather | solution.py:261
  7.9 17.3 %collective-permute-start.2 = (bf16[96,1024]{1,0:T(8,128)(2,1)}, bf16[96,1024]{1,0:T(8,128)(2,1)S(1)}, u32[]{:S(2)}, u32[]{:S(2)}) collective-permute-start(bf16[96,1024]{1,0:T(8,128)(2,1)} %param.7), channel_id=1, source_target_pairs={{0,32},{16,48},{32,0},{48,16},{1,33},{17,49},{33,1},{49,17},{2,34}... | collective-permute-start | bytes 589832 | tf_op jit(solution)/shard_map/ppermute | solution.py:30
  15.7 13.7 %collective-permute-start.1 = (bf16[96,1024]{1,0:T(8,128)(2,1)}, bf16[96,1024]{1,0:T(8,128)(2,1)S(1)}, u32[]{:S(2)}, u32[]{:S(2)}) collective-permute-start(bf16[96,1024]{1,0:T(8,128)(2,1)} %param.7), channel_id=1, source_target_pairs={{0,16},{16,32},{32,48},{48,0},{1,17},{17,33},{33,49},{49,1},{2,18}... | collective-permute-start | bytes 589832 | tf_op jit(solution)/shard_map/ppermute | solution.py:30
  16.9 19.7 %collective-permute-start = (bf16[96,1024]{1,0:T(8,128)(2,1)}, bf16[96,1024]{1,0:T(8,128)(2,1)S(1)}, u32[]{:S(2)}, u32[]{:S(2)}) collective-permute-start(bf16[96,1024]{1,0:T(8,128)(2,1)} %param.7), channel_id=1, source_target_pairs={{0,48},{16,0},{32,16},{48,32},{1,49},{17,1},{33,17},{49,33},{2,50}... | collective-permute-start | bytes 589832 | tf_op jit(solution)/shard_map/ppermute | solution.py:30
  19.3 2.3 copy-start.2
  24.0 12.6 %copy-start.14 = (bf16[96,1024]{1,0:T(8,128)(2,1)S(1)}, bf16[96,1024]{1,0:T(8,128)(2,1)}, u32[]{:S(2)}) copy-start(bf16[96,1024]{1,0:T(8,128)(2,1)} %param.7) | copy-start | bytes 589828
  36.7 51.9 %copy-start.3 = (bf16[384,1024]{1,0:T(8,128)(2,1)}, bf16[384,1024]{1,0:T(8,128)(2,1)S(1)}, u32[]{:S(2)}) copy-start(bf16[384,1024]{1,0:T(8,128)(2,1)S(1)} %pad_maximum_fusion.refs_0_) | copy-start | bytes 2359300
  36.7 21.8 %collective-permute-start.3 = (bf16[384,1024]{1,0:T(8,128)(2,1)S(1)}, bf16[384,1024]{1,0:T(8,128)(2,1)S(1)}, u32[]{:S(2)}, u32[]{:S(2)}) collective-permute-start(bf16[384,1024]{1,0:T(8,128)(2,1)S(1)} %pad_maximum_fusion.refs_0_), channel_id=1, source_target_pairs={{0,192},{64,0},{128,64},{192,128},{1,193},{65,1},{129,65},{193,129... | collective-permute-start | bytes 2359304 | tf_op jit(solution)/shard_map/ppermute | solution.py:30
  39.2 21.9 %collective-permute-start.4 = (bf16[384,1024]{1,0:T(8,128)(2,1)S(1)}, bf16[384,1024]{1,0:T(8,128)(2,1)S(1)}, u32[]{:S(2)}, u32[]{:S(2)}) collective-permute-start(bf16[384,1024]{1,0:T(8,128)(2,1)S(1)} %pad_maximum_fusion.refs_0_), channel_id=1, source_target_pairs={{0,64},{64,128},{128,192},{192,0},{1,65},{65,129},{129,193},{193,1... | collective-permute-start | bytes 2359304 | tf_op jit(solution)/shard_map/ppermute | solution.py:30
  39.2 21.9 %collective-permute-start.5 = (bf16[384,1024]{1,0:T(8,128)(2,1)S(1)}, bf16[384,1024]{1,0:T(8,128)(2,1)S(1)}, u32[]{:S(2)}, u32[]{:S(2)}) collective-permute-start(bf16[384,1024]{1,0:T(8,128)(2,1)S(1)} %pad_maximum_fusion.refs_0_), channel_id=1, source_target_pairs={{0,8},{8,0},{1,9},{9,1},{2,10},{10,2},{3,11},{11,3},{4,12},{12,4},... | collective-permute-start | bytes 2359304 | tf_op jit(solution)/shard_map/ppermute | solution.py:30
  58.5 30.1 %copy-start.5 = (bf16[384,1024]{1,0:T(8,128)(2,1)}, bf16[384,1024]{1,0:T(8,128)(2,1)S(1)}, u32[]{:S(2)}) copy-start(bf16[384,1024]{1,0:T(8,128)(2,1)S(1)} %collective-permute-done.3.refs_1_) | copy-start | bytes 2359300
  61.2 22.6 %copy-start.6 = (bf16[384,1024]{1,0:T(8,128)(2,1)}, bf16[384,1024]{1,0:T(8,128)(2,1)S(1)}, u32[]{:S(2)}) copy-start(bf16[384,1024]{1,0:T(8,128)(2,1)S(1)} %collective-permute-done.4.refs_2_) | copy-start | bytes 2359300
  61.2 0.9 copy-start.7
  62.1 21.7 %collective-permute-start.8 = (bf16[384,1024]{1,0:T(8,128)(2,1)S(1)}, bf16[384,1024]{1,0:T(8,128)(2,1)S(1)}, u32[]{:S(2)}, u32[]{:S(2)}) collective-permute-start(bf16[384,1024]{1,0:T(8,128)(2,1)S(1)} %collective-permute-done.3.refs_1_), channel_id=1, source_target_pairs={{0,8},{8,0},{1,9},{9,1},{2,10},{10,2},{3,11},{11,3},{4,12},{12,4},... | collective-permute-start | bytes 2359304 | tf_op jit(solution)/shard_map/ppermute | solution.py:30
  65.7 18.1 %collective-permute-start.9 = (bf16[384,1024]{1,0:T(8,128)(2,1)S(1)}, bf16[384,1024]{1,0:T(8,128)(2,1)S(1)}, u32[]{:S(2)}, u32[]{:S(2)}) collective-permute-start(bf16[384,1024]{1,0:T(8,128)(2,1)S(1)} %collective-permute-done.4.refs_2_), channel_id=1, source_target_pairs={{0,8},{8,0},{1,9},{9,1},{2,10},{10,2},{3,11},{11,3},{4,12},{12,4},... | collective-permute-start | bytes 2359304 | tf_op jit(solution)/shard_map/ppermute | solution.py:30
  65.8 16.7 %collective-permute-start.6 = (bf16[192,1024]{1,0:T(8,128)(2,1)S(1)}, bf16[192,1024]{1,0:T(8,128)(2,1)S(1)}, u32[]{:S(2)}, u32[]{:S(2)}) collective-permute-start(bf16[192,1024]{1,0:T(8,128)(2,1)S(1)} %slice.18), channel_id=1, source_target_pairs={{0,192},{64,0},{128,64},{192,128},{1,193},{65,1},{129,65},{193,129... | collective-permute-start | bytes 1179656 | tf_op jit(solution)/shard_map/ppermute | solution.py:30
  66.0 17.8 %collective-permute-start.7 = (bf16[192,1024]{1,0:T(8,128)(2,1)S(1)}, bf16[192,1024]{1,0:T(8,128)(2,1)S(1)}, u32[]{:S(2)}, u32[]{:S(2)}) collective-permute-start(bf16[192,1024]{1,0:T(8,128)(2,1)S(1)} %slice.19), channel_id=1, source_target_pairs={{0,64},{64,128},{128,192},{192,0},{1,65},{65,129},{129,193},{193,1... | collective-permute-start | bytes 1179656 | tf_op jit(solution)/shard_map/ppermute | solution.py:30
  82.5 6.0 %copy-start.10 = (bf16[192,1024]{1,0:T(8,128)(2,1)}, bf16[192,1024]{1,0:T(8,128)(2,1)S(1)}, u32[]{:S(2)}) copy-start(bf16[192,1024]{1,0:T(8,128)(2,1)S(1)} %collective-permute-done.6.refs_3_) | copy-start | bytes 1179652
  83.8 3.3 %copy-start.11 = (bf16[192,1024]{1,0:T(8,128)(2,1)}, bf16[192,1024]{1,0:T(8,128)(2,1)S(1)}, u32[]{:S(2)}) copy-start(bf16[192,1024]{1,0:T(8,128)(2,1)S(1)} %collective-permute-done.7.refs_4_) | copy-start | bytes 1179652
  83.8 0.9 copy-start.8
  84.7 0.9 copy-start.9
  84.7 2.3 collective-permute-start.10
  85.6 2.1 collective-permute-start.11
  87.0 0.8 copy-start.12
  87.8 0.8 copy-start.13
  99.1 25.3 %all-to-all-start = ((bf16[8,96,1024]{2,1,0:T(8,128)(2,1)}), bf16[8,96,1024]{2,1,0:T(8,128)(2,1)}, u32[]{:S(2)}, u32[]{:S(2)}) async-start(bf16[8,96,1024]{2,1,0:T(8,128)(2,1)} %shard_map.101), calls=%async_computation | async-start | bytes 3145728 | tf_op jit(solution)/shard_map/all_to_all | solution.py:25
  124.4 24.3 %all-to-all-start.1 = ((bf16[8,96,1024]{2,1,0:T(8,128)(2,1)}), bf16[8,96,1024]{2,1,0:T(8,128)(2,1)}, u32[]{:S(2)}, u32[]{:S(2)}) async-start(bf16[8,96,1024]{2,1,0:T(8,128)(2,1)} %bitcast.26), calls=%async_computation.1 | async-start | bytes 3145728 | tf_op jit(solution)/shard_map/all_to_all | solution.py:25
  154.7 31.0 %all-to-all-start.2 = ((bf16[32,3,32,96]{3,2,1,0:T(8,128)(2,1)}), bf16[32,3,32,96]{3,2,1,0:T(8,128)(2,1)S(1)}, u32[]{:S(2)}, u32[]{:S(2)}) async-start(bf16[32,3,32,96]{3,2,1,0:T(8,128)(2,1)} %maximum_bitcast_fusion), calls=%async_computation.2 | async-start | bytes 1572864 | tf_op jit(solution)/shard_map/all_to_all | solution.py:25
  185.7 0.9 copy-start.4
  212.9 1.0 copy-start.1
  225.9 2.6 %copy-start.15 = (f32[4,1024]{1,0:T(4,128)}, f32[4,1024]{1,0:T(4,128)S(1)}, u32[]{:S(2)}) copy-start(f32[4,1024]{1,0:T(4,128)S(1)} %get-tuple-element.40) | copy-start | bytes 49156
Sparse Core Ops, SparseCore 0:
  10.6 75.1 all-gather.1

commit v7 on v6

--- a/solution.py
+++ b/solution.py
@@ -40,16 +40,15 @@
 
 def lay_out(where, mine, others, panel, sems):
     rows = mine[0].shape[0] // 4
-    for k, dx in enumerate((0, 1, 3, 2, 2)):
+    for k, dx in enumerate(RING):
         for pieces, core in ((mine, where[2]), (others, 1 - where[2])):
-            for n in range(pieces[k].shape[0] // rows):
-                dz = RING[n + (2 if k == 4 else 0)]
+            for n, dz in enumerate(RING):
                 at = lax.rem(where[0] + dx, 4) * 4 + lax.rem(where[1] + dz, 4)
                 at = pl.multiple_of((at * 2 + core) * rows, 32)
                 pltpu.make_async_copy(
                     pieces[k].at[pl.ds(n * rows, rows)],
                     panel.at[pl.ds(at, rows)],
-                    sems.at[RING.index(dx)],
+                    sems.at[k],
                 ).start()
 
 
@@ -58,7 +57,7 @@
 
 
 def product_kernel(where, *refs):
-    z, out, panel, zcols, acc, result, sems, zsems, out_sem = refs[10:]
+    z, out, whole, panel, zcols, acc, result, sems, zsems, whole_sems, out_sem = refs[8:]
     depth = panel.shape[0] // 4
 
     def block(step):
@@ -67,13 +66,18 @@
     zcopies = [
         pltpu.make_async_copy(z.at[:, block(step)], zcols.at[step], zsems.at[step]) for step in range(4)
     ]
+    keeps = [
+        pltpu.make_async_copy(panel.at[block(step)], whole.at[block(step)], whole_sems.at[step])
+        for step in range(4)
+    ]
     for copy in zcopies:
         copy.start()
-    lay_out(where, refs[:5], refs[5:10], panel, sems)
+    lay_out(where, refs[:4], refs[4:8], panel, sems)
     for step in range(4):
         part = panel.at[block(step)]
         zcopies[step].wait()
         pltpu.make_async_copy(part, part, sems.at[step]).wait()
+        keeps[step].start()
         got = jnp.dot(zcols[step], part[...], preferred_element_type=F32)
         if step == 0:
             acc[...] = got
@@ -83,6 +87,8 @@
             result[...] = (acc[...] + got).astype(BF).reshape(result.shape)
     copy = pltpu.make_async_copy(result, out, out_sem)
     copy.start()
+    for keep in keeps:
+        keep.wait()
     copy.wait()
 
 
@@ -95,8 +101,8 @@
         grid_spec=pltpu.PrefetchScalarGridSpec(
             num_scalar_prefetch=1,
             grid=(),
-            in_specs=[hbm] * 11,
-            out_specs=hbm,
+            in_specs=[hbm] * 9,
+            out_specs=[hbm] * 2,
             scratch_shapes=[
                 pltpu.VMEM((depth, width), BF),
                 pltpu.VMEM((4, z.shape[0], depth // 4), BF),
@@ -104,53 +110,18 @@
                 pltpu.VMEM(blocks, BF),
                 pltpu.SemaphoreType.DMA((4,)),
                 pltpu.SemaphoreType.DMA((4,)),
+                pltpu.SemaphoreType.DMA((4,)),
                 pltpu.SemaphoreType.DMA(()),
             ],
         ),
-        out_shape=jax.ShapeDtypeStruct(blocks, BF),
-        compiler_params=pltpu.CompilerParams(vmem_limit_bytes=60 << 20),
+        out_shape=[jax.ShapeDtypeStruct(blocks, BF), jax.ShapeDtypeStruct((depth, width), BF)],
+        compiler_params=pltpu.CompilerParams(vmem_limit_bytes=40 << 20),
         cost_estimate=pl.CostEstimate(
             flops=2 * z.size * width,
             transcendentals=0,
             bytes_accessed=2 * z.size + 2 * depth * width + 2 * z.shape[0] * width,
         ),
     )(where, *mine, *others, z)
-
-
-def panel_kernel(where, *refs):
-    out, panel, sems, out_sem = refs[10:]
-    depth = panel.shape[0] // 4
-    lay_out(where, refs[:5], refs[5:10], panel, sems)
-    copies = []
-    for step in range(4):
-        at = pl.ds(pl.multiple_of(ring_block(step, where) * depth, 256), depth)
-        pltpu.make_async_copy(panel.at[at], panel.at[at], sems.at[step]).wait()
-        copies.append(pltpu.make_async_copy(panel.at[at], out.at[at], out_sem.at[step]))
-        copies[-1].start()
-    for copy in copies:
-        copy.wait()
-
-
-def whole_panel(where, mine, others, depth):
-    width = mine[0].shape[1]
-    hbm = pl.BlockSpec(memory_space=pltpu.HBM)
-    return pl.pallas_call(
-        panel_kernel,
-        grid_spec=pltpu.PrefetchScalarGridSpec(
-            num_scalar_prefetch=1,
-            grid=(),
-            in_specs=[hbm] * 10,
-            out_specs=hbm,
-            scratch_shapes=[
-                pltpu.VMEM((depth, width), BF),
-                pltpu.SemaphoreType.DMA((4,)),
-                pltpu.SemaphoreType.DMA((4,)),
-            ],
-        ),
-        out_shape=jax.ShapeDtypeStruct((depth, width), BF),
-        compiler_params=pltpu.CompilerParams(vmem_limit_bytes=60 << 20),
-        cost_estimate=pl.CostEstimate(flops=0, transcendentals=0, bytes_accessed=4 * depth * width),
-    )(where, *mine, *others)
 
 
 def slices_kernel(x, parent, child, cp, t, r, xt, pbuf, cbuf, cpbuf, big, psem, csem, cpsem):
@@ -250,6 +221,34 @@
     )(t, r)
 
 
+def ancestors_kernel(got, shifted, ut, st, anc, x):
+    nr, _, sl, rows = x.shape
+    low = got[0].astype(F32)
+    for n in range(1, got.shape[0]):
+        low += got[n].astype(F32)
+    low -= shifted[...]
+    anc[...] = -low
+    x[:, 0] = ut[...].reshape(nr, sl, rows)
+    x[:, 1] = st[...].reshape(nr, sl, rows)
+    x[:, 2] = low.T.astype(BF).reshape(nr, sl, rows)
+
+
+def ancestors(got, shifted, ut, st, nr):
+    rows, w = shifted.shape
+    vmem = pl.BlockSpec(memory_space=pltpu.VMEM)
+    return pl.pallas_call(
+        ancestors_kernel,
+        in_specs=[vmem] * 4,
+        out_specs=[vmem] * 2,
+        out_shape=[
+            jax.ShapeDtypeStruct((rows, w), F32),
+            jax.ShapeDtypeStruct((nr, 3, w // nr, rows), BF),
+        ],
+        compiler_params=pltpu.CompilerParams(vmem_limit_bytes=16 << 20),
+        cost_estimate=pl.CostEstimate(flops=9 * rows * w, transcendentals=0, bytes_accessed=40 * rows * w),
+    )(got, shifted, ut, st)
+
+
 def shards(z, pp, pdi, ca, cp, cdi):
     rows, w = pp.shape
     nr, nc = lax.axis_size(ROW), lax.axis_size(COL)
@@ -267,27 +266,17 @@
 
     here = jnp.concatenate(ring(pp, "zh"))
     here, diag_upper, diag_lower = hold((here, diag_upper, diag_lower))
-    after, before, here_other = hold((shift(here, "x", -1), shift(here, "x", 1), swap(here)))
-    half = here.shape[0] // 2
-    far = shift(after[:half], "x", -1), shift(before[half:], "x", 1), swap(after), swap(before)
-    far_top, far_bottom, after_other, before_other = hold(far)
-    pieces = [here, after, before, far_top, far_bottom]
-    others = [here_other, after_other, before_other, swap(far_top), swap(far_bottom)]
-
-    up = product(where, pieces, others, block, rows)
+    pieces = ring(here, "x")
+    others = [swap(piece) for piece in pieces]
+
+    up, parent = product(where, pieces, others, block, rows)
     upper = jnp.sum(exchange(up, COL).astype(F32), axis=0)
     u = upper.astype(BF)
     shifted = dot(u, cp)
     s = shifted.astype(BF)
 
     lp = dot(block, child).astype(BF).reshape(nc, rows, w)
-    others[0], lp = hold((others[0], lp))
-    parent = whole_panel(where, pieces, others, block.shape[1])
-    lower = jnp.sum(exchange(lp, COL).astype(F32), axis=0)
-    anc = lower - shifted
-    a = anc.astype(BF)
-
-    x = jnp.stack([u.T, s.T, a.T]).reshape(3, nr, sl, rows).transpose(1, 0, 2, 3)
+    anc, x = ancestors(exchange(lp, COL), shifted, u.T, s.T, nr)
     x = exchange(x, ROW)
     t, r = slices(x, parent, child, cp)
     t = exchange(t, ROW)
@@ -296,7 +285,7 @@
     pp_out = diag_upper + f[:own, :w]
     pc = f[own:, :w] - dot(pp_out.astype(BF), cp)
     cc = diag_lower + jnp.concatenate([f[:own, w:], f[own:, w:]], axis=1)
-    return -upper, pp_out, -anc, pc, cc
+    return -upper, pp_out, anc, pc, cc
 
 
 def solution(mesh):

time: 236 us -> 244 us (1.034)
  blocking collectives: 29.2 us -> 50.9 us
  waiting for transfers between devices: 96.2 us -> 82.7 us
  other arithmetic: 6.69 us -> 3.27 us
    all_to_all x2, blocking collectives: 29.2 us -> 50.9 us  [exchange(): return lax.all_to_all(a, axes, 0, 0, tiled=True)]
    all_to_all x3, waiting for transfers between devices: 45.9 us -> 33 us  [exchange(): return lax.all_to_all(a, axes, 0, 0, tiled=True)]
    ppermute x12 -> x10, starting transfers between devices: 21.6 us -> 26.9 us  [shift(): return lax.ppermute(a, axis, [(i, (i + by) % n) for i in range(n)])]
    pallas_call x1, Pallas kernels: 10.6 us -> 15.4 us  [product(): pl.pallas_call(product_kernel, grid_spec=pltpu.PrefetchScalarGridSpec(num...]
    all_to_all x3, starting transfers between devices: 16.4 us -> 12.1 us  [exchange(): return lax.all_to_all(a, axes, 0, 0, tiled=True)]
    pallas_call x1, Pallas kernels: 6.04 us -> 2.48 us  [ancestors(): pl.pallas_call(ancestors_kernel, in_specs=[vmem] * 4, out_specs=[vmem] *...]
    unnamed x32 -> x14, local copies, waits for them, and re-layouts: 4.69 us -> 2.1 us
    ppermute x12 -> x10, waiting for transfers between devices: 49.6 us -> 49.1 us  [shift(): return lax.ppermute(a, axis, [(i, (i + by) % n) for i in range(n)])]
  transfers between devices with their start and end apart: 16 -> 14, of which waited for: 10 -> 8; matrix products, arithmetic and copies ran while one was open for 8% -> 10% of each run, Pallas kernels for 7% -> 6%
where the time goes in v7:
time: 244 us; the launch traced here: 243 us
  waiting for transfers between devices  82.7 us (34%)
  blocking collectives  50.9 us (21%)
  starting transfers between devices  39.1 us (16%)
  Pallas kernels  27.1 us (11%)
  matrix products  22.3 us (9%)
  between operations  14.2 us (6%)
  local copies, waits for them, and re-layouts  3.37 us (1%)
  other arithmetic  3.27 us (1%)
    all_to_all x2, blocking collectives, exchange(): return lax.all_to_all(a, axes, 0, 0, tiled=True)  50.9 us
    ppermute x10, waiting for transfers between devices, shift(): return lax.ppermute(a, axis, [(i, (i + by) % n) for i in range(n)])  49.1 us
    all_to_all x3, waiting for transfers between devices, exchange(): return lax.all_to_all(a, axes, 0, 0, tiled=True)  33 us
    ppermute x10, starting transfers between devices, shift(): return lax.ppermute(a, axis, [(i, (i + by) % n) for i in range(n)])  26.9 us
    dot_general x7, matrix products, dot(): lax.dot_general(a, b, (((ca,), (cb,)), ((), ())), preferred_element_type=...  22.3 us
    pallas_call x1, Pallas kernels, product(): pl.pallas_call(product_kernel, grid_spec=pltpu.PrefetchScalarGridSpec(num...  15.4 us
    all_to_all x3, starting transfers between devices, exchange(): return lax.all_to_all(a, axes, 0, 0, tiled=True)  12.1 us
    pallas_call x1, Pallas kernels, slices(): pl.pallas_call(slices_kernel, in_specs=[vm, any_, any_, any_], out_specs=...  7.81 us
  transfers between devices with their start and end apart: 14, of which 8 were waited for; matrix products, arithmetic and copies ran while one was open for 10% of the time, Pallas kernels for 6%

profile of v7, /device:TPU:1, one launch (start us, length us, event | category | flops | bytes accessed | tf_op | source)
XLA Modules:
  0.0 242.9 jit_solution(11505099613432599662)
XLA Ops:
  7.2 0.0 copy-start
  7.2 0.0 all-gather.2.cloned.1.call-start
  7.2 0.7 all-gather.2.cloned.1.call-update
  7.9 7.8 %collective-permute-start.2 = (bf16[96,1024]{1,0:T(8,128)(2,1)}, bf16[96,1024]{1,0:T(8,128)(2,1)S(1)}, u32[]{:S(2)}, u32[]{:S(2)}) collective-permute-start(bf16[96,1024]{1,0:T(8,128)(2,1)} %param.7), channel_id=1, source_target_pairs={{0,32},{16,48},{32,0},{48,16},{1,33},{17,49},{33,1},{49,17},{2,34}... | collective-permute-start | bytes 589832 | tf_op jit(solution)/shard_map/ppermute | solution.py:30
  15.7 1.2 collective-permute-start.1
  16.9 2.4 collective-permute-start
  19.3 0.0 slice-start
  19.3 2.3 fusion
  21.6 0.0 copy-done
  21.6 0.0 slice-start.1
  21.6 4.0 %convolution_convert_fusion = bf16[1024,1024]{0,1:T(8,128)(2,1)S(1)} fusion(bf16[1024,1024]{1,0:T(8,128)(2,1)S(1)} %copy-done, bf16[1024,1024]{1,0:T(8,128)(2,1)} %cp.1), kind=kOutput, calls=%fused_computation.1 | convolution fusion | flops 2148532224 | bytes 6291456 | tf_op jit(solution)/shard_map/dot_general | solution.py:17
  25.7 0.0 copy-start.3
  25.7 0.6 convolution_add_fusion
  26.3 0.5 fusion.2
  26.8 0.0 collective-permute-done.2
  26.8 2.6 %collective-permute-done.1 = bf16[96,1024]{1,0:T(8,128)(2,1)S(1)} collective-permute-done((bf16[96,1024]{1,0:T(8,128)(2,1)}, bf16[96,1024]{1,0:T(8,128)(2,1)S(1)}, u32[]{:S(2)}, u32[]{:S(2)}) %collective-permute-start.1) | collective-permute-done | bytes 196640 | tf_op jit(solution)/shard_map/ppermute | solution.py:30
  29.5 7.1 %collective-permute-done = bf16[96,1024]{1,0:T(8,128)(2,1)S(1)} collective-permute-done((bf16[96,1024]{1,0:T(8,128)(2,1)}, bf16[96,1024]{1,0:T(8,128)(2,1)S(1)}, u32[]{:S(2)}, u32[]{:S(2)}) %collective-permute-start) | collective-permute-done | bytes 196640 | tf_op jit(solution)/shard_map/ppermute | solution.py:30
  36.6 0.0 copy-done.3
  36.6 0.1 pad_maximum_fusion.refs_0_
  36.7 2.6 %collective-permute-start.3 = (bf16[384,1024]{1,0:T(8,128)(2,1)S(1)}, bf16[384,1024]{1,0:T(8,128)(2,1)S(1)}, u32[]{:S(2)}, u32[]{:S(2)}) collective-permute-start(bf16[384,1024]{1,0:T(8,128)(2,1)S(1)} %pad_maximum_fusion.refs_0_), channel_id=1, source_target_pairs={{0,192},{64,0},{128,64},{192,128},{1,193},{65,1},{129,65},{193,129... | collective-permute-start | bytes 2359304 | tf_op jit(solution)/shard_map/ppermute | solution.py:30
  39.2 0.0 collective-permute-start.4
  39.2 1.7 collective-permute-start.5
  41.0 1.4 collective-permute-start.6
  42.4 16.4 %collective-permute-done.3.refs_1_ = bf16[384,1024]{1,0:T(8,128)(2,1)S(1)} collective-permute-done((bf16[384,1024]{1,0:T(8,128)(2,1)S(1)}, bf16[384,1024]{1,0:T(8,128)(2,1)S(1)}, u32[]{:S(2)}, u32[]{:S(2)}) %collective-permute-start.3) | collective-permute-done | bytes 786464 | tf_op jit(solution)/shard_map/ppermute | solution.py:30
  58.8 5.8 %collective-permute-start.7 = (bf16[384,1024]{1,0:T(8,128)(2,1)S(1)}, bf16[384,1024]{1,0:T(8,128)(2,1)S(1)}, u32[]{:S(2)}, u32[]{:S(2)}) collective-permute-start(bf16[384,1024]{1,0:T(8,128)(2,1)S(1)} %collective-permute-done.3.refs_1_), channel_id=1, source_target_pairs={{0,8},{8,0},{1,9},{9,1},{2,10},{10,2},{3,11},{11,3},{4,12},{12,4},... | collective-permute-start | bytes 2359304 | tf_op jit(solution)/shard_map/ppermute | solution.py:30
  64.6 0.0 collective-permute-done.4.refs_2_
  64.6 2.6 %collective-permute-start.8 = (bf16[384,1024]{1,0:T(8,128)(2,1)S(1)}, bf16[384,1024]{1,0:T(8,128)(2,1)S(1)}, u32[]{:S(2)}, u32[]{:S(2)}) collective-permute-start(bf16[384,1024]{1,0:T(8,128)(2,1)S(1)} %collective-permute-done.4.refs_2_), channel_id=1, source_target_pairs={{0,8},{8,0},{1,9},{9,1},{2,10},{10,2},{3,11},{11,3},{4,12},{12,4},... | collective-permute-start | bytes 2359304 | tf_op jit(solution)/shard_map/ppermute | solution.py:30
  67.2 21.1 %collective-permute-done.5.refs_3_ = bf16[384,1024]{1,0:T(8,128)(2,1)S(1)} collective-permute-done((bf16[384,1024]{1,0:T(8,128)(2,1)S(1)}, bf16[384,1024]{1,0:T(8,128)(2,1)S(1)}, u32[]{:S(2)}, u32[]{:S(2)}) %collective-permute-start.5) | collective-permute-done | bytes 786464 | tf_op jit(solution)/shard_map/ppermute | solution.py:30
  88.3 1.4 collective-permute-start.9
  89.7 0.1 pad_add_fusion.where
  89.8 0.0 collective-permute-done.6.refs_4_
  89.8 0.0 collective-permute-done.7.refs_5_
  89.8 0.0 collective-permute-done.8.refs_6_
  89.8 1.8 collective-permute-done.9.refs_7_
  91.6 0.0 slice-done
  91.6 0.0 slice-done.1
  91.6 15.4 %shard_map.101 = (bf16[8,96,1024]{2,1,0:T(8,128)(2,1)S(1)}, bf16[3072,1024]{1,0:T(8,128)(2,1)}) custom-call(s32[3]{0:T(128)S(1)} %pad_add_fusion.where, bf16[384,1024]{1,0:T(8,128)(2,1)S(1)} %pad_maximum_fusion.refs_0_, bf16[384,1024]{1,0:T(8,128)(2,1)S(1)} %collective-permute-done.3.refs_1_, bf16[384,1024]{1,0:T(8,128)(2,1)S(1)} %collective-permute-done.4.refs_2_, ...), custom_call_target="tpu_custom_call" | custom-call | flops 4831838208 | bytes 12582912 | tf_op jit(solution)/shard_map/pallas_call | solution.py:99
  107.0 0.0 copy-start.1
  107.1 1.1 copy-done.1
  108.2 4.4 %all-to-all-start = ((bf16[8,96,1024]{2,1,0:T(8,128)(2,1)}), bf16[8,96,1024]{2,1,0:T(8,128)(2,1)}, u32[]{:S(2)}, u32[]{:S(2)}) async-start(bf16[8,96,1024]{2,1,0:T(8,128)(2,1)} %copy-done.1), calls=%async_computation | async-start | bytes 3145728 | tf_op jit(solution)/shard_map/all_to_all | solution.py:25
  112.6 0.0 all-gather.2.cloned.1.call-done.child
  112.6 9.5 %convolution_convert_fusion.1 = bf16[768,1024]{1,0:T(8,128)(2,1)} fusion(bf16[3072,1024]{1,0:T(8,128)(2,1)} %all-gather.2.cloned.1.call-done.child, bf16[768,1,3072]{2,0,1:T(8,128)(2,1)} %param.6), kind=kOutput, calls=%fused_computation.2 | convolution fusion | flops 4832624640 | bytes 12582912 | tf_op jit(solution)/shard_map/dot_general | solution.py:17
  122.0 11.4 %all-to-all-done = bf16[8,96,1024]{2,1,0:T(8,128)(2,1)} async-done(((bf16[8,96,1024]{2,1,0:T(8,128)(2,1)}), bf16[8,96,1024]{2,1,0:T(8,128)(2,1)}, u32[]{:S(2)}, u32[]{:S(2)}) %all-to-all-start) | async-done | bytes 1572896 | tf_op jit(solution)/shard_map/all_to_all | solution.py:25
  133.4 4.3 %all-to-all-start.1 = ((bf16[8,96,1024]{2,1,0:T(8,128)(2,1)}), bf16[8,96,1024]{2,1,0:T(8,128)(2,1)}, u32[]{:S(2)}, u32[]{:S(2)}) async-start(bf16[8,96,1024]{2,1,0:T(8,128)(2,1)} %bitcast.25), calls=%async_computation.1 | async-start | bytes 3145728 | tf_op jit(solution)/shard_map/all_to_all | solution.py:25
  137.7 1.7 convert_reduce_fusion
  139.5 0.2 copy.15
  139.6 2.8 %fusion.13 = (bf16[96,1024]{1,0:T(8,128)(2,1)}, f32[96,1024]{1,0:T(8,128)S(1)}) fusion(bf16[96,1024]{0,1:T(8,128)(2,1)S(1)} %copy.15, bf16[1024,1024]{1,0:T(8,128)(2,1)} %cp.1), kind=kOutput, calls=%fused_computation.23 | convolution fusion | flops 201424896 | bytes 2883584 | tf_op jit(solution)/shard_map/dot_general | solution.py:17
  142.4 1.1 copy.16
  143.5 14.1 %all-to-all-done.1.got = bf16[8,96,1024]{2,1,0:T(8,128)(2,1)} async-done(((bf16[8,96,1024]{2,1,0:T(8,128)(2,1)}), bf16[8,96,1024]{2,1,0:T(8,128)(2,1)}, u32[]{:S(2)}, u32[]{:S(2)}) %all-to-all-start.1) | async-done | bytes 1572896 | tf_op jit(solution)/shard_map/all_to_all | solution.py:25
  157.6 2.5 %shard_map.102 = (f32[96,1024]{1,0:T(8,128)}, bf16[32,3,32,96]{3,2,1,0:T(8,128)(2,1)S(1)}) custom-call(bf16[8,96,1024]{2,1,0:T(8,128)(2,1)} %all-to-all-done.1.got, f32[96,1024]{1,0:T(8,128)S(1)} %get-tuple-element.31.shifted, bf16[1024,96]{1,0:T(8,128)(2,1)S(1)} %bitcast.20, bf16[1024,96]{1,0:T(8,128)(2,1)S(1)} %bitcast.21), custom_call_target="tpu_custom_call" | custom-call | flops 884736 | bytes 3932160 | tf_op jit(solution)/shard_map/pallas_call | solution.py:239
  160.1 32.4 %all_to_all.25.x = bf16[32,3,32,96]{3,2,1,0:T(8,128)(2,1)} all-to-all(bf16[32,3,32,96]{3,2,1,0:T(8,128)(2,1)S(1)} %get-tuple-element.17), channel_id=1, replica_groups=mesh['x'=4,'zh'=4,'core'=2,'y'=4,'zl'=2] {'x','zh','core'}, dimensions={0} | all-to-all | bytes 1179648 | tf_op jit(solution)/shard_map/all_to_all | solution.py:25
  192.5 7.8 %shard_map.103 = (f32[32,16,128]{2,1,0:T(8,128)}, f32[2,32,1024]{2,1,0:T(8,128)}) custom-call(bf16[32,3,32,96]{3,2,1,0:T(8,128)(2,1)} %all_to_all.25.x, bf16[3072,1024]{1,0:T(8,128)(2,1)} %get-tuple-element.18.parent, bf16[3072,1024]{1,0:T(8,128)(2,1)} %all-gather.2.cloned.1.call-done.child, bf16[1024,1024]{1,0:T(8,128)(2,1)} %cp.1), custom_call_target="tpu_custom_call" | custom-call | flops 1006632960 | bytes 12582912 | tf_op jit(solution)/shard_map/pallas_call | solution.py:176
  200.3 18.4 %all_to_all.26.t = f32[32,16,128]{2,1,0:T(8,128)S(1)} all-to-all(f32[32,16,128]{2,1,0:T(8,128)} %get-tuple-element.19), channel_id=1, replica_groups=mesh['x'=4,'zh'=4,'core'=2,'y'=4,'zl'=2] {'x','zh','core'}, dimensions={0} | all-to-all | bytes 524288 | tf_op jit(solution)/shard_map/all_to_all | solution.py:25
  218.8 0.0 copy-start.2
  218.8 0.9 copy-done.2
  219.7 1.4 shard_map.104
  221.1 3.5 %all-to-all-start.4 = ((f32[8,8,1536]{2,1,0:T(8,128)}), f32[8,8,1536]{2,1,0:T(8,128)S(1)}, u32[]{:S(2)}, u32[]{:S(2)}) async-start(f32[8,8,1536]{2,1,0:T(8,128)} %shard_map.104), calls=%async_computation.4 | async-start | bytes 786432 | tf_op jit(solution)/shard_map/all_to_all | solution.py:25
  224.6 0.8 neg.3
  225.3 7.5 %all-to-all-done.4 = f32[8,8,1536]{2,1,0:T(8,128)S(1)} async-done(((f32[8,8,1536]{2,1,0:T(8,128)}), f32[8,8,1536]{2,1,0:T(8,128)S(1)}, u32[]{:S(2)}, u32[]{:S(2)}) %all-to-all-start.4) | async-done | bytes 393248 | tf_op jit(solution)/shard_map/all_to_all | solution.py:25
  232.8 0.6 slice_add_fusion
  233.5 0.0 copy-start.4
  233.5 2.6 %convolution_subtract_fusion = f32[4,1024]{1,0:T(4,128)} fusion(bf16[1024,1024]{1,0:T(8,128)(2,1)} %cp.1, f32[8,1536]{1,0:T(8,128)S(1)} %reduce_sum.19, f32[4,1024]{1,0:T(4,128)S(1)} %get-tuple-element.32), kind=kOutput, calls=%fused_computation.3 | convolution fusion | flops 8396800 | bytes 2146304 | tf_op jit(solution)/shard_map/dot_general | solution.py:17
  236.1 0.0 copy-done.4
  (3 shorter events, 0.0 us)
Async XLA Ops:
  7.2 14.5 %copy-start = (bf16[1024,1024]{1,0:T(8,128)(2,1)S(1)}, bf16[1024,1024]{1,0:T(8,128)(2,1)}, u32[]{:S(2)}) copy-start(bf16[1024,1024]{1,0:T(8,128)(2,1)} %param.8) | copy-start | bytes 6291460
  7.2 105.4 %all-gather.2.cloned.1.call-start = ((), (), s32[]{:S(2)}) async-start(), calls=%async_computation.5 | async-start | bytes 6488064 | tf_op jit(solution)/shard_map/all_gather | solution.py:260
  7.9 18.9 %collective-permute-start.2 = (bf16[96,1024]{1,0:T(8,128)(2,1)}, bf16[96,1024]{1,0:T(8,128)(2,1)S(1)}, u32[]{:S(2)}, u32[]{:S(2)}) collective-permute-start(bf16[96,1024]{1,0:T(8,128)(2,1)} %param.7), channel_id=1, source_target_pairs={{0,32},{16,48},{32,0},{48,16},{1,33},{17,49},{33,1},{49,17},{2,34}... | collective-permute-start | bytes 589832 | tf_op jit(solution)/shard_map/ppermute | solution.py:30
  15.7 13.7 %collective-permute-start.1 = (bf16[96,1024]{1,0:T(8,128)(2,1)}, bf16[96,1024]{1,0:T(8,128)(2,1)S(1)}, u32[]{:S(2)}, u32[]{:S(2)}) collective-permute-start(bf16[96,1024]{1,0:T(8,128)(2,1)} %param.7), channel_id=1, source_target_pairs={{0,16},{16,32},{32,48},{48,0},{1,17},{17,33},{33,49},{49,1},{2,18}... | collective-permute-start | bytes 589832 | tf_op jit(solution)/shard_map/ppermute | solution.py:30
  16.9 19.7 %collective-permute-start = (bf16[96,1024]{1,0:T(8,128)(2,1)}, bf16[96,1024]{1,0:T(8,128)(2,1)S(1)}, u32[]{:S(2)}, u32[]{:S(2)}) collective-permute-start(bf16[96,1024]{1,0:T(8,128)(2,1)} %param.7), channel_id=1, source_target_pairs={{0,48},{16,0},{32,16},{48,32},{1,49},{17,1},{33,17},{49,33},{2,50}... | collective-permute-start | bytes 589832 | tf_op jit(solution)/shard_map/ppermute | solution.py:30
  19.3 72.3 %slice-start = ((s8[4718592]{0:T(1024)(128)(4,1)}), s8[4194304]{0:T(1024)(128)(4,1)S(1)}, s32[]{:S(2)}) async-start(s8[4718592]{0:T(1024)(128)(4,1)} %bitcast.22), calls=%async_computation.6 | async-start | bytes 8388608
  21.6 70.0 %slice-start.1 = ((s8[4718592]{0:T(1024)(128)(4,1)}), s8[524288]{0:T(1024)(128)(4,1)S(1)}, s32[]{:S(2)}) async-start(s8[4718592]{0:T(1024)(128)(4,1)} %bitcast.22), calls=%async_computation.7 | async-start | bytes 1048576
  25.7 10.9 %copy-start.3 = (bf16[96,1024]{1,0:T(8,128)(2,1)S(1)}, bf16[96,1024]{1,0:T(8,128)(2,1)}, u32[]{:S(2)}) copy-start(bf16[96,1024]{1,0:T(8,128)(2,1)} %param.7) | copy-start | bytes 589828
  36.7 22.2 %collective-permute-start.3 = (bf16[384,1024]{1,0:T(8,128)(2,1)S(1)}, bf16[384,1024]{1,0:T(8,128)(2,1)S(1)}, u32[]{:S(2)}, u32[]{:S(2)}) collective-permute-start(bf16[384,1024]{1,0:T(8,128)(2,1)S(1)} %pad_maximum_fusion.refs_0_), channel_id=1, source_target_pairs={{0,192},{64,0},{128,64},{192,128},{1,193},{65,1},{129,65},{193,129... | collective-permute-start | bytes 2359304 | tf_op jit(solution)/shard_map/ppermute | solution.py:30
  39.2 25.4 %collective-permute-start.4 = (bf16[384,1024]{1,0:T(8,128)(2,1)S(1)}, bf16[384,1024]{1,0:T(8,128)(2,1)S(1)}, u32[]{:S(2)}, u32[]{:S(2)}) collective-permute-start(bf16[384,1024]{1,0:T(8,128)(2,1)S(1)} %pad_maximum_fusion.refs_0_), channel_id=1, source_target_pairs={{0,64},{64,128},{128,192},{192,0},{1,65},{65,129},{129,193},{193,1... | collective-permute-start | bytes 2359304 | tf_op jit(solution)/shard_map/ppermute | solution.py:30
  39.2 49.1 %collective-permute-start.5 = (bf16[384,1024]{1,0:T(8,128)(2,1)S(1)}, bf16[384,1024]{1,0:T(8,128)(2,1)S(1)}, u32[]{:S(2)}, u32[]{:S(2)}) collective-permute-start(bf16[384,1024]{1,0:T(8,128)(2,1)S(1)} %pad_maximum_fusion.refs_0_), channel_id=1, source_target_pairs={{0,128},{64,192},{128,0},{192,64},{1,129},{65,193},{129,1},{193,65... | collective-permute-start | bytes 2359304 | tf_op jit(solution)/shard_map/ppermute | solution.py:30
  41.0 48.8 %collective-permute-start.6 = (bf16[384,1024]{1,0:T(8,128)(2,1)S(1)}, bf16[384,1024]{1,0:T(8,128)(2,1)S(1)}, u32[]{:S(2)}, u32[]{:S(2)}) collective-permute-start(bf16[384,1024]{1,0:T(8,128)(2,1)S(1)} %pad_maximum_fusion.refs_0_), channel_id=1, source_target_pairs={{0,8},{8,0},{1,9},{9,1},{2,10},{10,2},{3,11},{11,3},{4,12},{12,4},... | collective-permute-start | bytes 2359304 | tf_op jit(solution)/shard_map/ppermute | solution.py:30
  58.8 30.9 %collective-permute-start.7 = (bf16[384,1024]{1,0:T(8,128)(2,1)S(1)}, bf16[384,1024]{1,0:T(8,128)(2,1)S(1)}, u32[]{:S(2)}, u32[]{:S(2)}) collective-permute-start(bf16[384,1024]{1,0:T(8,128)(2,1)S(1)} %collective-permute-done.3.refs_1_), channel_id=1, source_target_pairs={{0,8},{8,0},{1,9},{9,1},{2,10},{10,2},{3,11},{11,3},{4,12},{12,4},... | collective-permute-start | bytes 2359304 | tf_op jit(solution)/shard_map/ppermute | solution.py:30
  64.6 25.2 %collective-permute-start.8 = (bf16[384,1024]{1,0:T(8,128)(2,1)S(1)}, bf16[384,1024]{1,0:T(8,128)(2,1)S(1)}, u32[]{:S(2)}, u32[]{:S(2)}) collective-permute-start(bf16[384,1024]{1,0:T(8,128)(2,1)S(1)} %collective-permute-done.4.refs_2_), channel_id=1, source_target_pairs={{0,8},{8,0},{1,9},{9,1},{2,10},{10,2},{3,11},{11,3},{4,12},{12,4},... | collective-permute-start | bytes 2359304 | tf_op jit(solution)/shard_map/ppermute | solution.py:30
  88.3 3.3 %collective-permute-start.9 = (bf16[384,1024]{1,0:T(8,128)(2,1)S(1)}, bf16[384,1024]{1,0:T(8,128)(2,1)S(1)}, u32[]{:S(2)}, u32[]{:S(2)}) collective-permute-start(bf16[384,1024]{1,0:T(8,128)(2,1)S(1)} %collective-permute-done.5.refs_3_), channel_id=1, source_target_pairs={{0,8},{8,0},{1,9},{9,1},{2,10},{10,2},{3,11},{11,3},{4,12},{12,4},... | collective-permute-start | bytes 2359304 | tf_op jit(solution)/shard_map/ppermute | solution.py:30
  107.0 1.1 copy-start.1
  108.2 25.3 %all-to-all-start = ((bf16[8,96,1024]{2,1,0:T(8,128)(2,1)}), bf16[8,96,1024]{2,1,0:T(8,128)(2,1)}, u32[]{:S(2)}, u32[]{:S(2)}) async-start(bf16[8,96,1024]{2,1,0:T(8,128)(2,1)} %copy-done.1), calls=%async_computation | async-start | bytes 3145728 | tf_op jit(solution)/shard_map/all_to_all | solution.py:25
  133.4 24.2 %all-to-all-start.1 = ((bf16[8,96,1024]{2,1,0:T(8,128)(2,1)}), bf16[8,96,1024]{2,1,0:T(8,128)(2,1)}, u32[]{:S(2)}, u32[]{:S(2)}) async-start(bf16[8,96,1024]{2,1,0:T(8,128)(2,1)} %bitcast.25), calls=%async_computation.1 | async-start | bytes 3145728 | tf_op jit(solution)/shard_map/all_to_all | solution.py:25
  218.8 1.0 copy-start.2
  221.1 11.7 %all-to-all-start.4 = ((f32[8,8,1536]{2,1,0:T(8,128)}), f32[8,8,1536]{2,1,0:T(8,128)S(1)}, u32[]{:S(2)}, u32[]{:S(2)}) async-start(f32[8,8,1536]{2,1,0:T(8,128)} %shard_map.104), calls=%async_computation.4 | async-start | bytes 786432 | tf_op jit(solution)/shard_map/all_to_all | solution.py:25
  233.5 2.6 %copy-start.4 = (f32[4,1024]{1,0:T(4,128)}, f32[4,1024]{1,0:T(4,128)S(1)}, u32[]{:S(2)}) copy-start(f32[4,1024]{1,0:T(4,128)S(1)} %get-tuple-element.32) | copy-start | bytes 49156
Sparse Core Ops, SparseCore 0:
  10.6 81.4 all-gather.1

commit v8 on v6

--- a/solution.py
+++ b/solution.py
@@ -38,83 +38,133 @@
     return [a, shift(a, axis, -1), shift(a, axis, 1), shift(a, axis, 2)]
 
 
-def lay_out(where, mine, others, panel, sems):
-    rows = mine[0].shape[0] // 4
-    for k, dx in enumerate((0, 1, 3, 2, 2)):
+def lay_out(where, mine, others, panel, sems, blocks=range(4)):
+    for n in blocks:
         for pieces, core in ((mine, where[2]), (others, 1 - where[2])):
-            for n in range(pieces[k].shape[0] // rows):
-                dz = RING[n + (2 if k == 4 else 0)]
-                at = lax.rem(where[0] + dx, 4) * 4 + lax.rem(where[1] + dz, 4)
+            rows = pieces[0].shape[0] // 4
+            for m, dz in enumerate(RING):
+                piece, start = (pieces[n], m) if n < 3 else (pieces[3 + m // 2], m % 2)
+                at = lax.rem(where[0] + RING[n], 4) * 4 + lax.rem(where[1] + dz, 4)
                 at = pl.multiple_of((at * 2 + core) * rows, 32)
                 pltpu.make_async_copy(
-                    pieces[k].at[pl.ds(n * rows, rows)],
-                    panel.at[pl.ds(at, rows)],
-                    sems.at[RING.index(dx)],
+                    piece.at[pl.ds(start * rows, rows)], panel.at[pl.ds(at, rows)], sems.at[n]
                 ).start()
 
 
-def ring_block(step, where):
-    return lax.rem(where[0] + jnp.where(step < 2, step, 5 - step), 4)
-
-
-def product_kernel(where, *refs):
-    z, out, panel, zcols, acc, result, sems, zsems, out_sem = refs[10:]
+def ring_block(n, where):
+    return lax.rem(where[0] + RING[n], 4)
+
+
+def near_kernel(where, *refs):
+    z, out, panel, zcols, acc, sems, zsems, out_sem = refs[6:]
     depth = panel.shape[0] // 4
 
-    def block(step):
-        return pl.ds(pl.multiple_of(ring_block(step, where) * depth, 256), depth)
-
-    zcopies = [
-        pltpu.make_async_copy(z.at[:, block(step)], zcols.at[step], zsems.at[step]) for step in range(4)
-    ]
+    def block(n):
+        return pl.ds(pl.multiple_of(ring_block(n, where) * depth, 256), depth)
+
+    zcopies = [pltpu.make_async_copy(z.at[:, block(n)], zcols.at[n], zsems.at[n]) for n in range(3)]
     for copy in zcopies:
         copy.start()
-    lay_out(where, refs[:5], refs[5:10], panel, sems)
-    for step in range(4):
-        part = panel.at[block(step)]
-        zcopies[step].wait()
-        pltpu.make_async_copy(part, part, sems.at[step]).wait()
-        got = jnp.dot(zcols[step], part[...], preferred_element_type=F32)
-        if step == 0:
+    lay_out(where, refs[:3], refs[3:6], panel, sems, range(3))
+    for n in range(3):
+        part = panel.at[block(n)]
+        zcopies[n].wait()
+        pltpu.make_async_copy(part, part, sems.at[n]).wait()
+        got = jnp.dot(zcols[n], part[...], preferred_element_type=F32)
+        if n == 0:
             acc[...] = got
-        elif step < 3:
+        else:
             acc[...] += got
-        else:
-            result[...] = (acc[...] + got).astype(BF).reshape(result.shape)
+    copy = pltpu.make_async_copy(acc, out, out_sem)
+    copy.start()
+    copy.wait()
+
+
+def far_kernel(where, *refs):
+    near, z, out, panel, zcols, acc, result, sem, zsem, near_sem, out_sem = refs[4:]
+    depth, rows = panel.shape[0], refs[0].shape[0] // 2
+    at = ring_block(3, where)
+    zcopy = pltpu.make_async_copy(
+        z.at[:, pl.ds(pl.multiple_of(at * depth, 256), depth)], zcols, zsem
+    )
+    zcopy.start()
+    for pieces, core in ((refs[:2], where[2]), (refs[2:4], 1 - where[2])):
+        for m, dz in enumerate(RING):
+            to = pl.multiple_of((lax.rem(where[1] + dz, 4) * 2 + core) * rows, 32)
+            pltpu.make_async_copy(
+                pieces[m // 2].at[pl.ds(m % 2 * rows, rows)], panel.at[pl.ds(to, rows)], sem
+            ).start()
+    ncopy = pltpu.make_async_copy(near, acc, near_sem)
+    ncopy.start()
+    zcopy.wait()
+    pltpu.make_async_copy(panel, panel, sem).wait()
+    got = jnp.dot(zcols[...], panel[...], preferred_element_type=F32)
+    ncopy.wait()
+    result[...] = (acc[...] + got).astype(BF).reshape(result.shape)
     copy = pltpu.make_async_copy(result, out, out_sem)
     copy.start()
     copy.wait()
 
 
-def product(where, mine, others, z, rows):
+def near_product(where, mine, others, z):
     depth, width = z.shape[1], mine[0].shape[1]
     hbm = pl.BlockSpec(memory_space=pltpu.HBM)
-    blocks = (z.shape[0] // rows, rows, width)
-    return pl.pallas_call(
-        product_kernel,
+    return pl.pallas_call(
+        near_kernel,
         grid_spec=pltpu.PrefetchScalarGridSpec(
             num_scalar_prefetch=1,
             grid=(),
-            in_specs=[hbm] * 11,
+            in_specs=[hbm] * 7,
             out_specs=hbm,
             scratch_shapes=[
                 pltpu.VMEM((depth, width), BF),
-                pltpu.VMEM((4, z.shape[0], depth // 4), BF),
+                pltpu.VMEM((3, z.shape[0], depth // 4), BF),
+                pltpu.VMEM((z.shape[0], width), F32),
+                pltpu.SemaphoreType.DMA((3,)),
+                pltpu.SemaphoreType.DMA((3,)),
+                pltpu.SemaphoreType.DMA(()),
+            ],
+        ),
+        out_shape=jax.ShapeDtypeStruct((z.shape[0], width), F32),
+        compiler_params=pltpu.CompilerParams(vmem_limit_bytes=60 << 20),
+        cost_estimate=pl.CostEstimate(
+            flops=3 * z.size * width // 2,
+            transcendentals=0,
+            bytes_accessed=3 * z.size // 2 + 3 * depth * width // 2 + 4 * z.shape[0] * width,
+        ),
+    )(where, *mine, *others, z)
+
+
+def far_product(where, mine, others, near, z, rows):
+    depth, width = z.shape[1] // 4, near.shape[1]
+    hbm = pl.BlockSpec(memory_space=pltpu.HBM)
+    blocks = (z.shape[0] // rows, rows, width)
+    return pl.pallas_call(
+        far_kernel,
+        grid_spec=pltpu.PrefetchScalarGridSpec(
+            num_scalar_prefetch=1,
+            grid=(),
+            in_specs=[hbm] * 6,
+            out_specs=hbm,
+            scratch_shapes=[
+                pltpu.VMEM((depth, width), BF),
+                pltpu.VMEM((z.shape[0], depth), BF),
                 pltpu.VMEM((z.shape[0], width), F32),
                 pltpu.VMEM(blocks, BF),
-                pltpu.SemaphoreType.DMA((4,)),
-                pltpu.SemaphoreType.DMA((4,)),
+                pltpu.SemaphoreType.DMA(()),
+                pltpu.SemaphoreType.DMA(()),
+                pltpu.SemaphoreType.DMA(()),
                 pltpu.SemaphoreType.DMA(()),
             ],
         ),
         out_shape=jax.ShapeDtypeStruct(blocks, BF),
         compiler_params=pltpu.CompilerParams(vmem_limit_bytes=60 << 20),
         cost_estimate=pl.CostEstimate(
-            flops=2 * z.size * width,
+            flops=z.size * width // 2,
             transcendentals=0,
-            bytes_accessed=2 * z.size + 2 * depth * width + 2 * z.shape[0] * width,
-        ),
-    )(where, *mine, *others, z)
+            bytes_accessed=z.size // 2 + 2 * depth * width + 6 * z.shape[0] * width,
+        ),
+    )(where, *mine, *others, near, z)
 
 
 def panel_kernel(where, *refs):
@@ -250,6 +300,34 @@
     )(t, r)
 
 
+def ancestors_kernel(got, shifted, ut, st, anc, x):
+    nr, _, sl, rows = x.shape
+    low = got[0].astype(F32)
+    for n in range(1, got.shape[0]):
+        low += got[n].astype(F32)
+    low -= shifted[...]
+    anc[...] = -low
+    x[:, 0] = ut[...].reshape(nr, sl, rows)
+    x[:, 1] = st[...].reshape(nr, sl, rows)
+    x[:, 2] = low.T.astype(BF).reshape(nr, sl, rows)
+
+
+def ancestors(got, shifted, ut, st, nr):
+    rows, w = shifted.shape
+    vmem = pl.BlockSpec(memory_space=pltpu.VMEM)
+    return pl.pallas_call(
+        ancestors_kernel,
+        in_specs=[vmem] * 4,
+        out_specs=[vmem] * 2,
+        out_shape=[
+            jax.ShapeDtypeStruct((rows, w), F32),
+            jax.ShapeDtypeStruct((nr, 3, w // nr, rows), BF),
+        ],
+        compiler_params=pltpu.CompilerParams(vmem_limit_bytes=16 << 20),
+        cost_estimate=pl.CostEstimate(flops=9 * rows * w, transcendentals=0, bytes_accessed=40 * rows * w),
+    )(got, shifted, ut, st)
+
+
 def shards(z, pp, pdi, ca, cp, cdi):
     rows, w = pp.shape
     nr, nc = lax.axis_size(ROW), lax.axis_size(COL)
@@ -269,26 +347,23 @@
     here, diag_upper, diag_lower = hold((here, diag_upper, diag_lower))
     after, before, here_other = hold((shift(here, "x", -1), shift(here, "x", 1), swap(here)))
     half = here.shape[0] // 2
-    far = shift(after[:half], "x", -1), shift(before[half:], "x", 1), swap(after), swap(before)
-    far_top, far_bottom, after_other, before_other = hold(far)
-    pieces = [here, after, before, far_top, far_bottom]
-    others = [here_other, after_other, before_other, swap(far_top), swap(far_bottom)]
-
-    up = product(where, pieces, others, block, rows)
+    pieces = [here, after, before, shift(after[:half], "x", -1), shift(before[half:], "x", 1)]
+    others = [here_other, swap(after), swap(before)]
+    near = near_product(where, pieces[:3], others, block)
+    pieces[3], pieces[4], near = hold((pieces[3], pieces[4], near))
+    others += [swap(pieces[3]), swap(pieces[4])]
+    up = far_product(where, pieces[3:], others[3:], near, block, rows)
     upper = jnp.sum(exchange(up, COL).astype(F32), axis=0)
     u = upper.astype(BF)
     shifted = dot(u, cp)
     s = shifted.astype(BF)
 
     lp = dot(block, child).astype(BF).reshape(nc, rows, w)
-    others[0], lp = hold((others[0], lp))
+    got = exchange(lp, COL)
+    anc, x = ancestors(got, shifted, u.T, s.T, nr)
+    others[0], x = hold((others[0], x))
+    x = exchange(x, ROW)
     parent = whole_panel(where, pieces, others, block.shape[1])
-    lower = jnp.sum(exchange(lp, COL).astype(F32), axis=0)
-    anc = lower - shifted
-    a = anc.astype(BF)
-
-    x = jnp.stack([u.T, s.T, a.T]).reshape(3, nr, sl, rows).transpose(1, 0, 2, 3)
-    x = exchange(x, ROW)
     t, r = slices(x, parent, child, cp)
     t = exchange(t, ROW)
     f = jnp.sum(exchange(rows_of(t, r, nc), COL), axis=0)
@@ -296,7 +371,7 @@
     pp_out = diag_upper + f[:own, :w]
     pc = f[own:, :w] - dot(pp_out.astype(BF), cp)
     cc = diag_lower + jnp.concatenate([f[:own, w:], f[own:, w:]], axis=1)
-    return -upper, pp_out, -anc, pc, cc
+    return -upper, pp_out, anc, pc, cc
 
 
 def solution(mesh):

time: 236 us -> 230 us (0.975)
  waiting for transfers between devices: 96.2 us -> 80 us
  starting transfers between devices: 38.1 us -> 51 us
  blocking collectives: 29.2 us -> 18.4 us
  Pallas kernels: 25 us -> 32.3 us
  local copies, waits for them, and re-layouts: 5.25 us -> 8.89 us
  other arithmetic: 6.69 us -> 3.85 us
    ppermute x12, waiting for transfers between devices: 49.6 us -> 29.2 us  [shift(): return lax.ppermute(a, axis, [(i, (i + by) % n) for i in range(n)])]
    all_to_all x3 -> x4, starting transfers between devices: 16.4 us -> 28 us  [exchange(): return lax.all_to_all(a, axes, 0, 0, tiled=True)]
    all_to_all x2 -> x1, blocking collectives: 29.2 us -> 18.4 us  [exchange(): return lax.all_to_all(a, axes, 0, 0, tiled=True)]
    pallas_call x1 -> x3, Pallas kernels: 10.6 us -> 17.1 us  [the longest x1 9.25 us: near_product(): pl.pallas_call(near_kernel, grid_spec=pltpu.PrefetchScalarGridSpec(num_sc...]
    all_to_all x3 -> x4, waiting for transfers between devices: 45.9 us -> 50.2 us  [exchange(): return lax.all_to_all(a, axes, 0, 0, tiled=True)]
  transfers between devices with their start and end apart: 16 -> 17, of which waited for: 10 -> 10; matrix products, arithmetic and copies ran while one was open for 8% -> 11% of each run, Pallas kernels for 7% -> 9%
where the time goes in v8:
time: 230 us; the launch traced here: 229 us
  waiting for transfers between devices  80 us (35%)
  starting transfers between devices  51 us (22%)
  Pallas kernels  32.3 us (14%)
  matrix products  20.7 us (9%)
  blocking collectives  18.4 us (8%)
  between operations  14.2 us (6%)
  local copies, waits for them, and re-layouts  8.89 us (4%)
  other arithmetic  3.85 us (2%)
    all_to_all x4, waiting for transfers between devices, exchange(): return lax.all_to_all(a, axes, 0, 0, tiled=True)  50.2 us
    ppermute x12, waiting for transfers between devices, shift(): return lax.ppermute(a, axis, [(i, (i + by) % n) for i in range(n)])  29.2 us
    all_to_all x4, starting transfers between devices, exchange(): return lax.all_to_all(a, axes, 0, 0, tiled=True)  28 us
    ppermute x12, starting transfers between devices, shift(): return lax.ppermute(a, axis, [(i, (i + by) % n) for i in range(n)])  22.9 us
    dot_general x7, matrix products, dot(): lax.dot_general(a, b, (((ca,), (cb,)), ((), ())), preferred_element_type=...  20.7 us
    all_to_all x1, blocking collectives, exchange(): return lax.all_to_all(a, axes, 0, 0, tiled=True)  18.4 us
    pallas_call x1, Pallas kernels, near_product(): pl.pallas_call(near_kernel, grid_spec=pltpu.PrefetchScalarGridSpec(num_sc...  9.25 us
    pallas_call x1, Pallas kernels, slices(): pl.pallas_call(slices_kernel, in_specs=[vm, any_, any_, any_], out_specs=...  7.81 us
  transfers between devices with their start and end apart: 17, of which 10 were waited for; matrix products, arithmetic and copies ran while one was open for 11% of the time, Pallas kernels for 9%

profile of v8, /device:TPU:1, one launch (start us, length us, event | category | flops | bytes accessed | tf_op | source)
XLA Modules:
  0.0 229.4 jit_solution(11196420415515771942)
XLA Ops:
  7.2 0.0 copy-start
  7.2 0.0 all-gather.2.cloned.1.call-start
  7.2 0.7 all-gather.2.cloned.1.call-update
  7.9 3.9 %collective-permute-start.1 = (bf16[96,1024]{1,0:T(8,128)(2,1)}, bf16[96,1024]{1,0:T(8,128)(2,1)S(1)}, u32[]{:S(2)}, u32[]{:S(2)}) collective-permute-start(bf16[96,1024]{1,0:T(8,128)(2,1)} %param.7), channel_id=1, source_target_pairs={{0,16},{16,32},{32,48},{48,0},{1,17},{17,33},{33,49},{49,1},{2,18}... | collective-permute-start | bytes 589832 | tf_op jit(solution)/shard_map/ppermute | solution.py:30
  11.8 3.1 %collective-permute-start = (bf16[96,1024]{1,0:T(8,128)(2,1)}, bf16[96,1024]{1,0:T(8,128)(2,1)S(1)}, u32[]{:S(2)}, u32[]{:S(2)}) collective-permute-start(bf16[96,1024]{1,0:T(8,128)(2,1)} %param.7), channel_id=1, source_target_pairs={{0,48},{16,0},{32,16},{48,32},{1,49},{17,1},{33,17},{49,33},{2,50}... | collective-permute-start | bytes 589832 | tf_op jit(solution)/shard_map/ppermute | solution.py:30
  14.9 4.4 %collective-permute-start.2 = (bf16[96,1024]{1,0:T(8,128)(2,1)}, bf16[96,1024]{1,0:T(8,128)(2,1)S(1)}, u32[]{:S(2)}, u32[]{:S(2)}) collective-permute-start(bf16[96,1024]{1,0:T(8,128)(2,1)} %param.7), channel_id=1, source_target_pairs={{0,32},{16,48},{32,0},{48,16},{1,33},{17,49},{33,1},{49,17},{2,34}... | collective-permute-start | bytes 589832 | tf_op jit(solution)/shard_map/ppermute | solution.py:30
  19.3 2.3 %fusion = f32[4,1024]{1,0:T(4,128)S(1)} fusion(bf16[1024,1024]{1,0:T(8,128)(2,1)} %param.11, s32[]{:T(128)S(6)} %select_n.2), kind=kOutput, calls=%fused_computation.6 | convolution fusion | flops 8388608 | bytes 2375684 | tf_op jit(solution)/shard_map/dot_general | solution.py:17
  21.6 2.4 %convolution_convert_fusion = bf16[1024,1024]{0,1:T(8,128)(2,1)S(1)} fusion(bf16[1024,1024]{1,0:T(8,128)(2,1)S(1)} %copy-done, bf16[1024,1024]{1,0:T(8,128)(2,1)S(1)} %copy-done.3), kind=kOutput, calls=%fused_computation.1 | convolution fusion | flops 2148532224 | bytes 6291456 | tf_op jit(solution)/shard_map/dot_general | solution.py:17
  24.0 0.0 copy-start.14
  24.0 0.6 convolution_add_fusion
  24.7 0.5 fusion.2
  25.2 0.0 collective-permute-done.1
  25.2 5.0 %collective-permute-done = bf16[96,1024]{1,0:T(8,128)(2,1)S(1)} collective-permute-done((bf16[96,1024]{1,0:T(8,128)(2,1)}, bf16[96,1024]{1,0:T(8,128)(2,1)S(1)}, u32[]{:S(2)}, u32[]{:S(2)}) %collective-permute-start) | collective-permute-done | bytes 196640 | tf_op jit(solution)/shard_map/ppermute | solution.py:30
  30.2 0.3 collective-permute-done.2
  30.5 0.1 pad_maximum_fusion.refs_0_
  30.6 2.5 %collective-permute-start.5 = (bf16[384,1024]{1,0:T(8,128)(2,1)S(1)}, bf16[384,1024]{1,0:T(8,128)(2,1)S(1)}, u32[]{:S(2)}, u32[]{:S(2)}) collective-permute-start(bf16[384,1024]{1,0:T(8,128)(2,1)S(1)} %pad_maximum_fusion.refs_0_), channel_id=1, source_target_pairs={{0,8},{8,0},{1,9},{9,1},{2,10},{10,2},{3,11},{11,3},{4,12},{12,4},... | collective-permute-start | bytes 2359304 | tf_op jit(solution)/shard_map/ppermute | solution.py:30
  33.1 1.2 collective-permute-start.4
  34.3 1.5 collective-permute-start.3
  35.7 0.0 collective-permute-done.5.refs_3_.refs_5_
  35.8 19.3 %collective-permute-done.4.refs_2_ = bf16[384,1024]{1,0:T(8,128)(2,1)S(1)} collective-permute-done((bf16[384,1024]{1,0:T(8,128)(2,1)S(1)}, bf16[384,1024]{1,0:T(8,128)(2,1)S(1)}, u32[]{:S(2)}, u32[]{:S(2)}) %collective-permute-start.4) | collective-permute-done | bytes 786464 | tf_op jit(solution)/shard_map/ppermute | solution.py:30
  55.1 1.0 collective-permute-start.8
  56.1 0.1 collective-permute-start.9
  56.2 0.8 slice.18
  56.9 0.8 slice.19
  57.7 1.0 collective-permute-start.7
  58.7 1.7 collective-permute-start.6
  60.4 0.7 pad_add_fusion.where
  61.0 0.0 collective-permute-done.9.refs_5_.refs_7_
  61.1 0.9 copy-done.12
  61.9 0.9 copy-done.13
  62.8 9.3 %shard_map.101.refs_4_ = f32[768,1024]{1,0:T(8,128)} custom-call(s32[3]{0:T(128)} %pad_add_fusion.where, bf16[384,1024]{1,0:T(8,128)(2,1)} %copy-done.4, bf16[384,1024]{1,0:T(8,128)(2,1)} %copy-done.7, bf16[384,1024]{1,0:T(8,128)(2,1)} %copy-done.6, bf16[384,1024]{1,0:T(8,128)(2,1)} %copy-done.11, bf16[384,1024]{1,0:T(8,128)(2,1)} %copy-done.12, ...), custom_call_target="tpu_custom_call" | custom-call | flops 3623878656 | bytes 11403264 | tf_op jit(solution)/shard_map/pallas_call | solution.py:112
  72.1 1.4 collective-permute-done.7.refs_1_.refs_4_
  73.5 1.0 collective-permute-done.6.refs_0_.refs_3_
  74.4 2.6 %collective-permute-start.10 = (bf16[192,1024]{1,0:T(8,128)(2,1)}, bf16[192,1024]{1,0:T(8,128)(2,1)S(1)}, u32[]{:S(2)}, u32[]{:S(2)}) collective-permute-start(bf16[192,1024]{1,0:T(8,128)(2,1)} %collective-permute-done.6.refs_0_.refs_3_), channel_id=1, source_target_pairs={{0,8},{8,0},{1,9},{9,1},{2,10},{10,2},{3,11},{11,3},{4,12},{12,4},... | collective-permute-start | bytes 1179656 | tf_op jit(solution)/shard_map/ppermute | solution.py:30
  77.0 0.0 collective-permute-start.11
  77.0 2.2 collective-permute-done.10.refs_2_.refs_8_
  79.2 0.7 copy-done.9
  80.0 0.8 copy-done.10
  80.7 5.4 %shard_map.102 = bf16[8,96,1024]{2,1,0:T(8,128)(2,1)} custom-call(s32[3]{0:T(128)} %pad_add_fusion.where, bf16[192,1024]{1,0:T(8,128)(2,1)} %collective-permute-done.6.refs_0_.refs_3_, bf16[192,1024]{1,0:T(8,128)(2,1)} %copy-done.8, bf16[192,1024]{1,0:T(8,128)(2,1)} %copy-done.9, bf16[192,1024]{1,0:T(8,128)(2,1)} %copy-done.10, ...), custom_call_target="tpu_custom_call" | custom-call | flops 1207959552 | bytes 7471104 | tf_op jit(solution)/shard_map/pallas_call | solution.py:142
  86.1 13.0 %all-to-all-start = ((bf16[8,96,1024]{2,1,0:T(8,128)(2,1)}), bf16[8,96,1024]{2,1,0:T(8,128)(2,1)}, u32[]{:S(2)}, u32[]{:S(2)}) async-start(bf16[8,96,1024]{2,1,0:T(8,128)(2,1)} %shard_map.102), calls=%async_computation | async-start | bytes 3145728 | tf_op jit(solution)/shard_map/all_to_all | solution.py:25
  99.1 0.0 all-gather.2.cloned.1.call-done.child
  99.1 9.5 %convolution_convert_fusion.1 = bf16[768,1024]{1,0:T(8,128)(2,1)} fusion(bf16[3072,1024]{1,0:T(8,128)(2,1)} %all-gather.2.cloned.1.call-done.child, bf16[768,1,3072]{2,0,1:T(8,128)(2,1)} %param.6), kind=kOutput, calls=%fused_computation.2 | convolution fusion | flops 4832624640 | bytes 12582912 | tf_op jit(solution)/shard_map/dot_general | solution.py:17
  108.5 11.4 %all-to-all-done = bf16[8,96,1024]{2,1,0:T(8,128)(2,1)} async-done(((bf16[8,96,1024]{2,1,0:T(8,128)(2,1)}), bf16[8,96,1024]{2,1,0:T(8,128)(2,1)}, u32[]{:S(2)}, u32[]{:S(2)}) %all-to-all-start) | async-done | bytes 1572896 | tf_op jit(solution)/shard_map/all_to_all | solution.py:25
  120.0 4.3 %all-to-all-start.1 = ((bf16[8,96,1024]{2,1,0:T(8,128)(2,1)}), bf16[8,96,1024]{2,1,0:T(8,128)(2,1)}, u32[]{:S(2)}, u32[]{:S(2)}) async-start(bf16[8,96,1024]{2,1,0:T(8,128)(2,1)} %bitcast.24), calls=%async_computation.1 | async-start | bytes 3145728 | tf_op jit(solution)/shard_map/all_to_all | solution.py:25
  124.3 1.7 convert_reduce_fusion
  126.0 0.2 copy.15
  126.2 2.8 %fusion.13 = (bf16[96,1024]{1,0:T(8,128)(2,1)}, f32[96,1024]{1,0:T(8,128)S(1)}) fusion(bf16[96,1024]{0,1:T(8,128)(2,1)S(1)} %copy.15, bf16[1024,1024]{1,0:T(8,128)(2,1)} %cp.1), kind=kOutput, calls=%fused_computation.23 | convolution fusion | flops 201424896 | bytes 2883584 | tf_op jit(solution)/shard_map/dot_general | solution.py:17
  128.9 1.1 copy.16
  130.0 14.1 %all-to-all-done.1.got = bf16[8,96,1024]{2,1,0:T(8,128)(2,1)} async-done(((bf16[8,96,1024]{2,1,0:T(8,128)(2,1)}), bf16[8,96,1024]{2,1,0:T(8,128)(2,1)}, u32[]{:S(2)}, u32[]{:S(2)}) %all-to-all-start.1) | async-done | bytes 1572896 | tf_op jit(solution)/shard_map/all_to_all | solution.py:25
  144.2 2.5 %shard_map.103 = (f32[96,1024]{1,0:T(8,128)}, bf16[32,3,32,96]{3,2,1,0:T(8,128)(2,1)S(1)}) custom-call(bf16[8,96,1024]{2,1,0:T(8,128)(2,1)} %all-to-all-done.1.got, f32[96,1024]{1,0:T(8,128)S(1)} %get-tuple-element.43.shifted, bf16[1024,96]{1,0:T(8,128)(2,1)S(1)} %bitcast.20, bf16[1024,96]{1,0:T(8,128)(2,1)S(1)} %bitcast.21), custom_call_target="tpu_custom_call" | custom-call | flops 884736 | bytes 3932160 | tf_op jit(solution)/shard_map/pallas_call | solution.py:318
  146.6 0.9 copy-done.1
  147.5 7.4 %all-to-all-start.2 = ((bf16[32,3,32,96]{3,2,1,0:T(8,128)(2,1)}), bf16[32,3,32,96]{3,2,1,0:T(8,128)(2,1)S(1)}, u32[]{:S(2)}, u32[]{:S(2)}) async-start(bf16[32,3,32,96]{3,2,1,0:T(8,128)(2,1)} %copy-done.1), calls=%async_computation.2 | async-start | bytes 1572864 | tf_op jit(solution)/shard_map/all_to_all | solution.py:25
  154.9 6.0 %shard_map.104.parent = bf16[3072,1024]{1,0:T(8,128)(2,1)} custom-call(s32[3]{0:T(128)} %pad_add_fusion.where, bf16[384,1024]{1,0:T(8,128)(2,1)} %copy-done.4, bf16[384,1024]{1,0:T(8,128)(2,1)} %copy-done.7, bf16[384,1024]{1,0:T(8,128)(2,1)} %copy-done.6, bf16[192,1024]{1,0:T(8,128)(2,1)} %collective-permute-done.6.refs_0_.refs_3_, ...), custom_call_target="tpu_custom_call" | custom-call | bytes 12582912 | tf_op jit(solution)/shard_map/pallas_call | solution.py:187
  160.9 17.1 %all-to-all-done.2.x = bf16[32,3,32,96]{3,2,1,0:T(8,128)(2,1)S(1)} async-done(((bf16[32,3,32,96]{3,2,1,0:T(8,128)(2,1)}), bf16[32,3,32,96]{3,2,1,0:T(8,128)(2,1)S(1)}, u32[]{:S(2)}, u32[]{:S(2)}) %all-to-all-start.2) | async-done | bytes 589856 | tf_op jit(solution)/shard_map/all_to_all | solution.py:25
  178.1 0.9 copy-done.5
  179.0 7.8 %shard_map.105 = (f32[32,16,128]{2,1,0:T(8,128)}, f32[2,32,1024]{2,1,0:T(8,128)}) custom-call(bf16[32,3,32,96]{3,2,1,0:T(8,128)(2,1)} %copy-done.5, bf16[3072,1024]{1,0:T(8,128)(2,1)} %shard_map.104.parent, bf16[3072,1024]{1,0:T(8,128)(2,1)} %all-gather.2.cloned.1.call-done.child, bf16[1024,1024]{1,0:T(8,128)(2,1)} %cp.1), custom_call_target="tpu_custom_call" | custom-call | flops 1006632960 | bytes 12582912 | tf_op jit(solution)/shard_map/pallas_call | solution.py:255
  186.8 18.4 %all_to_all.25.t = f32[32,16,128]{2,1,0:T(8,128)S(1)} all-to-all(f32[32,16,128]{2,1,0:T(8,128)} %get-tuple-element.31), channel_id=1, replica_groups=mesh['x'=4,'zh'=4,'core'=2,'y'=4,'zl'=2] {'x','zh','core'}, dimensions={0} | all-to-all | bytes 524288 | tf_op jit(solution)/shard_map/all_to_all | solution.py:25
  205.3 0.9 copy-done.2
  206.2 1.4 shard_map.106
  207.6 3.5 %all-to-all-start.4 = ((f32[8,8,1536]{2,1,0:T(8,128)}), f32[8,8,1536]{2,1,0:T(8,128)S(1)}, u32[]{:S(2)}, u32[]{:S(2)}) async-start(f32[8,8,1536]{2,1,0:T(8,128)} %shard_map.106), calls=%async_computation.4 | async-start | bytes 786432 | tf_op jit(solution)/shard_map/all_to_all | solution.py:25
  211.0 0.8 neg.3
  211.8 7.5 %all-to-all-done.4 = f32[8,8,1536]{2,1,0:T(8,128)S(1)} async-done(((f32[8,8,1536]{2,1,0:T(8,128)}), f32[8,8,1536]{2,1,0:T(8,128)S(1)}, u32[]{:S(2)}, u32[]{:S(2)}) %all-to-all-start.4) | async-done | bytes 393248 | tf_op jit(solution)/shard_map/all_to_all | solution.py:25
  219.3 0.6 slice_add_fusion
  220.0 2.6 %convolution_subtract_fusion = f32[4,1024]{1,0:T(4,128)} fusion(bf16[1024,1024]{1,0:T(8,128)(2,1)} %cp.1, f32[8,1536]{1,0:T(8,128)S(1)} %reduce_sum.19, f32[4,1024]{1,0:T(4,128)S(1)} %get-tuple-element.44), kind=kOutput, calls=%fused_computation.3 | convolution fusion | flops 8396800 | bytes 2146304 | tf_op jit(solution)/shard_map/dot_general | solution.py:17
  (28 shorter events, 0.1 us)
Async XLA Ops:
  7.2 14.5 %copy-start = (bf16[1024,1024]{1,0:T(8,128)(2,1)S(1)}, bf16[1024,1024]{1,0:T(8,128)(2,1)}, u32[]{:S(2)}) copy-start(bf16[1024,1024]{1,0:T(8,128)(2,1)} %param.8) | copy-start | bytes 6291460
  7.2 91.9 %all-gather.2.cloned.1.call-start = ((), (), s32[]{:S(2)}) async-start(), calls=%async_computation.5 | async-start | bytes 6488064 | tf_op jit(solution)/shard_map/all_gather | solution.py:339
  7.9 17.3 %collective-permute-start.1 = (bf16[96,1024]{1,0:T(8,128)(2,1)}, bf16[96,1024]{1,0:T(8,128)(2,1)S(1)}, u32[]{:S(2)}, u32[]{:S(2)}) collective-permute-start(bf16[96,1024]{1,0:T(8,128)(2,1)} %param.7), channel_id=1, source_target_pairs={{0,16},{16,32},{32,48},{48,0},{1,17},{17,33},{33,49},{49,1},{2,18}... | collective-permute-start | bytes 589832 | tf_op jit(solution)/shard_map/ppermute | solution.py:30
  11.8 18.4 %collective-permute-start = (bf16[96,1024]{1,0:T(8,128)(2,1)}, bf16[96,1024]{1,0:T(8,128)(2,1)S(1)}, u32[]{:S(2)}, u32[]{:S(2)}) collective-permute-start(bf16[96,1024]{1,0:T(8,128)(2,1)} %param.7), channel_id=1, source_target_pairs={{0,48},{16,0},{32,16},{48,32},{1,49},{17,1},{33,17},{49,33},{2,50}... | collective-permute-start | bytes 589832 | tf_op jit(solution)/shard_map/ppermute | solution.py:30
  14.9 15.6 %collective-permute-start.2 = (bf16[96,1024]{1,0:T(8,128)(2,1)}, bf16[96,1024]{1,0:T(8,128)(2,1)S(1)}, u32[]{:S(2)}, u32[]{:S(2)}) collective-permute-start(bf16[96,1024]{1,0:T(8,128)(2,1)} %param.7), channel_id=1, source_target_pairs={{0,32},{16,48},{32,0},{48,16},{1,33},{17,49},{33,1},{49,17},{2,34}... | collective-permute-start | bytes 589832 | tf_op jit(solution)/shard_map/ppermute | solution.py:30
  19.3 2.3 %copy-start.3 = (bf16[1024,1024]{1,0:T(8,128)(2,1)S(1)}, bf16[1024,1024]{1,0:T(8,128)(2,1)}, u32[]{:S(2)}) copy-start(bf16[1024,1024]{1,0:T(8,128)(2,1)} %cp.1) | copy-start | bytes 6291460
  24.0 6.5 %copy-start.14 = (bf16[96,1024]{1,0:T(8,128)(2,1)S(1)}, bf16[96,1024]{1,0:T(8,128)(2,1)}, u32[]{:S(2)}) copy-start(bf16[96,1024]{1,0:T(8,128)(2,1)} %param.7) | copy-start | bytes 589828
  30.5 32.3 %copy-start.4 = (bf16[384,1024]{1,0:T(8,128)(2,1)}, bf16[384,1024]{1,0:T(8,128)(2,1)S(1)}, u32[]{:S(2)}) copy-start(bf16[384,1024]{1,0:T(8,128)(2,1)S(1)} %pad_maximum_fusion.refs_0_) | copy-start | bytes 2359300
  30.6 5.2 %collective-permute-start.5 = (bf16[384,1024]{1,0:T(8,128)(2,1)S(1)}, bf16[384,1024]{1,0:T(8,128)(2,1)S(1)}, u32[]{:S(2)}, u32[]{:S(2)}) collective-permute-start(bf16[384,1024]{1,0:T(8,128)(2,1)S(1)} %pad_maximum_fusion.refs_0_), channel_id=1, source_target_pairs={{0,8},{8,0},{1,9},{9,1},{2,10},{10,2},{3,11},{11,3},{4,12},{12,4},... | collective-permute-start | bytes 2359304 | tf_op jit(solution)/shard_map/ppermute | solution.py:30
  33.1 22.0 %collective-permute-start.4 = (bf16[384,1024]{1,0:T(8,128)(2,1)S(1)}, bf16[384,1024]{1,0:T(8,128)(2,1)S(1)}, u32[]{:S(2)}, u32[]{:S(2)}) collective-permute-start(bf16[384,1024]{1,0:T(8,128)(2,1)S(1)} %pad_maximum_fusion.refs_0_), channel_id=1, source_target_pairs={{0,64},{64,128},{128,192},{192,0},{1,65},{65,129},{129,193},{193,1... | collective-permute-start | bytes 2359304 | tf_op jit(solution)/shard_map/ppermute | solution.py:30
  34.3 20.8 %collective-permute-start.3 = (bf16[384,1024]{1,0:T(8,128)(2,1)S(1)}, bf16[384,1024]{1,0:T(8,128)(2,1)S(1)}, u32[]{:S(2)}, u32[]{:S(2)}) collective-permute-start(bf16[384,1024]{1,0:T(8,128)(2,1)S(1)} %pad_maximum_fusion.refs_0_), channel_id=1, source_target_pairs={{0,192},{64,0},{128,64},{192,128},{1,193},{65,1},{129,65},{193,129... | collective-permute-start | bytes 2359304 | tf_op jit(solution)/shard_map/ppermute | solution.py:30
  35.7 19.3 %copy-start.11 = (bf16[384,1024]{1,0:T(8,128)(2,1)}, bf16[384,1024]{1,0:T(8,128)(2,1)S(1)}, u32[]{:S(2)}) copy-start(bf16[384,1024]{1,0:T(8,128)(2,1)S(1)} %collective-permute-done.5.refs_3_.refs_5_) | copy-start | bytes 2359300
  55.1 7.7 %copy-start.6 = (bf16[384,1024]{1,0:T(8,128)(2,1)}, bf16[384,1024]{1,0:T(8,128)(2,1)S(1)}, u32[]{:S(2)}) copy-start(bf16[384,1024]{1,0:T(8,128)(2,1)S(1)} %collective-permute-done.4.refs_2_) | copy-start | bytes 2359300
  55.1 6.0 %copy-start.7 = (bf16[384,1024]{1,0:T(8,128)(2,1)}, bf16[384,1024]{1,0:T(8,128)(2,1)S(1)}, u32[]{:S(2)}) copy-start(bf16[384,1024]{1,0:T(8,128)(2,1)S(1)} %collective-permute-done.3.refs_1_) | copy-start | bytes 2359300
  55.1 5.9 %collective-permute-start.8 = (bf16[384,1024]{1,0:T(8,128)(2,1)S(1)}, bf16[384,1024]{1,0:T(8,128)(2,1)S(1)}, u32[]{:S(2)}, u32[]{:S(2)}) collective-permute-start(bf16[384,1024]{1,0:T(8,128)(2,1)S(1)} %collective-permute-done.3.refs_1_), channel_id=1, source_target_pairs={{0,8},{8,0},{1,9},{9,1},{2,10},{10,2},{3,11},{11,3},{4,12},{12,4},... | collective-permute-start | bytes 2359304 | tf_op jit(solution)/shard_map/ppermute | solution.py:30
  56.1 5.0 %collective-permute-start.9 = (bf16[384,1024]{1,0:T(8,128)(2,1)S(1)}, bf16[384,1024]{1,0:T(8,128)(2,1)S(1)}, u32[]{:S(2)}, u32[]{:S(2)}) collective-permute-start(bf16[384,1024]{1,0:T(8,128)(2,1)S(1)} %collective-permute-done.4.refs_2_), channel_id=1, source_target_pairs={{0,8},{8,0},{1,9},{9,1},{2,10},{10,2},{3,11},{11,3},{4,12},{12,4},... | collective-permute-start | bytes 2359304 | tf_op jit(solution)/shard_map/ppermute | solution.py:30
  57.7 15.8 %collective-permute-start.7 = (bf16[192,1024]{1,0:T(8,128)(2,1)}, bf16[192,1024]{1,0:T(8,128)(2,1)S(1)}, u32[]{:S(2)}, u32[]{:S(2)}) collective-permute-start(bf16[192,1024]{1,0:T(8,128)(2,1)} %slice.19), channel_id=1, source_target_pairs={{0,64},{64,128},{128,192},{192,0},{1,65},{65,129},{129,193},{193,1... | collective-permute-start | bytes 1179656 | tf_op jit(solution)/shard_map/ppermute | solution.py:30
  58.7 15.8 %collective-permute-start.6 = (bf16[192,1024]{1,0:T(8,128)(2,1)}, bf16[192,1024]{1,0:T(8,128)(2,1)}, u32[]{:S(2)}, u32[]{:S(2)}) collective-permute-start(bf16[192,1024]{1,0:T(8,128)(2,1)} %slice.18), channel_id=1, source_target_pairs={{0,192},{64,0},{128,64},{192,128},{1,193},{65,1},{129,65},{193,129... | collective-permute-start | bytes 1179656 | tf_op jit(solution)/shard_map/ppermute | solution.py:30
  61.0 0.9 copy-start.12
  61.9 0.9 copy-start.13
  73.5 5.8 %copy-start.8 = (bf16[192,1024]{1,0:T(8,128)(2,1)}, bf16[192,1024]{1,0:T(8,128)(2,1)S(1)}, u32[]{:S(2)}) copy-start(bf16[192,1024]{1,0:T(8,128)(2,1)S(1)} %collective-permute-done.7.refs_1_.refs_4_) | copy-start | bytes 1179652
  74.4 4.8 %collective-permute-start.10 = (bf16[192,1024]{1,0:T(8,128)(2,1)}, bf16[192,1024]{1,0:T(8,128)(2,1)S(1)}, u32[]{:S(2)}, u32[]{:S(2)}) collective-permute-start(bf16[192,1024]{1,0:T(8,128)(2,1)} %collective-permute-done.6.refs_0_.refs_3_), channel_id=1, source_target_pairs={{0,8},{8,0},{1,9},{9,1},{2,10},{10,2},{3,11},{11,3},{4,12},{12,4},... | collective-permute-start | bytes 1179656 | tf_op jit(solution)/shard_map/ppermute | solution.py:30
  77.0 2.2 collective-permute-start.11
  79.2 0.7 copy-start.9
  80.0 0.8 copy-start.10
  86.1 33.9 %all-to-all-start = ((bf16[8,96,1024]{2,1,0:T(8,128)(2,1)}), bf16[8,96,1024]{2,1,0:T(8,128)(2,1)}, u32[]{:S(2)}, u32[]{:S(2)}) async-start(bf16[8,96,1024]{2,1,0:T(8,128)(2,1)} %shard_map.102), calls=%async_computation | async-start | bytes 3145728 | tf_op jit(solution)/shard_map/all_to_all | solution.py:25
  120.0 24.2 %all-to-all-start.1 = ((bf16[8,96,1024]{2,1,0:T(8,128)(2,1)}), bf16[8,96,1024]{2,1,0:T(8,128)(2,1)}, u32[]{:S(2)}, u32[]{:S(2)}) async-start(bf16[8,96,1024]{2,1,0:T(8,128)(2,1)} %bitcast.24), calls=%async_computation.1 | async-start | bytes 3145728 | tf_op jit(solution)/shard_map/all_to_all | solution.py:25
  146.6 0.9 copy-start.1
  147.5 30.5 %all-to-all-start.2 = ((bf16[32,3,32,96]{3,2,1,0:T(8,128)(2,1)}), bf16[32,3,32,96]{3,2,1,0:T(8,128)(2,1)S(1)}, u32[]{:S(2)}, u32[]{:S(2)}) async-start(bf16[32,3,32,96]{3,2,1,0:T(8,128)(2,1)} %copy-done.1), calls=%async_computation.2 | async-start | bytes 1572864 | tf_op jit(solution)/shard_map/all_to_all | solution.py:25
  178.1 0.9 copy-start.5
  205.3 1.0 copy-start.2
  207.6 11.7 %all-to-all-start.4 = ((f32[8,8,1536]{2,1,0:T(8,128)}), f32[8,8,1536]{2,1,0:T(8,128)S(1)}, u32[]{:S(2)}, u32[]{:S(2)}) async-start(f32[8,8,1536]{2,1,0:T(8,128)} %shard_map.106), calls=%async_computation.4 | async-start | bytes 786432 | tf_op jit(solution)/shard_map/all_to_all | solution.py:25
  220.0 2.6 %copy-start.15 = (f32[4,1024]{1,0:T(4,128)}, f32[4,1024]{1,0:T(4,128)S(1)}, u32[]{:S(2)}) copy-start(f32[4,1024]{1,0:T(4,128)S(1)} %get-tuple-element.44) | copy-start | bytes 49156
Sparse Core Ops, SparseCore 0:
  10.6 75.2 all-gather.1

commit v9 on v8

--- a/solution.py
+++ b/solution.py
@@ -81,7 +81,7 @@
 
 
 def far_kernel(where, *refs):
-    near, z, out, panel, zcols, acc, result, sem, zsem, near_sem, out_sem = refs[4:]
+    near, z, out, own, panel, zcols, acc, result, sem, zsem, near_sem, out_sem, own_sem = refs[4:]
     depth, rows = panel.shape[0], refs[0].shape[0] // 2
     at = ring_block(3, where)
     zcopy = pltpu.make_async_copy(
@@ -100,10 +100,16 @@
     pltpu.make_async_copy(panel, panel, sem).wait()
     got = jnp.dot(zcols[...], panel[...], preferred_element_type=F32)
     ncopy.wait()
-    result[...] = (acc[...] + got).astype(BF).reshape(result.shape)
+    got += acc[...]
+    acc[...] = got
+    result[...] = got.astype(BF).reshape(result.shape)
     copy = pltpu.make_async_copy(result, out, out_sem)
     copy.start()
+    at = pl.multiple_of(where[3] * rows, 32)
+    keep = pltpu.make_async_copy(acc.at[pl.ds(at, rows)], own, own_sem)
+    keep.start()
     copy.wait()
+    keep.wait()
 
 
 def near_product(where, mine, others, z):
@@ -145,7 +151,7 @@
             num_scalar_prefetch=1,
             grid=(),
             in_specs=[hbm] * 6,
-            out_specs=hbm,
+            out_specs=[hbm] * 2,
             scratch_shapes=[
                 pltpu.VMEM((depth, width), BF),
                 pltpu.VMEM((z.shape[0], depth), BF),
@@ -155,9 +161,10 @@
                 pltpu.SemaphoreType.DMA(()),
                 pltpu.SemaphoreType.DMA(()),
                 pltpu.SemaphoreType.DMA(()),
+                pltpu.SemaphoreType.DMA(()),
             ],
         ),
-        out_shape=jax.ShapeDtypeStruct(blocks, BF),
+        out_shape=[jax.ShapeDtypeStruct(blocks, BF), jax.ShapeDtypeStruct((rows, width), F32)],
         compiler_params=pltpu.CompilerParams(vmem_limit_bytes=60 << 20),
         cost_estimate=pl.CostEstimate(
             flops=z.size * width // 2,
@@ -244,7 +251,7 @@
                 v = big[g * 16 : (g + 1) * 16, q * 128 : (q + 1) * 128]
                 v = pltpu.roll(v, ((g - d) * sl) % 128, 1) if g != d else v
                 out = v if out is None else jnp.where(lane == g, v, out)
-            t[q * 4 + d] = out
+            t[q * 4 + d] = out.astype(BF)
 
 def slices(x, parent, child, cp):
     nr, kinds, sl, rows = x.shape
@@ -256,7 +263,7 @@
         slices_kernel,
         in_specs=[vm, any_, any_, any_],
         out_specs=[vm, vm],
-        out_shape=[jax.ShapeDtypeStruct((nr, 16, 128), F32), jax.ShapeDtypeStruct((2, sl, w), F32)],
+        out_shape=[jax.ShapeDtypeStruct((nr, 16, 128), BF), jax.ShapeDtypeStruct((2, sl, w), F32)],
         scratch_shapes=[pltpu.VMEM((kinds * sl, depth), BF), pltpu.VMEM((depth, w), BF), pltpu.VMEM((depth, w), BF), pltpu.VMEM(cp.shape, BF), pltpu.VMEM((5 * sl, w), F32),
             pltpu.SemaphoreType.DMA((parts,)), pltpu.SemaphoreType.DMA((parts,)), pltpu.SemaphoreType.DMA(())],
         compiler_params=pltpu.CompilerParams(vmem_limit_bytes=60 << 20),
@@ -272,7 +279,7 @@
             tall = []
             for d in range(4):
                 for h in range(2):
-                    v = t[q * 4 + d]
+                    v = t[q * 4 + d].astype(F32)
                     g = kind * 2 + h
                     tall.append(pltpu.roll(v, (128 - g * sl) % 128, 1) if g else v)
             tall = jnp.concatenate(tall, axis=0)
@@ -300,24 +307,23 @@
     )(t, r)
 
 
-def ancestors_kernel(got, shifted, ut, st, anc, x):
+def ancestors_kernel(where, got, own, shifted, ut, st, anc, x):
     nr, _, sl, rows = x.shape
-    low = got[0].astype(F32)
-    for n in range(1, got.shape[0]):
-        low += got[n].astype(F32)
-    low -= shifted[...]
+    low = own[...] - shifted[...]
+    for n in range(got.shape[0]):
+        low += jnp.where(where[3] == n, 0.0, got[n].astype(F32))
     anc[...] = -low
     x[:, 0] = ut[...].reshape(nr, sl, rows)
     x[:, 1] = st[...].reshape(nr, sl, rows)
     x[:, 2] = low.T.astype(BF).reshape(nr, sl, rows)
 
 
-def ancestors(got, shifted, ut, st, nr):
+def ancestors(where, got, own, shifted, ut, st, nr):
     rows, w = shifted.shape
     vmem = pl.BlockSpec(memory_space=pltpu.VMEM)
     return pl.pallas_call(
         ancestors_kernel,
-        in_specs=[vmem] * 4,
+        in_specs=[pl.BlockSpec(memory_space=pltpu.SMEM)] + [vmem] * 5,
         out_specs=[vmem] * 2,
         out_shape=[
             jax.ShapeDtypeStruct((rows, w), F32),
@@ -325,7 +331,7 @@
         ],
         compiler_params=pltpu.CompilerParams(vmem_limit_bytes=16 << 20),
         cost_estimate=pl.CostEstimate(flops=9 * rows * w, transcendentals=0, bytes_accessed=40 * rows * w),
-    )(got, shifted, ut, st)
+    )(where, got, own, shifted, ut, st)
 
 
 def shards(z, pp, pdi, ca, cp, cdi):
@@ -333,7 +339,7 @@
     nr, nc = lax.axis_size(ROW), lax.axis_size(COL)
     sl = w // nr
     own = sl // nc
-    where = jnp.stack([lax.axis_index(a) for a in ROW]).astype(jnp.int32)
+    where = jnp.stack([lax.axis_index(a) for a in ROW + (COL,)]).astype(jnp.int32)
     block = z.reshape(z.shape[0], -1)
 
     child = lax.all_gather(ca, ROW, axis=0, tiled=True)
@@ -352,15 +358,17 @@
     near = near_product(where, pieces[:3], others, block)
     pieces[3], pieces[4], near = hold((pieces[3], pieces[4], near))
     others += [swap(pieces[3]), swap(pieces[4])]
-    up = far_product(where, pieces[3:], others[3:], near, block, rows)
-    upper = jnp.sum(exchange(up, COL).astype(F32), axis=0)
+    up, own_up = far_product(where, pieces[3:], others[3:], near, block, rows)
+    foreign = (jnp.arange(nc) != where[3])[:, None, None]
+    upper = own_up + jnp.sum(jnp.where(foreign, exchange(up, COL).astype(F32), 0.0), axis=0)
     u = upper.astype(BF)
     shifted = dot(u, cp)
     s = shifted.astype(BF)
 
     lp = dot(block, child).astype(BF).reshape(nc, rows, w)
     got = exchange(lp, COL)
-    anc, x = ancestors(got, shifted, u.T, s.T, nr)
+    own_lp = dot(lax.dynamic_slice_in_dim(block, where[3] * rows, rows, 0), child)
+    anc, x = ancestors(where, got, own_lp, shifted, u.T, s.T, nr)
     others[0], x = hold((others[0], x))
     x = exchange(x, ROW)
     parent = whole_panel(where, pieces, others, block.shape[1])

time: 230 us -> 229 us (level)
  waiting for transfers between devices: 80 us -> 74.4 us
  matrix products: 20.7 us -> 24.1 us
    all_to_all x4, waiting for transfers between devices: 50.2 us -> 44.5 us  [exchange(): return lax.all_to_all(a, axes, 0, 0, tiled=True)]
    dot_general x7 -> x8, matrix products: 20.7 us -> 24.1 us  [dot(): lax.dot_general(a, b, (((ca,), (cb,)), ((), ())), preferred_element_type=...]
    unnamed x32 -> x39, local copies, waits for them, and re-layouts: 6.08 us -> 7.03 us
  transfers between devices with their start and end apart: 17 -> 17, of which waited for: 10 -> 10; matrix products, arithmetic and copies ran while one was open for 11% -> 13% of each run, Pallas kernels for 9% -> 9%
where the time goes in v9:
time: 229 us; the launch traced here: 228 us
  waiting for transfers between devices  74.4 us (32%)
  starting transfers between devices  50.9 us (22%)
  Pallas kernels  33.2 us (14%)
  matrix products  24.1 us (11%)
  blocking collectives  16.2 us (7%)
  between operations  14.2 us (6%)
  local copies, waits for them, and re-layouts  10.1 us (4%)
  other arithmetic  4.83 us (2%)
    all_to_all x4, waiting for transfers between devices, exchange(): return lax.all_to_all(a, axes, 0, 0, tiled=True)  44.5 us
    ppermute x12, waiting for transfers between devices, shift(): return lax.ppermute(a, axis, [(i, (i + by) % n) for i in range(n)])  29.2 us
    all_to_all x4, starting transfers between devices, exchange(): return lax.all_to_all(a, axes, 0, 0, tiled=True)  28 us
    dot_general x8, matrix products, dot(): lax.dot_general(a, b, (((ca,), (cb,)), ((), ())), preferred_element_type=...  24.1 us
    ppermute x12, starting transfers between devices, shift(): return lax.ppermute(a, axis, [(i, (i + by) % n) for i in range(n)])  22.9 us
    all_to_all x1, blocking collectives, exchange(): return lax.all_to_all(a, axes, 0, 0, tiled=True)  16.2 us
    pallas_call x1, Pallas kernels, near_product(): pl.pallas_call(near_kernel, grid_spec=pltpu.PrefetchScalarGridSpec(num_sc...  9.25 us
    pallas_call x1, Pallas kernels, slices(): pl.pallas_call(slices_kernel, in_specs=[vm, any_, any_, any_], out_specs=...  7.8 us
  transfers between devices with their start and end apart: 17, of which 10 were waited for; matrix products, arithmetic and copies ran while one was open for 13% of the time, Pallas kernels for 9%

profile of v9, /device:TPU:1, one launch (start us, length us, event | category | flops | bytes accessed | tf_op | source)
XLA Modules:
  0.0 228.1 jit_solution(11080468028987525711)
XLA Ops:
  7.2 0.0 copy-start
  7.2 0.0 all-gather.2.cloned.1.call-start
  7.2 0.7 all-gather.2.cloned.1.call-update
  7.9 3.9 %collective-permute-start.1 = (bf16[96,1024]{1,0:T(8,128)(2,1)}, bf16[96,1024]{1,0:T(8,128)(2,1)S(1)}, u32[]{:S(2)}, u32[]{:S(2)}) collective-permute-start(bf16[96,1024]{1,0:T(8,128)(2,1)} %param.7), channel_id=1, source_target_pairs={{0,16},{16,32},{32,48},{48,0},{1,17},{17,33},{33,49},{49,1},{2,18}... | collective-permute-start | bytes 589832 | tf_op jit(solution)/shard_map/ppermute | solution.py:30
  11.8 3.1 %collective-permute-start = (bf16[96,1024]{1,0:T(8,128)(2,1)}, bf16[96,1024]{1,0:T(8,128)(2,1)S(1)}, u32[]{:S(2)}, u32[]{:S(2)}) collective-permute-start(bf16[96,1024]{1,0:T(8,128)(2,1)} %param.7), channel_id=1, source_target_pairs={{0,48},{16,0},{32,16},{48,32},{1,49},{17,1},{33,17},{49,33},{2,50}... | collective-permute-start | bytes 589832 | tf_op jit(solution)/shard_map/ppermute | solution.py:30
  14.9 4.4 %collective-permute-start.2 = (bf16[96,1024]{1,0:T(8,128)(2,1)}, bf16[96,1024]{1,0:T(8,128)(2,1)S(1)}, u32[]{:S(2)}, u32[]{:S(2)}) collective-permute-start(bf16[96,1024]{1,0:T(8,128)(2,1)} %param.7), channel_id=1, source_target_pairs={{0,32},{16,48},{32,0},{48,16},{1,33},{17,49},{33,1},{49,17},{2,34}... | collective-permute-start | bytes 589832 | tf_op jit(solution)/shard_map/ppermute | solution.py:30
  19.3 2.3 %fusion.3 = f32[4,1024]{1,0:T(4,128)S(1)} fusion(bf16[1024,1024]{1,0:T(8,128)(2,1)} %param.11, s32[]{:T(128)S(6)} %select_n.12), kind=kOutput, calls=%fused_computation.9 | convolution fusion | flops 8388608 | bytes 2375684 | tf_op jit(solution)/shard_map/dot_general | solution.py:17
  21.6 2.4 %convolution_convert_fusion = bf16[1024,1024]{0,1:T(8,128)(2,1)S(1)} fusion(bf16[1024,1024]{1,0:T(8,128)(2,1)S(1)} %copy-done, bf16[1024,1024]{1,0:T(8,128)(2,1)S(1)} %copy-done.4), kind=kOutput, calls=%fused_computation.1 | convolution fusion | flops 2148532224 | bytes 6291456 | tf_op jit(solution)/shard_map/dot_general | solution.py:17
  24.0 0.0 copy-start.17
  24.0 0.6 convolution_add_fusion
  24.7 0.5 fusion.5
  25.2 5.0 %collective-permute-done = bf16[96,1024]{1,0:T(8,128)(2,1)S(1)} collective-permute-done((bf16[96,1024]{1,0:T(8,128)(2,1)}, bf16[96,1024]{1,0:T(8,128)(2,1)S(1)}, u32[]{:S(2)}, u32[]{:S(2)}) %collective-permute-start) | collective-permute-done | bytes 196640 | tf_op jit(solution)/shard_map/ppermute | solution.py:30
  30.2 0.3 collective-permute-done.2
  30.5 0.1 pad_maximum_fusion.refs_0_
  30.6 2.5 %collective-permute-start.5 = (bf16[384,1024]{1,0:T(8,128)(2,1)S(1)}, bf16[384,1024]{1,0:T(8,128)(2,1)S(1)}, u32[]{:S(2)}, u32[]{:S(2)}) collective-permute-start(bf16[384,1024]{1,0:T(8,128)(2,1)S(1)} %pad_maximum_fusion.refs_0_), channel_id=1, source_target_pairs={{0,8},{8,0},{1,9},{9,1},{2,10},{10,2},{3,11},{11,3},{4,12},{12,4},... | collective-permute-start | bytes 2359304 | tf_op jit(solution)/shard_map/ppermute | solution.py:30
  33.1 1.2 collective-permute-start.4
  34.3 1.5 collective-permute-start.3
  35.8 19.3 %collective-permute-done.4.refs_2_ = bf16[384,1024]{1,0:T(8,128)(2,1)S(1)} collective-permute-done((bf16[384,1024]{1,0:T(8,128)(2,1)S(1)}, bf16[384,1024]{1,0:T(8,128)(2,1)S(1)}, u32[]{:S(2)}, u32[]{:S(2)}) %collective-permute-start.4) | collective-permute-done | bytes 786464 | tf_op jit(solution)/shard_map/ppermute | solution.py:30
  55.1 0.0 collective-permute-done.3.refs_1_
  55.1 1.0 collective-permute-start.8
  56.1 0.1 collective-permute-start.9
  56.2 0.8 slice.18
  56.9 0.8 slice.19
  57.7 1.0 collective-permute-start.7
  58.7 1.7 collective-permute-start.6
  60.4 0.7 pad_add_fusion.where
  61.1 0.9 copy-done.14
  61.9 0.9 copy-done.15
  62.8 9.3 %shard_map.101.refs_4_ = f32[768,1024]{1,0:T(8,128)} custom-call(s32[4]{0:T(128)} %pad_add_fusion.where, bf16[384,1024]{1,0:T(8,128)(2,1)} %copy-done.5, bf16[384,1024]{1,0:T(8,128)(2,1)} %copy-done.9, bf16[384,1024]{1,0:T(8,128)(2,1)} %copy-done.8, bf16[384,1024]{1,0:T(8,128)(2,1)} %copy-done.13, bf16[384,1024]{1,0:T(8,128)(2,1)} %copy-done.14, ...), custom_call_target="tpu_custom_call" | custom-call | flops 3623878656 | bytes 11403264 | tf_op jit(solution)/shard_map/pallas_call | solution.py:118
  72.1 1.4 collective-permute-done.7.refs_1_.refs_4_
  73.5 1.0 collective-permute-done.6.refs_0_.refs_3_
  74.4 2.6 %collective-permute-start.10 = (bf16[192,1024]{1,0:T(8,128)(2,1)}, bf16[192,1024]{1,0:T(8,128)(2,1)S(1)}, u32[]{:S(2)}, u32[]{:S(2)}) collective-permute-start(bf16[192,1024]{1,0:T(8,128)(2,1)} %collective-permute-done.6.refs_0_.refs_3_), channel_id=1, source_target_pairs={{0,8},{8,0},{1,9},{9,1},{2,10},{10,2},{3,11},{11,3},{4,12},{12,4},... | collective-permute-start | bytes 1179656 | tf_op jit(solution)/shard_map/ppermute | solution.py:30
  77.0 2.2 collective-permute-done.10.refs_2_.refs_8_
  79.2 0.7 copy-done.11
  80.0 0.7 copy-done.12
  80.7 6.4 %shard_map.102 = (bf16[8,96,1024]{2,1,0:T(8,128)(2,1)}, f32[96,1024]{1,0:T(8,128)}) custom-call(s32[4]{0:T(128)} %pad_add_fusion.where, bf16[192,1024]{1,0:T(8,128)(2,1)} %collective-permute-done.6.refs_0_.refs_3_, bf16[192,1024]{1,0:T(8,128)(2,1)} %copy-done.10, bf16[192,1024]{1,0:T(8,128)(2,1)} %copy-done.11, bf16[192,1024]{1,0:T(8,128)(2,1)} %copy-done.12, ...), custom_call_target="tpu_custom_call" | custom-call | flops 1207959552 | bytes 7471104 | tf_op jit(solution)/shard_map/pallas_call | solution.py:148
  87.1 12.9 %all-to-all-start = ((bf16[8,96,1024]{2,1,0:T(8,128)(2,1)}), bf16[8,96,1024]{2,1,0:T(8,128)(2,1)}, u32[]{:S(2)}, u32[]{:S(2)}) async-start(bf16[8,96,1024]{2,1,0:T(8,128)(2,1)} %get-tuple-element.30), calls=%async_computation | async-start | bytes 3145728 | tf_op jit(solution)/shard_map/all_to_all | solution.py:25
  100.0 0.0 all-gather.2.cloned.1.call-done.child
  100.0 9.5 %convolution_convert_fusion.1 = bf16[768,1024]{1,0:T(8,128)(2,1)} fusion(bf16[3072,1024]{1,0:T(8,128)(2,1)} %all-gather.2.cloned.1.call-done.child, bf16[768,1,3072]{2,0,1:T(8,128)(2,1)} %param.6), kind=kOutput, calls=%fused_computation.2 | convolution fusion | flops 4832624640 | bytes 12582912 | tf_op jit(solution)/shard_map/dot_general | solution.py:17
  109.5 11.4 %all-to-all-done = bf16[8,96,1024]{2,1,0:T(8,128)(2,1)} async-done(((bf16[8,96,1024]{2,1,0:T(8,128)(2,1)}), bf16[8,96,1024]{2,1,0:T(8,128)(2,1)}, u32[]{:S(2)}, u32[]{:S(2)}) %all-to-all-start) | async-done | bytes 1572896 | tf_op jit(solution)/shard_map/all_to_all | solution.py:25
  120.9 4.3 %all-to-all-start.1 = ((bf16[8,96,1024]{2,1,0:T(8,128)(2,1)}), bf16[8,96,1024]{2,1,0:T(8,128)(2,1)}, u32[]{:S(2)}, u32[]{:S(2)}) async-start(bf16[8,96,1024]{2,1,0:T(8,128)(2,1)} %bitcast.27), calls=%async_computation.1 | async-start | bytes 3145728 | tf_op jit(solution)/shard_map/all_to_all | solution.py:25
  125.2 0.2 copy.18
  125.4 2.6 %select_reduce_fusion = f32[96,1024]{1,0:T(8,128)} fusion(bf16[8,96,1024]{2,1,0:T(8,128)(2,1)} %all-to-all-done, pred[8]{0:T(512)(128)(4,1)S(1)} %iota_compare_fusion), kind=kLoop, calls=%fused_computation | loop fusion | flops 2260992 | bytes 1966088 | tf_op jit(solution)/shard_map/reduce_sum | solution.py:363
  128.0 1.2 copy.19
  129.2 0.9 add_convert_fusion
  130.0 2.1 fusion.15
  132.1 0.2 copy.20
  132.3 4.1 %fusion.own = f32[96,1024]{1,0:T(8,128)S(1)} fusion(bf16[3072,1024]{1,0:T(8,128)(2,1)} %all-gather.2.cloned.1.call-done.child, bf16[768,1,3072]{2,0,1:T(8,128)(2,1)} %param.6, s32[]{:T(128)S(6)} %select_n.14), kind=kOutput, calls=%fused_computation.6 | convolution fusion | flops 603979776 | bytes 7274500 | tf_op jit(solution)/shard_map/dot_general | solution.py:17
  136.4 8.6 %all-to-all-done.1.got = bf16[8,96,1024]{2,1,0:T(8,128)(2,1)} async-done(((bf16[8,96,1024]{2,1,0:T(8,128)(2,1)}), bf16[8,96,1024]{2,1,0:T(8,128)(2,1)}, u32[]{:S(2)}, u32[]{:S(2)}) %all-to-all-start.1) | async-done | bytes 1572896 | tf_op jit(solution)/shard_map/all_to_all | solution.py:25
  145.1 2.6 %shard_map.103 = (f32[96,1024]{1,0:T(8,128)}, bf16[32,3,32,96]{3,2,1,0:T(8,128)(2,1)S(1)}) custom-call(s32[4]{0:T(128)S(1)} %copy-done.3, bf16[8,96,1024]{2,1,0:T(8,128)(2,1)} %all-to-all-done.1.got, f32[96,1024]{1,0:T(8,128)S(1)} %fusion.own, f32[96,1024]{1,0:T(8,128)S(1)} %get-tuple-element.59.shifted, bf16[1024,96]{1,0:T(8,128)(2,1)S(1)} %bitcast.23, ...), custom_call_target="tpu_custom_call" | custom-call | flops 884736 | bytes 3932160 | tf_op jit(solution)/shard_map/pallas_call | solution.py:324
  147.7 0.9 copy-done.1
  148.6 7.4 %all-to-all-start.2 = ((bf16[32,3,32,96]{3,2,1,0:T(8,128)(2,1)}), bf16[32,3,32,96]{3,2,1,0:T(8,128)(2,1)S(1)}, u32[]{:S(2)}, u32[]{:S(2)}) async-start(bf16[32,3,32,96]{3,2,1,0:T(8,128)(2,1)} %copy-done.1), calls=%async_computation.2 | async-start | bytes 1572864 | tf_op jit(solution)/shard_map/all_to_all | solution.py:25
  156.0 6.0 %shard_map.104.parent = bf16[3072,1024]{1,0:T(8,128)(2,1)} custom-call(s32[4]{0:T(128)} %pad_add_fusion.where, bf16[384,1024]{1,0:T(8,128)(2,1)} %copy-done.5, bf16[384,1024]{1,0:T(8,128)(2,1)} %copy-done.9, bf16[384,1024]{1,0:T(8,128)(2,1)} %copy-done.8, bf16[192,1024]{1,0:T(8,128)(2,1)} %collective-permute-done.6.refs_0_.refs_3_, ...), custom_call_target="tpu_custom_call" | custom-call | bytes 12582912 | tf_op jit(solution)/shard_map/pallas_call | solution.py:194
  162.0 17.1 %all-to-all-done.2.x = bf16[32,3,32,96]{3,2,1,0:T(8,128)(2,1)S(1)} async-done(((bf16[32,3,32,96]{3,2,1,0:T(8,128)(2,1)}), bf16[32,3,32,96]{3,2,1,0:T(8,128)(2,1)S(1)}, u32[]{:S(2)}, u32[]{:S(2)}) %all-to-all-start.2) | async-done | bytes 589856 | tf_op jit(solution)/shard_map/all_to_all | solution.py:25
  179.2 0.9 copy-done.6
  180.1 7.8 %shard_map.105 = (bf16[32,16,128]{2,1,0:T(8,128)(2,1)}, f32[2,32,1024]{2,1,0:T(8,128)}) custom-call(bf16[32,3,32,96]{3,2,1,0:T(8,128)(2,1)} %copy-done.6, bf16[3072,1024]{1,0:T(8,128)(2,1)} %shard_map.104.parent, bf16[3072,1024]{1,0:T(8,128)(2,1)} %all-gather.2.cloned.1.call-done.child, bf16[1024,1024]{1,0:T(8,128)(2,1)} %cp.1), custom_call_target="tpu_custom_call" | custom-call | flops 1006632960 | bytes 12582912 | tf_op jit(solution)/shard_map/pallas_call | solution.py:262
  187.9 16.2 %all_to_all.25.t = bf16[32,16,128]{2,1,0:T(8,128)(2,1)S(1)} all-to-all(bf16[32,16,128]{2,1,0:T(8,128)(2,1)} %get-tuple-element.35), channel_id=1, replica_groups=mesh['x'=4,'zh'=4,'core'=2,'y'=4,'zl'=2] {'x','zh','core'}, dimensions={0} | all-to-all | bytes 262144 | tf_op jit(solution)/shard_map/all_to_all | solution.py:25
  204.1 0.9 copy-done.2
  205.0 1.2 shard_map.106
  206.2 3.5 %all-to-all-start.4 = ((f32[8,8,1536]{2,1,0:T(8,128)}), f32[8,8,1536]{2,1,0:T(8,128)S(1)}, u32[]{:S(2)}, u32[]{:S(2)}) async-start(f32[8,8,1536]{2,1,0:T(8,128)} %shard_map.106), calls=%async_computation.4 | async-start | bytes 786432 | tf_op jit(solution)/shard_map/all_to_all | solution.py:25
  209.7 0.9 copy.21
  210.7 7.4 %all-to-all-done.4 = f32[8,8,1536]{2,1,0:T(8,128)S(1)} async-done(((f32[8,8,1536]{2,1,0:T(8,128)}), f32[8,8,1536]{2,1,0:T(8,128)S(1)}, u32[]{:S(2)}, u32[]{:S(2)}) %all-to-all-start.4) | async-done | bytes 393248 | tf_op jit(solution)/shard_map/all_to_all | solution.py:25
  218.1 0.6 slice_add_fusion
  218.7 2.6 %convolution_subtract_fusion = f32[4,1024]{1,0:T(4,128)} fusion(bf16[1024,1024]{1,0:T(8,128)(2,1)} %cp.1, f32[8,1536]{1,0:T(8,128)S(1)} %reduce_sum.19, f32[4,1024]{1,0:T(4,128)S(1)} %get-tuple-element.60), kind=kOutput, calls=%fused_computation.3 | convolution fusion | flops 8396800 | bytes 2146304 | tf_op jit(solution)/shard_map/dot_general | solution.py:17
  (38 shorter events, 0.1 us)
Async XLA Ops:
  7.2 14.5 %copy-start = (bf16[1024,1024]{1,0:T(8,128)(2,1)S(1)}, bf16[1024,1024]{1,0:T(8,128)(2,1)}, u32[]{:S(2)}) copy-start(bf16[1024,1024]{1,0:T(8,128)(2,1)} %param.8) | copy-start | bytes 6291460
  7.2 92.8 %all-gather.2.cloned.1.call-start = ((), (), s32[]{:S(2)}) async-start(), calls=%async_computation.5 | async-start | bytes 6488064 | tf_op jit(solution)/shard_map/all_gather | solution.py:345
  7.9 17.3 %collective-permute-start.1 = (bf16[96,1024]{1,0:T(8,128)(2,1)}, bf16[96,1024]{1,0:T(8,128)(2,1)S(1)}, u32[]{:S(2)}, u32[]{:S(2)}) collective-permute-start(bf16[96,1024]{1,0:T(8,128)(2,1)} %param.7), channel_id=1, source_target_pairs={{0,16},{16,32},{32,48},{48,0},{1,17},{17,33},{33,49},{49,1},{2,18}... | collective-permute-start | bytes 589832 | tf_op jit(solution)/shard_map/ppermute | solution.py:30
  11.8 18.4 %collective-permute-start = (bf16[96,1024]{1,0:T(8,128)(2,1)}, bf16[96,1024]{1,0:T(8,128)(2,1)S(1)}, u32[]{:S(2)}, u32[]{:S(2)}) collective-permute-start(bf16[96,1024]{1,0:T(8,128)(2,1)} %param.7), channel_id=1, source_target_pairs={{0,48},{16,0},{32,16},{48,32},{1,49},{17,1},{33,17},{49,33},{2,50}... | collective-permute-start | bytes 589832 | tf_op jit(solution)/shard_map/ppermute | solution.py:30
  14.9 15.6 %collective-permute-start.2 = (bf16[96,1024]{1,0:T(8,128)(2,1)}, bf16[96,1024]{1,0:T(8,128)(2,1)S(1)}, u32[]{:S(2)}, u32[]{:S(2)}) collective-permute-start(bf16[96,1024]{1,0:T(8,128)(2,1)} %param.7), channel_id=1, source_target_pairs={{0,32},{16,48},{32,0},{48,16},{1,33},{17,49},{33,1},{49,17},{2,34}... | collective-permute-start | bytes 589832 | tf_op jit(solution)/shard_map/ppermute | solution.py:30
  19.3 2.3 %copy-start.4 = (bf16[1024,1024]{1,0:T(8,128)(2,1)S(1)}, bf16[1024,1024]{1,0:T(8,128)(2,1)}, u32[]{:S(2)}) copy-start(bf16[1024,1024]{1,0:T(8,128)(2,1)} %cp.1) | copy-start | bytes 6291460
  24.0 6.5 %copy-start.17 = (bf16[96,1024]{1,0:T(8,128)(2,1)S(1)}, bf16[96,1024]{1,0:T(8,128)(2,1)}, u32[]{:S(2)}) copy-start(bf16[96,1024]{1,0:T(8,128)(2,1)} %param.7) | copy-start | bytes 589828
  30.5 32.3 %copy-start.5 = (bf16[384,1024]{1,0:T(8,128)(2,1)}, bf16[384,1024]{1,0:T(8,128)(2,1)S(1)}, u32[]{:S(2)}) copy-start(bf16[384,1024]{1,0:T(8,128)(2,1)S(1)} %pad_maximum_fusion.refs_0_) | copy-start | bytes 2359300
  30.6 5.2 %collective-permute-start.5 = (bf16[384,1024]{1,0:T(8,128)(2,1)S(1)}, bf16[384,1024]{1,0:T(8,128)(2,1)S(1)}, u32[]{:S(2)}, u32[]{:S(2)}) collective-permute-start(bf16[384,1024]{1,0:T(8,128)(2,1)S(1)} %pad_maximum_fusion.refs_0_), channel_id=1, source_target_pairs={{0,8},{8,0},{1,9},{9,1},{2,10},{10,2},{3,11},{11,3},{4,12},{12,4},... | collective-permute-start | bytes 2359304 | tf_op jit(solution)/shard_map/ppermute | solution.py:30
  33.1 22.0 %collective-permute-start.4 = (bf16[384,1024]{1,0:T(8,128)(2,1)S(1)}, bf16[384,1024]{1,0:T(8,128)(2,1)S(1)}, u32[]{:S(2)}, u32[]{:S(2)}) collective-permute-start(bf16[384,1024]{1,0:T(8,128)(2,1)S(1)} %pad_maximum_fusion.refs_0_), channel_id=1, source_target_pairs={{0,64},{64,128},{128,192},{192,0},{1,65},{65,129},{129,193},{193,1... | collective-permute-start | bytes 2359304 | tf_op jit(solution)/shard_map/ppermute | solution.py:30
  34.3 20.8 %collective-permute-start.3 = (bf16[384,1024]{1,0:T(8,128)(2,1)S(1)}, bf16[384,1024]{1,0:T(8,128)(2,1)S(1)}, u32[]{:S(2)}, u32[]{:S(2)}) collective-permute-start(bf16[384,1024]{1,0:T(8,128)(2,1)S(1)} %pad_maximum_fusion.refs_0_), channel_id=1, source_target_pairs={{0,192},{64,0},{128,64},{192,128},{1,193},{65,1},{129,65},{193,129... | collective-permute-start | bytes 2359304 | tf_op jit(solution)/shard_map/ppermute | solution.py:30
  35.7 19.3 %copy-start.13 = (bf16[384,1024]{1,0:T(8,128)(2,1)}, bf16[384,1024]{1,0:T(8,128)(2,1)S(1)}, u32[]{:S(2)}) copy-start(bf16[384,1024]{1,0:T(8,128)(2,1)S(1)} %collective-permute-done.5.refs_3_.refs_5_) | copy-start | bytes 2359300
  55.1 7.8 %copy-start.8 = (bf16[384,1024]{1,0:T(8,128)(2,1)}, bf16[384,1024]{1,0:T(8,128)(2,1)S(1)}, u32[]{:S(2)}) copy-start(bf16[384,1024]{1,0:T(8,128)(2,1)S(1)} %collective-permute-done.4.refs_2_) | copy-start | bytes 2359300
  55.1 6.0 %copy-start.9 = (bf16[384,1024]{1,0:T(8,128)(2,1)}, bf16[384,1024]{1,0:T(8,128)(2,1)S(1)}, u32[]{:S(2)}) copy-start(bf16[384,1024]{1,0:T(8,128)(2,1)S(1)} %collective-permute-done.3.refs_1_) | copy-start | bytes 2359300
  55.1 5.9 %collective-permute-start.8 = (bf16[384,1024]{1,0:T(8,128)(2,1)S(1)}, bf16[384,1024]{1,0:T(8,128)(2,1)S(1)}, u32[]{:S(2)}, u32[]{:S(2)}) collective-permute-start(bf16[384,1024]{1,0:T(8,128)(2,1)S(1)} %collective-permute-done.3.refs_1_), channel_id=1, source_target_pairs={{0,8},{8,0},{1,9},{9,1},{2,10},{10,2},{3,11},{11,3},{4,12},{12,4},... | collective-permute-start | bytes 2359304 | tf_op jit(solution)/shard_map/ppermute | solution.py:30
  56.1 5.0 %collective-permute-start.9 = (bf16[384,1024]{1,0:T(8,128)(2,1)S(1)}, bf16[384,1024]{1,0:T(8,128)(2,1)S(1)}, u32[]{:S(2)}, u32[]{:S(2)}) collective-permute-start(bf16[384,1024]{1,0:T(8,128)(2,1)S(1)} %collective-permute-done.4.refs_2_), channel_id=1, source_target_pairs={{0,8},{8,0},{1,9},{9,1},{2,10},{10,2},{3,11},{11,3},{4,12},{12,4},... | collective-permute-start | bytes 2359304 | tf_op jit(solution)/shard_map/ppermute | solution.py:30
  57.7 15.8 %collective-permute-start.7 = (bf16[192,1024]{1,0:T(8,128)(2,1)}, bf16[192,1024]{1,0:T(8,128)(2,1)S(1)}, u32[]{:S(2)}, u32[]{:S(2)}) collective-permute-start(bf16[192,1024]{1,0:T(8,128)(2,1)} %slice.19), channel_id=1, source_target_pairs={{0,64},{64,128},{128,192},{192,0},{1,65},{65,129},{129,193},{193,1... | collective-permute-start | bytes 1179656 | tf_op jit(solution)/shard_map/ppermute | solution.py:30
  58.7 15.8 %collective-permute-start.6 = (bf16[192,1024]{1,0:T(8,128)(2,1)}, bf16[192,1024]{1,0:T(8,128)(2,1)}, u32[]{:S(2)}, u32[]{:S(2)}) collective-permute-start(bf16[192,1024]{1,0:T(8,128)(2,1)} %slice.18), channel_id=1, source_target_pairs={{0,192},{64,0},{128,64},{192,128},{1,193},{65,1},{129,65},{193,129... | collective-permute-start | bytes 1179656 | tf_op jit(solution)/shard_map/ppermute | solution.py:30
  61.0 0.9 copy-start.14
  61.9 0.9 copy-start.15
  73.5 5.7 %copy-start.10 = (bf16[192,1024]{1,0:T(8,128)(2,1)}, bf16[192,1024]{1,0:T(8,128)(2,1)S(1)}, u32[]{:S(2)}) copy-start(bf16[192,1024]{1,0:T(8,128)(2,1)S(1)} %collective-permute-done.7.refs_1_.refs_4_) | copy-start | bytes 1179652
  74.4 4.8 %collective-permute-start.10 = (bf16[192,1024]{1,0:T(8,128)(2,1)}, bf16[192,1024]{1,0:T(8,128)(2,1)S(1)}, u32[]{:S(2)}, u32[]{:S(2)}) collective-permute-start(bf16[192,1024]{1,0:T(8,128)(2,1)} %collective-permute-done.6.refs_0_.refs_3_), channel_id=1, source_target_pairs={{0,8},{8,0},{1,9},{9,1},{2,10},{10,2},{3,11},{11,3},{4,12},{12,4},... | collective-permute-start | bytes 1179656 | tf_op jit(solution)/shard_map/ppermute | solution.py:30
  77.0 2.2 collective-permute-start.11
  79.2 0.8 copy-start.11
  80.0 0.8 copy-start.12
  87.1 33.8 %all-to-all-start = ((bf16[8,96,1024]{2,1,0:T(8,128)(2,1)}), bf16[8,96,1024]{2,1,0:T(8,128)(2,1)}, u32[]{:S(2)}, u32[]{:S(2)}) async-start(bf16[8,96,1024]{2,1,0:T(8,128)(2,1)} %get-tuple-element.30), calls=%async_computation | async-start | bytes 3145728 | tf_op jit(solution)/shard_map/all_to_all | solution.py:25
  109.5 15.7 %copy-start.16 = (f32[96,1024]{1,0:T(8,128)S(1)}, f32[96,1024]{1,0:T(8,128)}, u32[]{:S(2)}) copy-start(f32[96,1024]{1,0:T(8,128)} %get-tuple-element.29) | copy-start | bytes 1179652
  120.9 24.2 %all-to-all-start.1 = ((bf16[8,96,1024]{2,1,0:T(8,128)(2,1)}), bf16[8,96,1024]{2,1,0:T(8,128)(2,1)}, u32[]{:S(2)}, u32[]{:S(2)}) async-start(bf16[8,96,1024]{2,1,0:T(8,128)(2,1)} %bitcast.27), calls=%async_computation.1 | async-start | bytes 3145728 | tf_op jit(solution)/shard_map/all_to_all | solution.py:25
  132.3 12.7 %copy-start.3 = (s32[4]{0:T(128)S(1)}, s32[4]{0:T(128)}, u32[]{:S(2)}) copy-start(s32[4]{0:T(128)} %pad_add_fusion.where) | copy-start | bytes 52
  147.7 0.9 copy-start.1
  148.6 30.6 %all-to-all-start.2 = ((bf16[32,3,32,96]{3,2,1,0:T(8,128)(2,1)}), bf16[32,3,32,96]{3,2,1,0:T(8,128)(2,1)S(1)}, u32[]{:S(2)}, u32[]{:S(2)}) async-start(bf16[32,3,32,96]{3,2,1,0:T(8,128)(2,1)} %copy-done.1), calls=%async_computation.2 | async-start | bytes 1572864 | tf_op jit(solution)/shard_map/all_to_all | solution.py:25
  179.2 0.9 copy-start.6
  180.1 29.6 %copy-start.7 = (f32[96,1024]{0,1:T(8,128)S(1)}, f32[96,1024]{0,1:T(8,128)}, u32[]{:S(2)}) copy-start(f32[96,1024]{0,1:T(8,128)} %get-tuple-element.55) | copy-start | bytes 1179652
  204.1 1.0 copy-start.2
  206.2 11.8 %all-to-all-start.4 = ((f32[8,8,1536]{2,1,0:T(8,128)}), f32[8,8,1536]{2,1,0:T(8,128)S(1)}, u32[]{:S(2)}, u32[]{:S(2)}) async-start(f32[8,8,1536]{2,1,0:T(8,128)} %shard_map.106), calls=%async_computation.4 | async-start | bytes 786432 | tf_op jit(solution)/shard_map/all_to_all | solution.py:25
  218.7 2.6 %copy-start.18 = (f32[4,1024]{1,0:T(4,128)}, f32[4,1024]{1,0:T(4,128)S(1)}, u32[]{:S(2)}) copy-start(f32[4,1024]{1,0:T(4,128)S(1)} %get-tuple-element.60) | copy-start | bytes 49156
Sparse Core Ops, SparseCore 0:
  10.6 75.2 all-gather.1

commit v10 on v9

--- a/solution.py
+++ b/solution.py
@@ -132,7 +132,7 @@
             ],
         ),
         out_shape=jax.ShapeDtypeStruct((z.shape[0], width), F32),
-        compiler_params=pltpu.CompilerParams(vmem_limit_bytes=60 << 20),
+        compiler_params=pltpu.CompilerParams(vmem_limit_bytes=24 << 20),
         cost_estimate=pl.CostEstimate(
             flops=3 * z.size * width // 2,
             transcendentals=0,
@@ -165,7 +165,7 @@
             ],
         ),
         out_shape=[jax.ShapeDtypeStruct(blocks, BF), jax.ShapeDtypeStruct((rows, width), F32)],
-        compiler_params=pltpu.CompilerParams(vmem_limit_bytes=60 << 20),
+        compiler_params=pltpu.CompilerParams(vmem_limit_bytes=24 << 20),
         cost_estimate=pl.CostEstimate(
             flops=z.size * width // 2,
             transcendentals=0,

time: 229 us -> 227 us (level)
  local copies, waits for them, and re-layouts: 10.1 us -> 5.57 us
  matrix products: 24.1 us -> 27 us
    dot_general x8, matrix products: 24.1 us -> 27 us  [dot(): lax.dot_general(a, b, (((ca,), (cb,)), ((), ())), preferred_element_type=...]
    ppermute x12, waiting for transfers between devices: 29.2 us -> 26.4 us  [shift(): return lax.ppermute(a, axis, [(i, (i + by) % n) for i in range(n)])]
    pallas_call x1, Pallas kernels: 9.25 us -> 11.8 us  [near_product(): pl.pallas_call(near_kernel, grid_spec=pltpu.PrefetchScalarGridSpec(num_sc...]
    unnamed x39 -> x47, local copies, waits for them, and re-layouts: 7.03 us -> 4.95 us
  transfers between devices with their start and end apart: 17 -> 17, of which waited for: 10 -> 10; matrix products, arithmetic and copies ran while one was open for 13% -> 13% of each run, Pallas kernels for 9% -> 10%
where the time goes in v10:
time: 227 us; the launch traced here: 226 us
  waiting for transfers between devices  73.3 us (32%)
  starting transfers between devices  51.7 us (23%)
  Pallas kernels  34.4 us (15%)
  matrix products  27 us (12%)
  blocking collectives  16.2 us (7%)
  between operations  14.4 us (6%)
  local copies, waits for them, and re-layouts  5.57 us (2%)
  other arithmetic  3.51 us (2%)
    all_to_all x4, waiting for transfers between devices, exchange(): return lax.all_to_all(a, axes, 0, 0, tiled=True)  46.2 us
    all_to_all x4, starting transfers between devices, exchange(): return lax.all_to_all(a, axes, 0, 0, tiled=True)  30 us
    dot_general x8, matrix products, dot(): lax.dot_general(a, b, (((ca,), (cb,)), ((), ())), preferred_element_type=...  27 us
    ppermute x12, waiting for transfers between devices, shift(): return lax.ppermute(a, axis, [(i, (i + by) % n) for i in range(n)])  26.4 us
    ppermute x12, starting transfers between devices, shift(): return lax.ppermute(a, axis, [(i, (i + by) % n) for i in range(n)])  21.6 us
    all_to_all x1, blocking collectives, exchange(): return lax.all_to_all(a, axes, 0, 0, tiled=True)  16.2 us
    pallas_call x1, Pallas kernels, near_product(): pl.pallas_call(near_kernel, grid_spec=pltpu.PrefetchScalarGridSpec(num_sc...  11.8 us
    pallas_call x1, Pallas kernels, slices(): pl.pallas_call(slices_kernel, in_specs=[vm, any_, any_, any_], out_specs=...  7.8 us
  transfers between devices with their start and end apart: 17, of which 10 were waited for; matrix products, arithmetic and copies ran while one was open for 13% of the time, Pallas kernels for 10%

profile of v10, /device:TPU:1, one launch (start us, length us, event | category | flops | bytes accessed | tf_op | source)
XLA Modules:
  0.0 226.1 jit_solution(17276969445320829825)
XLA Ops:
  7.2 0.0 copy-start
  7.2 0.0 all-gather.2.cloned.1.call-start
  7.2 0.7 all-gather.2.cloned.1.call-update
  7.9 3.9 %collective-permute-start.1 = (bf16[96,1024]{1,0:T(8,128)(2,1)}, bf16[96,1024]{1,0:T(8,128)(2,1)S(1)}, u32[]{:S(2)}, u32[]{:S(2)}) collective-permute-start(bf16[96,1024]{1,0:T(8,128)(2,1)} %param.7), channel_id=1, source_target_pairs={{0,16},{16,32},{32,48},{48,0},{1,17},{17,33},{33,49},{49,1},{2,18}... | collective-permute-start | bytes 589832 | tf_op jit(solution)/shard_map/ppermute | solution.py:30
  11.8 3.1 %collective-permute-start = (bf16[96,1024]{1,0:T(8,128)(2,1)}, bf16[96,1024]{1,0:T(8,128)(2,1)S(1)}, u32[]{:S(2)}, u32[]{:S(2)}) collective-permute-start(bf16[96,1024]{1,0:T(8,128)(2,1)} %param.7), channel_id=1, source_target_pairs={{0,48},{16,0},{32,16},{48,32},{1,49},{17,1},{33,17},{49,33},{2,50}... | collective-permute-start | bytes 589832 | tf_op jit(solution)/shard_map/ppermute | solution.py:30
  14.9 4.4 %collective-permute-start.2 = (bf16[96,1024]{1,0:T(8,128)(2,1)}, bf16[96,1024]{1,0:T(8,128)(2,1)S(1)}, u32[]{:S(2)}, u32[]{:S(2)}) collective-permute-start(bf16[96,1024]{1,0:T(8,128)(2,1)} %param.7), channel_id=1, source_target_pairs={{0,32},{16,48},{32,0},{48,16},{1,33},{17,49},{33,1},{49,17},{2,34}... | collective-permute-start | bytes 589832 | tf_op jit(solution)/shard_map/ppermute | solution.py:30
  19.3 2.3 %fusion.3 = f32[4,1024]{1,0:T(4,128)S(1)} fusion(bf16[1024,1024]{1,0:T(8,128)(2,1)} %param.11, s32[]{:T(128)S(6)} %select_n.12), kind=kOutput, calls=%fused_computation.9 | convolution fusion | flops 8388608 | bytes 2375684 | tf_op jit(solution)/shard_map/dot_general | solution.py:17
  21.6 4.0 %convolution_convert_fusion = bf16[1024,1024]{0,1:T(8,128)(2,1)S(1)} fusion(bf16[1024,1024]{1,0:T(8,128)(2,1)S(1)} %copy-done, bf16[1024,1024]{1,0:T(8,128)(2,1)} %cp.1), kind=kOutput, calls=%fused_computation.1 | convolution fusion | flops 2148532224 | bytes 6291456 | tf_op jit(solution)/shard_map/dot_general | solution.py:17
  25.7 0.0 copy-start.17
  25.7 1.3 convolution_add_fusion
  27.0 1.1 fusion.5
  28.1 0.0 collective-permute-done.1
  28.1 2.1 collective-permute-done
  30.2 0.3 collective-permute-done.2
  30.5 0.1 pad_maximum_fusion.refs_0_
  30.6 2.5 %collective-permute-start.5 = (bf16[384,1024]{1,0:T(8,128)(2,1)S(1)}, bf16[384,1024]{1,0:T(8,128)(2,1)S(1)}, u32[]{:S(2)}, u32[]{:S(2)}) collective-permute-start(bf16[384,1024]{1,0:T(8,128)(2,1)S(1)} %pad_maximum_fusion.refs_0_), channel_id=1, source_target_pairs={{0,8},{8,0},{1,9},{9,1},{2,10},{10,2},{3,11},{11,3},{4,12},{12,4},... | collective-permute-start | bytes 2359304 | tf_op jit(solution)/shard_map/ppermute | solution.py:30
  33.1 1.2 collective-permute-start.4
  34.3 1.5 collective-permute-start.3
  35.8 19.4 %collective-permute-done.4.refs_2_ = bf16[384,1024]{1,0:T(8,128)(2,1)S(1)} collective-permute-done((bf16[384,1024]{1,0:T(8,128)(2,1)S(1)}, bf16[384,1024]{1,0:T(8,128)(2,1)S(1)}, u32[]{:S(2)}, u32[]{:S(2)}) %collective-permute-start.4) | collective-permute-done | bytes 786464 | tf_op jit(solution)/shard_map/ppermute | solution.py:30
  55.2 0.0 collective-permute-done.3.refs_1_
  55.2 0.9 collective-permute-start.8
  56.0 0.1 collective-permute-start.9
  56.2 0.7 collective-permute-start.7
  56.9 2.0 collective-permute-start.6
  59.0 0.1 pad_add_fusion.where
  59.0 0.0 collective-permute-done.9.refs_5_.refs_7_
  59.1 11.8 %shard_map.101.refs_4_ = f32[768,1024]{1,0:T(8,128)S(1)} custom-call(s32[4]{0:T(128)S(1)} %pad_add_fusion.where, bf16[384,1024]{1,0:T(8,128)(2,1)S(1)} %pad_maximum_fusion.refs_0_, bf16[384,1024]{1,0:T(8,128)(2,1)S(1)} %collective-permute-done.3.refs_1_, bf16[384,1024]{1,0:T(8,128)(2,1)S(1)} %collective-permute-done.4.refs_2_, ...), custom_call_target="tpu_custom_call" | custom-call | flops 3623878656 | bytes 11403264 | tf_op jit(solution)/shard_map/pallas_call | solution.py:118
  71.0 2.7 %collective-permute-done.7.refs_1_.refs_4_ = bf16[192,1024]{1,0:T(8,128)(2,1)S(1)} collective-permute-done((bf16[192,1024]{1,0:T(8,128)(2,1)S(1)}, bf16[192,1024]{1,0:T(8,128)(2,1)S(1)}, u32[]{:S(2)}, u32[]{:S(2)}) %collective-permute-start.7) | collective-permute-done | bytes 393248 | tf_op jit(solution)/shard_map/ppermute | solution.py:30
  73.7 1.2 collective-permute-start.10
  74.9 0.1 collective-permute-start.11
  75.0 1.2 collective-permute-done.10.refs_2_.refs_8_
  76.3 0.6 collective-permute-done.11.refs_3_.refs_9_
  76.8 4.9 %shard_map.102 = (bf16[8,96,1024]{2,1,0:T(8,128)(2,1)S(1)}, f32[96,1024]{1,0:T(8,128)S(1)}) custom-call(s32[4]{0:T(128)S(1)} %pad_add_fusion.where, bf16[192,1024]{1,0:T(8,128)(2,1)S(1)} %collective-permute-done.6.refs_0_.refs_3_, bf16[192,1024]{1,0:T(8,128)(2,1)S(1)} %collective-permute-done.7.refs_1_.refs_4_, ...), custom_call_target="tpu_custom_call" | custom-call | flops 1207959552 | bytes 7471104 | tf_op jit(solution)/shard_map/pallas_call | solution.py:148
  81.8 1.2 copy-done.8
  82.9 15.1 %all-to-all-start = ((bf16[8,96,1024]{2,1,0:T(8,128)(2,1)}), bf16[8,96,1024]{2,1,0:T(8,128)(2,1)}, u32[]{:S(2)}, u32[]{:S(2)}) async-start(bf16[8,96,1024]{2,1,0:T(8,128)(2,1)} %copy-done.8), calls=%async_computation | async-start | bytes 3145728 | tf_op jit(solution)/shard_map/all_to_all | solution.py:25
  98.0 0.0 all-gather.2.cloned.1.call-done.child
  98.1 9.5 %convolution_convert_fusion.1 = bf16[768,1024]{1,0:T(8,128)(2,1)} fusion(bf16[3072,1024]{1,0:T(8,128)(2,1)} %all-gather.2.cloned.1.call-done.child, bf16[768,1,3072]{2,0,1:T(8,128)(2,1)} %param.6), kind=kOutput, calls=%fused_computation.2 | convolution fusion | flops 4832624640 | bytes 12582912 | tf_op jit(solution)/shard_map/dot_general | solution.py:17
  107.6 11.4 %all-to-all-done = bf16[8,96,1024]{2,1,0:T(8,128)(2,1)} async-done(((bf16[8,96,1024]{2,1,0:T(8,128)(2,1)}), bf16[8,96,1024]{2,1,0:T(8,128)(2,1)}, u32[]{:S(2)}, u32[]{:S(2)}) %all-to-all-start) | async-done | bytes 1572896 | tf_op jit(solution)/shard_map/all_to_all | solution.py:25
  118.9 4.3 %all-to-all-start.1 = ((bf16[8,96,1024]{2,1,0:T(8,128)(2,1)}), bf16[8,96,1024]{2,1,0:T(8,128)(2,1)}, u32[]{:S(2)}, u32[]{:S(2)}) async-start(bf16[8,96,1024]{2,1,0:T(8,128)(2,1)} %bitcast.29), calls=%async_computation.1 | async-start | bytes 3145728 | tf_op jit(solution)/shard_map/all_to_all | solution.py:25
  123.3 0.2 copy.18
  123.5 1.9 select_reduce_fusion
  125.3 0.2 copy.19
  125.5 0.9 add_convert_fusion
  126.4 2.1 fusion.15
  128.5 0.2 copy.20
  128.7 4.1 %fusion.own = f32[96,1024]{1,0:T(8,128)S(1)} fusion(bf16[3072,1024]{1,0:T(8,128)(2,1)} %all-gather.2.cloned.1.call-done.child, bf16[768,1,3072]{2,0,1:T(8,128)(2,1)} %param.6, s32[]{:T(128)S(6)} %select_n.14), kind=kOutput, calls=%fused_computation.6 | convolution fusion | flops 603979776 | bytes 7274500 | tf_op jit(solution)/shard_map/dot_general | solution.py:17
  132.8 10.3 %all-to-all-done.1.got = bf16[8,96,1024]{2,1,0:T(8,128)(2,1)} async-done(((bf16[8,96,1024]{2,1,0:T(8,128)(2,1)}), bf16[8,96,1024]{2,1,0:T(8,128)(2,1)}, u32[]{:S(2)}, u32[]{:S(2)}) %all-to-all-start.1) | async-done | bytes 1572896 | tf_op jit(solution)/shard_map/all_to_all | solution.py:25
  143.1 2.6 %shard_map.103 = (f32[96,1024]{1,0:T(8,128)}, bf16[32,3,32,96]{3,2,1,0:T(8,128)(2,1)S(1)}) custom-call(s32[4]{0:T(128)S(1)} %pad_add_fusion.where, bf16[8,96,1024]{2,1,0:T(8,128)(2,1)} %all-to-all-done.1.got, f32[96,1024]{1,0:T(8,128)S(1)} %fusion.own, f32[96,1024]{1,0:T(8,128)S(1)} %get-tuple-element.59.shifted, bf16[1024,96]{1,0:T(8,128)(2,1)S(1)} %bitcast.27, ...), custom_call_target="tpu_custom_call" | custom-call | flops 884736 | bytes 3932160 | tf_op jit(solution)/shard_map/pallas_call | solution.py:324
  145.8 0.9 copy-done.12
  146.7 7.2 %all-to-all-start.2 = ((bf16[32,3,32,96]{3,2,1,0:T(8,128)(2,1)}), bf16[32,3,32,96]{3,2,1,0:T(8,128)(2,1)S(1)}, u32[]{:S(2)}, u32[]{:S(2)}) async-start(bf16[32,3,32,96]{3,2,1,0:T(8,128)(2,1)} %copy-done.12), calls=%async_computation.2 | async-start | bytes 1572864 | tf_op jit(solution)/shard_map/all_to_all | solution.py:25
  153.9 6.1 %shard_map.104.parent = bf16[3072,1024]{1,0:T(8,128)(2,1)} custom-call(s32[4]{0:T(128)} %copy-done.14, bf16[384,1024]{1,0:T(8,128)(2,1)} %copy-done.1, bf16[384,1024]{1,0:T(8,128)(2,1)} %copy-done.3, bf16[384,1024]{1,0:T(8,128)(2,1)} %copy-done.2, bf16[192,1024]{1,0:T(8,128)(2,1)} %copy-done.5, bf16[192,1024]{1,0:T(8,128)(2,1)} %copy-done.4, ...), custom_call_target="tpu_custom_call" | custom-call | bytes 12582912 | tf_op jit(solution)/shard_map/pallas_call | solution.py:194
  160.0 17.1 %all-to-all-done.2.x = bf16[32,3,32,96]{3,2,1,0:T(8,128)(2,1)S(1)} async-done(((bf16[32,3,32,96]{3,2,1,0:T(8,128)(2,1)}), bf16[32,3,32,96]{3,2,1,0:T(8,128)(2,1)S(1)}, u32[]{:S(2)}, u32[]{:S(2)}) %all-to-all-start.2) | async-done | bytes 589856 | tf_op jit(solution)/shard_map/all_to_all | solution.py:25
  177.1 0.9 copy-done.15
  178.0 7.8 %shard_map.105 = (bf16[32,16,128]{2,1,0:T(8,128)(2,1)}, f32[2,32,1024]{2,1,0:T(8,128)}) custom-call(bf16[32,3,32,96]{3,2,1,0:T(8,128)(2,1)} %copy-done.15, bf16[3072,1024]{1,0:T(8,128)(2,1)} %shard_map.104.parent, bf16[3072,1024]{1,0:T(8,128)(2,1)} %all-gather.2.cloned.1.call-done.child, bf16[1024,1024]{1,0:T(8,128)(2,1)} %cp.1), custom_call_target="tpu_custom_call" | custom-call | flops 1006632960 | bytes 12582912 | tf_op jit(solution)/shard_map/pallas_call | solution.py:262
  185.8 0.0 copy-start.18
  185.8 0.0 copy-start.19
  185.8 16.2 %all_to_all.25.t = bf16[32,16,128]{2,1,0:T(8,128)(2,1)S(1)} all-to-all(bf16[32,16,128]{2,1,0:T(8,128)(2,1)} %get-tuple-element.35), channel_id=1, replica_groups=mesh['x'=4,'zh'=4,'core'=2,'y'=4,'zl'=2] {'x','zh','core'}, dimensions={0} | all-to-all | bytes 262144 | tf_op jit(solution)/shard_map/all_to_all | solution.py:25
  202.0 0.9 copy-done.13
  203.0 1.2 shard_map.106
  204.2 3.5 %all-to-all-start.4 = ((f32[8,8,1536]{2,1,0:T(8,128)}), f32[8,8,1536]{2,1,0:T(8,128)S(1)}, u32[]{:S(2)}, u32[]{:S(2)}) async-start(f32[8,8,1536]{2,1,0:T(8,128)} %shard_map.106), calls=%async_computation.4 | async-start | bytes 786432 | tf_op jit(solution)/shard_map/all_to_all | solution.py:25
  207.6 0.9 copy.21
  208.6 7.4 %all-to-all-done.4 = f32[8,8,1536]{2,1,0:T(8,128)S(1)} async-done(((f32[8,8,1536]{2,1,0:T(8,128)}), f32[8,8,1536]{2,1,0:T(8,128)S(1)}, u32[]{:S(2)}, u32[]{:S(2)}) %all-to-all-start.4) | async-done | bytes 393248 | tf_op jit(solution)/shard_map/all_to_all | solution.py:25
  216.0 0.6 slice_add_fusion
  216.6 2.6 %convolution_subtract_fusion = f32[4,1024]{1,0:T(4,128)} fusion(bf16[1024,1024]{1,0:T(8,128)(2,1)} %cp.1, f32[8,1536]{1,0:T(8,128)S(1)} %reduce_sum.19, f32[4,1024]{1,0:T(4,128)S(1)} %get-tuple-element.60), kind=kOutput, calls=%fused_computation.3 | convolution fusion | flops 8396800 | bytes 2146304 | tf_op jit(solution)/shard_map/dot_general | solution.py:17
  (47 shorter events, 0.2 us)
Async XLA Ops:
  7.2 14.5 %copy-start = (bf16[1024,1024]{1,0:T(8,128)(2,1)S(1)}, bf16[1024,1024]{1,0:T(8,128)(2,1)}, u32[]{:S(2)}) copy-start(bf16[1024,1024]{1,0:T(8,128)(2,1)} %param.8) | copy-start | bytes 6291460
  7.2 90.9 %all-gather.2.cloned.1.call-start = ((), (), s32[]{:S(2)}) async-start(), calls=%async_computation.5 | async-start | bytes 6488064 | tf_op jit(solution)/shard_map/all_gather | solution.py:345
  7.9 20.1 %collective-permute-start.1 = (bf16[96,1024]{1,0:T(8,128)(2,1)}, bf16[96,1024]{1,0:T(8,128)(2,1)S(1)}, u32[]{:S(2)}, u32[]{:S(2)}) collective-permute-start(bf16[96,1024]{1,0:T(8,128)(2,1)} %param.7), channel_id=1, source_target_pairs={{0,16},{16,32},{32,48},{48,0},{1,17},{17,33},{33,49},{49,1},{2,18}... | collective-permute-start | bytes 589832 | tf_op jit(solution)/shard_map/ppermute | solution.py:30
  11.8 18.4 %collective-permute-start = (bf16[96,1024]{1,0:T(8,128)(2,1)}, bf16[96,1024]{1,0:T(8,128)(2,1)S(1)}, u32[]{:S(2)}, u32[]{:S(2)}) collective-permute-start(bf16[96,1024]{1,0:T(8,128)(2,1)} %param.7), channel_id=1, source_target_pairs={{0,48},{16,0},{32,16},{48,32},{1,49},{17,1},{33,17},{49,33},{2,50}... | collective-permute-start | bytes 589832 | tf_op jit(solution)/shard_map/ppermute | solution.py:30
  14.9 15.6 %collective-permute-start.2 = (bf16[96,1024]{1,0:T(8,128)(2,1)}, bf16[96,1024]{1,0:T(8,128)(2,1)S(1)}, u32[]{:S(2)}, u32[]{:S(2)}) collective-permute-start(bf16[96,1024]{1,0:T(8,128)(2,1)} %param.7), channel_id=1, source_target_pairs={{0,32},{16,48},{32,0},{48,16},{1,33},{17,49},{33,1},{49,17},{2,34}... | collective-permute-start | bytes 589832 | tf_op jit(solution)/shard_map/ppermute | solution.py:30
  19.3 39.8 %slice-start = ((s8[4718592]{0:T(1024)(128)(4,1)}), s8[4194304]{0:T(1024)(128)(4,1)S(1)}, s32[]{:S(2)}) async-start(s8[4718592]{0:T(1024)(128)(4,1)} %bitcast.23), calls=%async_computation.6 | async-start | bytes 8388608
  21.6 37.5 %slice-start.1 = ((s8[4718592]{0:T(1024)(128)(4,1)}), s8[524288]{0:T(1024)(128)(4,1)S(1)}, s32[]{:S(2)}) async-start(s8[4718592]{0:T(1024)(128)(4,1)} %bitcast.23), calls=%async_computation.7 | async-start | bytes 1048576
  25.7 4.8 %copy-start.17 = (bf16[96,1024]{1,0:T(8,128)(2,1)S(1)}, bf16[96,1024]{1,0:T(8,128)(2,1)}, u32[]{:S(2)}) copy-start(bf16[96,1024]{1,0:T(8,128)(2,1)} %param.7) | copy-start | bytes 589828
  30.5 40.4 %copy-start.1 = (bf16[384,1024]{1,0:T(8,128)(2,1)}, bf16[384,1024]{1,0:T(8,128)(2,1)S(1)}, u32[]{:S(2)}) copy-start(bf16[384,1024]{1,0:T(8,128)(2,1)S(1)} %pad_maximum_fusion.refs_0_) | copy-start | bytes 2359300
  30.6 5.2 %collective-permute-start.5 = (bf16[384,1024]{1,0:T(8,128)(2,1)S(1)}, bf16[384,1024]{1,0:T(8,128)(2,1)S(1)}, u32[]{:S(2)}, u32[]{:S(2)}) collective-permute-start(bf16[384,1024]{1,0:T(8,128)(2,1)S(1)} %pad_maximum_fusion.refs_0_), channel_id=1, source_target_pairs={{0,8},{8,0},{1,9},{9,1},{2,10},{10,2},{3,11},{11,3},{4,12},{12,4},... | collective-permute-start | bytes 2359304 | tf_op jit(solution)/shard_map/ppermute | solution.py:30
  33.1 22.1 %collective-permute-start.4 = (bf16[384,1024]{1,0:T(8,128)(2,1)S(1)}, bf16[384,1024]{1,0:T(8,128)(2,1)S(1)}, u32[]{:S(2)}, u32[]{:S(2)}) collective-permute-start(bf16[384,1024]{1,0:T(8,128)(2,1)S(1)} %pad_maximum_fusion.refs_0_), channel_id=1, source_target_pairs={{0,64},{64,128},{128,192},{192,0},{1,65},{65,129},{129,193},{193,1... | collective-permute-start | bytes 2359304 | tf_op jit(solution)/shard_map/ppermute | solution.py:30
  34.3 20.9 %collective-permute-start.3 = (bf16[384,1024]{1,0:T(8,128)(2,1)S(1)}, bf16[384,1024]{1,0:T(8,128)(2,1)S(1)}, u32[]{:S(2)}, u32[]{:S(2)}) collective-permute-start(bf16[384,1024]{1,0:T(8,128)(2,1)S(1)} %pad_maximum_fusion.refs_0_), channel_id=1, source_target_pairs={{0,192},{64,0},{128,64},{192,128},{1,193},{65,1},{129,65},{193,129... | collective-permute-start | bytes 2359304 | tf_op jit(solution)/shard_map/ppermute | solution.py:30
  35.7 35.2 %copy-start.9 = (bf16[384,1024]{1,0:T(8,128)(2,1)}, bf16[384,1024]{1,0:T(8,128)(2,1)S(1)}, u32[]{:S(2)}) copy-start(bf16[384,1024]{1,0:T(8,128)(2,1)S(1)} %collective-permute-done.5.refs_3_.refs_5_) | copy-start | bytes 2359300
  55.2 15.8 %copy-start.2 = (bf16[384,1024]{1,0:T(8,128)(2,1)}, bf16[384,1024]{1,0:T(8,128)(2,1)S(1)}, u32[]{:S(2)}) copy-start(bf16[384,1024]{1,0:T(8,128)(2,1)S(1)} %collective-permute-done.4.refs_2_) | copy-start | bytes 2359300
  55.2 15.8 %copy-start.3 = (bf16[384,1024]{1,0:T(8,128)(2,1)}, bf16[384,1024]{1,0:T(8,128)(2,1)S(1)}, u32[]{:S(2)}) copy-start(bf16[384,1024]{1,0:T(8,128)(2,1)S(1)} %collective-permute-done.3.refs_1_) | copy-start | bytes 2359300
  55.2 3.9 %collective-permute-start.8 = (bf16[384,1024]{1,0:T(8,128)(2,1)S(1)}, bf16[384,1024]{1,0:T(8,128)(2,1)S(1)}, u32[]{:S(2)}, u32[]{:S(2)}) collective-permute-start(bf16[384,1024]{1,0:T(8,128)(2,1)S(1)} %collective-permute-done.3.refs_1_), channel_id=1, source_target_pairs={{0,8},{8,0},{1,9},{9,1},{2,10},{10,2},{3,11},{11,3},{4,12},{12,4},... | collective-permute-start | bytes 2359304 | tf_op jit(solution)/shard_map/ppermute | solution.py:30
  56.0 3.0 %collective-permute-start.9 = (bf16[384,1024]{1,0:T(8,128)(2,1)S(1)}, bf16[384,1024]{1,0:T(8,128)(2,1)S(1)}, u32[]{:S(2)}, u32[]{:S(2)}) collective-permute-start(bf16[384,1024]{1,0:T(8,128)(2,1)S(1)} %collective-permute-done.4.refs_2_), channel_id=1, source_target_pairs={{0,8},{8,0},{1,9},{9,1},{2,10},{10,2},{3,11},{11,3},{4,12},{12,4},... | collective-permute-start | bytes 2359304 | tf_op jit(solution)/shard_map/ppermute | solution.py:30
  56.2 17.5 %collective-permute-start.7 = (bf16[192,1024]{1,0:T(8,128)(2,1)S(1)}, bf16[192,1024]{1,0:T(8,128)(2,1)S(1)}, u32[]{:S(2)}, u32[]{:S(2)}) collective-permute-start(bf16[192,1024]{1,0:T(8,128)(2,1)S(1)} %slice.19), channel_id=1, source_target_pairs={{0,64},{64,128},{128,192},{192,0},{1,65},{65,129},{129,193},{193,1... | collective-permute-start | bytes 1179656 | tf_op jit(solution)/shard_map/ppermute | solution.py:30
  56.9 16.7 %collective-permute-start.6 = (bf16[192,1024]{1,0:T(8,128)(2,1)S(1)}, bf16[192,1024]{1,0:T(8,128)(2,1)S(1)}, u32[]{:S(2)}, u32[]{:S(2)}) collective-permute-start(bf16[192,1024]{1,0:T(8,128)(2,1)S(1)} %slice.18), channel_id=1, source_target_pairs={{0,192},{64,0},{128,64},{192,128},{1,193},{65,1},{129,65},{193,129... | collective-permute-start | bytes 1179656 | tf_op jit(solution)/shard_map/ppermute | solution.py:30
  59.0 84.1 %copy-start.14 = (s32[4]{0:T(128)}, s32[4]{0:T(128)S(1)}, u32[]{:S(2)}) copy-start(s32[4]{0:T(128)S(1)} %pad_add_fusion.where) | copy-start | bytes 52
  59.0 11.9 %copy-start.10 = (bf16[384,1024]{1,0:T(8,128)(2,1)}, bf16[384,1024]{1,0:T(8,128)(2,1)S(1)}, u32[]{:S(2)}) copy-start(bf16[384,1024]{1,0:T(8,128)(2,1)S(1)} %collective-permute-done.8.refs_4_.refs_6_) | copy-start | bytes 2359300
  59.1 11.9 %copy-start.11 = (bf16[384,1024]{1,0:T(8,128)(2,1)}, bf16[384,1024]{1,0:T(8,128)(2,1)S(1)}, u32[]{:S(2)}) copy-start(bf16[384,1024]{1,0:T(8,128)(2,1)S(1)} %collective-permute-done.9.refs_5_.refs_7_) | copy-start | bytes 2359300
  73.7 8.1 %copy-start.4 = (bf16[192,1024]{1,0:T(8,128)(2,1)}, bf16[192,1024]{1,0:T(8,128)(2,1)S(1)}, u32[]{:S(2)}) copy-start(bf16[192,1024]{1,0:T(8,128)(2,1)S(1)} %collective-permute-done.7.refs_1_.refs_4_) | copy-start | bytes 1179652
  73.7 8.1 %copy-start.5 = (bf16[192,1024]{1,0:T(8,128)(2,1)}, bf16[192,1024]{1,0:T(8,128)(2,1)S(1)}, u32[]{:S(2)}) copy-start(bf16[192,1024]{1,0:T(8,128)(2,1)S(1)} %collective-permute-done.6.refs_0_.refs_3_) | copy-start | bytes 1179652
  73.7 2.6 %collective-permute-start.10 = (bf16[192,1024]{1,0:T(8,128)(2,1)S(1)}, bf16[192,1024]{1,0:T(8,128)(2,1)S(1)}, u32[]{:S(2)}, u32[]{:S(2)}) collective-permute-start(bf16[192,1024]{1,0:T(8,128)(2,1)S(1)} %collective-permute-done.6.refs_0_.refs_3_), channel_id=1, source_target_pairs={{0,8},{8,0},{1,9},{9,1},{2,10},{10,2},{3,11},{11,3},{4,12},{12,4},... | collective-permute-start | bytes 1179656 | tf_op jit(solution)/shard_map/ppermute | solution.py:30
  74.9 1.9 collective-permute-start.11
  76.3 5.5 %copy-start.6 = (bf16[192,1024]{1,0:T(8,128)(2,1)}, bf16[192,1024]{1,0:T(8,128)(2,1)S(1)}, u32[]{:S(2)}) copy-start(bf16[192,1024]{1,0:T(8,128)(2,1)S(1)} %collective-permute-done.10.refs_2_.refs_8_) | copy-start | bytes 1179652
  76.8 5.0 %copy-start.7 = (bf16[192,1024]{1,0:T(8,128)(2,1)}, bf16[192,1024]{1,0:T(8,128)(2,1)S(1)}, u32[]{:S(2)}) copy-start(bf16[192,1024]{1,0:T(8,128)(2,1)S(1)} %collective-permute-done.11.refs_3_.refs_9_) | copy-start | bytes 1179652
  81.8 1.2 copy-start.8
  82.9 36.0 %all-to-all-start = ((bf16[8,96,1024]{2,1,0:T(8,128)(2,1)}), bf16[8,96,1024]{2,1,0:T(8,128)(2,1)}, u32[]{:S(2)}, u32[]{:S(2)}) async-start(bf16[8,96,1024]{2,1,0:T(8,128)(2,1)} %copy-done.8), calls=%async_computation | async-start | bytes 3145728 | tf_op jit(solution)/shard_map/all_to_all | solution.py:25
  118.9 24.2 %all-to-all-start.1 = ((bf16[8,96,1024]{2,1,0:T(8,128)(2,1)}), bf16[8,96,1024]{2,1,0:T(8,128)(2,1)}, u32[]{:S(2)}, u32[]{:S(2)}) async-start(bf16[8,96,1024]{2,1,0:T(8,128)(2,1)} %bitcast.29), calls=%async_computation.1 | async-start | bytes 3145728 | tf_op jit(solution)/shard_map/all_to_all | solution.py:25
  145.8 0.9 copy-start.12
  146.7 30.4 %all-to-all-start.2 = ((bf16[32,3,32,96]{3,2,1,0:T(8,128)(2,1)}), bf16[32,3,32,96]{3,2,1,0:T(8,128)(2,1)S(1)}, u32[]{:S(2)}, u32[]{:S(2)}) async-start(bf16[32,3,32,96]{3,2,1,0:T(8,128)(2,1)} %copy-done.12), calls=%async_computation.2 | async-start | bytes 1572864 | tf_op jit(solution)/shard_map/all_to_all | solution.py:25
  177.1 0.9 copy-start.15
  178.0 29.7 %copy-start.16 = (f32[96,1024]{0,1:T(8,128)S(1)}, f32[96,1024]{0,1:T(8,128)}, u32[]{:S(2)}) copy-start(f32[96,1024]{0,1:T(8,128)} %get-tuple-element.55) | copy-start | bytes 1179652
  185.8 30.2 %copy-start.18 = (f32[4,1024]{1,0:T(4,128)S(1)}, f32[4,1024]{1,0:T(4,128)}, u32[]{:S(2)}) copy-start(f32[4,1024]{1,0:T(4,128)} %convolution_add_fusion) | copy-start | bytes 49156
  185.8 30.2 %copy-start.19 = (f32[4,1024]{1,0:T(4,128)S(1)}, f32[4,1024]{1,0:T(4,128)}, u32[]{:S(2)}) copy-start(f32[4,1024]{1,0:T(4,128)} %fusion.5) | copy-start | bytes 49156
  202.0 1.0 copy-start.13
  204.2 11.8 %all-to-all-start.4 = ((f32[8,8,1536]{2,1,0:T(8,128)}), f32[8,8,1536]{2,1,0:T(8,128)S(1)}, u32[]{:S(2)}, u32[]{:S(2)}) async-start(f32[8,8,1536]{2,1,0:T(8,128)} %shard_map.106), calls=%async_computation.4 | async-start | bytes 786432 | tf_op jit(solution)/shard_map/all_to_all | solution.py:25
  216.6 2.6 %copy-start.20 = (f32[4,1024]{1,0:T(4,128)}, f32[4,1024]{1,0:T(4,128)S(1)}, u32[]{:S(2)}) copy-start(f32[4,1024]{1,0:T(4,128)S(1)} %get-tuple-element.60) | copy-start | bytes 49156
Sparse Core Ops, SparseCore 0:
  10.6 75.1 all-gather.1

commit v11 on v10

--- a/solution.py
+++ b/solution.py
@@ -266,7 +266,7 @@
         out_shape=[jax.ShapeDtypeStruct((nr, 16, 128), BF), jax.ShapeDtypeStruct((2, sl, w), F32)],
         scratch_shapes=[pltpu.VMEM((kinds * sl, depth), BF), pltpu.VMEM((depth, w), BF), pltpu.VMEM((depth, w), BF), pltpu.VMEM(cp.shape, BF), pltpu.VMEM((5 * sl, w), F32),
             pltpu.SemaphoreType.DMA((parts,)), pltpu.SemaphoreType.DMA((parts,)), pltpu.SemaphoreType.DMA(())],
-        compiler_params=pltpu.CompilerParams(vmem_limit_bytes=60 << 20),
+        compiler_params=pltpu.CompilerParams(vmem_limit_bytes=52 << 20),
         cost_estimate=pl.CostEstimate(flops=10 * sl * depth * w, transcendentals=0, bytes_accessed=4 * depth * w),
     )(x, parent, child, cp)
 

time: 227 us -> 224 us (0.987)
    unnamed x47 -> x43, local copies, waits for them, and re-layouts: 4.95 us -> 3.11 us
where the time goes in v11:
time: 224 us; the launch traced here: 223 us
  waiting for transfers between devices  73.3 us (33%)
  starting transfers between devices  51.7 us (23%)
  Pallas kernels  33.2 us (15%)
  matrix products  27 us (12%)
  blocking collectives  16.1 us (7%)
  between operations  14.4 us (6%)
  local copies, waits for them, and re-layouts  3.74 us (2%)
  other arithmetic  3.51 us (2%)
    all_to_all x4, waiting for transfers between devices, exchange(): return lax.all_to_all(a, axes, 0, 0, tiled=True)  46.2 us
    all_to_all x4, starting transfers between devices, exchange(): return lax.all_to_all(a, axes, 0, 0, tiled=True)  30 us
    dot_general x8, matrix products, dot(): lax.dot_general(a, b, (((ca,), (cb,)), ((), ())), preferred_element_type=...  27 us
    ppermute x12, waiting for transfers between devices, shift(): return lax.ppermute(a, axis, [(i, (i + by) % n) for i in range(n)])  26.4 us
    ppermute x12, starting transfers between devices, shift(): return lax.ppermute(a, axis, [(i, (i + by) % n) for i in range(n)])  21.6 us
    all_to_all x1, blocking collectives, exchange(): return lax.all_to_all(a, axes, 0, 0, tiled=True)  16.1 us
    pallas_call x1, Pallas kernels, near_product(): pl.pallas_call(near_kernel, grid_spec=pltpu.PrefetchScalarGridSpec(num_sc...  11.8 us
    pallas_call x1, Pallas kernels, slices(): pl.pallas_call(slices_kernel, in_specs=[vm, any_, any_, any_], out_specs=...  6.58 us
  transfers between devices with their start and end apart: 17, of which 10 were waited for; matrix products, arithmetic and copies ran while one was open for 13% of the time, Pallas kernels for 10%

profile of v11, /device:TPU:1, one launch (start us, length us, event | category | flops | bytes accessed | tf_op | source)
XLA Modules:
  0.0 223.0 jit_solution(5173002128283541883)
XLA Ops:
  7.2 0.0 copy-start
  7.2 0.0 all-gather.2.cloned.1.call-start
  7.2 0.7 all-gather.2.cloned.1.call-update
  7.9 3.9 %collective-permute-start.1 = (bf16[96,1024]{1,0:T(8,128)(2,1)}, bf16[96,1024]{1,0:T(8,128)(2,1)S(1)}, u32[]{:S(2)}, u32[]{:S(2)}) collective-permute-start(bf16[96,1024]{1,0:T(8,128)(2,1)} %param.7), channel_id=1, source_target_pairs={{0,16},{16,32},{32,48},{48,0},{1,17},{17,33},{33,49},{49,1},{2,18}... | collective-permute-start | bytes 589832 | tf_op jit(solution)/shard_map/ppermute | solution.py:30
  11.8 3.1 %collective-permute-start = (bf16[96,1024]{1,0:T(8,128)(2,1)}, bf16[96,1024]{1,0:T(8,128)(2,1)S(1)}, u32[]{:S(2)}, u32[]{:S(2)}) collective-permute-start(bf16[96,1024]{1,0:T(8,128)(2,1)} %param.7), channel_id=1, source_target_pairs={{0,48},{16,0},{32,16},{48,32},{1,49},{17,1},{33,17},{49,33},{2,50}... | collective-permute-start | bytes 589832 | tf_op jit(solution)/shard_map/ppermute | solution.py:30
  14.9 4.4 %collective-permute-start.2 = (bf16[96,1024]{1,0:T(8,128)(2,1)}, bf16[96,1024]{1,0:T(8,128)(2,1)S(1)}, u32[]{:S(2)}, u32[]{:S(2)}) collective-permute-start(bf16[96,1024]{1,0:T(8,128)(2,1)} %param.7), channel_id=1, source_target_pairs={{0,32},{16,48},{32,0},{48,16},{1,33},{17,49},{33,1},{49,17},{2,34}... | collective-permute-start | bytes 589832 | tf_op jit(solution)/shard_map/ppermute | solution.py:30
  19.3 2.3 %fusion.3 = f32[4,1024]{1,0:T(4,128)S(1)} fusion(bf16[1024,1024]{1,0:T(8,128)(2,1)} %param.11, s32[]{:T(128)S(6)} %select_n.12), kind=kOutput, calls=%fused_computation.9 | convolution fusion | flops 8388608 | bytes 2375684 | tf_op jit(solution)/shard_map/dot_general | solution.py:17
  21.6 4.0 %convolution_convert_fusion = bf16[1024,1024]{0,1:T(8,128)(2,1)S(1)} fusion(bf16[1024,1024]{1,0:T(8,128)(2,1)S(1)} %copy-done, bf16[1024,1024]{1,0:T(8,128)(2,1)} %cp.1), kind=kOutput, calls=%fused_computation.1 | convolution fusion | flops 2148532224 | bytes 6291456 | tf_op jit(solution)/shard_map/dot_general | solution.py:17
  25.7 0.0 copy-start.15
  25.7 1.3 convolution_add_fusion
  27.0 1.1 fusion.5
  28.1 0.0 collective-permute-done.1
  28.1 2.1 collective-permute-done
  30.2 0.3 collective-permute-done.2
  30.5 0.1 pad_maximum_fusion.refs_0_
  30.6 2.5 %collective-permute-start.5 = (bf16[384,1024]{1,0:T(8,128)(2,1)S(1)}, bf16[384,1024]{1,0:T(8,128)(2,1)S(1)}, u32[]{:S(2)}, u32[]{:S(2)}) collective-permute-start(bf16[384,1024]{1,0:T(8,128)(2,1)S(1)} %pad_maximum_fusion.refs_0_), channel_id=1, source_target_pairs={{0,8},{8,0},{1,9},{9,1},{2,10},{10,2},{3,11},{11,3},{4,12},{12,4},... | collective-permute-start | bytes 2359304 | tf_op jit(solution)/shard_map/ppermute | solution.py:30
  33.1 1.2 collective-permute-start.4
  34.3 1.5 collective-permute-start.3
  35.7 0.0 collective-permute-done.5.refs_3_.refs_5_
  35.8 19.4 %collective-permute-done.4.refs_2_ = bf16[384,1024]{1,0:T(8,128)(2,1)S(1)} collective-permute-done((bf16[384,1024]{1,0:T(8,128)(2,1)S(1)}, bf16[384,1024]{1,0:T(8,128)(2,1)S(1)}, u32[]{:S(2)}, u32[]{:S(2)}) %collective-permute-start.4) | collective-permute-done | bytes 786464 | tf_op jit(solution)/shard_map/ppermute | solution.py:30
  55.2 0.0 collective-permute-done.3.refs_1_
  55.2 0.9 collective-permute-start.8
  56.0 0.1 collective-permute-start.9
  56.2 0.7 collective-permute-start.7
  56.9 2.0 collective-permute-start.6
  59.0 0.1 pad_add_fusion.where
  59.0 0.0 collective-permute-done.8.refs_4_.refs_6_
  59.0 0.0 collective-permute-done.9.refs_5_.refs_7_
  59.1 11.8 %shard_map.101.refs_4_ = f32[768,1024]{1,0:T(8,128)S(1)} custom-call(s32[4]{0:T(128)S(1)} %pad_add_fusion.where, bf16[384,1024]{1,0:T(8,128)(2,1)S(1)} %pad_maximum_fusion.refs_0_, bf16[384,1024]{1,0:T(8,128)(2,1)S(1)} %collective-permute-done.3.refs_1_, bf16[384,1024]{1,0:T(8,128)(2,1)S(1)} %collective-permute-done.4.refs_2_, ...), custom_call_target="tpu_custom_call" | custom-call | flops 3623878656 | bytes 11403264 | tf_op jit(solution)/shard_map/pallas_call | solution.py:118
  71.0 2.7 %collective-permute-done.7.refs_1_.refs_4_ = bf16[192,1024]{1,0:T(8,128)(2,1)S(1)} collective-permute-done((bf16[192,1024]{1,0:T(8,128)(2,1)S(1)}, bf16[192,1024]{1,0:T(8,128)(2,1)S(1)}, u32[]{:S(2)}, u32[]{:S(2)}) %collective-permute-start.7) | collective-permute-done | bytes 393248 | tf_op jit(solution)/shard_map/ppermute | solution.py:30
  73.7 1.2 collective-permute-start.10
  74.9 0.1 collective-permute-start.11
  75.0 1.2 collective-permute-done.10.refs_2_.refs_8_
  76.3 0.6 collective-permute-done.11.refs_3_.refs_9_
  76.8 4.9 %shard_map.102 = (bf16[8,96,1024]{2,1,0:T(8,128)(2,1)S(1)}, f32[96,1024]{1,0:T(8,128)S(1)}) custom-call(s32[4]{0:T(128)S(1)} %pad_add_fusion.where, bf16[192,1024]{1,0:T(8,128)(2,1)S(1)} %collective-permute-done.6.refs_0_.refs_3_, bf16[192,1024]{1,0:T(8,128)(2,1)S(1)} %collective-permute-done.7.refs_1_.refs_4_, ...), custom_call_target="tpu_custom_call" | custom-call | flops 1207959552 | bytes 7471104 | tf_op jit(solution)/shard_map/pallas_call | solution.py:148
  81.8 1.1 copy-done.8
  82.9 15.1 %all-to-all-start = ((bf16[8,96,1024]{2,1,0:T(8,128)(2,1)}), bf16[8,96,1024]{2,1,0:T(8,128)(2,1)}, u32[]{:S(2)}, u32[]{:S(2)}) async-start(bf16[8,96,1024]{2,1,0:T(8,128)(2,1)} %copy-done.8), calls=%async_computation | async-start | bytes 3145728 | tf_op jit(solution)/shard_map/all_to_all | solution.py:25
  98.0 0.0 all-gather.2.cloned.1.call-done.child
  98.1 9.5 %convolution_convert_fusion.1 = bf16[768,1024]{1,0:T(8,128)(2,1)} fusion(bf16[3072,1024]{1,0:T(8,128)(2,1)} %all-gather.2.cloned.1.call-done.child, bf16[768,1,3072]{2,0,1:T(8,128)(2,1)} %param.6), kind=kOutput, calls=%fused_computation.2 | convolution fusion | flops 4832624640 | bytes 12582912 | tf_op jit(solution)/shard_map/dot_general | solution.py:17
  107.6 11.4 %all-to-all-done = bf16[8,96,1024]{2,1,0:T(8,128)(2,1)} async-done(((bf16[8,96,1024]{2,1,0:T(8,128)(2,1)}), bf16[8,96,1024]{2,1,0:T(8,128)(2,1)}, u32[]{:S(2)}, u32[]{:S(2)}) %all-to-all-start) | async-done | bytes 1572896 | tf_op jit(solution)/shard_map/all_to_all | solution.py:25
  118.9 4.3 %all-to-all-start.1 = ((bf16[8,96,1024]{2,1,0:T(8,128)(2,1)}), bf16[8,96,1024]{2,1,0:T(8,128)(2,1)}, u32[]{:S(2)}, u32[]{:S(2)}) async-start(bf16[8,96,1024]{2,1,0:T(8,128)(2,1)} %bitcast.29), calls=%async_computation.1 | async-start | bytes 3145728 | tf_op jit(solution)/shard_map/all_to_all | solution.py:25
  123.3 0.2 copy.18
  123.5 1.9 select_reduce_fusion
  125.3 0.2 copy.19
  125.5 0.9 add_convert_fusion
  126.4 2.1 fusion.15
  128.5 0.2 copy.20
  128.7 4.1 %fusion.own = f32[96,1024]{1,0:T(8,128)S(1)} fusion(bf16[3072,1024]{1,0:T(8,128)(2,1)} %all-gather.2.cloned.1.call-done.child, bf16[768,1,3072]{2,0,1:T(8,128)(2,1)} %param.6, s32[]{:T(128)S(6)} %select_n.14), kind=kOutput, calls=%fused_computation.6 | convolution fusion | flops 603979776 | bytes 7274500 | tf_op jit(solution)/shard_map/dot_general | solution.py:17
  132.8 10.3 %all-to-all-done.1.got = bf16[8,96,1024]{2,1,0:T(8,128)(2,1)} async-done(((bf16[8,96,1024]{2,1,0:T(8,128)(2,1)}), bf16[8,96,1024]{2,1,0:T(8,128)(2,1)}, u32[]{:S(2)}, u32[]{:S(2)}) %all-to-all-start.1) | async-done | bytes 1572896 | tf_op jit(solution)/shard_map/all_to_all | solution.py:25
  143.1 2.6 %shard_map.103 = (f32[96,1024]{1,0:T(8,128)}, bf16[32,3,32,96]{3,2,1,0:T(8,128)(2,1)S(1)}) custom-call(s32[4]{0:T(128)S(1)} %pad_add_fusion.where, bf16[8,96,1024]{2,1,0:T(8,128)(2,1)} %all-to-all-done.1.got, f32[96,1024]{1,0:T(8,128)S(1)} %fusion.own, f32[96,1024]{1,0:T(8,128)S(1)} %get-tuple-element.59.shifted, bf16[1024,96]{1,0:T(8,128)(2,1)S(1)} %bitcast.27, ...), custom_call_target="tpu_custom_call" | custom-call | flops 884736 | bytes 3932160 | tf_op jit(solution)/shard_map/pallas_call | solution.py:324
  145.8 0.9 copy-done.12
  146.7 7.2 %all-to-all-start.2 = ((bf16[32,3,32,96]{3,2,1,0:T(8,128)(2,1)}), bf16[32,3,32,96]{3,2,1,0:T(8,128)(2,1)S(1)}, u32[]{:S(2)}, u32[]{:S(2)}) async-start(bf16[32,3,32,96]{3,2,1,0:T(8,128)(2,1)} %copy-done.12), calls=%async_computation.2 | async-start | bytes 1572864 | tf_op jit(solution)/shard_map/all_to_all | solution.py:25
  153.9 6.0 %shard_map.104.parent = bf16[3072,1024]{1,0:T(8,128)(2,1)} custom-call(s32[4]{0:T(128)} %copy-done.13, bf16[384,1024]{1,0:T(8,128)(2,1)} %copy-done.1, bf16[384,1024]{1,0:T(8,128)(2,1)} %copy-done.3, bf16[384,1024]{1,0:T(8,128)(2,1)} %copy-done.2, bf16[192,1024]{1,0:T(8,128)(2,1)} %copy-done.5, bf16[192,1024]{1,0:T(8,128)(2,1)} %copy-done.4, ...), custom_call_target="tpu_custom_call" | custom-call | bytes 12582912 | tf_op jit(solution)/shard_map/pallas_call | solution.py:194
  159.9 17.1 %all-to-all-done.2.x = bf16[32,3,32,96]{3,2,1,0:T(8,128)(2,1)S(1)} async-done(((bf16[32,3,32,96]{3,2,1,0:T(8,128)(2,1)}), bf16[32,3,32,96]{3,2,1,0:T(8,128)(2,1)S(1)}, u32[]{:S(2)}, u32[]{:S(2)}) %all-to-all-start.2) | async-done | bytes 589856 | tf_op jit(solution)/shard_map/all_to_all | solution.py:25
  177.1 6.6 %shard_map.105 = (bf16[32,16,128]{2,1,0:T(8,128)(2,1)S(1)}, f32[2,32,1024]{2,1,0:T(8,128)S(1)}) custom-call(bf16[32,3,32,96]{3,2,1,0:T(8,128)(2,1)S(1)} %all-to-all-done.2.x, bf16[3072,1024]{1,0:T(8,128)(2,1)} %shard_map.104.parent, bf16[3072,1024]{1,0:T(8,128)(2,1)} %all-gather.2.cloned.1.call-done.child, bf16[1024,1024]{1,0:T(8,128)(2,1)} %cp.1), custom_call_target="tpu_custom_call" | custom-call | flops 1006632960 | bytes 12582912 | tf_op jit(solution)/shard_map/pallas_call | solution.py:262
  183.7 0.0 copy-start.16
  183.7 0.0 copy-start.17
  183.7 16.1 %all_to_all.25.t = bf16[32,16,128]{2,1,0:T(8,128)(2,1)S(1)} all-to-all(bf16[32,16,128]{2,1,0:T(8,128)(2,1)S(1)} %get-tuple-element.35), channel_id=1, replica_groups=mesh['x'=4,'zh'=4,'core'=2,'y'=4,'zl'=2] {'x','zh','core'}, dimensions={0} | all-to-all | bytes 262144 | tf_op jit(solution)/shard_map/all_to_all | solution.py:25
  199.9 1.2 shard_map.106
  201.1 3.5 %all-to-all-start.4 = ((f32[8,8,1536]{2,1,0:T(8,128)}), f32[8,8,1536]{2,1,0:T(8,128)S(1)}, u32[]{:S(2)}, u32[]{:S(2)}) async-start(f32[8,8,1536]{2,1,0:T(8,128)} %shard_map.106), calls=%async_computation.4 | async-start | bytes 786432 | tf_op jit(solution)/shard_map/all_to_all | solution.py:25
  204.5 0.9 copy.21
  205.5 7.4 %all-to-all-done.4 = f32[8,8,1536]{2,1,0:T(8,128)S(1)} async-done(((f32[8,8,1536]{2,1,0:T(8,128)}), f32[8,8,1536]{2,1,0:T(8,128)S(1)}, u32[]{:S(2)}, u32[]{:S(2)}) %all-to-all-start.4) | async-done | bytes 393248 | tf_op jit(solution)/shard_map/all_to_all | solution.py:25
  212.9 0.6 slice_add_fusion
  213.5 2.6 %convolution_subtract_fusion = f32[4,1024]{1,0:T(4,128)} fusion(bf16[1024,1024]{1,0:T(8,128)(2,1)} %cp.1, f32[8,1536]{1,0:T(8,128)S(1)} %reduce_sum.19, f32[4,1024]{1,0:T(4,128)S(1)} %get-tuple-element.60), kind=kOutput, calls=%fused_computation.3 | convolution fusion | flops 8396800 | bytes 2146304 | tf_op jit(solution)/shard_map/dot_general | solution.py:17
  (43 shorter events, 0.2 us)
Async XLA Ops:
  7.2 14.5 %copy-start = (bf16[1024,1024]{1,0:T(8,128)(2,1)S(1)}, bf16[1024,1024]{1,0:T(8,128)(2,1)}, u32[]{:S(2)}) copy-start(bf16[1024,1024]{1,0:T(8,128)(2,1)} %param.8) | copy-start | bytes 6291460
  7.2 90.9 %all-gather.2.cloned.1.call-start = ((), (), s32[]{:S(2)}) async-start(), calls=%async_computation.5 | async-start | bytes 6488064 | tf_op jit(solution)/shard_map/all_gather | solution.py:345
  7.9 20.1 %collective-permute-start.1 = (bf16[96,1024]{1,0:T(8,128)(2,1)}, bf16[96,1024]{1,0:T(8,128)(2,1)S(1)}, u32[]{:S(2)}, u32[]{:S(2)}) collective-permute-start(bf16[96,1024]{1,0:T(8,128)(2,1)} %param.7), channel_id=1, source_target_pairs={{0,16},{16,32},{32,48},{48,0},{1,17},{17,33},{33,49},{49,1},{2,18}... | collective-permute-start | bytes 589832 | tf_op jit(solution)/shard_map/ppermute | solution.py:30
  11.8 18.4 %collective-permute-start = (bf16[96,1024]{1,0:T(8,128)(2,1)}, bf16[96,1024]{1,0:T(8,128)(2,1)S(1)}, u32[]{:S(2)}, u32[]{:S(2)}) collective-permute-start(bf16[96,1024]{1,0:T(8,128)(2,1)} %param.7), channel_id=1, source_target_pairs={{0,48},{16,0},{32,16},{48,32},{1,49},{17,1},{33,17},{49,33},{2,50}... | collective-permute-start | bytes 589832 | tf_op jit(solution)/shard_map/ppermute | solution.py:30
  14.9 15.6 %collective-permute-start.2 = (bf16[96,1024]{1,0:T(8,128)(2,1)}, bf16[96,1024]{1,0:T(8,128)(2,1)S(1)}, u32[]{:S(2)}, u32[]{:S(2)}) collective-permute-start(bf16[96,1024]{1,0:T(8,128)(2,1)} %param.7), channel_id=1, source_target_pairs={{0,32},{16,48},{32,0},{48,16},{1,33},{17,49},{33,1},{49,17},{2,34}... | collective-permute-start | bytes 589832 | tf_op jit(solution)/shard_map/ppermute | solution.py:30
  19.3 39.8 %slice-start = ((s8[4718592]{0:T(1024)(128)(4,1)}), s8[4194304]{0:T(1024)(128)(4,1)S(1)}, s32[]{:S(2)}) async-start(s8[4718592]{0:T(1024)(128)(4,1)} %bitcast.23), calls=%async_computation.6 | async-start | bytes 8388608
  21.6 37.5 %slice-start.1 = ((s8[4718592]{0:T(1024)(128)(4,1)}), s8[524288]{0:T(1024)(128)(4,1)S(1)}, s32[]{:S(2)}) async-start(s8[4718592]{0:T(1024)(128)(4,1)} %bitcast.23), calls=%async_computation.7 | async-start | bytes 1048576
  25.7 4.8 %copy-start.15 = (bf16[96,1024]{1,0:T(8,128)(2,1)S(1)}, bf16[96,1024]{1,0:T(8,128)(2,1)}, u32[]{:S(2)}) copy-start(bf16[96,1024]{1,0:T(8,128)(2,1)} %param.7) | copy-start | bytes 589828
  30.5 40.4 %copy-start.1 = (bf16[384,1024]{1,0:T(8,128)(2,1)}, bf16[384,1024]{1,0:T(8,128)(2,1)S(1)}, u32[]{:S(2)}) copy-start(bf16[384,1024]{1,0:T(8,128)(2,1)S(1)} %pad_maximum_fusion.refs_0_) | copy-start | bytes 2359300
  30.6 5.2 %collective-permute-start.5 = (bf16[384,1024]{1,0:T(8,128)(2,1)S(1)}, bf16[384,1024]{1,0:T(8,128)(2,1)S(1)}, u32[]{:S(2)}, u32[]{:S(2)}) collective-permute-start(bf16[384,1024]{1,0:T(8,128)(2,1)S(1)} %pad_maximum_fusion.refs_0_), channel_id=1, source_target_pairs={{0,8},{8,0},{1,9},{9,1},{2,10},{10,2},{3,11},{11,3},{4,12},{12,4},... | collective-permute-start | bytes 2359304 | tf_op jit(solution)/shard_map/ppermute | solution.py:30
  33.1 22.1 %collective-permute-start.4 = (bf16[384,1024]{1,0:T(8,128)(2,1)S(1)}, bf16[384,1024]{1,0:T(8,128)(2,1)S(1)}, u32[]{:S(2)}, u32[]{:S(2)}) collective-permute-start(bf16[384,1024]{1,0:T(8,128)(2,1)S(1)} %pad_maximum_fusion.refs_0_), channel_id=1, source_target_pairs={{0,64},{64,128},{128,192},{192,0},{1,65},{65,129},{129,193},{193,1... | collective-permute-start | bytes 2359304 | tf_op jit(solution)/shard_map/ppermute | solution.py:30
  34.3 20.9 %collective-permute-start.3 = (bf16[384,1024]{1,0:T(8,128)(2,1)S(1)}, bf16[384,1024]{1,0:T(8,128)(2,1)S(1)}, u32[]{:S(2)}, u32[]{:S(2)}) collective-permute-start(bf16[384,1024]{1,0:T(8,128)(2,1)S(1)} %pad_maximum_fusion.refs_0_), channel_id=1, source_target_pairs={{0,192},{64,0},{128,64},{192,128},{1,193},{65,1},{129,65},{193,129... | collective-permute-start | bytes 2359304 | tf_op jit(solution)/shard_map/ppermute | solution.py:30
  35.7 35.2 %copy-start.9 = (bf16[384,1024]{1,0:T(8,128)(2,1)}, bf16[384,1024]{1,0:T(8,128)(2,1)S(1)}, u32[]{:S(2)}) copy-start(bf16[384,1024]{1,0:T(8,128)(2,1)S(1)} %collective-permute-done.5.refs_3_.refs_5_) | copy-start | bytes 2359300
  55.2 15.8 %copy-start.2 = (bf16[384,1024]{1,0:T(8,128)(2,1)}, bf16[384,1024]{1,0:T(8,128)(2,1)S(1)}, u32[]{:S(2)}) copy-start(bf16[384,1024]{1,0:T(8,128)(2,1)S(1)} %collective-permute-done.4.refs_2_) | copy-start | bytes 2359300
  55.2 15.8 %copy-start.3 = (bf16[384,1024]{1,0:T(8,128)(2,1)}, bf16[384,1024]{1,0:T(8,128)(2,1)S(1)}, u32[]{:S(2)}) copy-start(bf16[384,1024]{1,0:T(8,128)(2,1)S(1)} %collective-permute-done.3.refs_1_) | copy-start | bytes 2359300
  55.2 3.9 %collective-permute-start.8 = (bf16[384,1024]{1,0:T(8,128)(2,1)S(1)}, bf16[384,1024]{1,0:T(8,128)(2,1)S(1)}, u32[]{:S(2)}, u32[]{:S(2)}) collective-permute-start(bf16[384,1024]{1,0:T(8,128)(2,1)S(1)} %collective-permute-done.3.refs_1_), channel_id=1, source_target_pairs={{0,8},{8,0},{1,9},{9,1},{2,10},{10,2},{3,11},{11,3},{4,12},{12,4},... | collective-permute-start | bytes 2359304 | tf_op jit(solution)/shard_map/ppermute | solution.py:30
  56.0 3.0 %collective-permute-start.9 = (bf16[384,1024]{1,0:T(8,128)(2,1)S(1)}, bf16[384,1024]{1,0:T(8,128)(2,1)S(1)}, u32[]{:S(2)}, u32[]{:S(2)}) collective-permute-start(bf16[384,1024]{1,0:T(8,128)(2,1)S(1)} %collective-permute-done.4.refs_2_), channel_id=1, source_target_pairs={{0,8},{8,0},{1,9},{9,1},{2,10},{10,2},{3,11},{11,3},{4,12},{12,4},... | collective-permute-start | bytes 2359304 | tf_op jit(solution)/shard_map/ppermute | solution.py:30
  56.2 17.5 %collective-permute-start.7 = (bf16[192,1024]{1,0:T(8,128)(2,1)S(1)}, bf16[192,1024]{1,0:T(8,128)(2,1)S(1)}, u32[]{:S(2)}, u32[]{:S(2)}) collective-permute-start(bf16[192,1024]{1,0:T(8,128)(2,1)S(1)} %slice.19), channel_id=1, source_target_pairs={{0,64},{64,128},{128,192},{192,0},{1,65},{65,129},{129,193},{193,1... | collective-permute-start | bytes 1179656 | tf_op jit(solution)/shard_map/ppermute | solution.py:30
  56.9 16.7 %collective-permute-start.6 = (bf16[192,1024]{1,0:T(8,128)(2,1)S(1)}, bf16[192,1024]{1,0:T(8,128)(2,1)S(1)}, u32[]{:S(2)}, u32[]{:S(2)}) collective-permute-start(bf16[192,1024]{1,0:T(8,128)(2,1)S(1)} %slice.18), channel_id=1, source_target_pairs={{0,192},{64,0},{128,64},{192,128},{1,193},{65,1},{129,65},{193,129... | collective-permute-start | bytes 1179656 | tf_op jit(solution)/shard_map/ppermute | solution.py:30
  59.0 84.1 %copy-start.13 = (s32[4]{0:T(128)}, s32[4]{0:T(128)S(1)}, u32[]{:S(2)}) copy-start(s32[4]{0:T(128)S(1)} %pad_add_fusion.where) | copy-start | bytes 52
  59.0 11.9 %copy-start.10 = (bf16[384,1024]{1,0:T(8,128)(2,1)}, bf16[384,1024]{1,0:T(8,128)(2,1)S(1)}, u32[]{:S(2)}) copy-start(bf16[384,1024]{1,0:T(8,128)(2,1)S(1)} %collective-permute-done.8.refs_4_.refs_6_) | copy-start | bytes 2359300
  59.1 11.9 %copy-start.11 = (bf16[384,1024]{1,0:T(8,128)(2,1)}, bf16[384,1024]{1,0:T(8,128)(2,1)S(1)}, u32[]{:S(2)}) copy-start(bf16[384,1024]{1,0:T(8,128)(2,1)S(1)} %collective-permute-done.9.refs_5_.refs_7_) | copy-start | bytes 2359300
  73.7 8.1 %copy-start.4 = (bf16[192,1024]{1,0:T(8,128)(2,1)}, bf16[192,1024]{1,0:T(8,128)(2,1)S(1)}, u32[]{:S(2)}) copy-start(bf16[192,1024]{1,0:T(8,128)(2,1)S(1)} %collective-permute-done.7.refs_1_.refs_4_) | copy-start | bytes 1179652
  73.7 8.1 %copy-start.5 = (bf16[192,1024]{1,0:T(8,128)(2,1)}, bf16[192,1024]{1,0:T(8,128)(2,1)S(1)}, u32[]{:S(2)}) copy-start(bf16[192,1024]{1,0:T(8,128)(2,1)S(1)} %collective-permute-done.6.refs_0_.refs_3_) | copy-start | bytes 1179652
  73.7 2.6 %collective-permute-start.10 = (bf16[192,1024]{1,0:T(8,128)(2,1)S(1)}, bf16[192,1024]{1,0:T(8,128)(2,1)S(1)}, u32[]{:S(2)}, u32[]{:S(2)}) collective-permute-start(bf16[192,1024]{1,0:T(8,128)(2,1)S(1)} %collective-permute-done.6.refs_0_.refs_3_), channel_id=1, source_target_pairs={{0,8},{8,0},{1,9},{9,1},{2,10},{10,2},{3,11},{11,3},{4,12},{12,4},... | collective-permute-start | bytes 1179656 | tf_op jit(solution)/shard_map/ppermute | solution.py:30
  74.9 1.9 collective-permute-start.11
  76.3 5.5 %copy-start.6 = (bf16[192,1024]{1,0:T(8,128)(2,1)}, bf16[192,1024]{1,0:T(8,128)(2,1)S(1)}, u32[]{:S(2)}) copy-start(bf16[192,1024]{1,0:T(8,128)(2,1)S(1)} %collective-permute-done.10.refs_2_.refs_8_) | copy-start | bytes 1179652
  76.8 5.0 %copy-start.7 = (bf16[192,1024]{1,0:T(8,128)(2,1)}, bf16[192,1024]{1,0:T(8,128)(2,1)S(1)}, u32[]{:S(2)}) copy-start(bf16[192,1024]{1,0:T(8,128)(2,1)S(1)} %collective-permute-done.11.refs_3_.refs_9_) | copy-start | bytes 1179652
  81.8 1.2 copy-start.8
  82.9 36.0 %all-to-all-start = ((bf16[8,96,1024]{2,1,0:T(8,128)(2,1)}), bf16[8,96,1024]{2,1,0:T(8,128)(2,1)}, u32[]{:S(2)}, u32[]{:S(2)}) async-start(bf16[8,96,1024]{2,1,0:T(8,128)(2,1)} %copy-done.8), calls=%async_computation | async-start | bytes 3145728 | tf_op jit(solution)/shard_map/all_to_all | solution.py:25
  118.9 24.2 %all-to-all-start.1 = ((bf16[8,96,1024]{2,1,0:T(8,128)(2,1)}), bf16[8,96,1024]{2,1,0:T(8,128)(2,1)}, u32[]{:S(2)}, u32[]{:S(2)}) async-start(bf16[8,96,1024]{2,1,0:T(8,128)(2,1)} %bitcast.29), calls=%async_computation.1 | async-start | bytes 3145728 | tf_op jit(solution)/shard_map/all_to_all | solution.py:25
  145.8 0.9 copy-start.12
  146.7 30.4 %all-to-all-start.2 = ((bf16[32,3,32,96]{3,2,1,0:T(8,128)(2,1)}), bf16[32,3,32,96]{3,2,1,0:T(8,128)(2,1)S(1)}, u32[]{:S(2)}, u32[]{:S(2)}) async-start(bf16[32,3,32,96]{3,2,1,0:T(8,128)(2,1)} %copy-done.12), calls=%async_computation.2 | async-start | bytes 1572864 | tf_op jit(solution)/shard_map/all_to_all | solution.py:25
  183.7 20.9 %copy-start.14 = (f32[96,1024]{0,1:T(8,128)S(1)}, f32[96,1024]{0,1:T(8,128)}, u32[]{:S(2)}) copy-start(f32[96,1024]{0,1:T(8,128)} %get-tuple-element.55) | copy-start | bytes 1179652
  183.7 29.2 %copy-start.16 = (f32[4,1024]{1,0:T(4,128)S(1)}, f32[4,1024]{1,0:T(4,128)}, u32[]{:S(2)}) copy-start(f32[4,1024]{1,0:T(4,128)} %convolution_add_fusion) | copy-start | bytes 49156
  183.7 29.2 %copy-start.17 = (f32[4,1024]{1,0:T(4,128)S(1)}, f32[4,1024]{1,0:T(4,128)}, u32[]{:S(2)}) copy-start(f32[4,1024]{1,0:T(4,128)} %fusion.5) | copy-start | bytes 49156
  201.1 11.8 %all-to-all-start.4 = ((f32[8,8,1536]{2,1,0:T(8,128)}), f32[8,8,1536]{2,1,0:T(8,128)S(1)}, u32[]{:S(2)}, u32[]{:S(2)}) async-start(f32[8,8,1536]{2,1,0:T(8,128)} %shard_map.106), calls=%async_computation.4 | async-start | bytes 786432 | tf_op jit(solution)/shard_map/all_to_all | solution.py:25
  213.5 2.6 %copy-start.18 = (f32[4,1024]{1,0:T(4,128)}, f32[4,1024]{1,0:T(4,128)S(1)}, u32[]{:S(2)}) copy-start(f32[4,1024]{1,0:T(4,128)S(1)} %get-tuple-element.60) | copy-start | bytes 49156
Sparse Core Ops, SparseCore 0:
  10.6 75.1 all-gather.1

commit v12 on v11

--- a/solution.py
+++ b/solution.py
@@ -329,7 +329,7 @@
             jax.ShapeDtypeStruct((rows, w), F32),
             jax.ShapeDtypeStruct((nr, 3, w // nr, rows), BF),
         ],
-        compiler_params=pltpu.CompilerParams(vmem_limit_bytes=16 << 20),
+        compiler_params=pltpu.CompilerParams(vmem_limit_bytes=54 << 20),
         cost_estimate=pl.CostEstimate(flops=9 * rows * w, transcendentals=0, bytes_accessed=40 * rows * w),
     )(where, got, own, shifted, ut, st)
 

time: 224 us -> 223 us (level)
  waiting for transfers between devices: 73.3 us -> 70.4 us
    all_to_all x4, waiting for transfers between devices: 46.2 us -> 42.1 us  [exchange(): return lax.all_to_all(a, axes, 0, 0, tiled=True)]
  transfers between devices with their start and end apart: 17 -> 17, of which waited for: 10 -> 10; matrix products, arithmetic and copies ran while one was open for 13% -> 14% of each run, Pallas kernels for 10% -> 10%
where the time goes in v12:
time: 223 us; the launch traced here: 222 us
  waiting for transfers between devices  70.4 us (32%)
  starting transfers between devices  51.7 us (23%)
  Pallas kernels  33.7 us (15%)
  matrix products  27.4 us (12%)
  blocking collectives  16 us (7%)
  between operations  14.3 us (6%)
  local copies, waits for them, and re-layouts  5.09 us (2%)
  other arithmetic  3.79 us (2%)
    all_to_all x4, waiting for transfers between devices, exchange(): return lax.all_to_all(a, axes, 0, 0, tiled=True)  42.1 us
    all_to_all x4, starting transfers between devices, exchange(): return lax.all_to_all(a, axes, 0, 0, tiled=True)  30 us
    ppermute x12, waiting for transfers between devices, shift(): return lax.ppermute(a, axis, [(i, (i + by) % n) for i in range(n)])  27.6 us
    dot_general x8, matrix products, dot(): lax.dot_general(a, b, (((ca,), (cb,)), ((), ())), preferred_element_type=...  27.4 us
    ppermute x12, starting transfers between devices, shift(): return lax.ppermute(a, axis, [(i, (i + by) % n) for i in range(n)])  21.6 us
    all_to_all x1, blocking collectives, exchange(): return lax.all_to_all(a, axes, 0, 0, tiled=True)  16 us
    pallas_call x1, Pallas kernels, near_product(): pl.pallas_call(near_kernel, grid_spec=pltpu.PrefetchScalarGridSpec(num_sc...  11.8 us
    pallas_call x1, Pallas kernels, slices(): pl.pallas_call(slices_kernel, in_specs=[vm, any_, any_, any_], out_specs=...  6.58 us
  transfers between devices with their start and end apart: 17, of which 10 were waited for; matrix products, arithmetic and copies ran while one was open for 14% of the time, Pallas kernels for 10%

profile of v12, /device:TPU:1, one launch (start us, length us, event | category | flops | bytes accessed | tf_op | source)
XLA Modules:
  0.0 222.4 jit_solution(16071369667893308468)
XLA Ops:
  7.2 0.0 copy-start
  7.2 0.0 all-gather.2.cloned.1.call-start
  7.2 0.7 all-gather.2.cloned.1.call-update
  7.9 3.9 %collective-permute-start.1 = (bf16[96,1024]{1,0:T(8,128)(2,1)}, bf16[96,1024]{1,0:T(8,128)(2,1)S(1)}, u32[]{:S(2)}, u32[]{:S(2)}) collective-permute-start(bf16[96,1024]{1,0:T(8,128)(2,1)} %param.7), channel_id=1, source_target_pairs={{0,16},{16,32},{32,48},{48,0},{1,17},{17,33},{33,49},{49,1},{2,18}... | collective-permute-start | bytes 589832 | tf_op jit(solution)/shard_map/ppermute | solution.py:30
  11.8 3.1 %collective-permute-start = (bf16[96,1024]{1,0:T(8,128)(2,1)}, bf16[96,1024]{1,0:T(8,128)(2,1)S(1)}, u32[]{:S(2)}, u32[]{:S(2)}) collective-permute-start(bf16[96,1024]{1,0:T(8,128)(2,1)} %param.7), channel_id=1, source_target_pairs={{0,48},{16,0},{32,16},{48,32},{1,49},{17,1},{33,17},{49,33},{2,50}... | collective-permute-start | bytes 589832 | tf_op jit(solution)/shard_map/ppermute | solution.py:30
  14.9 4.4 %collective-permute-start.2 = (bf16[96,1024]{1,0:T(8,128)(2,1)}, bf16[96,1024]{1,0:T(8,128)(2,1)S(1)}, u32[]{:S(2)}, u32[]{:S(2)}) collective-permute-start(bf16[96,1024]{1,0:T(8,128)(2,1)} %param.7), channel_id=1, source_target_pairs={{0,32},{16,48},{32,0},{48,16},{1,33},{17,49},{33,1},{49,17},{2,34}... | collective-permute-start | bytes 589832 | tf_op jit(solution)/shard_map/ppermute | solution.py:30
  19.3 2.3 %fusion.3 = f32[4,1024]{1,0:T(4,128)S(1)} fusion(bf16[1024,1024]{1,0:T(8,128)(2,1)} %param.11, s32[]{:T(128)S(6)} %select_n.12), kind=kOutput, calls=%fused_computation.9 | convolution fusion | flops 8388608 | bytes 2375684 | tf_op jit(solution)/shard_map/dot_general | solution.py:17
  21.6 4.0 %convolution_convert_fusion = bf16[1024,1024]{0,1:T(8,128)(2,1)S(1)} fusion(bf16[1024,1024]{1,0:T(8,128)(2,1)S(1)} %copy-done, bf16[1024,1024]{1,0:T(8,128)(2,1)} %cp.1), kind=kOutput, calls=%fused_computation.1 | convolution fusion | flops 2148532224 | bytes 6291456 | tf_op jit(solution)/shard_map/dot_general | solution.py:17
  25.7 0.0 copy-start.15
  25.7 0.6 convolution_add_fusion
  26.3 0.5 fusion.5
  26.8 0.0 collective-permute-done.1
  26.8 3.3 %collective-permute-done = bf16[96,1024]{1,0:T(8,128)(2,1)S(1)} collective-permute-done((bf16[96,1024]{1,0:T(8,128)(2,1)}, bf16[96,1024]{1,0:T(8,128)(2,1)S(1)}, u32[]{:S(2)}, u32[]{:S(2)}) %collective-permute-start) | collective-permute-done | bytes 196640 | tf_op jit(solution)/shard_map/ppermute | solution.py:30
  30.2 0.3 collective-permute-done.2
  30.5 0.0 copy-done.15
  30.5 0.1 pad_maximum_fusion.refs_0_
  30.5 0.0 copy-start.1
  30.6 2.5 %collective-permute-start.5 = (bf16[384,1024]{1,0:T(8,128)(2,1)S(1)}, bf16[384,1024]{1,0:T(8,128)(2,1)S(1)}, u32[]{:S(2)}, u32[]{:S(2)}) collective-permute-start(bf16[384,1024]{1,0:T(8,128)(2,1)S(1)} %pad_maximum_fusion.refs_0_), channel_id=1, source_target_pairs={{0,8},{8,0},{1,9},{9,1},{2,10},{10,2},{3,11},{11,3},{4,12},{12,4},... | collective-permute-start | bytes 2359304 | tf_op jit(solution)/shard_map/ppermute | solution.py:30
  33.1 1.2 collective-permute-start.4
  34.3 1.5 collective-permute-start.3
  35.7 0.0 collective-permute-done.5.refs_3_.refs_5_
  35.8 19.4 %collective-permute-done.4.refs_2_ = bf16[384,1024]{1,0:T(8,128)(2,1)S(1)} collective-permute-done((bf16[384,1024]{1,0:T(8,128)(2,1)S(1)}, bf16[384,1024]{1,0:T(8,128)(2,1)S(1)}, u32[]{:S(2)}, u32[]{:S(2)}) %collective-permute-start.4) | collective-permute-done | bytes 786464 | tf_op jit(solution)/shard_map/ppermute | solution.py:30
  55.2 0.0 collective-permute-done.3.refs_1_
  55.2 0.9 collective-permute-start.8
  56.0 0.1 collective-permute-start.9
  56.2 0.7 collective-permute-start.7
  56.9 2.0 collective-permute-start.6
  59.0 0.1 pad_add_fusion.where
  59.0 0.0 collective-permute-done.8.refs_4_.refs_6_
  59.0 0.0 collective-permute-done.9.refs_5_.refs_7_
  59.1 11.8 %shard_map.101.refs_4_ = f32[768,1024]{1,0:T(8,128)S(1)} custom-call(s32[4]{0:T(128)S(1)} %pad_add_fusion.where, bf16[384,1024]{1,0:T(8,128)(2,1)S(1)} %pad_maximum_fusion.refs_0_, bf16[384,1024]{1,0:T(8,128)(2,1)S(1)} %collective-permute-done.3.refs_1_, bf16[384,1024]{1,0:T(8,128)(2,1)S(1)} %collective-permute-done.4.refs_2_, ...), custom_call_target="tpu_custom_call" | custom-call | flops 3623878656 | bytes 11403264 | tf_op jit(solution)/shard_map/pallas_call | solution.py:118
  71.0 2.7 %collective-permute-done.7.refs_1_.refs_4_ = bf16[192,1024]{1,0:T(8,128)(2,1)S(1)} collective-permute-done((bf16[192,1024]{1,0:T(8,128)(2,1)S(1)}, bf16[192,1024]{1,0:T(8,128)(2,1)S(1)}, u32[]{:S(2)}, u32[]{:S(2)}) %collective-permute-start.7) | collective-permute-done | bytes 393248 | tf_op jit(solution)/shard_map/ppermute | solution.py:30
  73.7 0.0 collective-permute-done.6.refs_0_.refs_3_
  73.7 1.2 collective-permute-start.10
  74.9 0.1 collective-permute-start.11
  75.0 1.2 collective-permute-done.10.refs_2_.refs_8_
  76.3 0.6 collective-permute-done.11.refs_3_.refs_9_
  76.8 4.9 %shard_map.102 = (bf16[8,96,1024]{2,1,0:T(8,128)(2,1)S(1)}, f32[96,1024]{1,0:T(8,128)S(1)}) custom-call(s32[4]{0:T(128)S(1)} %pad_add_fusion.where, bf16[192,1024]{1,0:T(8,128)(2,1)S(1)} %collective-permute-done.6.refs_0_.refs_3_, bf16[192,1024]{1,0:T(8,128)(2,1)S(1)} %collective-permute-done.7.refs_1_.refs_4_, ...), custom_call_target="tpu_custom_call" | custom-call | flops 1207959552 | bytes 7471104 | tf_op jit(solution)/shard_map/pallas_call | solution.py:148
  81.8 1.2 copy-done.8
  83.0 15.1 %all-to-all-start = ((bf16[8,96,1024]{2,1,0:T(8,128)(2,1)}), bf16[8,96,1024]{2,1,0:T(8,128)(2,1)}, u32[]{:S(2)}, u32[]{:S(2)}) async-start(bf16[8,96,1024]{2,1,0:T(8,128)(2,1)} %copy-done.8), calls=%async_computation | async-start | bytes 3145728 | tf_op jit(solution)/shard_map/all_to_all | solution.py:25
  98.1 0.0 all-gather.2.cloned.1.call-done.child
  98.1 9.5 %convolution_convert_fusion.1 = bf16[768,1024]{1,0:T(8,128)(2,1)} fusion(bf16[3072,1024]{1,0:T(8,128)(2,1)} %all-gather.2.cloned.1.call-done.child, bf16[768,1,3072]{2,0,1:T(8,128)(2,1)} %param.6), kind=kOutput, calls=%fused_computation.2 | convolution fusion | flops 4832624640 | bytes 12582912 | tf_op jit(solution)/shard_map/dot_general | solution.py:17
  107.6 11.4 %all-to-all-done = bf16[8,96,1024]{2,1,0:T(8,128)(2,1)} async-done(((bf16[8,96,1024]{2,1,0:T(8,128)(2,1)}), bf16[8,96,1024]{2,1,0:T(8,128)(2,1)}, u32[]{:S(2)}, u32[]{:S(2)}) %all-to-all-start) | async-done | bytes 1572896 | tf_op jit(solution)/shard_map/all_to_all | solution.py:25
  118.9 4.3 %all-to-all-start.1 = ((bf16[8,96,1024]{2,1,0:T(8,128)(2,1)}), bf16[8,96,1024]{2,1,0:T(8,128)(2,1)}, u32[]{:S(2)}, u32[]{:S(2)}) async-start(bf16[8,96,1024]{2,1,0:T(8,128)(2,1)} %bitcast.28), calls=%async_computation.1 | async-start | bytes 3145728 | tf_op jit(solution)/shard_map/all_to_all | solution.py:25
  123.3 1.0 copy.18
  124.3 1.9 select_reduce_fusion
  126.2 1.0 copy.19
  127.2 1.1 add_convert_fusion
  128.3 2.9 %fusion.15 = (bf16[96,1024]{1,0:T(8,128)(2,1)S(1)}, f32[96,1024]{1,0:T(8,128)}) fusion(bf16[96,1024]{0,1:T(8,128)(2,1)S(1)} %get-tuple-element.54, bf16[1024,1024]{1,0:T(8,128)(2,1)} %cp.1), kind=kOutput, calls=%fused_computation.27 | convolution fusion | flops 201424896 | bytes 2883584 | tf_op jit(solution)/shard_map/dot_general | solution.py:17
  131.2 0.8 copy.20
  132.1 4.9 %fusion.own = f32[96,1024]{1,0:T(8,128)} fusion(bf16[3072,1024]{1,0:T(8,128)(2,1)} %all-gather.2.cloned.1.call-done.child, bf16[768,1,3072]{2,0,1:T(8,128)(2,1)} %param.6, s32[]{:T(128)S(6)} %select_n.14), kind=kOutput, calls=%fused_computation.6 | convolution fusion | flops 603979776 | bytes 7274500 | tf_op jit(solution)/shard_map/dot_general | solution.py:17
  136.9 6.2 %all-to-all-done.1.got = bf16[8,96,1024]{2,1,0:T(8,128)(2,1)} async-done(((bf16[8,96,1024]{2,1,0:T(8,128)(2,1)}), bf16[8,96,1024]{2,1,0:T(8,128)(2,1)}, u32[]{:S(2)}, u32[]{:S(2)}) %all-to-all-start.1) | async-done | bytes 1572896 | tf_op jit(solution)/shard_map/all_to_all | solution.py:25
  143.1 3.2 %shard_map.103 = (f32[96,1024]{1,0:T(8,128)}, bf16[32,3,32,96]{3,2,1,0:T(8,128)(2,1)}) custom-call(s32[4]{0:T(128)} %copy-done.12, bf16[8,96,1024]{2,1,0:T(8,128)(2,1)} %all-to-all-done.1.got, f32[96,1024]{1,0:T(8,128)} %fusion.own, f32[96,1024]{1,0:T(8,128)} %get-tuple-element.59.shifted, bf16[1024,96]{1,0:T(8,128)(2,1)} %bitcast.27, bf16[1024,96]{1,0:T(8,128)(2,1)} %bitcast.29), custom_call_target="tpu_custom_call" | custom-call | flops 884736 | bytes 3932160 | tf_op jit(solution)/shard_map/pallas_call | solution.py:324
  146.3 7.2 %all-to-all-start.2 = ((bf16[32,3,32,96]{3,2,1,0:T(8,128)(2,1)}), bf16[32,3,32,96]{3,2,1,0:T(8,128)(2,1)S(1)}, u32[]{:S(2)}, u32[]{:S(2)}) async-start(bf16[32,3,32,96]{3,2,1,0:T(8,128)(2,1)} %get-tuple-element.33), calls=%async_computation.2 | async-start | bytes 1572864 | tf_op jit(solution)/shard_map/all_to_all | solution.py:25
  153.5 6.0 %shard_map.104.parent = bf16[3072,1024]{1,0:T(8,128)(2,1)} custom-call(s32[4]{0:T(128)} %copy-done.12, bf16[384,1024]{1,0:T(8,128)(2,1)} %copy-done.1, bf16[384,1024]{1,0:T(8,128)(2,1)} %copy-done.3, bf16[384,1024]{1,0:T(8,128)(2,1)} %copy-done.2, bf16[192,1024]{1,0:T(8,128)(2,1)} %copy-done.5, bf16[192,1024]{1,0:T(8,128)(2,1)} %copy-done.4, ...), custom_call_target="tpu_custom_call" | custom-call | bytes 12582912 | tf_op jit(solution)/shard_map/pallas_call | solution.py:194
  159.5 17.1 %all-to-all-done.2.x = bf16[32,3,32,96]{3,2,1,0:T(8,128)(2,1)S(1)} async-done(((bf16[32,3,32,96]{3,2,1,0:T(8,128)(2,1)}), bf16[32,3,32,96]{3,2,1,0:T(8,128)(2,1)S(1)}, u32[]{:S(2)}, u32[]{:S(2)}) %all-to-all-start.2) | async-done | bytes 589856 | tf_op jit(solution)/shard_map/all_to_all | solution.py:25
  176.7 6.6 %shard_map.105 = (bf16[32,16,128]{2,1,0:T(8,128)(2,1)S(1)}, f32[2,32,1024]{2,1,0:T(8,128)S(1)}) custom-call(bf16[32,3,32,96]{3,2,1,0:T(8,128)(2,1)S(1)} %all-to-all-done.2.x, bf16[3072,1024]{1,0:T(8,128)(2,1)} %shard_map.104.parent, bf16[3072,1024]{1,0:T(8,128)(2,1)} %all-gather.2.cloned.1.call-done.child, bf16[1024,1024]{1,0:T(8,128)(2,1)} %cp.1), custom_call_target="tpu_custom_call" | custom-call | flops 1006632960 | bytes 12582912 | tf_op jit(solution)/shard_map/pallas_call | solution.py:262
  183.3 16.0 %all_to_all.25.t = bf16[32,16,128]{2,1,0:T(8,128)(2,1)S(1)} all-to-all(bf16[32,16,128]{2,1,0:T(8,128)(2,1)S(1)} %get-tuple-element.35), channel_id=1, replica_groups=mesh['x'=4,'zh'=4,'core'=2,'y'=4,'zl'=2] {'x','zh','core'}, dimensions={0} | all-to-all | bytes 262144 | tf_op jit(solution)/shard_map/all_to_all | solution.py:25
  199.3 1.2 shard_map.106
  200.5 3.5 %all-to-all-start.4 = ((f32[8,8,1536]{2,1,0:T(8,128)}), f32[8,8,1536]{2,1,0:T(8,128)S(1)}, u32[]{:S(2)}, u32[]{:S(2)}) async-start(f32[8,8,1536]{2,1,0:T(8,128)} %shard_map.106), calls=%async_computation.4 | async-start | bytes 786432 | tf_op jit(solution)/shard_map/all_to_all | solution.py:25
  203.9 0.9 copy.21
  204.9 7.4 %all-to-all-done.4 = f32[8,8,1536]{2,1,0:T(8,128)S(1)} async-done(((f32[8,8,1536]{2,1,0:T(8,128)}), f32[8,8,1536]{2,1,0:T(8,128)S(1)}, u32[]{:S(2)}, u32[]{:S(2)}) %all-to-all-start.4) | async-done | bytes 393248 | tf_op jit(solution)/shard_map/all_to_all | solution.py:25
  212.3 0.6 slice_add_fusion
  212.9 2.6 %convolution_subtract_fusion = f32[4,1024]{1,0:T(4,128)} fusion(bf16[1024,1024]{1,0:T(8,128)(2,1)} %cp.1, f32[8,1536]{1,0:T(8,128)S(1)} %reduce_sum.19, f32[4,1024]{1,0:T(4,128)S(1)} %get-tuple-element.60), kind=kOutput, calls=%fused_computation.3 | convolution fusion | flops 8396800 | bytes 2146304 | tf_op jit(solution)/shard_map/dot_general | solution.py:17
  (39 shorter events, 0.2 us)
Async XLA Ops:
  7.2 14.5 %copy-start = (bf16[1024,1024]{1,0:T(8,128)(2,1)S(1)}, bf16[1024,1024]{1,0:T(8,128)(2,1)}, u32[]{:S(2)}) copy-start(bf16[1024,1024]{1,0:T(8,128)(2,1)} %param.8) | copy-start | bytes 6291460
  7.2 90.9 %all-gather.2.cloned.1.call-start = ((), (), s32[]{:S(2)}) async-start(), calls=%async_computation.5 | async-start | bytes 6488064 | tf_op jit(solution)/shard_map/all_gather | solution.py:345
  7.9 18.9 %collective-permute-start.1 = (bf16[96,1024]{1,0:T(8,128)(2,1)}, bf16[96,1024]{1,0:T(8,128)(2,1)S(1)}, u32[]{:S(2)}, u32[]{:S(2)}) collective-permute-start(bf16[96,1024]{1,0:T(8,128)(2,1)} %param.7), channel_id=1, source_target_pairs={{0,16},{16,32},{32,48},{48,0},{1,17},{17,33},{33,49},{49,1},{2,18}... | collective-permute-start | bytes 589832 | tf_op jit(solution)/shard_map/ppermute | solution.py:30
  11.8 18.4 %collective-permute-start = (bf16[96,1024]{1,0:T(8,128)(2,1)}, bf16[96,1024]{1,0:T(8,128)(2,1)S(1)}, u32[]{:S(2)}, u32[]{:S(2)}) collective-permute-start(bf16[96,1024]{1,0:T(8,128)(2,1)} %param.7), channel_id=1, source_target_pairs={{0,48},{16,0},{32,16},{48,32},{1,49},{17,1},{33,17},{49,33},{2,50}... | collective-permute-start | bytes 589832 | tf_op jit(solution)/shard_map/ppermute | solution.py:30
  14.9 15.6 %collective-permute-start.2 = (bf16[96,1024]{1,0:T(8,128)(2,1)}, bf16[96,1024]{1,0:T(8,128)(2,1)S(1)}, u32[]{:S(2)}, u32[]{:S(2)}) collective-permute-start(bf16[96,1024]{1,0:T(8,128)(2,1)} %param.7), channel_id=1, source_target_pairs={{0,32},{16,48},{32,0},{48,16},{1,33},{17,49},{33,1},{49,17},{2,34}... | collective-permute-start | bytes 589832 | tf_op jit(solution)/shard_map/ppermute | solution.py:30
  19.3 39.8 %slice-start = ((s8[4718592]{0:T(1024)(128)(4,1)}), s8[4194304]{0:T(1024)(128)(4,1)S(1)}, s32[]{:S(2)}) async-start(s8[4718592]{0:T(1024)(128)(4,1)} %bitcast.23), calls=%async_computation.6 | async-start | bytes 8388608
  21.6 37.5 %slice-start.1 = ((s8[4718592]{0:T(1024)(128)(4,1)}), s8[524288]{0:T(1024)(128)(4,1)S(1)}, s32[]{:S(2)}) async-start(s8[4718592]{0:T(1024)(128)(4,1)} %bitcast.23), calls=%async_computation.7 | async-start | bytes 1048576
  25.7 4.8 %copy-start.15 = (bf16[96,1024]{1,0:T(8,128)(2,1)S(1)}, bf16[96,1024]{1,0:T(8,128)(2,1)}, u32[]{:S(2)}) copy-start(bf16[96,1024]{1,0:T(8,128)(2,1)} %param.7) | copy-start | bytes 589828
  30.5 40.4 %copy-start.1 = (bf16[384,1024]{1,0:T(8,128)(2,1)}, bf16[384,1024]{1,0:T(8,128)(2,1)S(1)}, u32[]{:S(2)}) copy-start(bf16[384,1024]{1,0:T(8,128)(2,1)S(1)} %pad_maximum_fusion.refs_0_) | copy-start | bytes 2359300
  30.6 5.2 %collective-permute-start.5 = (bf16[384,1024]{1,0:T(8,128)(2,1)S(1)}, bf16[384,1024]{1,0:T(8,128)(2,1)S(1)}, u32[]{:S(2)}, u32[]{:S(2)}) collective-permute-start(bf16[384,1024]{1,0:T(8,128)(2,1)S(1)} %pad_maximum_fusion.refs_0_), channel_id=1, source_target_pairs={{0,8},{8,0},{1,9},{9,1},{2,10},{10,2},{3,11},{11,3},{4,12},{12,4},... | collective-permute-start | bytes 2359304 | tf_op jit(solution)/shard_map/ppermute | solution.py:30
  33.1 22.1 %collective-permute-start.4 = (bf16[384,1024]{1,0:T(8,128)(2,1)S(1)}, bf16[384,1024]{1,0:T(8,128)(2,1)S(1)}, u32[]{:S(2)}, u32[]{:S(2)}) collective-permute-start(bf16[384,1024]{1,0:T(8,128)(2,1)S(1)} %pad_maximum_fusion.refs_0_), channel_id=1, source_target_pairs={{0,64},{64,128},{128,192},{192,0},{1,65},{65,129},{129,193},{193,1... | collective-permute-start | bytes 2359304 | tf_op jit(solution)/shard_map/ppermute | solution.py:30
  34.3 20.9 %collective-permute-start.3 = (bf16[384,1024]{1,0:T(8,128)(2,1)S(1)}, bf16[384,1024]{1,0:T(8,128)(2,1)S(1)}, u32[]{:S(2)}, u32[]{:S(2)}) collective-permute-start(bf16[384,1024]{1,0:T(8,128)(2,1)S(1)} %pad_maximum_fusion.refs_0_), channel_id=1, source_target_pairs={{0,192},{64,0},{128,64},{192,128},{1,193},{65,1},{129,65},{193,129... | collective-permute-start | bytes 2359304 | tf_op jit(solution)/shard_map/ppermute | solution.py:30
  35.7 35.2 %copy-start.9 = (bf16[384,1024]{1,0:T(8,128)(2,1)}, bf16[384,1024]{1,0:T(8,128)(2,1)S(1)}, u32[]{:S(2)}) copy-start(bf16[384,1024]{1,0:T(8,128)(2,1)S(1)} %collective-permute-done.5.refs_3_.refs_5_) | copy-start | bytes 2359300
  55.2 15.8 %copy-start.2 = (bf16[384,1024]{1,0:T(8,128)(2,1)}, bf16[384,1024]{1,0:T(8,128)(2,1)S(1)}, u32[]{:S(2)}) copy-start(bf16[384,1024]{1,0:T(8,128)(2,1)S(1)} %collective-permute-done.4.refs_2_) | copy-start | bytes 2359300
  55.2 15.8 %copy-start.3 = (bf16[384,1024]{1,0:T(8,128)(2,1)}, bf16[384,1024]{1,0:T(8,128)(2,1)S(1)}, u32[]{:S(2)}) copy-start(bf16[384,1024]{1,0:T(8,128)(2,1)S(1)} %collective-permute-done.3.refs_1_) | copy-start | bytes 2359300
  55.2 3.9 %collective-permute-start.8 = (bf16[384,1024]{1,0:T(8,128)(2,1)S(1)}, bf16[384,1024]{1,0:T(8,128)(2,1)S(1)}, u32[]{:S(2)}, u32[]{:S(2)}) collective-permute-start(bf16[384,1024]{1,0:T(8,128)(2,1)S(1)} %collective-permute-done.3.refs_1_), channel_id=1, source_target_pairs={{0,8},{8,0},{1,9},{9,1},{2,10},{10,2},{3,11},{11,3},{4,12},{12,4},... | collective-permute-start | bytes 2359304 | tf_op jit(solution)/shard_map/ppermute | solution.py:30
  56.0 3.0 %collective-permute-start.9 = (bf16[384,1024]{1,0:T(8,128)(2,1)S(1)}, bf16[384,1024]{1,0:T(8,128)(2,1)S(1)}, u32[]{:S(2)}, u32[]{:S(2)}) collective-permute-start(bf16[384,1024]{1,0:T(8,128)(2,1)S(1)} %collective-permute-done.4.refs_2_), channel_id=1, source_target_pairs={{0,8},{8,0},{1,9},{9,1},{2,10},{10,2},{3,11},{11,3},{4,12},{12,4},... | collective-permute-start | bytes 2359304 | tf_op jit(solution)/shard_map/ppermute | solution.py:30
  56.2 17.5 %collective-permute-start.7 = (bf16[192,1024]{1,0:T(8,128)(2,1)S(1)}, bf16[192,1024]{1,0:T(8,128)(2,1)S(1)}, u32[]{:S(2)}, u32[]{:S(2)}) collective-permute-start(bf16[192,1024]{1,0:T(8,128)(2,1)S(1)} %slice.19), channel_id=1, source_target_pairs={{0,64},{64,128},{128,192},{192,0},{1,65},{65,129},{129,193},{193,1... | collective-permute-start | bytes 1179656 | tf_op jit(solution)/shard_map/ppermute | solution.py:30
  56.9 16.7 %collective-permute-start.6 = (bf16[192,1024]{1,0:T(8,128)(2,1)S(1)}, bf16[192,1024]{1,0:T(8,128)(2,1)S(1)}, u32[]{:S(2)}, u32[]{:S(2)}) collective-permute-start(bf16[192,1024]{1,0:T(8,128)(2,1)S(1)} %slice.18), channel_id=1, source_target_pairs={{0,192},{64,0},{128,64},{192,128},{1,193},{65,1},{129,65},{193,129... | collective-permute-start | bytes 1179656 | tf_op jit(solution)/shard_map/ppermute | solution.py:30
  59.0 17.8 %copy-start.12 = (s32[4]{0:T(128)}, s32[4]{0:T(128)S(1)}, u32[]{:S(2)}) copy-start(s32[4]{0:T(128)S(1)} %pad_add_fusion.where) | copy-start | bytes 52
  59.0 11.9 %copy-start.10 = (bf16[384,1024]{1,0:T(8,128)(2,1)}, bf16[384,1024]{1,0:T(8,128)(2,1)S(1)}, u32[]{:S(2)}) copy-start(bf16[384,1024]{1,0:T(8,128)(2,1)S(1)} %collective-permute-done.8.refs_4_.refs_6_) | copy-start | bytes 2359300
  59.1 11.9 %copy-start.11 = (bf16[384,1024]{1,0:T(8,128)(2,1)}, bf16[384,1024]{1,0:T(8,128)(2,1)S(1)}, u32[]{:S(2)}) copy-start(bf16[384,1024]{1,0:T(8,128)(2,1)S(1)} %collective-permute-done.9.refs_5_.refs_7_) | copy-start | bytes 2359300
  73.7 8.1 %copy-start.4 = (bf16[192,1024]{1,0:T(8,128)(2,1)}, bf16[192,1024]{1,0:T(8,128)(2,1)S(1)}, u32[]{:S(2)}) copy-start(bf16[192,1024]{1,0:T(8,128)(2,1)S(1)} %collective-permute-done.7.refs_1_.refs_4_) | copy-start | bytes 1179652
  73.7 8.1 %copy-start.5 = (bf16[192,1024]{1,0:T(8,128)(2,1)}, bf16[192,1024]{1,0:T(8,128)(2,1)S(1)}, u32[]{:S(2)}) copy-start(bf16[192,1024]{1,0:T(8,128)(2,1)S(1)} %collective-permute-done.6.refs_0_.refs_3_) | copy-start | bytes 1179652
  73.7 2.6 %collective-permute-start.10 = (bf16[192,1024]{1,0:T(8,128)(2,1)S(1)}, bf16[192,1024]{1,0:T(8,128)(2,1)S(1)}, u32[]{:S(2)}, u32[]{:S(2)}) collective-permute-start(bf16[192,1024]{1,0:T(8,128)(2,1)S(1)} %collective-permute-done.6.refs_0_.refs_3_), channel_id=1, source_target_pairs={{0,8},{8,0},{1,9},{9,1},{2,10},{10,2},{3,11},{11,3},{4,12},{12,4},... | collective-permute-start | bytes 1179656 | tf_op jit(solution)/shard_map/ppermute | solution.py:30
  74.9 1.9 collective-permute-start.11
  76.3 5.5 %copy-start.6 = (bf16[192,1024]{1,0:T(8,128)(2,1)}, bf16[192,1024]{1,0:T(8,128)(2,1)S(1)}, u32[]{:S(2)}) copy-start(bf16[192,1024]{1,0:T(8,128)(2,1)S(1)} %collective-permute-done.10.refs_2_.refs_8_) | copy-start | bytes 1179652
  76.8 5.0 %copy-start.7 = (bf16[192,1024]{1,0:T(8,128)(2,1)}, bf16[192,1024]{1,0:T(8,128)(2,1)S(1)}, u32[]{:S(2)}) copy-start(bf16[192,1024]{1,0:T(8,128)(2,1)S(1)} %collective-permute-done.11.refs_3_.refs_9_) | copy-start | bytes 1179652
  81.8 1.2 copy-start.8
  83.0 36.0 %all-to-all-start = ((bf16[8,96,1024]{2,1,0:T(8,128)(2,1)}), bf16[8,96,1024]{2,1,0:T(8,128)(2,1)}, u32[]{:S(2)}, u32[]{:S(2)}) async-start(bf16[8,96,1024]{2,1,0:T(8,128)(2,1)} %copy-done.8), calls=%async_computation | async-start | bytes 3145728 | tf_op jit(solution)/shard_map/all_to_all | solution.py:25
  118.9 24.2 %all-to-all-start.1 = ((bf16[8,96,1024]{2,1,0:T(8,128)(2,1)}), bf16[8,96,1024]{2,1,0:T(8,128)(2,1)}, u32[]{:S(2)}, u32[]{:S(2)}) async-start(bf16[8,96,1024]{2,1,0:T(8,128)(2,1)} %bitcast.28), calls=%async_computation.1 | async-start | bytes 3145728 | tf_op jit(solution)/shard_map/all_to_all | solution.py:25
  124.3 2.9 %copy-start.14 = (f32[96,1024]{0,1:T(8,128)S(1)}, f32[96,1024]{0,1:T(8,128)}, u32[]{:S(2)}) copy-start(f32[96,1024]{0,1:T(8,128)} %copy.18) | copy-start | bytes 1179652
  128.3 8.6 %copy-start.13 = (bf16[96,1024]{0,1:T(8,128)(2,1)}, bf16[96,1024]{0,1:T(8,128)(2,1)S(1)}, u32[]{:S(2)}) copy-start(bf16[96,1024]{0,1:T(8,128)(2,1)S(1)} %get-tuple-element.54) | copy-start | bytes 589828
  146.3 30.4 %all-to-all-start.2 = ((bf16[32,3,32,96]{3,2,1,0:T(8,128)(2,1)}), bf16[32,3,32,96]{3,2,1,0:T(8,128)(2,1)S(1)}, u32[]{:S(2)}, u32[]{:S(2)}) async-start(bf16[32,3,32,96]{3,2,1,0:T(8,128)(2,1)} %get-tuple-element.33), calls=%async_computation.2 | async-start | bytes 1572864 | tf_op jit(solution)/shard_map/all_to_all | solution.py:25
  200.5 11.8 %all-to-all-start.4 = ((f32[8,8,1536]{2,1,0:T(8,128)}), f32[8,8,1536]{2,1,0:T(8,128)S(1)}, u32[]{:S(2)}, u32[]{:S(2)}) async-start(f32[8,8,1536]{2,1,0:T(8,128)} %shard_map.106), calls=%async_computation.4 | async-start | bytes 786432 | tf_op jit(solution)/shard_map/all_to_all | solution.py:25
  212.9 2.6 %copy-start.16 = (f32[4,1024]{1,0:T(4,128)}, f32[4,1024]{1,0:T(4,128)S(1)}, u32[]{:S(2)}) copy-start(f32[4,1024]{1,0:T(4,128)S(1)} %get-tuple-element.60) | copy-start | bytes 49156
Sparse Core Ops, SparseCore 0:
  10.6 75.1 all-gather.1
